TPU v7x, 32 devices: a whole 2x2x4 slice. The times are simulated.
32 devices in a mesh: dp: 8 (over y, x, core), seq: 4 (over z).
Axes of the slice: x: 2, y: 2, z: 4, core: 2. Of those that a mesh axis runs over, the one named last changes fastest.
Arguments:
- layer_input: bfloat16 [8, 1024, 2048], P('dp', 'seq'), may hold values from -6 to 6
- segments: int32 [8, 1024], P('dp'), may hold values from 0 to 3, never falling along the last dimension, each value on 1 to 512 neighbouring positions
- w_query: bfloat16 [2048, 2048], P(('dp', 'seq')), may hold values from -0.125 to 0.125
- w_key: bfloat16 [2048, 2048], P(('dp', 'seq')), may hold values from -0.125 to 0.125
- w_value: bfloat16 [2048, 2048], P(('dp', 'seq')), may hold values from -0.125 to 0.125
- w_output: bfloat16 [2048, 2048], P(('dp', 'seq')), may hold values from -0.125 to 0.125
- w_gate: bfloat16 [2048, 8192], P(('dp', 'seq')), may hold values from -0.125 to 0.125
- w_up: bfloat16 [2048, 8192], P(('dp', 'seq')), may hold values from -0.125 to 0.125
- w_down: bfloat16 [8192, 2048], P(None, ('dp', 'seq')), may hold values from -0.0625 to 0.0625
- query_gain: float32 [2048], replicated, may hold values from 0.1 to 1.9
- key_gain: float32 [2048], replicated, may hold values from 0.1 to 1.9
- attn_gain: float32 [2048], replicated, may hold values from 0.1 to 1.9
- ff_gain: float32 [2048], replicated, may hold values from 0.1 to 1.9
- cotangent: bfloat16 [8, 1024, 2048], P('dp', 'seq'), may hold values from -6 to 6
Outputs:
- activation: bfloat16 [8, 1024, 2048], P('dp', 'seq')
- input_grad: bfloat16 [8, 1024, 2048], P('dp', 'seq')
- grad_query: float32 [2048, 2048], P(('dp', 'seq'))
- grad_key: float32 [2048, 2048], P(('dp', 'seq'))
- grad_value: float32 [2048, 2048], P(('dp', 'seq'))
- grad_output: float32 [2048, 2048], P(('dp', 'seq'))
- grad_gate: float32 [2048, 8192], P(('dp', 'seq'))
- grad_up: float32 [2048, 8192], P(('dp', 'seq'))
- grad_down: float32 [8192, 2048], P(None, ('dp', 'seq'))
- grad_query_gain: float32 [2048], P(('dp', 'seq'))
- grad_key_gain: float32 [2048], P(('dp', 'seq'))
- grad_attn_gain: float32 [2048], P(('dp', 'seq'))
- grad_ff_gain: float32 [2048], P(('dp', 'seq'))
Inputs may be any that keep to these rules, and one draw needn't show every extreme that they name: `segments`: segment numbers never fall along a row, and a document holds at most half of 1024 tokens.
All inputs are finite; a program needn't handle non-finite values.
Results may differ from a plain program's by a relative error of at most 0.017.
Values may be sent and summed in bfloat16 or wider, within the bound.
No kernel may reach another device: no remote copies, remote signals or barrier semaphores. Data moves between devices by JAX's collectives and lax.ppermute only.
A program may use at most 384 MiB of HBM per device.

v0:
```python
import jax
import jax.numpy as jnp
from jax import lax
from jax.sharding import PartitionSpec as P

HD = 128


EPSILON = 1e-06
ROPE_BASE = 500000.0
MASKED = -1e30


def rms_norm(values, gain_vec):
    factor = lax.rsqrt(jnp.mean(values * values, axis=-1, keepdims=True) + EPSILON)
    return values * factor * gain_vec


def rope_tables(positions):
    half_dim = HD // 2
    frequency = jnp.power(
        jnp.float32(ROPE_BASE), -jnp.arange(half_dim, dtype=jnp.float32) * (2.0 / HD)
    )
    angles = positions[:, None] * frequency[None, :]
    angles = jnp.concatenate([angles, angles], axis=-1)
    return (jnp.cos(angles), jnp.sin(angles))


def rotate(values, cosine_table, sine_table):
    shaped = values.reshape(values.shape[:-1] + (values.shape[-1] // HD, HD))
    first_half = shaped[..., : HD // 2]
    second = shaped[..., HD // 2 :]
    turned = jnp.concatenate([-second, first_half], axis=-1)
    rotated = shaped * cosine_table[:, None, :] + turned * sine_table[:, None, :]
    return rotated.reshape(values.shape)


def project(left, weight):
    return jnp.dot(left, weight, preferred_element_type=jnp.float32)


def back_project(grad_in, weight):
    return lax.dot_general(
        grad_in, weight, (((grad_in.ndim - 1,), (1,)), ((), ())), preferred_element_type=jnp.float32
    )


def rows_product(left, right):
    return lax.dot_general(
        left, right, (((0,), (0,)), ((), ())), preferred_element_type=jnp.float32
    )


def block_mask(segments, row_start, block_rows):
    seq_length = segments.shape[1]
    query_pos = row_start + jnp.arange(block_rows, dtype=jnp.int32)
    query_seg = lax.dynamic_slice_in_dim(segments, row_start, block_rows, 1)
    key_pos = jnp.arange(seq_length, dtype=jnp.int32)
    causal = key_pos[None, None, :] <= query_pos[None, :, None]
    return causal & (segments[:, None, :] == query_seg[:, :, None])


def block_scores(query_block, key_heads, segments, row_start, block_rows):
    score_scale = HD ** (-0.5)
    scores = (
        jnp.einsum("rqhd,rkhd->rhqk", query_block, key_heads, preferred_element_type=jnp.float32)
        * score_scale
    )
    allowed = block_mask(segments, row_start, block_rows)
    return jnp.where(allowed[:, None], scores, MASKED)


def attend(query_all, key_all, value_all, segments):
    row_count, seq_length, local_width = query_all.shape
    head_count = local_width // HD
    block_rows = min(512, seq_length)
    block_count = seq_length // block_rows
    query_split = query_all.reshape(row_count, block_count, block_rows, head_count, HD)
    key_heads = key_all.reshape(row_count, seq_length, head_count, HD)
    value_heads = value_all.reshape(row_count, seq_length, head_count, HD)

    def one_block(block_index):
        query_block = lax.dynamic_index_in_dim(query_split, block_index, 1, keepdims=False)
        scores = block_scores(
            query_block, key_heads, segments, block_index * block_rows, block_rows
        )
        top_score = jnp.max(scores, axis=-1, keepdims=True)
        exp_scores = jnp.exp(scores - top_score)
        row_total = jnp.sum(exp_scores, axis=-1, keepdims=True)
        probs_full = exp_scores / row_total
        log_total = top_score + jnp.log(row_total)
        mixed = jnp.einsum(
            "rhqk,rkhd->rqhd",
            probs_full.astype(jnp.bfloat16),
            value_heads,
            preferred_element_type=jnp.float32,
        )
        return (mixed.astype(jnp.bfloat16), log_total[..., 0])

    mixed_blocks, log_totals = lax.map(one_block, jnp.arange(block_count, dtype=jnp.int32))
    mixed_all = jnp.moveaxis(mixed_blocks, 0, 1).reshape(row_count, seq_length, local_width)
    return (mixed_all, log_totals)


def attend_back(query_all, key_all, value_all, grad_mixed, log_totals, segments):
    row_count, seq_length, local_width = query_all.shape
    head_count = local_width // HD
    block_rows = min(512, seq_length)
    block_count = seq_length // block_rows
    score_scale = HD ** (-0.5)
    query_split = query_all.reshape(row_count, block_count, block_rows, head_count, HD)
    grad_split = grad_mixed.reshape(row_count, block_count, block_rows, head_count, HD)
    key_heads = key_all.reshape(row_count, seq_length, head_count, HD)
    value_heads = value_all.reshape(row_count, seq_length, head_count, HD)

    def one_block(totals, step_item):
        block_index, log_total = step_item
        grad_keys, grad_values = totals
        query_block = lax.dynamic_index_in_dim(query_split, block_index, 1, keepdims=False)
        grad_block = lax.dynamic_index_in_dim(grad_split, block_index, 1, keepdims=False)
        scores = block_scores(
            query_block, key_heads, segments, block_index * block_rows, block_rows
        )
        probs_full = jnp.exp(scores - log_total[..., None])
        grad_probs = jnp.einsum(
            "rqhd,rkhd->rhqk", grad_block, value_heads, preferred_element_type=jnp.float32
        )
        grad_values = grad_values + jnp.einsum(
            "rhqk,rqhd->rkhd",
            probs_full.astype(jnp.bfloat16),
            grad_block,
            preferred_element_type=jnp.float32,
        )
        inner = jnp.sum(probs_full * grad_probs, axis=-1, keepdims=True)
        grad_scores = (probs_full * (grad_probs - inner)).astype(jnp.bfloat16)
        grad_query = (
            jnp.einsum(
                "rhqk,rkhd->rqhd", grad_scores, key_heads, preferred_element_type=jnp.float32
            )
            * score_scale
        )
        grad_keys = (
            grad_keys
            + jnp.einsum(
                "rhqk,rqhd->rkhd", grad_scores, query_block, preferred_element_type=jnp.float32
            )
            * score_scale
        )
        return ((grad_keys, grad_values), grad_query.astype(jnp.bfloat16))

    zeros_heads = jnp.zeros((row_count, seq_length, head_count, HD), jnp.float32)
    (grad_keys, grad_values), grad_queries = lax.scan(
        one_block,
        (zeros_heads, zeros_heads),
        (jnp.arange(block_count, dtype=jnp.int32), log_totals),
    )
    grad_queries = jnp.moveaxis(grad_queries, 0, 1).reshape(row_count, seq_length, local_width)
    grad_keys = grad_keys.reshape(row_count, seq_length, local_width).astype(jnp.bfloat16)
    grad_values = grad_values.reshape(row_count, seq_length, local_width).astype(jnp.bfloat16)
    return (grad_queries, grad_keys, grad_values)


def silu_mix(gate_in, up_in):
    return jax.nn.silu(gate_in) * up_in


def shards(
    layer_input,
    segments,
    w_query,
    w_key,
    w_value,
    w_output,
    w_gate,
    w_up,
    w_down,
    query_gain,
    key_gain,
    attn_gain,
    ff_gain,
    cotangent,
):
    row_count, local_len, model_width = layer_input.shape
    offset = lax.axis_index("seq") * local_len
    positions = (offset + jnp.arange(local_len, dtype=jnp.int32)).astype(jnp.float32)
    cosine_table, sine_table = rope_tables(positions)

    def front(values, gain_vec):
        return rotate(rms_norm(values, gain_vec), cosine_table, sine_table)

    wq_all, wk_all, wv_all, wo_all = (
        lax.all_gather(w_query, ("dp", "seq"), axis=0, tiled=True),
        lax.all_gather(w_key, ("dp", "seq"), axis=0, tiled=True),
        lax.all_gather(w_value, ("dp", "seq"), axis=0, tiled=True),
        lax.all_gather(w_output, ("dp", "seq"), axis=0, tiled=True),
    )
    q_proj = project(layer_input, wq_all)
    k_proj = project(layer_input, wk_all)
    v_proj = project(layer_input, wv_all)
    q_rot, query_back = jax.vjp(front, q_proj, query_gain)
    k_rot, key_back = jax.vjp(front, k_proj, key_gain)
    q_low = q_rot.astype(jnp.bfloat16)
    k_low = k_rot.astype(jnp.bfloat16)
    v_low = v_proj.astype(jnp.bfloat16)
    q_heads, k_heads, v_heads = (
        lax.all_to_all(q_low, "seq", split_axis=2, concat_axis=1, tiled=True),
        lax.all_to_all(k_low, "seq", split_axis=2, concat_axis=1, tiled=True),
        lax.all_to_all(v_low, "seq", split_axis=2, concat_axis=1, tiled=True),
    )
    mixed_heads, log_totals = attend(q_heads, k_heads, v_heads, segments)
    mixed_local = lax.all_to_all(mixed_heads, "seq", split_axis=1, concat_axis=2, tiled=True)
    attn_out = project(mixed_local, wo_all)
    attn_normed, attn_back = jax.vjp(rms_norm, attn_out, attn_gain)
    residual = layer_input.astype(jnp.float32) + attn_normed
    residual_low = residual.astype(jnp.bfloat16)
    grad_top = cotangent.astype(jnp.float32)
    gate_part, up_part, down_part = (
        lax.all_to_all(w_gate, "seq", split_axis=1, concat_axis=0, tiled=True),
        lax.all_to_all(w_up, "seq", split_axis=1, concat_axis=0, tiled=True),
        lax.all_to_all(w_down.T, "seq", split_axis=1, concat_axis=0, tiled=True),
    )
    wg_blk, wu_blk, wd_blk = (
        lax.all_gather(gate_part, "dp", axis=0, tiled=True),
        lax.all_gather(up_part, "dp", axis=0, tiled=True),
        lax.all_gather(down_part, "dp", axis=0, tiled=True),
    )
    resid_full, cot_full = (
        lax.all_gather(residual_low, "seq", axis=1, tiled=True),
        lax.all_gather(cotangent, "seq", axis=1, tiled=True),
    )
    gate_act = project(resid_full, wg_blk)
    up_act = project(resid_full, wu_blk)
    hidden_low = silu_mix(gate_act, up_act).astype(jnp.bfloat16)
    ff_full = lax.psum(back_project(hidden_low, wd_blk).astype(jnp.bfloat16), "seq").astype(
        jnp.float32
    )
    ff_own = lax.dynamic_slice_in_dim(ff_full, offset, local_len, 1)
    ff_normed, ff_back = jax.vjp(rms_norm, ff_own, ff_gain)
    activation = (residual + ff_normed).astype(jnp.bfloat16)
    _, grad_ffg = ff_back(grad_top)
    _, full_back = jax.vjp(rms_norm, ff_full, ff_gain)
    grad_ff32, _ = full_back(cot_full.astype(jnp.float32))
    grad_ff = grad_ff32.astype(jnp.bfloat16)
    grad_hidden = project(grad_ff, wd_blk)
    _, mix_back = jax.vjp(silu_mix, gate_act, up_act)
    grad_gate32, grad_up32 = mix_back(grad_hidden)
    grad_gate_low = grad_gate32.astype(jnp.bfloat16)
    grad_up_low = grad_up32.astype(jnp.bfloat16)
    partial_resid = back_project(grad_gate_low, wg_blk) + back_project(grad_up_low, wu_blk)
    grad_resid = grad_top + lax.psum_scatter(partial_resid, "seq", scatter_dimension=1, tiled=True)
    residual_flat = resid_full.reshape(-1, model_width)
    grad_ff_flat = grad_ff.reshape(-1, model_width)
    hidden_flat = hidden_low.reshape(-1, hidden_low.shape[-1])
    grad_gate_flat = grad_gate_low.reshape(-1, hidden_low.shape[-1])
    grad_up_flat = grad_up_low.reshape(-1, hidden_low.shape[-1])
    block_width = hidden_low.shape[-1]
    mlp_blocks = lax.psum_scatter(
        jnp.concatenate(
            [
                rows_product(residual_flat, grad_gate_flat),
                rows_product(residual_flat, grad_up_flat),
                rows_product(grad_ff_flat, hidden_flat),
            ],
            axis=1,
        ).astype(jnp.bfloat16),
        "dp",
        scatter_dimension=0,
        tiled=True,
    ).astype(jnp.float32)
    grad_gate, grad_up, grad_down_rows = (
        lax.all_to_all(
            mlp_blocks[:, :block_width].astype(jnp.bfloat16),
            "seq",
            split_axis=0,
            concat_axis=1,
            tiled=True,
        ).astype(jnp.float32),
        lax.all_to_all(
            mlp_blocks[:, block_width : 2 * block_width].astype(jnp.bfloat16),
            "seq",
            split_axis=0,
            concat_axis=1,
            tiled=True,
        ).astype(jnp.float32),
        lax.all_to_all(
            mlp_blocks[:, 2 * block_width :].astype(jnp.bfloat16),
            "seq",
            split_axis=0,
            concat_axis=1,
            tiled=True,
        ).astype(jnp.float32),
    )
    grad_down = grad_down_rows.T
    grad_attn32, grad_attng = attn_back(grad_resid)
    grad_attn = grad_attn32.astype(jnp.bfloat16)
    grad_mixed = back_project(grad_attn, wo_all).astype(jnp.bfloat16)
    grad_mixed_heads = lax.all_to_all(grad_mixed, "seq", split_axis=2, concat_axis=1, tiled=True)
    grad_qh, grad_kh, grad_vh = attend_back(
        q_heads, k_heads, v_heads, grad_mixed_heads, log_totals, segments
    )
    grad_q_rot, grad_k_rot, grad_value_low = (
        lax.all_to_all(grad_qh, "seq", split_axis=1, concat_axis=2, tiled=True),
        lax.all_to_all(grad_kh, "seq", split_axis=1, concat_axis=2, tiled=True),
        lax.all_to_all(grad_vh, "seq", split_axis=1, concat_axis=2, tiled=True),
    )
    grad_q32, grad_qg = query_back(grad_q_rot.astype(jnp.float32))
    grad_k32, grad_kg = key_back(grad_k_rot.astype(jnp.float32))
    grad_query_low = grad_q32.astype(jnp.bfloat16)
    grad_key_low = grad_k32.astype(jnp.bfloat16)
    input_grad = (
        grad_resid
        + back_project(grad_query_low, wq_all)
        + back_project(grad_key_low, wk_all)
        + back_project(grad_value_low, wv_all)
    ).astype(jnp.bfloat16)
    input_flat = layer_input.reshape(-1, model_width)
    mixed_flat = mixed_local.reshape(-1, model_width)
    grad_query_flat = grad_query_low.reshape(-1, model_width)
    grad_key_flat = grad_key_low.reshape(-1, model_width)
    grad_value_flat = grad_value_low.reshape(-1, model_width)
    grad_attn_flat = grad_attn.reshape(-1, model_width)
    attn_part = lax.psum_scatter(
        jnp.concatenate(
            [
                rows_product(input_flat, grad_query_flat),
                rows_product(input_flat, grad_key_flat),
                rows_product(input_flat, grad_value_flat),
                rows_product(mixed_flat, grad_attn_flat),
            ],
            axis=1,
        ),
        ("dp", "seq"),
        scatter_dimension=0,
        tiled=True,
    )
    gain_stack = jnp.stack([grad_qg, grad_kg, grad_attng, grad_ffg])
    gain_shares = lax.psum_scatter(gain_stack, ("dp", "seq"), scatter_dimension=1, tiled=True)
    grad_query = attn_part[:, :model_width]
    grad_key = attn_part[:, model_width : 2 * model_width]
    grad_value = attn_part[:, 2 * model_width : 3 * model_width]
    grad_output = attn_part[:, 3 * model_width :]
    return (
        activation,
        input_grad,
        grad_query,
        grad_key,
        grad_value,
        grad_output,
        grad_gate,
        grad_up,
        grad_down,
        gain_shares[0],
        gain_shares[1],
        gain_shares[2],
        gain_shares[3],
    )


def solution(mesh):
    placed = (
        P("dp", "seq", None),
        P("dp", None),
        P(("dp", "seq"), None),
        P(("dp", "seq"), None),
        P(("dp", "seq"), None),
        P(("dp", "seq"), None),
        P(("dp", "seq"), None),
        P(("dp", "seq"), None),
        P(None, ("dp", "seq")),
        P(),
        P(),
        P(),
        P(),
        P("dp", "seq", None),
    )
    return jax.shard_map(
        shards,
        mesh=mesh,
        in_specs=placed,
        out_specs=(
            P("dp", "seq", None),
            P("dp", "seq", None),
            P(("dp", "seq"), None),
            P(("dp", "seq"), None),
            P(("dp", "seq"), None),
            P(("dp", "seq"), None),
            P(("dp", "seq"), None),
            P(("dp", "seq"), None),
            P(None, ("dp", "seq")),
            P(("dp", "seq")),
            P(("dp", "seq")),
            P(("dp", "seq")),
            P(("dp", "seq")),
        ),
        check_vma=False,
    )
```

profile of v0, /device:TPU:0, one launch (start us, length us, event | category | flops | bytes accessed | tf_op | source)
XLA Modules:
  0.0 3019.1 jit_solution(3999838460059790055)
XLA Ops:
  19.4 30.5 %all-to-all-done.4 = bf16[64,4,2048]{2,0,1:T(8,128)(2,1)S(1)} async-done(((bf16[64,4,2048]{2,0,1:T(8,128)(2,1)}), bf16[64,4,2048]{2,0,1:T(8,128)(2,1)S(1)}, u32[]{:S(2)}, u32[]{:S(2)}) %all-to-all-start.4) | async-done | bytes 1048608 | tf_op jit(solution)/shard_map/all_to_all | solution.py:218
  50.9 51.7 %all-gather.14.cloned.1.call-done = bf16[2048,2048]{1,0:T(8,128)(2,1)} async-done(((bf16[64,2048]{1,0:T(8,128)(2,1)}), bf16[2048,2048]{1,0:T(8,128)(2,1)}) %all-gather.14.cloned.1.call-update) | async-done | bytes 8388624 | tf_op jit(solution)/shard_map/all_gather | solution.py:194
  134.0 58.4 %all-gather.12.cloned.1.call-done = bf16[2048,2048]{1,0:T(8,128)(2,1)} async-done(((bf16[64,2048]{1,0:T(8,128)(2,1)}), bf16[2048,2048]{1,0:T(8,128)(2,1)}) %all-gather.12.cloned.1.call-update) | async-done | bytes 8388624 | tf_op jit(solution)/shard_map/all_gather | solution.py:193
  201.6 69.9 %all-gather.10.cloned.1.call-done = bf16[2048,2048]{1,0:T(8,128)(2,1)} async-done(((bf16[64,2048]{1,0:T(8,128)(2,1)}), bf16[2048,2048]{1,0:T(8,128)(2,1)}) %all-gather.10.cloned.1.call-update) | async-done | bytes 8388624 | tf_op jit(solution)/shard_map/all_gather | solution.py:192
  325.9 32.2 %all-to-all-done.1 = bf16[4,2,65536]{2,1,0:T(2,128)(2,1)} async-done(((bf16[4,2,65536]{2,1,0:T(2,128)(2,1)}), bf16[4,2,65536]{2,1,0:T(2,128)(2,1)}, u32[]{:S(2)}, u32[]{:S(2)}) %all-to-all-start.1) | async-done | bytes 1048608 | tf_op jit(solution)/shard_map/all_to_all | solution.py:207
  372.0 15.0 all-to-all-done
  399.5 25.0 while.27
  444.4 28.9 all_to_all.204
  485.9 55.2 %all_to_all.205 = bf16[64,4,2048]{2,0,1:T(8,128)(2,1)} all-to-all(bf16[64,4,2048]{2,0,1:T(8,128)(2,1)S(1)} %bitcast.443), channel_id=1, replica_groups=mesh['dp'=8,'seq'=4] {'seq'}, dimensions={1} | all-to-all | bytes 2097152 | tf_op jit(solution)/shard_map/all_to_all | solution.py:219
  541.3 52.8 %all_to_all.206 = bf16[64,4,2048]{2,0,1:T(8,128)(2,1)} all-to-all(bf16[64,4,2048]{2,0,1:T(8,128)(2,1)S(1)} %bitcast.444), channel_id=1, replica_groups=mesh['dp'=8,'seq'=4] {'seq'}, dimensions={1} | all-to-all | bytes 2097152 | tf_op jit(solution)/shard_map/all_to_all | solution.py:220
  604.0 14.7 fusion.49
  618.7 39.7 %all-gather.22.cloned.1.call-done = bf16[2048,2048]{1,0:T(8,128)(2,1)} async-done(((bf16[256,2048]{1,0:T(8,128)(2,1)}), bf16[2048,2048]{1,0:T(8,128)(2,1)}) %all-gather.22.cloned.1.call-update) | async-done | bytes 8388624 | tf_op jit(solution)/shard_map/all_gather | solution.py:224
  658.4 17.0 multiply_convert_fusion.2
  675.4 39.3 %all-gather.24.cloned.1.call-done = bf16[2048,2048]{1,0:T(8,128)(2,1)} async-done(((bf16[256,2048]{1,0:T(8,128)(2,1)}), bf16[2048,2048]{1,0:T(8,128)(2,1)}) %all-gather.24.cloned.1.call-update) | async-done | bytes 8388624 | tf_op jit(solution)/shard_map/all_gather | solution.py:225
  714.8 14.0 convert_bitcast_fusion
  728.8 68.3 %all-gather.26.cloned.1.call-done = bf16[1,1024,2048]{2,1,0:T(8,128)(2,1)} async-done(((bf16[1,256,2048]{2,1,0:T(8,128)(2,1)}), bf16[1,1024,2048]{2,1,0:T(8,128)(2,1)}) %all-gather.26.cloned.1.call-update) | async-done | bytes 4194320 | tf_op jit(solution)/shard_map/all_gather | solution.py:229
  797.1 155.8 %all-reduce.6.cloned.1.call-done = bf16[1,1024,2048]{2,1,0:T(8,128)(2,1)} async-done(((bf16[1,1024,2048]{2,1,0:T(8,128)(2,1)}), bf16[1,1024,2048]{2,1,0:T(8,128)(2,1)}) %all-reduce.6.cloned.1.call-update) | async-done | bytes 4194320 | tf_op jit(solution)/shard_map/psum | solution.py:234
  958.0 23.0 multiply_convert_fusion.1
  993.7 13.8 add_bitcast_fusion
  1007.5 14.5 convolution_convert_fusion.1
  1033.3 13.6 convolution_convert_fusion
  1046.9 18.1 pad_maximum_fusion.1
  1072.3 78.8 %reduce-scatter.9.cloned.1.call-done = f32[1,256,2048]{2,1,0:T(8,128)} async-done(((f32[1,1024,2048]{2,1,0:T(8,128)}), f32[1,256,2048]{2,1,0:T(8,128)}) %reduce-scatter.9.cloned.1.call-update) | async-done | bytes 2097168 | tf_op jit(solution)/shard_map/reduce_scatter | solution.py:250
  1184.4 25.7 all-to-all-done.7
  1221.0 43.4 %while.28 = (s32[]{:T(128)}, f32[1,1024,4,128]{1,3,2,0:T(8,128)S(1)}, f32[1,1024,4,128]{1,3,2,0:T(8,128)}, bf16[2,1,512,4,128]{4,3,2,0,1:T(4,128)(2,1)}, s32[2]{...) while((s32[]{:T(128)}, ...), condition=%wide.region_15.16_spmd.clone, body=%wide.region_13.15_spmd.clone.sunk | while | flops 2720528896 | bytes 98113936 | solution.py:152
  1297.3 14.4 all-to-all-done.8
  1420.9 45.1 %pad_maximum_fusion = f32[2048,8192]{0,1:T(8,128)} fusion(f32[2048,2048]{0,1:T(8,128)} %fusion.92, f32[2048,2048]{0,1:T(8,128)} %convolution_bitcast_fusion, f32[2048,2048]{0,1:T(8,128)} %convolution_bitcast_fusion.1, f32[2048,2048]{0,1:T(8,128)} %convolution_bitcast_fusion.2), kind=kLoop, calls=%fused_computation.57 | loop fusion | flops 50331648 | bytes 134217728 | tf_op jit(solution)/shard_map/concatenate | solution.py:323
  1466.0 61.3 %copy.230 = f32[2048,8192]{1,0:T(8,128)} copy(f32[2048,8192]{0,1:T(8,128)} %pad_maximum_fusion) | data formatting | bytes 134217728
  1539.3 24.2 all-to-all-done.13
  1584.8 37.2 %all-to-all-done.12 = bf16[4,64,2048]{2,1,0:T(8,128)(2,1)} async-done(((bf16[4,64,2048]{2,1,0:T(8,128)(2,1)}), bf16[4,64,2048]{2,1,0:T(8,128)(2,1)}, u32[]{:S(2)}, u32[]{:S(2)}) %all-to-all-start.12) | async-done | bytes 1048608 | tf_op jit(solution)/shard_map/all_to_all | solution.py:278
  1643.8 37.9 %all-to-all-done.11 = bf16[4,64,2048]{2,1,0:T(8,128)(2,1)} async-done(((bf16[4,64,2048]{2,1,0:T(8,128)(2,1)}), bf16[4,64,2048]{2,1,0:T(8,128)(2,1)}, u32[]{:S(2)}, u32[]{:S(2)}) %all-to-all-start.11) | async-done | bytes 1048608 | tf_op jit(solution)/shard_map/all_to_all | solution.py:271
  1684.6 1324.6 %reduce-scatter.13.cloned.1.call-done = f32[64,8192]{1,0:T(8,128)} async-done(((f32[2048,8192]{1,0:T(8,128)}), f32[64,8192]{1,0:T(8,128)}) %reduce-scatter.13.cloned.1.call-update) | async-done | bytes 2097168
  (399 shorter events, 517.1 us)
Async XLA Ops:
  7.2 95.5 %copy-start.13 = (bf16[1,256,2048]{2,1,0:T(8,128)(2,1)S(1)}, bf16[1,256,2048]{2,1,0:T(8,128)(2,1)}, u32[]{:S(2)}) copy-start(bf16[1,256,2048]{2,1,0:T(8,128)(2,1)} %param.18) | copy-start | bytes 3145732
  7.2 95.5 %all-gather.14.cloned.1.call-start = ((), (), s32[]{:S(2)}) async-start(), calls=%async_computation.20 | async-start | bytes 8650752 | tf_op jit(solution)/shard_map/all_gather | solution.py:194
  7.9 184.5 %all-gather.12.cloned.1.call-start = ((), (), s32[]{:S(2)}) async-start(), calls=%async_computation.19 | async-start | bytes 8650752 | tf_op jit(solution)/shard_map/all_gather | solution.py:193
  8.7 262.8 %all-gather.10.cloned.1.call-start = ((), (), s32[]{:S(2)}) async-start(), calls=%async_computation.18 | async-start | bytes 8650752 | tf_op jit(solution)/shard_map/all_gather | solution.py:192
  9.4 467.4 %all-gather.16.cloned.1.call-start = ((), (), s32[]{:S(2)}) async-start(), calls=%async_computation.21 | async-start | bytes 8650752 | tf_op jit(solution)/shard_map/all_gather | solution.py:195
  12.3 37.6 %all-to-all-start.4 = ((bf16[64,4,2048]{2,0,1:T(8,128)(2,1)}), bf16[64,4,2048]{2,0,1:T(8,128)(2,1)S(1)}, u32[]{:S(2)}, u32[]{:S(2)}) async-start(bf16[64,4,2048]{2,0,1:T(8,128)(2,1)} %bitcast.345), calls=%async_computation.4 | async-start | bytes 2097152 | tf_op jit(solution)/shard_map/all_to_all | solution.py:218
  18.6 576.3 %all-gather.20.cloned.1.call-start = ((), (), s32[]{:S(2)}) async-start(), calls=%async_computation.23 | async-start | bytes 9437184 | tf_op jit(solution)/shard_map/all_gather | solution.py:223
  129.5 178.2 %all-to-all-start.2 = ((bf16[4,2,65536]{2,1,0:T(2,128)(2,1)}), bf16[4,2,65536]{2,1,0:T(2,128)(2,1)}, u32[]{:S(2)}, u32[]{:S(2)}) async-start(bf16[4,2,65536]{2,1,0:T(2,128)(2,1)} %reshape.886), calls=%async_computation.2 | async-start | bytes 2097152 | tf_op jit(solution)/shard_map/all_to_all | solution.py:208
  307.7 50.4 %all-to-all-start.1 = ((bf16[4,2,65536]{2,1,0:T(2,128)(2,1)}), bf16[4,2,65536]{2,1,0:T(2,128)(2,1)}, u32[]{:S(2)}, u32[]{:S(2)}) async-start(bf16[4,2,65536]{2,1,0:T(2,128)(2,1)} %reshape.884), calls=%async_computation.1 | async-start | bytes 2097152 | tf_op jit(solution)/shard_map/all_to_all | solution.py:207
  358.1 28.9 all-to-all-start
  362.4 241.6 %all-gather.18.cloned.1.call-start = ((), (), s32[]{:S(2)}) async-start(), calls=%async_computation.22 | async-start | bytes 5242880 | tf_op jit(solution)/shard_map/all_gather | solution.py:228
  485.7 172.7 %all-gather.22.cloned.1.call-start = ((), (), s32[]{:S(2)}) async-start(), calls=%async_computation.24 | async-start | bytes 9437184 | tf_op jit(solution)/shard_map/all_gather | solution.py:224
  541.1 173.7 %all-gather.24.cloned.1.call-start = ((), (), s32[]{:S(2)}) async-start(), calls=%async_computation.25 | async-start | bytes 9437184 | tf_op jit(solution)/shard_map/all_gather | solution.py:225
  594.1 203.0 %all-gather.26.cloned.1.call-start = ((), (), s32[]{:S(2)}) async-start(), calls=%async_computation.27 | async-start | bytes 5242880 | tf_op jit(solution)/shard_map/all_gather | solution.py:229
  594.8 358.1 %all-reduce.6.cloned.1.call-start = ((), (), s32[]{:S(2)}) async-start(), calls=%async_computation.26 | async-start | bytes 8388608 | tf_op jit(solution)/shard_map/psum | solution.py:234
  728.7 224.2 %copy-start.60 = (f32[2048]{0:T(1024)S(1)}, f32[2048]{0:T(1024)}, u32[]{:S(2)}) copy-start(f32[2048]{0:T(1024)} %param.30) | copy-start | bytes 24580
  728.8 422.3 %reduce-scatter.9.cloned.1.call-start = ((), (), s32[]{:S(2)}) async-start(), calls=%async_computation.28 | async-start | bytes 10485760 | tf_op jit(solution)/shard_map/reduce_scatter | solution.py:250
  1007.5 519.9 %reduce-scatter.11.cloned.1.call-start = ((), (), s32[]{:S(2)}) async-start(), calls=%async_computation.29 | async-start | bytes 28311552 | tf_op jit(solution)/shard_map/reduce_scatter | solution.py:257
  1065.0 86.1 %copy-start.12 = (f32[256,2048]{1,0:T(8,128)S(1)}, f32[256,2048]{1,0:T(8,128)}, u32[]{:S(2)}) copy-start(f32[256,2048]{1,0:T(8,128)} %copy-done.11) | copy-start | bytes 6291460
  1065.0 86.1 %copy-start.15 = (bf16[1,256,2048]{2,1,0:T(8,128)(2,1)S(1)}, bf16[1,256,2048]{2,1,0:T(8,128)(2,1)}, u32[]{:S(2)}) copy-start(bf16[1,256,2048]{2,1,0:T(8,128)(2,1)} %param.18) | copy-start | bytes 3145732
  1065.0 86.1 %copy-start.51 = (f32[2048]{0:T(1024)S(1)}, f32[2048]{0:T(1024)}, u32[]{:S(2)}) copy-start(f32[2048]{0:T(1024)} %param.29) | copy-start | bytes 24580
  1065.0 86.1 %copy-start.66 = (f32[256]{0:T(256)S(1)}, f32[256]{0:T(256)}, u32[]{:S(2)}) copy-start(f32[256]{0:T(256)} %copy-done.65) | copy-start | bytes 3076
  1072.3 85.2 %copy-start.68 = (f32[256]{0:T(256)S(1)}, f32[256]{0:T(256)}, u32[]{:S(2)}) copy-start(f32[256]{0:T(256)} %copy-done.67) | copy-start | bytes 3076
  1180.0 30.2 %all-to-all-start.7 = ((bf16[4,2,65536]{2,1,0:T(2,128)(2,1)}), bf16[4,2,65536]{2,1,0:T(2,128)(2,1)S(1)}, u32[]{:S(2)}, u32[]{:S(2)}) async-start(bf16[4,2,65536]{2,1,0:T(2,128)(2,1)} %reshape.890), calls=%async_computation.8 | async-start | bytes 2097152 | tf_op jit(solution)/shard_map/all_to_all | solution.py:297
  1281.5 30.1 all-to-all-start.8
  1311.7 29.7 all-to-all-start.9
  1341.4 28.7 all-to-all-start.10
  1344.9 289.8 %reduce-scatter.15.cloned.1.call-start = ((), (), s32[]{:S(2)}) async-start(), calls=%async_computation.31 | async-start | bytes 1081344
  1420.9 1588.4 %reduce-scatter.13.cloned.1.call-start = ((), (), s32[]{:S(2)}) async-start(), calls=%async_computation.30 | async-start | bytes 69206016
  1532.2 31.3 %all-to-all-start.13 = ((bf16[4,64,2048]{2,1,0:T(8,128)(2,1)}), bf16[4,64,2048]{2,1,0:T(8,128)(2,1)S(1)}, u32[]{:S(2)}, u32[]{:S(2)}) async-start(bf16[4,64,2048]{2,1,0:T(8,128)(2,1)} %bitcast.442), calls=%async_computation.15 | async-start | bytes 2097152 | tf_op jit(solution)/shard_map/all_to_all | solution.py:285
  1563.5 58.4 %all-to-all-start.12 = ((bf16[4,64,2048]{2,1,0:T(8,128)(2,1)}), bf16[4,64,2048]{2,1,0:T(8,128)(2,1)}, u32[]{:S(2)}, u32[]{:S(2)}) async-start(bf16[4,64,2048]{2,1,0:T(8,128)(2,1)} %bitcast.441), calls=%async_computation.14 | async-start | bytes 2097152 | tf_op jit(solution)/shard_map/all_to_all | solution.py:278
  1622.0 59.8 %all-to-all-start.11 = ((bf16[4,64,2048]{2,1,0:T(8,128)(2,1)}), bf16[4,64,2048]{2,1,0:T(8,128)(2,1)}, u32[]{:S(2)}, u32[]{:S(2)}) async-start(bf16[4,64,2048]{2,1,0:T(8,128)(2,1)} %bitcast.438), calls=%async_computation.13 | async-start | bytes 2097152 | tf_op jit(solution)/shard_map/all_to_all | solution.py:271
  (76 other events, 1037.8 us)
Sparse Core Ops, SparseCore 0:
  11.0 91.6 all-gather.13
  105.6 86.8 all-gather.11
  195.4 76.0 all-gather.9
  274.3 89.3 all-gather.15
  365.4 52.4 all-gather.19
  485.8 118.1 all-gather.17
  605.9 52.5 all-gather.21
  660.3 54.3 all-gather.23
  716.3 80.7 all-gather.25
  799.3 153.5 all-reduce.5
  1007.6 143.4 reduce-scatter.8
  1155.0 157.5 reduce-scatter.10
  1421.0 137.4 reduce-scatter.14
  1560.7 1448.5 reduce-scatter.12
where the time goes:
time: 3030 us; the launch traced here: 3020 us
  waiting for transfers between devices  2130 us (70%)
  matrix products  256 us (8%)
  local copies, waits for them, and re-layouts  223 us (7%)
  other arithmetic  199 us (7%)
  blocking collectives  137 us (5%)
  starting transfers between devices  50.6 us (2%)
    unnamed x16, waiting for transfers between devices  1330 us
    psum x1, waiting for transfers between devices, shards(): lax.psum(back_project(hidden_low, wd_blk).astype(jnp.bfloat16), 'seq')  156 us
    unnamed x173, local copies, waits for them, and re-layouts  131 us
    unnamed x15, other arithmetic  81.6 us
    dot_general x7, matrix products, project(): return jnp.dot(left, weight, preferred_element_type=jnp.float32)  79.2 us
    reduce_scatter x1, waiting for transfers between devices, shards(): lax.psum_scatter(partial_resid, 'seq', scatter_dimension=1, tiled=True)  78.8 us
    dot_general x7, matrix products, rows_product(): lax.dot_general(left, right, (((0,), (0,)), ((), ())), preferred_element_...  71.9 us
    dot_general x7, matrix products, back_project(): lax.dot_general(grad_in, weight, (((grad_in.ndim - 1,), (1,)), ((), ())),...  69.9 us
  transfers between devices with their start and end apart: 25, of which 20 were waited for; matrix products, arithmetic and copies ran while one was open for 20% of the time, Pallas kernels for 0%

commit v1 on v0

v1 whole, which is shorter than its diff:
```python
import jax
import jax.numpy as jnp
from jax import lax
from jax.sharding import PartitionSpec as P

HD = 128
EPSILON = 1e-06
ROPE_BASE = 500000.0
MASKED = -1e30
BF = jnp.bfloat16
F32 = jnp.float32


def project(left, weight):
    return jnp.dot(left, weight, preferred_element_type=F32)


def back_project(grad_in, weight):
    return lax.dot_general(
        grad_in, weight, (((grad_in.ndim - 1,), (1,)), ((), ())), preferred_element_type=F32
    )


def rows_product(left, right):
    return lax.dot_general(left, right, (((0,), (0,)), ((), ())), preferred_element_type=F32)


def inv_rms(values):
    return lax.rsqrt(jnp.mean(values * values, axis=-1, keepdims=True) + EPSILON)


def rms_back(normed, factor, gain, grad):
    scaled = grad * gain
    inner = jnp.mean(scaled * normed, axis=-1, keepdims=True)
    return (scaled - normed * inner) * factor


def rope_tables(positions):
    half_dim = HD // 2
    frequency = jnp.power(F32(ROPE_BASE), -jnp.arange(half_dim, dtype=F32) * (2.0 / HD))
    angles = positions[:, None] * frequency[None, :]
    angles = jnp.concatenate([angles, angles], axis=-1)
    return (jnp.cos(angles), jnp.sin(angles))


def rotate(values, cosine, sine):
    shaped = values.reshape(values.shape[:-1] + (values.shape[-1] // HD, HD))
    first = shaped[..., : HD // 2]
    second = shaped[..., HD // 2 :]
    turned = jnp.concatenate([-second, first], axis=-1)
    return (shaped * cosine[:, None, :] + turned * sine[:, None, :]).reshape(values.shape)


def shift(values, count, step):
    return lax.ppermute(values, "seq", [((i + step) % count, i) for i in range(count)])


def gather_cyclic(values, count):
    if count != 4:
        return [values] + [shift(values, count, p) for p in range(1, count)]
    me = lax.axis_index("seq")
    far = lax.ppermute(values, "seq", [(i ^ 2, i) for i in range(4)])
    after = lax.ppermute(values, "seq", [(i + 1, i) for i in range(3)])
    before = lax.ppermute(values, "seq", [(i, i + 1) for i in range(3)])
    ends = lax.ppermute(far, "seq", [(2, 3), (1, 0)])
    return [values, jnp.where(me == 3, ends, after), far, jnp.where(me == 0, ends, before)]


def scatter_cyclic(parts, count):
    low = [part.astype(BF) for part in parts]
    if count != 4:
        total = parts[0]
        for p in range(1, count):
            got = lax.ppermute(low[p], "seq", [(i, (i + p) % count) for i in range(count)])
            total = total + got.astype(F32)
        return total
    me = lax.axis_index("seq")
    ends = lax.ppermute(jnp.where(me == 0, low[3], low[1]), "seq", [(0, 1), (3, 2)])
    after = lax.ppermute(low[1], "seq", [(i, i + 1) for i in range(3)])
    before = lax.ppermute(low[3], "seq", [(i + 1, i) for i in range(3)])
    far_sum = (parts[2] + ends.astype(F32)).astype(BF)
    far = lax.ppermute(far_sum, "seq", [(i, i ^ 2) for i in range(4)])
    return parts[0] + after.astype(F32) + before.astype(F32) + far.astype(F32)


def sum_stats(stats, count):
    total = stats
    for p in range(1, count):
        total = total + jnp.roll(shift(stats, count, p), p, axis=1)
    return total


def sum_everywhere(values, dp_count, seq_count):
    for name, count in (("seq", seq_count), ("dp", dp_count)):
        if count & (count - 1):
            values = lax.psum(values, name)
            continue
        bit = 1
        while bit < count:
            values = values + lax.ppermute(values, name, [(i, i ^ bit) for i in range(count)])
            bit *= 2
    return values


def swap_blocks(values):
    return lax.all_to_all(values, "seq", split_axis=0, concat_axis=0, tiled=True)


def gather_dp(values):
    return lax.all_gather(values, "dp", axis=0, tiled=True)


def scatter_dp(values):
    return lax.psum_scatter(values, "dp", scatter_dimension=0, tiled=True)


def attend(query, key, value, segments, positions, heads):
    length = query.shape[0]
    block_rows = min(512, length)
    blocks = length // block_rows
    scale = HD ** (-0.5)
    key_heads = key.reshape(length, heads, HD)
    value_heads = value.reshape(length, heads, HD)
    split = lambda v: v.reshape((blocks, block_rows) + v.shape[1:])

    def one_block(item):
        q, seg, pos = item
        scores = jnp.einsum("qhd,khd->hqk", q, key_heads, preferred_element_type=F32) * scale
        allowed = (positions[None, :] <= pos[:, None]) & (segments[None, :] == seg[:, None])
        scores = jnp.where(allowed[None], scores, MASKED)
        top = jnp.max(scores, axis=-1, keepdims=True)
        exps = jnp.exp(scores - top)
        total = jnp.sum(exps, axis=-1, keepdims=True)
        probs = exps / total
        mixed = jnp.einsum("hqk,khd->qhd", probs.astype(BF), value_heads, preferred_element_type=F32)
        return (mixed.astype(BF), (top + jnp.log(total))[..., 0])

    items = (split(query.reshape(length, heads, HD)), split(segments), split(positions))
    mixed, logs = lax.map(one_block, items)
    return (mixed.reshape(length, heads * HD), logs)


def attend_back(query, key, value, grad_mixed, logs, segments, positions, heads):
    length = query.shape[0]
    block_rows = min(512, length)
    blocks = length // block_rows
    scale = HD ** (-0.5)
    key_heads = key.reshape(length, heads, HD)
    value_heads = value.reshape(length, heads, HD)
    split = lambda v: v.reshape((blocks, block_rows) + v.shape[1:])

    def one_block(totals, item):
        grad_keys, grad_values = totals
        q, grad, log_total, seg, pos = item
        scores = jnp.einsum("qhd,khd->hqk", q, key_heads, preferred_element_type=F32) * scale
        allowed = (positions[None, :] <= pos[:, None]) & (segments[None, :] == seg[:, None])
        scores = jnp.where(allowed[None], scores, MASKED)
        probs = jnp.exp(scores - log_total[..., None])
        grad_probs = jnp.einsum("qhd,khd->hqk", grad, value_heads, preferred_element_type=F32)
        grad_values = grad_values + jnp.einsum(
            "hqk,qhd->khd", probs.astype(BF), grad, preferred_element_type=F32
        )
        inner = jnp.sum(probs * grad_probs, axis=-1, keepdims=True)
        grad_scores = (probs * (grad_probs - inner)).astype(BF)
        grad_q = jnp.einsum("hqk,khd->qhd", grad_scores, key_heads, preferred_element_type=F32) * scale
        grad_keys = grad_keys + scale * jnp.einsum(
            "hqk,qhd->khd", grad_scores, q, preferred_element_type=F32
        )
        return ((grad_keys, grad_values), grad_q.astype(BF))

    zeros = jnp.zeros((length, heads, HD), F32)
    by_head = lambda v: split(v.reshape(length, heads, HD))
    items = (by_head(query), by_head(grad_mixed), logs, split(segments), split(positions))
    (grad_keys, grad_values), grad_q = lax.scan(one_block, (zeros, zeros), items)
    flat = lambda v: v.reshape(length, heads * HD).astype(BF)
    return (flat(grad_q), flat(grad_keys), flat(grad_values))


def build(dp_count, seq_count):
    def shards(
        layer_input,
        segments,
        w_query,
        w_key,
        w_value,
        w_output,
        w_gate,
        w_up,
        w_down,
        query_gain,
        key_gain,
        attn_gain,
        ff_gain,
        cotangent,
    ):
        n = seq_count
        tokens, width = layer_input.shape[1:]
        shard_rows = w_query.shape[0]
        part = width // n
        ff_width = w_gate.shape[1]
        ff_part = ff_width // n
        heads = part // HD
        length = n * tokens
        me = lax.axis_index("seq")
        dp_me = lax.axis_index("dp")
        x_own = layer_input[0]
        cot = cotangent[0].astype(F32)

        by_part = lambda w: w.reshape(shard_rows, n, -1).transpose(1, 0, 2)
        qkv_blocks = jnp.concatenate([by_part(w_query), by_part(w_key), by_part(w_value)], axis=2)
        w_qkv = gather_dp(swap_blocks(qkv_blocks).reshape(n * shard_rows, 3 * part))
        devices = dp_count * n
        to_heads = [(b, (b % dp_count) * n + b // dp_count) for b in range(devices)]
        from_heads = [(dst, src) for src, dst in to_heads]
        w_out = gather_dp(lax.ppermute(w_output, ("dp", "seq"), to_heads))
        w_gate_part, w_up_part, w_down_part = (
            gather_dp(swap_blocks(by_part(w)).reshape(n * shard_rows, ff_part))
            for w in (w_gate, w_up, w_down.T)
        )

        x_all = jnp.concatenate(gather_cyclic(x_own, n), axis=0)
        natural = jnp.arange(length, dtype=jnp.int32)
        positions = (natural + me * tokens) % length
        seg_row = segments[0]
        seg_cyclic = lax.dynamic_slice_in_dim(
            jnp.concatenate([seg_row, seg_row]), me * tokens, length, 0
        )
        cosine, sine = rope_tables(positions.astype(F32))
        own_gain = lambda g: lax.dynamic_slice_in_dim(g, me * part, part, 0)
        q_gain = own_gain(query_gain)
        k_gain = own_gain(key_gain)

        qkv = project(x_all, w_qkv)
        q_proj, k_proj, v_proj = (qkv[:, j * part : (j + 1) * part] for j in range(3))
        squares = jnp.stack([jnp.sum(q_proj * q_proj, axis=-1), jnp.sum(k_proj * k_proj, axis=-1)])
        squares = sum_stats(squares.reshape(2, n, tokens), n).reshape(2, length, 1)
        factors = lax.rsqrt(squares / width + EPSILON)
        q_low = rotate(q_proj * factors[0] * q_gain, cosine, sine).astype(BF)
        k_low = rotate(k_proj * factors[1] * k_gain, cosine, sine).astype(BF)
        v_low = v_proj.astype(BF)
        mixed, logs = attend(q_low, k_low, v_low, seg_cyclic, positions, heads)

        chunks = lambda v: [v[p * tokens : (p + 1) * tokens] for p in range(n)]
        attn_out = scatter_cyclic(chunks(project(mixed, w_out)), n)
        attn_factor = inv_rms(attn_out)
        attn_normed = attn_out * attn_factor
        residual = x_own.astype(F32) + attn_normed * attn_gain
        residual_all = jnp.concatenate(gather_cyclic(residual.astype(BF), n), axis=0)

        gate_act = project(residual_all, w_gate_part)
        up_act = project(residual_all, w_up_part)
        hidden = (jax.nn.silu(gate_act) * up_act).astype(BF)
        ff_out = scatter_cyclic(chunks(back_project(hidden, w_down_part)), n)
        ff_factor = inv_rms(ff_out)
        ff_normed = ff_out * ff_factor
        activation = (residual + ff_normed * ff_gain).astype(BF)
        grad_ff_gain = jnp.sum(cot * ff_normed, axis=0)
        d_ff = rms_back(ff_normed, ff_factor, ff_gain, cot).astype(BF)
        d_ff_all = jnp.concatenate(gather_cyclic(d_ff, n), axis=0)

        d_hidden = project(d_ff_all, w_down_part)
        sig = 1.0 / (1.0 + jnp.exp(-gate_act))
        d_gate = (d_hidden * up_act * sig * (1.0 + gate_act * (1.0 - sig))).astype(BF)
        d_up = (d_hidden * gate_act * sig).astype(BF)
        d_res = back_project(d_gate, w_gate_part) + back_project(d_up, w_up_part)
        d_res = cot + scatter_cyclic(chunks(d_res), n)

        def back_to_rows(grad):
            return swap_blocks(scatter_dp(grad.astype(BF)).reshape(n, shard_rows, -1))

        joined = lambda g: g.transpose(1, 0, 2).reshape(shard_rows, -1).astype(F32)
        grad_down = joined(back_to_rows(rows_product(d_ff_all, hidden))).T
        grad_gate = joined(back_to_rows(rows_product(residual_all, d_gate)))
        grad_up = joined(back_to_rows(rows_product(residual_all, d_up)))

        grad_attn_gain = jnp.sum(d_res * attn_normed, axis=0)
        d_attn = rms_back(attn_normed, attn_factor, attn_gain, d_res).astype(BF)
        d_attn_all = jnp.concatenate(gather_cyclic(d_attn, n), axis=0)
        d_mixed = back_project(d_attn_all, w_out).astype(BF)
        out_rows = scatter_dp(rows_product(mixed, d_attn_all).astype(BF))
        grad_output = lax.ppermute(out_rows, ("dp", "seq"), from_heads).astype(F32)
        d_q, d_k, d_v = attend_back(
            q_low, k_low, v_low, d_mixed, logs, seg_cyclic, positions, heads
        )

        back_q = rotate(d_q.astype(F32), cosine, -sine)
        back_k = rotate(d_k.astype(F32), cosine, -sine)
        q_normed = q_proj * factors[0]
        k_normed = k_proj * factors[1]
        grad_q_gain = jnp.sum(back_q * q_normed, axis=0)
        grad_k_gain = jnp.sum(back_k * k_normed, axis=0)
        inner = jnp.stack(
            [
                jnp.sum(back_q * q_gain * q_normed, axis=-1),
                jnp.sum(back_k * k_gain * k_normed, axis=-1),
            ]
        )
        inner = sum_stats(inner.reshape(2, n, tokens), n).reshape(2, length, 1) / width
        d_q_proj = ((back_q * q_gain - q_normed * inner[0]) * factors[0]).astype(BF)
        d_k_proj = ((back_k * k_gain - k_normed * inner[1]) * factors[1]).astype(BF)
        d_qkv = jnp.concatenate([d_q_proj, d_k_proj, d_v], axis=1)
        input_grad = d_res + scatter_cyclic(chunks(back_project(d_qkv, w_qkv)), n)
        qkv_rows = back_to_rows(rows_product(x_all, d_qkv))
        grad_query, grad_key, grad_value = (
            joined(qkv_rows[:, :, j * part : (j + 1) * part]) for j in range(3)
        )

        spread = lambda g: lax.dynamic_update_slice(jnp.zeros(width, F32), g, (me * part,))
        gains = jnp.stack([spread(grad_q_gain), spread(grad_k_gain), grad_attn_gain, grad_ff_gain])
        gains = sum_everywhere(gains, dp_count, n)
        share = width // devices
        gains = lax.dynamic_slice_in_dim(gains, (dp_me * n + me) * share, share, 1)
        return (
            activation[None],
            input_grad.astype(BF)[None],
            grad_query,
            grad_key,
            grad_value,
            grad_output,
            grad_gate,
            grad_up,
            grad_down,
            gains[0],
            gains[1],
            gains[2],
            gains[3],
        )

    return shards


def solution(mesh):
    both = P(("dp", "seq"), None)
    tokens = P("dp", "seq", None)
    columns = P(None, ("dp", "seq"))
    gain = P(("dp", "seq"))
    return jax.shard_map(
        build(mesh.shape["dp"], mesh.shape["seq"]),
        mesh=mesh,
        in_specs=(tokens, P("dp", None)) + (both,) * 6 + (columns,) + (P(),) * 4 + (tokens,),
        out_specs=(tokens, tokens) + (both,) * 6 + (columns,) + (gain,) * 4,
        check_vma=False,
    )
```

time: 3030 us -> 1160 us (0.38)
  waiting for transfers between devices: 2130 us -> 435 us
  starting transfers between devices: 50.6 us -> 231 us
  local copies, waits for them, and re-layouts: 223 us -> 55.9 us
  other arithmetic: 199 us -> 75 us
  blocking collectives: 137 us -> 103 us
    unnamed x16 -> x10, waiting for transfers between devices: 1330 us -> 0.16 us
    ppermute x0 -> x45, waiting for transfers between devices: none -> 418 us  [the longest x4 103 us: gather_cyclic(): far = lax.ppermute(values, 'seq', [(i ^ 2, i) for i in range(4)])]
    all_gather x9 -> x5, waiting for transfers between devices: 337 us -> 0.07 us  [gather_dp(): return lax.all_gather(values, 'dp', axis=0, tiled=True)]
    all_to_all x11 -> x5, waiting for transfers between devices: 227 us -> 17.3 us  [swap_blocks(): lax.all_to_all(values, 'seq', split_axis=0, concat_axis=0, tiled=True)]
    ppermute x0 -> x45, starting transfers between devices: none -> 202 us  [the longest x4 86.2 us: gather_cyclic(): before = lax.ppermute(values, 'seq', [(i, i + 1) for i in range(3)])]
    psum x1 -> x0, waiting for transfers between devices: 156 us -> none  [shards(): lax.psum(back_project(hidden_low, wd_blk).astype(jnp.bfloat16), 'seq')]
    unnamed x173 -> x154, local copies, waits for them, and re-layouts: 131 us -> 14.5 us
    reduce_scatter x2 -> x5, waiting for transfers between devices: 78.9 us -> 0.03 us  [scatter_dp(): return lax.psum_scatter(values, 'dp', scatter_dimension=0, tiled=True)]
  transfers between devices with their start and end apart: 25 -> 60, of which waited for: 20 -> 29; matrix products, arithmetic and copies ran while one was open for 20% -> 25% of each run, Pallas kernels for 0% -> 0%
where the time goes in v1:
time: 1160 us; the launch traced here: 1150 us
  waiting for transfers between devices  435 us (38%)
  matrix products  232 us (20%)
  starting transfers between devices  231 us (20%)
  blocking collectives  103 us (9%)
  other arithmetic  75 us (6%)
  local copies, waits for them, and re-layouts  55.9 us (5%)
  between operations  16 us (1%)
    all_to_all x3, blocking collectives, swap_blocks(): lax.all_to_all(values, 'seq', split_axis=0, concat_axis=0, tiled=True)  103 us
    ppermute x4, waiting for transfers between devices, gather_cyclic(): far = lax.ppermute(values, 'seq', [(i ^ 2, i) for i in range(4)])  103 us
    ppermute x4, waiting for transfers between devices, scatter_cyclic(): far = lax.ppermute(far_sum, 'seq', [(i, i ^ 2) for i in range(4)])  91.4 us
    ppermute x4, starting transfers between devices, gather_cyclic(): before = lax.ppermute(values, 'seq', [(i, i + 1) for i in range(3)])  86.2 us
    dot_general x5, matrix products, project(): return jnp.dot(left, weight, preferred_element_type=F32)  78.1 us
    ppermute x5, waiting for transfers between devices, sum_everywhere(): lax.ppermute(values, name, [(i, i ^ bit) for i in range(count)])  76.5 us
    ppermute x4, waiting for transfers between devices, scatter_cyclic(): lax.ppermute(jnp.where(me == 0, low[3], low[1]), 'seq', [(0, 1), (3, 2)])  59 us
    dot_general x5, matrix products, back_project(): lax.dot_general(grad_in, weight, (((grad_in.ndim - 1,), (1,)), ((), ())),...  58.6 us
  transfers between devices with their start and end apart: 60, of which 29 were waited for; matrix products, arithmetic and copies ran while one was open for 25% of the time, Pallas kernels for 0%

profile of v1, /device:TPU:0, one launch (start us, length us, event | category | flops | bytes accessed | tf_op | source)
XLA Modules:
  0.0 1149.2 jit_solution(5856948661134835691)
XLA Ops:
  11.2 26.3 %all_to_all.40 = bf16[4,64,1536]{2,1,0:T(8,128)(2,1)} all-to-all(bf16[4,64,1536]{2,1,0:T(8,128)(2,1)S(1)} %copy.145), channel_id=1, replica_groups=mesh['dp'=8,'seq'=4] {'seq'}, dimensions={0} | all-to-all | bytes 1572864 | tf_op jit(solution)/shard_map/all_to_all | solution.py:106
  40.7 46.4 %all_to_all.41 = bf16[4,64,2048]{2,1,0:T(8,128)(2,1)} all-to-all(bf16[4,64,2048]{2,1,0:T(8,128)(2,1)S(1)} %copy.153), channel_id=1, replica_groups=mesh['dp'=8,'seq'=4] {'seq'}, dimensions={0} | all-to-all | bytes 2097152 | tf_op jit(solution)/shard_map/all_to_all | solution.py:106
  88.6 30.2 %all_to_all.42 = bf16[4,64,2048]{2,1,0:T(8,128)(2,1)} all-to-all(bf16[4,64,2048]{2,1,0:T(8,128)(2,1)S(1)} %copy.154), channel_id=1, replica_groups=mesh['dp'=8,'seq'=4] {'seq'}, dimensions={0} | all-to-all | bytes 2097152 | tf_op jit(solution)/shard_map/all_to_all | solution.py:106
  132.3 45.9 %collective-permute-done = bf16[256,2048]{1,0:T(8,128)(2,1)} collective-permute-done((bf16[256,2048]{1,0:T(8,128)(2,1)S(1)}, bf16[256,2048]{1,0:T(8,128)(2,1)}, u32[]{:S(2)}, u32[]{:S(2)}) %collective-permute-start) | collective-permute-done | bytes 1048608 | tf_op jit(solution)/shard_map/ppermute | solution.py:62
  191.4 20.6 %collective-permute-done.1 = bf16[256,2048]{1,0:T(8,128)(2,1)} collective-permute-done((bf16[256,2048]{1,0:T(8,128)(2,1)}, bf16[256,2048]{1,0:T(8,128)(2,1)}, u32[]{:S(2)}, u32[]{:S(2)}) %collective-permute-start.1) | collective-permute-done | bytes 1048608 | tf_op jit(solution)/shard_map/ppermute | solution.py:65
  257.4 18.5 %while.28 = (s32[]{:T(128)}, bf16[2,512,4,128]{3,2,1,0:T(4,128)(2,1)}, f32[2,4,512]{2,1,0:T(4,128)S(1)}, s32[2,512]{1,0:T(2,128)S(1)}, s32[1024]{0:T(1024)S(1)},...) while((s32[]{:T(128)}, ...), condition=%wide.region_5.6_spmd.clone, body=%wide.region_2.5_spmd.clone.sunk | while | flops 1100752896 | bytes 39936192 | solution.py:139
  291.2 17.6 %collective-permute-done.10 = bf16[256,2048]{1,0:T(8,128)(2,1)S(1)} collective-permute-done((bf16[256,2048]{1,0:T(8,128)(2,1)S(1)}, bf16[256,2048]{1,0:T(8,128)(2,1)S(1)}, u32[]{:S(2)}, u32[]{:S(2)}) %collective-permute-start.10) | collective-permute-done | bytes 1048608 | tf_op jit(solution)/shard_map/ppermute | solution.py:78
  311.9 18.2 %collective-permute-done.9 = bf16[256,2048]{1,0:T(8,128)(2,1)S(1)} collective-permute-done((bf16[256,2048]{1,0:T(8,128)(2,1)S(1)}, bf16[256,2048]{1,0:T(8,128)(2,1)S(1)}, u32[]{:S(2)}, u32[]{:S(2)}) %collective-permute-start.9) | collective-permute-done | bytes 1048608 | tf_op jit(solution)/shard_map/ppermute | solution.py:80
  331.3 22.4 %collective-permute-done.11 = bf16[256,2048]{1,0:T(8,128)(2,1)S(1)} collective-permute-done((bf16[256,2048]{1,0:T(8,128)(2,1)S(1)}, bf16[256,2048]{1,0:T(8,128)(2,1)S(1)}, u32[]{:S(2)}, u32[]{:S(2)}) %collective-permute-start.11) | collective-permute-done | bytes 1048608 | tf_op jit(solution)/shard_map/ppermute | solution.py:82
  357.6 30.1 %collective-permute-start.15 = (bf16[256,2048]{1,0:T(8,128)(2,1)S(1)}, bf16[256,2048]{1,0:T(8,128)(2,1)S(1)}, u32[]{:S(2)}, u32[]{:S(2)}) collective-permute-start(bf16[256,2048]{1,0:T(8,128)(2,1)S(1)} %fusion.75), channel_id=1, source_target_pairs={{0,1},{1,2},{2,3},{4,5},{5,6},{6,7},{8,9},{9,10},{10,11},{12,13},{... | collective-permute-start | bytes 3145736 | tf_op jit(solution)/shard_map/ppermute | solution.py:64
  387.8 16.0 %collective-permute-done.12 = bf16[256,2048]{1,0:T(8,128)(2,1)S(1)} collective-permute-done((bf16[256,2048]{1,0:T(8,128)(2,1)S(1)}, bf16[256,2048]{1,0:T(8,128)(2,1)S(1)}, u32[]{:S(2)}, u32[]{:S(2)}) %collective-permute-start.12) | collective-permute-done | bytes 1048608 | tf_op jit(solution)/shard_map/ppermute | solution.py:62
  405.1 19.7 %collective-permute-done.13 = bf16[256,2048]{1,0:T(8,128)(2,1)S(1)} collective-permute-done((bf16[256,2048]{1,0:T(8,128)(2,1)S(1)}, bf16[256,2048]{1,0:T(8,128)(2,1)S(1)}, u32[]{:S(2)}, u32[]{:S(2)}) %collective-permute-start.13) | collective-permute-done | bytes 1048608 | tf_op jit(solution)/shard_map/ppermute | solution.py:65
  425.0 22.3 %fusion.112 = f32[1024,2048]{1,0:T(8,128)} fusion(bf16[2048,2048]{1,0:T(8,128)(2,1)} %all-gather.10.cloned.1.call-done, bf16[256,2048]{1,0:T(8,128)(2,1)S(1)} %get-tuple-element.428, bf16[256,2048]{1,0:T(8,128)(2,1)} %copy-done.85, bf16[256,2048]{1,0:T(8,128)(2,1)S(1)} %get-tuple-element.427, bf16[256,2048]{1,0:T(8,128)(2,1)S(1)} %fusion.75), kind=kOutput, calls=%fused_computation.250 | convolution fusion | flops 8606711808 | bytes 20971520 | tf_op jit(solution)/shard_map/dot_general | solution.py:15
  447.4 19.3 %multiply_convert_fusion.3 = (bf16[1024,2048]{1,0:T(8,128)(2,1)}, f32[1024,2048]{1,0:T(8,128)}) fusion(f32[1024,2048]{1,0:T(8,128)} %fusion.112, bf16[2048,2048]{1,0:T(8,128)(2,1)} %all-gather.12.cloned.1.call-done, bf16[256,2048]{1,0:T(8,128)(2,1)S(1)} %get-tuple-element.428, bf16[256,2048]{1,0:T(8,128)(2,1)} %copy-done.85, ...), kind=kOutput, calls=%fused_computation.68 | convolution fusion | flops 8619294720 | bytes 33554432 | tf_op jit(solution)/shard_map/dot_general | solution.py:15
  487.1 17.4 %collective-permute-done.18 = bf16[256,2048]{1,0:T(8,128)(2,1)S(1)} collective-permute-done((bf16[256,2048]{1,0:T(8,128)(2,1)S(1)}, bf16[256,2048]{1,0:T(8,128)(2,1)S(1)}, u32[]{:S(2)}, u32[]{:S(2)}) %collective-permute-start.18) | collective-permute-done | bytes 1048608 | tf_op jit(solution)/shard_map/ppermute | solution.py:78
  504.8 13.7 %collective-permute-start.19 = (bf16[256,2048]{1,0:T(8,128)(2,1)S(1)}, bf16[256,2048]{1,0:T(8,128)(2,1)S(1)}, u32[]{:S(2)}, u32[]{:S(2)}) collective-permute-start(bf16[256,2048]{1,0:T(8,128)(2,1)S(1)} %fusion.63), channel_id=1, source_target_pairs={{0,2},{1,3},{2,0},{3,1},{4,6},{5,7},{6,4},{7,5},{8,10},{9,11},{10,... | collective-permute-start | bytes 3145736 | tf_op jit(solution)/shard_map/ppermute | solution.py:82
  527.0 27.8 %collective-permute-done.19 = bf16[256,2048]{1,0:T(8,128)(2,1)S(1)} collective-permute-done((bf16[256,2048]{1,0:T(8,128)(2,1)S(1)}, bf16[256,2048]{1,0:T(8,128)(2,1)S(1)}, u32[]{:S(2)}, u32[]{:S(2)}) %collective-permute-start.19) | collective-permute-done | bytes 1048608 | tf_op jit(solution)/shard_map/ppermute | solution.py:82
  558.7 34.6 %collective-permute-start.23 = (bf16[256,2048]{1,0:T(8,128)(2,1)S(1)}, bf16[256,2048]{1,0:T(8,128)(2,1)S(1)}, u32[]{:S(2)}, u32[]{:S(2)}) collective-permute-start(bf16[256,2048]{1,0:T(8,128)(2,1)S(1)} %fusion.49), channel_id=1, source_target_pairs={{0,1},{1,2},{2,3},{4,5},{5,6},{6,7},{8,9},{9,10},{10,11},{12,13},{... | collective-permute-start | bytes 3145736 | tf_op jit(solution)/shard_map/ppermute | solution.py:64
  593.4 13.5 %collective-permute-done.20 = bf16[256,2048]{1,0:T(8,128)(2,1)S(1)} collective-permute-done((bf16[256,2048]{1,0:T(8,128)(2,1)S(1)}, bf16[256,2048]{1,0:T(8,128)(2,1)S(1)}, u32[]{:S(2)}, u32[]{:S(2)}) %collective-permute-start.20) | collective-permute-done | bytes 1048608 | tf_op jit(solution)/shard_map/ppermute | solution.py:62
  628.7 20.7 %multiply_convert_fusion.1 = (bf16[1024,2048]{1,0:T(8,128)(2,1)}, bf16[1024,2048]{1,0:T(8,128)(2,1)}) fusion(f32[1024,2048]{1,0:T(8,128)} %fusion.112, f32[1024,2048]{1,0:T(8,128)} %get-tuple-element.456, bf16[2048,2048]{1,0:T(8,128)(2,1)} %all-gather.14.cloned.1.call-done, bf16[256,2048]{1,0:T(8,128)(2,1)} %get-tuple-element.426, ...), kind=kOutput, calls=%fused_computation.66 | convolution fusion | flops 8633974784 | bytes 37748736 | tf_op jit(solution)/shard_map/dot_general | solution.py:15
  649.4 14.0 %convolution_convert_fusion.2 = bf16[2048,2048]{1,0:T(8,128)(2,1)} fusion(bf16[1024,2048]{1,0:T(8,128)(2,1)} %get-tuple-element.396, bf16[256,2048]{1,0:T(8,128)(2,1)} %copy-done.56, bf16[256,2048]{1,0:T(8,128)(2,1)} %copy-done.85, bf16[256,2048]{1,0:T(8,128)(2,1)} %copy-done.55, bf16[256,2048]{1,0:T(8,128)(2,1)} %copy-done.37), kind=kOutput, calls=%fused_computation.72 | convolution fusion | flops 8610906112 | bytes 16777216 | tf_op jit(solution)/shard_map/dot_general | solution.py:25
  663.6 14.1 %convolution_convert_fusion.1 = bf16[2048,2048]{1,0:T(8,128)(2,1)} fusion(bf16[1024,2048]{1,0:T(8,128)(2,1)} %get-tuple-element.395, bf16[256,2048]{1,0:T(8,128)(2,1)} %copy-done.56, bf16[256,2048]{1,0:T(8,128)(2,1)} %copy-done.85, bf16[256,2048]{1,0:T(8,128)(2,1)} %copy-done.55, bf16[256,2048]{1,0:T(8,128)(2,1)} %copy-done.37), kind=kOutput, calls=%fused_computation.71 | convolution fusion | flops 8610906112 | bytes 16777216 | tf_op jit(solution)/shard_map/dot_general | solution.py:25
  677.8 14.6 %fusion.128 = f32[1024,2048]{1,0:T(8,128)} fusion(bf16[1024,2048]{1,0:T(8,128)(2,1)} %get-tuple-element.396, bf16[2048,2048]{1,0:T(8,128)(2,1)} %all-gather.10.cloned.1.call-done), kind=kOutput, calls=%fused_computation.263 | convolution fusion | flops 8589934592 | bytes 20971520 | tf_op jit(solution)/shard_map/dot_general | solution.py:19
  692.4 15.3 %fusion.126 = (bf16[1024,2048]{1,0:T(8,128)(2,1)}, f32[1024,2048]{1,0:T(8,128)S(1)}) fusion(f32[1024,2048]{1,0:T(8,128)} %fusion.128, bf16[1024,2048]{1,0:T(8,128)(2,1)} %get-tuple-element.395, bf16[2048,2048]{1,0:T(8,128)(2,1)} %all-gather.12.cloned.1.call-done), kind=kOutput, calls=%fused_computation.261 | convolution fusion | flops 8594128896 | bytes 33554432 | tf_op jit(solution)/shard_map/dot_general | solution.py:19
  718.0 14.4 %collective-permute-done.26 = bf16[256,2048]{1,0:T(8,128)(2,1)S(1)} collective-permute-done((bf16[256,2048]{1,0:T(8,128)(2,1)S(1)}, bf16[256,2048]{1,0:T(8,128)(2,1)S(1)}, u32[]{:S(2)}, u32[]{:S(2)}) %collective-permute-start.26) | collective-permute-done | bytes 1048608 | tf_op jit(solution)/shard_map/ppermute | solution.py:78
  732.7 20.5 %collective-permute-start.27 = (bf16[256,2048]{1,0:T(8,128)(2,1)S(1)}, bf16[256,2048]{1,0:T(8,128)(2,1)S(1)}, u32[]{:S(2)}, u32[]{:S(2)}) collective-permute-start(bf16[256,2048]{1,0:T(8,128)(2,1)S(1)} %fusion.60), channel_id=1, source_target_pairs={{0,2},{1,3},{2,0},{3,1},{4,6},{5,7},{6,4},{7,5},{8,10},{9,11},{10,... | collective-permute-start | bytes 3145736 | tf_op jit(solution)/shard_map/ppermute | solution.py:82
  753.3 41.3 %collective-permute-done.27 = bf16[256,2048]{1,0:T(8,128)(2,1)S(1)} collective-permute-done((bf16[256,2048]{1,0:T(8,128)(2,1)S(1)}, bf16[256,2048]{1,0:T(8,128)(2,1)S(1)}, u32[]{:S(2)}, u32[]{:S(2)}) %collective-permute-start.27) | collective-permute-done | bytes 1048608 | tf_op jit(solution)/shard_map/ppermute | solution.py:82
  800.3 15.9 %collective-permute-start.31 = (bf16[256,2048]{1,0:T(8,128)(2,1)}, bf16[256,2048]{1,0:T(8,128)(2,1)}, u32[]{:S(2)}, u32[]{:S(2)}) collective-permute-start(bf16[256,2048]{1,0:T(8,128)(2,1)} %get-tuple-element.413), channel_id=1, source_target_pairs={{0,1},{1,2},{2,3},{4,5},{5,6},{6,7},{8,9},{9,10},{10,11},{12,13},{... | collective-permute-start | bytes 3145736 | tf_op jit(solution)/shard_map/ppermute | solution.py:64
  816.2 27.1 %collective-permute-done.28 = bf16[256,2048]{1,0:T(8,128)(2,1)} collective-permute-done((bf16[256,2048]{1,0:T(8,128)(2,1)}, bf16[256,2048]{1,0:T(8,128)(2,1)}, u32[]{:S(2)}, u32[]{:S(2)}) %collective-permute-start.28) | collective-permute-done | bytes 1048608 | tf_op jit(solution)/shard_map/ppermute | solution.py:62
  844.6 13.9 %convolution_convert_fusion = bf16[2048,2048]{1,0:T(8,128)(2,1)} fusion(bf16[1024,2048]{1,0:T(8,128)(2,1)} %get-tuple-element.455, bf16[256,2048]{1,0:T(8,128)(2,1)} %get-tuple-element.426, bf16[256,2048]{1,0:T(8,128)(2,1)} %copy-done.86, bf16[256,2048]{1,0:T(8,128)(2,1)} %get-tuple-element.425, bf16[256,2048]{1,0:T(8,128)(2,1)S(1)} %copy-done.51), kind=kOutput, calls=%fused_computation.70 | convolution fusion | flops 8610906112 | bytes 16777216 | tf_op jit(solution)/shard_map/dot_general | solution.py:25
  870.8 43.6 %while.29 = (s32[]{:T(128)}, f32[1024,4,128]{0,2,1:T(8,128)S(1)}, f32[1024,4,128]{0,2,1:T(8,128)}, bf16[2,512,4,128]{3,1,0,2:T(8,128)(2,1)}, bf16[2,512,4,128]{3...) while((s32[]{:T(128)}, f32[1024,4,128]{0,2,1:T(8,128)S(1)}, ...), condition=%wide.region_12.13_spmd.clone, body=%wide.region_10.12_spmd.clone.sunk | while | flops 2720540672 | bytes 206127696 | solution.py:174
  1030.9 59.4 %collective-permute-done.41 = f32[4,2048]{1,0:T(4,128)S(1)} collective-permute-done((f32[4,2048]{1,0:T(4,128)S(1)}, f32[4,2048]{1,0:T(4,128)S(1)}, u32[]{:S(2)}, u32[]{:S(2)}) %collective-permute-start.41) | collective-permute-done | bytes 32800 | tf_op jit(solution)/shard_map/ppermute | solution.py:100
  (495 shorter events, 419.3 us)
Async XLA Ops:
  7.2 206.7 %all-gather.6.cloned.1.call-start = ((), (), s32[]{:S(2)}) async-start(), calls=%async_computation.13 | async-start | bytes 7077888 | tf_op jit(solution)/shard_map/all_gather | solution.py:110
  37.6 238.4 %all-gather.8.cloned.1.call-start = ((), (), s32[]{:S(2)}) async-start(), calls=%async_computation.14 | async-start | bytes 2359296 | tf_op jit(solution)/shard_map/all_gather | solution.py:110
  39.2 385.8 %all-gather.10.cloned.1.call-start = ((), (), s32[]{:S(2)}) async-start(), calls=%async_computation.15 | async-start | bytes 9437184 | tf_op jit(solution)/shard_map/all_gather | solution.py:110
  87.1 360.2 %all-gather.12.cloned.1.call-start = ((), (), s32[]{:S(2)}) async-start(), calls=%async_computation.16 | async-start | bytes 9437184 | tf_op jit(solution)/shard_map/all_gather | solution.py:110
  118.9 59.3 %collective-permute-start = (bf16[256,2048]{1,0:T(8,128)(2,1)S(1)}, bf16[256,2048]{1,0:T(8,128)(2,1)}, u32[]{:S(2)}, u32[]{:S(2)}) collective-permute-start(bf16[256,2048]{1,0:T(8,128)(2,1)S(1)} %bitcast.277), channel_id=1, source_target_pairs={{2,0},{3,1},{0,2},{1,3},{6,4},{7,5},{4,6},{5,7},{10,8},{11,9},{8,1... | collective-permute-start | bytes 3145736 | tf_op jit(solution)/shard_map/ppermute | solution.py:62
  121.3 68.0 %all-to-all-start.3 = ((bf16[4,64,2048]{2,1,0:T(8,128)(2,1)}), bf16[4,64,2048]{2,1,0:T(8,128)(2,1)S(1)}, u32[]{:S(2)}, u32[]{:S(2)}) async-start(bf16[4,64,2048]{2,1,0:T(8,128)(2,1)} %copy.155), calls=%async_computation.3 | async-start | bytes 2097152 | tf_op jit(solution)/shard_map/all_to_all | solution.py:106
  125.5 341.2 %all-gather.14.cloned.1.call-start = ((), (), s32[]{:S(2)}) async-start(), calls=%async_computation.17 | async-start | bytes 9437184 | tf_op jit(solution)/shard_map/all_gather | solution.py:110
  125.5 64.9 %collective-permute-start.2 = (bf16[256,2048]{1,0:T(8,128)(2,1)S(1)}, bf16[256,2048]{1,0:T(8,128)(2,1)S(1)}, u32[]{:S(2)}, u32[]{:S(2)}) collective-permute-start(bf16[256,2048]{1,0:T(8,128)(2,1)S(1)} %bitcast.278), channel_id=1, source_target_pairs={{1,0},{2,1},{3,2},{5,4},{6,5},{7,6},{9,8},{10,9},{11,10},{13,12},{... | collective-permute-start | bytes 3145736 | tf_op jit(solution)/shard_map/ppermute | solution.py:63
  126.8 63.7 %collective-permute-start.3 = (bf16[256,2048]{1,0:T(8,128)(2,1)S(1)}, bf16[256,2048]{1,0:T(8,128)(2,1)}, u32[]{:S(2)}, u32[]{:S(2)}) collective-permute-start(bf16[256,2048]{1,0:T(8,128)(2,1)S(1)} %bitcast.279), channel_id=1, source_target_pairs={{0,1},{1,2},{2,3},{4,5},{5,6},{6,7},{8,9},{9,10},{10,11},{12,13},{... | collective-permute-start | bytes 3145736 | tf_op jit(solution)/shard_map/ppermute | solution.py:64
  190.4 770.6 %reduce-scatter.10.cloned.1.call-start = ((), (), s32[]{:S(2)}) async-start(), calls=%async_computation.20 | async-start | bytes 9437184 | tf_op jit(solution)/shard_map/reduce_scatter | solution.py:114
  285.3 44.9 %collective-permute-start.9 = (bf16[256,2048]{1,0:T(8,128)(2,1)S(1)}, bf16[256,2048]{1,0:T(8,128)(2,1)S(1)}, u32[]{:S(2)}, u32[]{:S(2)}) collective-permute-start(bf16[256,2048]{1,0:T(8,128)(2,1)S(1)} %get-tuple-element.412), channel_id=1, source_target_pairs={{1,0},{2,1},{3,2},{5,4},{6,5},{7,6},{9,8},{10,9},{11,10},{13,12},{... | collective-permute-start | bytes 3145736 | tf_op jit(solution)/shard_map/ppermute | solution.py:80
  286.6 44.7 %collective-permute-start.8 = (bf16[256,2048]{1,0:T(8,128)(2,1)S(1)}, bf16[256,2048]{1,0:T(8,128)(2,1)S(1)}, u32[]{:S(2)}, u32[]{:S(2)}) collective-permute-start(bf16[256,2048]{1,0:T(8,128)(2,1)S(1)} %get-tuple-element.410), channel_id=1, source_target_pairs={{0,1},{1,2},{2,3},{4,5},{5,6},{6,7},{8,9},{9,10},{10,11},{12,13},{... | collective-permute-start | bytes 3145736 | tf_op jit(solution)/shard_map/ppermute | solution.py:79
  309.1 44.5 %collective-permute-start.11 = (bf16[256,2048]{1,0:T(8,128)(2,1)S(1)}, bf16[256,2048]{1,0:T(8,128)(2,1)S(1)}, u32[]{:S(2)}, u32[]{:S(2)}) collective-permute-start(bf16[256,2048]{1,0:T(8,128)(2,1)S(1)} %fusion.66), channel_id=1, source_target_pairs={{0,2},{1,3},{2,0},{3,1},{4,6},{5,7},{6,4},{7,5},{8,10},{9,11},{10,... | collective-permute-start | bytes 3145736 | tf_op jit(solution)/shard_map/ppermute | solution.py:82
  356.1 47.7 %collective-permute-start.12 = (bf16[256,2048]{1,0:T(8,128)(2,1)S(1)}, bf16[256,2048]{1,0:T(8,128)(2,1)S(1)}, u32[]{:S(2)}, u32[]{:S(2)}) collective-permute-start(bf16[256,2048]{1,0:T(8,128)(2,1)S(1)} %fusion.75), channel_id=1, source_target_pairs={{2,0},{3,1},{0,2},{1,3},{6,4},{7,5},{4,6},{5,7},{10,8},{11,9},{8,1... | collective-permute-start | bytes 3145736 | tf_op jit(solution)/shard_map/ppermute | solution.py:62
  356.3 48.7 %collective-permute-start.14 = (bf16[256,2048]{1,0:T(8,128)(2,1)S(1)}, bf16[256,2048]{1,0:T(8,128)(2,1)S(1)}, u32[]{:S(2)}, u32[]{:S(2)}) collective-permute-start(bf16[256,2048]{1,0:T(8,128)(2,1)S(1)} %fusion.75), channel_id=1, source_target_pairs={{1,0},{2,1},{3,2},{5,4},{6,5},{7,6},{9,8},{10,9},{11,10},{13,12},{... | collective-permute-start | bytes 3145736 | tf_op jit(solution)/shard_map/ppermute | solution.py:63
  357.6 47.5 %collective-permute-start.15 = (bf16[256,2048]{1,0:T(8,128)(2,1)S(1)}, bf16[256,2048]{1,0:T(8,128)(2,1)S(1)}, u32[]{:S(2)}, u32[]{:S(2)}) collective-permute-start(bf16[256,2048]{1,0:T(8,128)(2,1)S(1)} %fusion.75), channel_id=1, source_target_pairs={{0,1},{1,2},{2,3},{4,5},{5,6},{6,7},{8,9},{9,10},{10,11},{12,13},{... | collective-permute-start | bytes 3145736 | tf_op jit(solution)/shard_map/ppermute | solution.py:64
  504.8 49.9 %collective-permute-start.19 = (bf16[256,2048]{1,0:T(8,128)(2,1)S(1)}, bf16[256,2048]{1,0:T(8,128)(2,1)S(1)}, u32[]{:S(2)}, u32[]{:S(2)}) collective-permute-start(bf16[256,2048]{1,0:T(8,128)(2,1)S(1)} %fusion.63), channel_id=1, source_target_pairs={{0,2},{1,3},{2,0},{3,1},{4,6},{5,7},{6,4},{7,5},{8,10},{9,11},{10,... | collective-permute-start | bytes 3145736 | tf_op jit(solution)/shard_map/ppermute | solution.py:82
  557.3 49.6 %collective-permute-start.20 = (bf16[256,2048]{1,0:T(8,128)(2,1)S(1)}, bf16[256,2048]{1,0:T(8,128)(2,1)S(1)}, u32[]{:S(2)}, u32[]{:S(2)}) collective-permute-start(bf16[256,2048]{1,0:T(8,128)(2,1)S(1)} %fusion.49), channel_id=1, source_target_pairs={{2,0},{3,1},{0,2},{1,3},{6,4},{7,5},{4,6},{5,7},{10,8},{11,9},{8,1... | collective-permute-start | bytes 3145736 | tf_op jit(solution)/shard_map/ppermute | solution.py:62
  557.4 58.5 %collective-permute-start.22 = (bf16[256,2048]{1,0:T(8,128)(2,1)S(1)}, bf16[256,2048]{1,0:T(8,128)(2,1)S(1)}, u32[]{:S(2)}, u32[]{:S(2)}) collective-permute-start(bf16[256,2048]{1,0:T(8,128)(2,1)S(1)} %fusion.49), channel_id=1, source_target_pairs={{1,0},{2,1},{3,2},{5,4},{6,5},{7,6},{9,8},{10,9},{11,10},{13,12},{... | collective-permute-start | bytes 3145736 | tf_op jit(solution)/shard_map/ppermute | solution.py:63
  558.7 57.2 %collective-permute-start.23 = (bf16[256,2048]{1,0:T(8,128)(2,1)S(1)}, bf16[256,2048]{1,0:T(8,128)(2,1)S(1)}, u32[]{:S(2)}, u32[]{:S(2)}) collective-permute-start(bf16[256,2048]{1,0:T(8,128)(2,1)S(1)} %fusion.49), channel_id=1, source_target_pairs={{0,1},{1,2},{2,3},{4,5},{5,6},{6,7},{8,9},{9,10},{10,11},{12,13},{... | collective-permute-start | bytes 3145736 | tf_op jit(solution)/shard_map/ppermute | solution.py:64
  663.4 319.4 %reduce-scatter.12.cloned.1.call-start = ((), (), s32[]{:S(2)}) async-start(), calls=%async_computation.21 | async-start | bytes 9437184 | tf_op jit(solution)/shard_map/reduce_scatter | solution.py:114
  677.7 348.9 %reduce-scatter.14.cloned.1.call-start = ((), (), s32[]{:S(2)}) async-start(), calls=%async_computation.22 | async-start | bytes 9437184 | tf_op jit(solution)/shard_map/reduce_scatter | solution.py:114
  732.7 61.8 %collective-permute-start.27 = (bf16[256,2048]{1,0:T(8,128)(2,1)S(1)}, bf16[256,2048]{1,0:T(8,128)(2,1)S(1)}, u32[]{:S(2)}, u32[]{:S(2)}) collective-permute-start(bf16[256,2048]{1,0:T(8,128)(2,1)S(1)} %fusion.60), channel_id=1, source_target_pairs={{0,2},{1,3},{2,0},{3,1},{4,6},{5,7},{6,4},{7,5},{8,10},{9,11},{10,... | collective-permute-start | bytes 3145736 | tf_op jit(solution)/shard_map/ppermute | solution.py:82
  799.0 60.0 %collective-permute-start.30 = (bf16[256,2048]{1,0:T(8,128)(2,1)}, bf16[256,2048]{1,0:T(8,128)(2,1)}, u32[]{:S(2)}, u32[]{:S(2)}) collective-permute-start(bf16[256,2048]{1,0:T(8,128)(2,1)} %get-tuple-element.413), channel_id=1, source_target_pairs={{1,0},{2,1},{3,2},{5,4},{6,5},{7,6},{9,8},{10,9},{11,10},{13,12},{... | collective-permute-start | bytes 3145736 | tf_op jit(solution)/shard_map/ppermute | solution.py:63
  800.3 58.7 %collective-permute-start.31 = (bf16[256,2048]{1,0:T(8,128)(2,1)}, bf16[256,2048]{1,0:T(8,128)(2,1)}, u32[]{:S(2)}, u32[]{:S(2)}) collective-permute-start(bf16[256,2048]{1,0:T(8,128)(2,1)} %get-tuple-element.413), channel_id=1, source_target_pairs={{0,1},{1,2},{2,3},{4,5},{5,6},{6,7},{8,9},{9,10},{10,11},{12,13},{... | collective-permute-start | bytes 3145736 | tf_op jit(solution)/shard_map/ppermute | solution.py:64
  858.6 242.7 %reduce-scatter.8.cloned.1.call-start = ((), (), s32[]{:S(2)}) async-start(), calls=%async_computation.19 | async-start | bytes 2359296 | tf_op jit(solution)/shard_map/reduce_scatter | solution.py:114
  930.8 177.2 %reduce-scatter.6.cloned.1.call-start = ((), (), s32[]{:S(2)}) async-start(), calls=%async_computation.18 | async-start | bytes 7077888 | tf_op jit(solution)/shard_map/reduce_scatter | solution.py:114
  989.3 113.5 %collective-permute-start.36 = (bf16[256,2048]{1,0:T(8,128)(2,1)}, bf16[256,2048]{1,0:T(8,128)(2,1)}, u32[]{:S(2)}, u32[]{:S(2)}) collective-permute-start(bf16[256,2048]{1,0:T(8,128)(2,1)} %get-tuple-element.403), channel_id=1, source_target_pairs={{1,0},{2,1},{3,2},{5,4},{6,5},{7,6},{9,8},{10,9},{11,10},{13,12},{... | collective-permute-start | bytes 3145736 | tf_op jit(solution)/shard_map/ppermute | solution.py:80
  990.6 112.3 %collective-permute-start.35 = (bf16[256,2048]{1,0:T(8,128)(2,1)}, bf16[256,2048]{1,0:T(8,128)(2,1)}, u32[]{:S(2)}, u32[]{:S(2)}) collective-permute-start(bf16[256,2048]{1,0:T(8,128)(2,1)} %get-tuple-element.401), channel_id=1, source_target_pairs={{0,1},{1,2},{2,3},{4,5},{5,6},{6,7},{8,9},{9,10},{10,11},{12,13},{... | collective-permute-start | bytes 3145736 | tf_op jit(solution)/shard_map/ppermute | solution.py:79
  1009.4 93.5 %collective-permute-start.38 = (bf16[256,2048]{1,0:T(8,128)(2,1)}, bf16[256,2048]{1,0:T(8,128)(2,1)}, u32[]{:S(2)}, u32[]{:S(2)}) collective-permute-start(bf16[256,2048]{1,0:T(8,128)(2,1)} %fusion.55), channel_id=1, source_target_pairs={{0,2},{1,3},{2,0},{3,1},{4,6},{5,7},{6,4},{7,5},{8,10},{9,11},{10,... | collective-permute-start | bytes 3145736 | tf_op jit(solution)/shard_map/ppermute | solution.py:82
  1023.2 67.2 %collective-permute-start.41 = (f32[4,2048]{1,0:T(4,128)S(1)}, f32[4,2048]{1,0:T(4,128)S(1)}, u32[]{:S(2)}, u32[]{:S(2)}) collective-permute-start(f32[4,2048]{1,0:T(4,128)S(1)} %fusion.109), channel_id=1, source_target_pairs={{0,2},{1,3},{2,0},{3,1},{4,6},{5,7},{6,4},{7,5},{8,10},{9,11},{10,... | collective-permute-start | bytes 98312 | tf_op jit(solution)/shard_map/ppermute | solution.py:100
  1026.7 81.3 %all-to-all-start.7 = ((bf16[4,64,2048]{2,1,0:T(8,128)(2,1)}), bf16[4,64,2048]{2,1,0:T(8,128)(2,1)}, u32[]{:S(2)}, u32[]{:S(2)}) async-start(bf16[4,64,2048]{2,1,0:T(8,128)(2,1)} %bitcast.287), calls=%async_computation.12 | async-start | bytes 2097152 | tf_op jit(solution)/shard_map/all_to_all | solution.py:106
  (133 other events, 2179.5 us)
Sparse Core Ops, SparseCore 0:
  37.7 50.0 all-gather.5
  90.3 27.8 all-gather.7
  120.1 54.3 all-gather.9
  176.2 54.3 all-gather.11
  232.4 54.3 all-gather.13
  663.5 84.0 reduce-scatter.9
  751.5 71.2 reduce-scatter.11
  858.7 72.2 reduce-scatter.13
  934.7 45.2 reduce-scatter.7
  983.2 61.7 reduce-scatter.5

commit v2 on v1

v2 whole, which is shorter than its diff:
```python
import functools

import jax
import jax.numpy as jnp
from jax import lax
from jax.experimental import pallas as pl
from jax.experimental.pallas import tpu as pltpu
from jax.sharding import PartitionSpec as P

HD = 128
EPSILON = 1e-06
ROPE_BASE = 500000.0
MASKED = -1e30
LOG2E = 1.4426950408889634
BF = jnp.bfloat16
F32 = jnp.float32


def project(left, weight):
    return jnp.dot(left, weight, preferred_element_type=F32)


def back_project(grad_in, weight):
    return lax.dot_general(
        grad_in, weight, (((grad_in.ndim - 1,), (1,)), ((), ())), preferred_element_type=F32
    )


def rows_product(left, right):
    return lax.dot_general(left, right, (((0,), (0,)), ((), ())), preferred_element_type=F32)


def inv_rms(values):
    return lax.rsqrt(jnp.mean(values * values, axis=-1, keepdims=True) + EPSILON)


def rms_back(normed, factor, gain, grad):
    scaled = grad * gain
    inner = jnp.mean(scaled * normed, axis=-1, keepdims=True)
    return (scaled - normed * inner) * factor


def rope_tables(positions):
    half_dim = HD // 2
    frequency = jnp.power(F32(ROPE_BASE), -jnp.arange(half_dim, dtype=F32) * (2.0 / HD))
    angles = positions[:, None] * frequency[None, :]
    cosine, sine = jnp.cos(angles), jnp.sin(angles)
    return (jnp.concatenate([cosine, cosine], axis=-1), jnp.concatenate([-sine, sine], axis=-1))


def shift(values, count, step):
    return lax.ppermute(values, "seq", [((i + step) % count, i) for i in range(count)])


def gather_cyclic(values, count):
    if count != 4:
        return [values] + [shift(values, count, p) for p in range(1, count)]
    me = lax.axis_index("seq")
    far = lax.ppermute(values, "seq", [(i ^ 2, i) for i in range(4)])
    after = lax.ppermute(values, "seq", [(i + 1, i) for i in range(3)])
    before = lax.ppermute(values, "seq", [(i, i + 1) for i in range(3)])
    ends = lax.ppermute(far, "seq", [(2, 3), (1, 0)])
    return [values, jnp.where(me == 3, ends, after), far, jnp.where(me == 0, ends, before)]


def scatter_start(after, before, count):
    me = lax.axis_index("seq")
    ends = lax.ppermute(jnp.where(me == 0, before, after), "seq", [(0, 1), (count - 1, count - 2)])
    step = [(i, i + 1) for i in range(count - 1)]
    after = lax.ppermute(after, "seq", step)
    before = lax.ppermute(before, "seq", [(j, i) for i, j in step])
    return [ends, after, before]


def scatter_far(far, ends, count):
    far_sum = (far + ends.astype(F32)).astype(BF)
    return lax.ppermute(far_sum, "seq", [(i, i ^ 2) for i in range(count)])


def scatter_end(own, got):
    for part in got:
        own = own + part.astype(F32)
    return own


def sum_stats(stats, count):
    total = stats
    for p in range(1, count):
        total = total + jnp.roll(shift(stats, count, p), p, axis=1)
    return total


def sum_everywhere(values, dp_count, seq_count):
    for name, count in (("dp", dp_count), ("seq", seq_count)):
        if count & (count - 1):
            values = lax.psum(values, name)
            continue
        bit = 1
        while bit < count:
            values = values + lax.ppermute(values, name, [(i, i ^ bit) for i in range(count)])
            bit *= 2
    return values


def swap_blocks(values):
    return lax.all_to_all(values, "seq", split_axis=0, concat_axis=0, tiled=True)


def send_columns(values, me, count):
    part = values.shape[1] // count
    columns = lambda p: lax.dynamic_slice_in_dim(values, (me + p) % count * part, part, 1)
    return [columns(0)] + [
        lax.ppermute(columns(p), "seq", [(i, (i + p) % count) for i in range(count)])
        for p in range(1, count)
    ]


def place_blocks(blocks, me, first, width, total=None):
    count = len(blocks)
    rows = blocks[0].shape[0]
    if total is None:
        total = jnp.zeros((count * rows, width), blocks[0].dtype)
    for p, block in enumerate(blocks):
        total = lax.dynamic_update_slice(total, block, ((me - p) % count * rows, first))
    return total


def send_rows(values, me, count):
    size = values.shape[0] // count
    rows = lambda p: lax.dynamic_slice_in_dim(values, (me + p) % count * size, size, 0)
    return [rows(0)] + [
        lax.ppermute(rows(p), "seq", [(i, (i + p) % count) for i in range(count)])
        for p in range(1, count)
    ]


def join_columns(blocks, me):
    count = len(blocks)
    rows, part = blocks[0].shape
    total = jnp.zeros((rows, count * part), F32)
    for p, block in enumerate(blocks):
        total = lax.dynamic_update_slice(total, block.astype(F32), (0, (me - p) % count * part))
    return total


def gather_dp(values):
    return lax.all_gather(values, "dp", axis=0, tiled=True)


def scatter_dp(values):
    return lax.psum_scatter(values, "dp", scatter_dimension=0, tiled=True)


def softmax_window(q, k_ref, seg_q, seg_row_ref, valid_from, place, tokens, count, span):
    parts = []
    for w in range(span):
        at = ((place - w) % count) * tokens
        scores = lax.dot_general(
            q, k_ref[at : at + tokens, :], (((1,), (1,)), ((), ())), preferred_element_type=F32
        )
        seg = seg_q if w == 0 else jnp.where(valid_from >= w, seg_q, -1)
        allowed = seg == seg_row_ref[:, at : at + tokens]
        if w == 0:
            rows = lax.broadcasted_iota(jnp.int32, (tokens, tokens), 0)
            cols = lax.broadcasted_iota(jnp.int32, (tokens, tokens), 1)
            allowed = allowed & (cols <= rows)
        parts.append(jnp.where(allowed, scores, MASKED))
    top = parts[0]
    for part in parts[1:]:
        top = jnp.maximum(top, part)
    top = jnp.max(top, axis=-1, keepdims=True)
    exps = [jnp.exp2((part - top) * (HD**-0.5 * LOG2E)) for part in parts]
    total = exps[0]
    for part in exps[1:]:
        total = total + part
    inverse = 1.0 / jnp.sum(total, axis=-1, keepdims=True)
    return [part * inverse for part in exps]


def turn(values, cosine, sine):
    return values * cosine + pltpu.roll(values, HD // 2, 1) * sine


def attend_kernel(
    tokens, count, span,
    me_ref, q_ref, k_ref, v_ref, f_ref, qg_ref, kg_ref, cos_ref, sin_ref, segc_ref, segr_ref,
    o_ref, qb_ref, kb_ref, vb_ref,
):
    cosine, sine = cos_ref[...], sin_ref[...]
    factors = f_ref[...]
    qb_ref[...] = turn(q_ref[...] * factors[:, 0:1] * qg_ref[...], cosine, sine).astype(BF)
    kb_ref[...] = turn(k_ref[...] * factors[:, 1:2] * kg_ref[...], cosine, sine).astype(BF)
    vb_ref[...] = v_ref[...].astype(BF)
    for place in range(count):
        rows = slice(place * tokens, (place + 1) * tokens)
        chunk = (me_ref[0] + place) % count
        probs = softmax_window(
            qb_ref[rows, :], kb_ref, segc_ref[rows, :], segr_ref, chunk, place, tokens, count, span
        )
        mixed = None
        for w in range(span):
            at = ((place - w) % count) * tokens
            part = jnp.dot(probs[w].astype(BF), vb_ref[at : at + tokens, :], preferred_element_type=F32)
            mixed = part if mixed is None else mixed + part
        o_ref[rows, :] = mixed.astype(BF)


def attend_back_kernel(
    tokens, count, span, me_ref, *refs
):
    grads_in = refs[:count]
    (q_ref, k_ref, v_ref, qp_ref, kp_ref, f_ref, qg_ref, kg_ref, cos_ref, sin_ref, segc_ref, segr_ref,
     dq_ref, dk_ref, dv_ref, inner_ref, gain_ref, dk_sum, dv_sum) = refs[count:]
    scale = HD**-0.5
    dk_sum[...] = jnp.zeros_like(dk_sum)
    dv_sum[...] = jnp.zeros_like(dv_sum)
    for place in range(count):
        rows = slice(place * tokens, (place + 1) * tokens)
        chunk = (me_ref[0] + place) % count
        q = q_ref[rows, :]
        grad = grads_in[place][...]
        probs = softmax_window(
            q, k_ref, segc_ref[rows, :], segr_ref, chunk, place, tokens, count, span
        )
        grads = []
        inner = None
        for w in range(span):
            at = ((place - w) % count) * tokens
            part = nt_dot(grad, v_ref[at : at + tokens, :])
            grads.append(part)
            inner = probs[w] * part if inner is None else inner + probs[w] * part
            dv_sum[at : at + tokens, :] += lax.dot_general(
                probs[w].astype(BF), grad, (((0,), (0,)), ((), ())), preferred_element_type=F32
            )
        inner = jnp.sum(inner, axis=-1, keepdims=True)
        dq = None
        for w in range(span):
            at = ((place - w) % count) * tokens
            ds = (probs[w] * (grads[w] - inner)).astype(BF)
            part = jnp.dot(ds, k_ref[at : at + tokens, :], preferred_element_type=F32)
            dq = part if dq is None else dq + part
            dk_sum[at : at + tokens, :] += lax.dot_general(
                ds, q, (((0,), (0,)), ((), ())), preferred_element_type=F32
            )
        dq_ref[rows, :] = dq
    ones = jnp.ones((8, HD), F32)
    first = pl.program_id(0) == 0
    sides = ((dq_ref, dq_ref, qp_ref, qg_ref), (dk_sum, dk_ref, kp_ref, kg_ref))
    for j, (raw_ref, out_ref, proj_ref, g_ref) in enumerate(sides):
        raw = (raw_ref[...] * scale).astype(BF).astype(F32)
        back = turn(raw, cos_ref[...], -sin_ref[...])
        normed = proj_ref[...] * f_ref[:, j : j + 1]
        gain_ref[j] = jnp.broadcast_to(jnp.sum(back * normed, axis=0, keepdims=True), (8, HD))
        back = back * g_ref[...]
        out_ref[...] = back
        sums = lax.dot_general(
            ones, back * normed, (((1,), (1,)), ((), ())),
            precision=lax.Precision.HIGHEST, preferred_element_type=F32,
        )
        inner_ref[j] = jnp.where(first, sums, inner_ref[j] + sums)
    dv_ref[...] = dv_sum[...].astype(BF)


def attend_specs(length, heads):
    head = lambda j: pl.BlockSpec((length, HD), lambda h, me: (0, j * heads + h))
    whole = lambda *shape: pl.BlockSpec(shape, lambda h, me: (0, 0))
    gain = pl.BlockSpec((1, HD), lambda h, me: (0, h))
    return head, whole, gain


def attend(me, qkv, factors, q_gain, k_gain, tables, seg, count):
    length = qkv.shape[0]
    part = qkv.shape[1] // 3
    heads = part // HD
    tokens = length // count
    span = min(count, (length // 2 - 1 + tokens - 1) // tokens + 1)
    head, whole, gain = attend_specs(length, heads)
    low = jax.ShapeDtypeStruct((length, part), BF)
    return pl.pallas_call(
        functools.partial(attend_kernel, tokens, count, span),
        grid_spec=pltpu.PrefetchScalarGridSpec(
            num_scalar_prefetch=1,
            grid=(heads,),
            in_specs=[head(0), head(1), head(2), whole(length, 2), gain, gain]
            + [whole(length, HD)] * 2
            + [whole(length, 1), whole(1, length)],
            out_specs=[head(0)] * 4,
        ),
        out_shape=[low] * 4,
        compiler_params=params(),
        cost_estimate=cost(4 * length * length * part, 16 << 20, length * length * heads),
        name="attend",
    )(me, qkv, qkv, qkv, factors, q_gain[None], k_gain[None], *tables, seg[:, None], seg[None])


def attend_back(me, pieces, query, key, value, qkv, factors, q_gain, k_gain, tables, seg, count):
    length, part = query.shape
    heads = part // HD
    tokens = length // count
    span = min(count, (length // 2 - 1 + tokens - 1) // tokens + 1)
    head, whole, gain = attend_specs(length, heads)
    return pl.pallas_call(
        functools.partial(attend_back_kernel, tokens, count, span),
        grid_spec=pltpu.PrefetchScalarGridSpec(
            num_scalar_prefetch=1,
            grid=(heads,),
            in_specs=[pl.BlockSpec((tokens, HD), lambda h, me: (0, h))] * count
            + [head(0)] * 3
            + [head(0), head(1), whole(length, 2), gain, gain]
            + [whole(length, HD)] * 2
            + [whole(length, 1), whole(1, length)],
            out_specs=[head(0)] * 3
            + [
                pl.BlockSpec((2, 8, length), lambda h, me: (0, 0, 0)),
                pl.BlockSpec((2, 8, HD), lambda h, me: (0, 0, h)),
            ],
            scratch_shapes=[pltpu.VMEM((length, HD), F32)] * 2,
        ),
        out_shape=[jax.ShapeDtypeStruct((length, part), t) for t in (F32, F32, BF)]
        + [jax.ShapeDtypeStruct((2, 8, m), F32) for m in (length, part)],
        compiler_params=params(),
        cost_estimate=cost(10 * length * length * part, 24 << 20, length * length * heads),
        name="attend_back",
    )(me, *pieces, query, key, value, qkv, qkv, factors, q_gain[None], k_gain[None], *tables,
      seg[:, None], seg[None])


def mixed_back_kernel(me_ref, d_ref, w_ref, *refs):
    for p, out in enumerate(refs):

        @pl.when(pl.program_id(0) == p)
        def _(out=out):
            out[...] = nt_dot(d_ref[...], w_ref[...]).astype(BF)


def mixed_back(me, d_attn, w_first, count):
    tokens, width = d_attn.shape
    part = width // count
    piece = pl.BlockSpec((tokens, part), lambda p, me: (0, 0))
    return pl.pallas_call(
        mixed_back_kernel,
        grid_spec=pltpu.PrefetchScalarGridSpec(
            num_scalar_prefetch=1,
            grid=(count,),
            in_specs=[
                pl.BlockSpec((tokens, width), lambda p, me: (0, 0)),
                pl.BlockSpec((part, width), lambda p, me: ((me[0] + p) % count, 0)),
            ],
            out_specs=[piece] * count,
        ),
        out_shape=[jax.ShapeDtypeStruct((tokens, part), BF)] * count,
        compiler_params=params(),
        cost_estimate=cost(2 * tokens * width * width, 10 << 20),
        name="mixed_back",
    )(me, d_attn, w_first)


def input_back_kernel(part, order, q_ref, k_ref, v_ref, qp_ref, kp_ref, in_ref, f_ref, w_ref, d_ref, *outs):
    for j, (grad, proj) in enumerate(((q_ref, qp_ref), (k_ref, kp_ref))):
        factor = f_ref[:, j : j + 1]
        normed = proj[...] * factor
        low = ((grad[...] - normed * in_ref[:, j : j + 1]) * factor).astype(BF)
        d_ref[:, j * part : (j + 1) * part] = low
    d_ref[:, 2 * part :] = v_ref[...]
    total = nt_dot(d_ref[...], w_ref[...])
    for step, out in enumerate(outs):

        @pl.when(pl.program_id(0) == step)
        def _(out=out):
            out[...] = total.astype(out.dtype)


def input_back(d_query, d_key, d_v, qkv, inner, factors, w_qkv, count):
    length, part = d_query.shape
    width = w_qkv.shape[0]
    tokens = length // count
    place = lambda t: jnp.where(t == 0, 1, jnp.where(t == 1, 3, jnp.where(t == 2, 2, 0)))
    rows = lambda columns, at=0: pl.BlockSpec((tokens, columns), lambda t: (place(t), at))
    kinds = (BF, BF, F32, F32)
    return pl.pallas_call(
        functools.partial(input_back_kernel, part, None),
        grid=(count,),
        in_specs=[rows(part)] * 3
        + [rows(part), rows(part, 1), rows(2), rows(2)]
        + [once((width, 3 * part), lambda t: (0, 0))],
        out_specs=[rows(3 * part)] + [pl.BlockSpec((tokens, width), lambda t: (0, 0))] * count,
        out_shape=[jax.ShapeDtypeStruct((length, 3 * part), BF)]
        + [jax.ShapeDtypeStruct((tokens, width), kind) for kind in kinds],
        compiler_params=params(),
        cost_estimate=cost(6 * length * width * part, 24 << 20),
        name="input_back",
    )(d_query, d_key, d_v, qkv, qkv, inner, factors, w_qkv)


def cost(flops, moved, exps=0):
    return pl.CostEstimate(flops=flops, bytes_accessed=moved, transcendentals=exps)


def params():
    return pltpu.CompilerParams(vmem_limit_bytes=56 << 20)


def once(shape, index):
    return pl.BlockSpec(shape, index, pipeline_mode=pl.Buffered(1))


def nt_dot(left, right):
    return lax.dot_general(left, right, (((1,), (1,)), ((), ())), preferred_element_type=F32)


def qkv_kernel(count, part, me_ref, *refs):
    chunks, (w_ref, x_ref, qkv_ref, sq_ref) = refs[:-4], refs[-4:]
    ones = jnp.ones((8, part), F32)
    for q in range(count):

        @pl.when(pl.program_id(0) == q)
        def _(q=q):
            x = chunks[q][...]
            x_ref[...] = x
            qkv = jnp.dot(x, w_ref[...], preferred_element_type=F32)
            qkv_ref[...] = qkv
            for j in range(2):
                values = qkv[:, j * part : (j + 1) * part]
                sq_ref[j] = lax.dot_general(
                    ones, values * values, (((1,), (1,)), ((), ())),
                    precision=lax.Precision.HIGHEST, preferred_element_type=F32,
                )


def qkv_project(me, chunks, w_qkv):
    count = len(chunks)
    tokens, width = chunks[0].shape
    columns = w_qkv.shape[1]
    length = count * tokens
    return pl.pallas_call(
        functools.partial(qkv_kernel, count, columns // 3),
        grid_spec=pltpu.PrefetchScalarGridSpec(
            num_scalar_prefetch=1,
            grid=(count,),
            in_specs=[once((tokens, width), lambda q, me: (0, 0))] * count
            + [once((width, columns), lambda q, me: (0, 0))],
            out_specs=[
                pl.BlockSpec((tokens, width), lambda q, me: (q, 0)),
                pl.BlockSpec((tokens, columns), lambda q, me: (q, 0)),
                pl.BlockSpec((2, 8, tokens), lambda q, me: (0, 0, q)),
            ],
        ),
        out_shape=[
            jax.ShapeDtypeStruct((length, width), BF),
            jax.ShapeDtypeStruct((length, columns), F32),
            jax.ShapeDtypeStruct((2, 8, length), F32),
        ],
        compiler_params=params(),
        cost_estimate=cost(2 * length * width * columns, 20 << 20),
        name="qkv_project",
    )(me, *chunks, w_qkv)


FF_TILE = 512


def ff_finish(step, product, acc, outs):
    @pl.when(step == 0)
    def _():
        acc[...] = product

    @pl.when(step > 0)
    def _():
        acc[...] += product

    @pl.when(step == pl.num_programs(0) - 1)
    def _():
        tokens = acc.shape[0] // len(outs)
        for j, out in enumerate(outs):
            out[...] = acc[j * tokens : (j + 1) * tokens].astype(out.dtype)


def ff_kernel(saved, h_ref, wg_ref, wu_ref, wd_ref, *refs):
    gate_ref, up_ref, hid_ref = refs[saved : saved + 3]
    h = h_ref[...]
    gate = jnp.dot(h, wg_ref[...], preferred_element_type=F32)
    up = jnp.dot(h, wu_ref[...], preferred_element_type=F32)
    hidden = (gate * (1.0 / (1.0 + jnp.exp(-gate))) * up).astype(BF)
    gate_ref[...] = gate
    up_ref[...] = up
    hid_ref[...] = hidden
    ff_finish(pl.program_id(0), nt_dot(hidden, wd_ref[...]), refs[-1], refs[saved + 3 : -1])


def ff_back_kernel(saved, d_ref, wg_ref, wu_ref, wd_ref, gate_ref, up_ref, *refs):
    dgu_ref = refs[saved]
    tile = wg_ref.shape[1]
    d_hidden = jnp.dot(d_ref[...], wd_ref[...], preferred_element_type=F32)
    gate = gate_ref[...]
    sig = 1.0 / (1.0 + jnp.exp(-gate))
    d_gate = (d_hidden * up_ref[...] * sig * (1.0 + gate * (1.0 - sig))).astype(BF)
    d_up = (d_hidden * gate * sig).astype(BF)
    dgu_ref[:, :tile] = d_gate
    dgu_ref[:, tile:] = d_up
    product = nt_dot(d_gate, wg_ref[...]) + nt_dot(d_up, wu_ref[...])
    ff_finish(pl.program_id(0), product, refs[-1], refs[saved + 1 : -1])


def ff_specs(width, tile, gate_at, down_at):
    return [
        pl.BlockSpec((width, tile), lambda t: (0, gate_at // tile + t)),
        pl.BlockSpec((width, tile), lambda t: (0, t)),
        pl.BlockSpec((width, tile), lambda t: (0, down_at // tile + t)),
    ]


def ff_forward(residual_all, w_first, w_second, place, kinds, saved=()):
    length, width = residual_all.shape
    tokens = length // 4
    rows = len(kinds) * tokens
    ff_part = w_second.shape[1] // 2
    tile = min(FF_TILE, ff_part)
    block = pl.BlockSpec((rows, tile), lambda t: (place // len(kinds), t))
    whole = pl.BlockSpec((tokens, width), lambda t: (0, 0))
    shape = lambda kind: jax.ShapeDtypeStruct((length, ff_part), kind)
    return pl.pallas_call(
        functools.partial(ff_kernel, len(saved)),
        grid=(ff_part // tile,),
        in_specs=[once((rows, width), lambda t: (place // len(kinds), 0))]
        + ff_specs(width, tile, w_first.shape[1] - ff_part, ff_part)
        + [pl.BlockSpec(memory_space=pl.ANY)] * len(saved),
        out_specs=[block] * 3 + [whole] * len(kinds),
        out_shape=[shape(F32), shape(F32), shape(BF)]
        + [jax.ShapeDtypeStruct((tokens, width), kind) for kind in kinds],
        scratch_shapes=[pltpu.VMEM((rows, width), F32)],
        input_output_aliases={4 + j: j for j in range(len(saved))},
        compiler_params=params(),
        cost_estimate=cost(6 * rows * width * ff_part, 40 << 20, rows * ff_part),
        name="ff_forward",
    )(residual_all, w_first, w_second, w_second, *saved)


def ff_backward(d_ff, w_first, w_second, gate, up, place, kinds, saved=()):
    rows, width = d_ff.shape
    length = gate.shape[0]
    tokens = length // 4
    ff_part = w_second.shape[1] // 2
    tile = min(FF_TILE, ff_part)
    block = pl.BlockSpec((rows, tile), lambda t: (place // len(kinds), t))
    whole = pl.BlockSpec((tokens, width), lambda t: (0, 0))
    return pl.pallas_call(
        functools.partial(ff_back_kernel, len(saved)),
        grid=(ff_part // tile,),
        in_specs=[once((rows, width), lambda t: (0, 0))]
        + ff_specs(width, tile, w_first.shape[1] - ff_part, ff_part)
        + [block, block]
        + [pl.BlockSpec(memory_space=pl.ANY)] * len(saved),
        out_specs=[pl.BlockSpec((rows, 2 * tile), lambda t: (place // len(kinds), t))]
        + [whole] * len(kinds),
        out_shape=[jax.ShapeDtypeStruct((length, 2 * ff_part), BF)]
        + [jax.ShapeDtypeStruct((tokens, width), kind) for kind in kinds],
        scratch_shapes=[pltpu.VMEM((rows, width), F32)],
        input_output_aliases={6 + j: j for j in range(len(saved))},
        compiler_params=params(),
        cost_estimate=cost(6 * rows * width * ff_part, 40 << 20, rows * ff_part),
        name="ff_backward",
    )(d_ff, w_first, w_second, w_second, gate, up, *saved)


def out_kernel(count, part, *refs):
    me_ref, pieces, (w_ref, x_ref, g_ref, res_ref, own_ref) = refs[0], refs[1:-5], refs[-5:]
    total = None
    for p, piece in enumerate(pieces):
        rows = pl.ds(pl.multiple_of((me_ref[0] + p) % count * part, part), part)
        product = jnp.dot(piece[...], w_ref[rows, :], preferred_element_type=F32)
        total = product if total is None else total + product
    normed = total * inv_rms(total)
    res_ref[...] = (x_ref[...].astype(F32) + normed * g_ref[...]).astype(BF)

    @pl.when(pl.program_id(0) == 0)
    def _():
        own_ref[...] = total


def ff_place(q):
    return jnp.where(q == 0, 3, jnp.where(q == 3, 1, jnp.where(q == 2, 2, 0)))


def out_project(me, pieces, w_out, x_all, gain, count):
    length, width = x_all.shape
    tokens = length // count
    part = pieces[0].shape[1]
    rolled = lambda p: pl.BlockSpec((tokens, part), lambda q, me: ((q + count - p) % count, 0))
    chunk = pl.BlockSpec((tokens, width), lambda q, me: (q, 0))
    moved = pl.BlockSpec((tokens, width), lambda q, me: (ff_place(q), 0))
    return pl.pallas_call(
        functools.partial(out_kernel, count, part),
        grid_spec=pltpu.PrefetchScalarGridSpec(
            num_scalar_prefetch=1,
            grid=(count,),
            in_specs=[rolled(p) for p in range(count)]
            + [pl.BlockSpec((width, width), lambda q, me: (0, 0), pipeline_mode=pl.Buffered(1))]
            + [chunk, pl.BlockSpec((1, width), lambda q, me: (0, 0))],
            out_specs=[moved, pl.BlockSpec((tokens, width), lambda q, me: (0, 0))],
        ),
        out_shape=[
            jax.ShapeDtypeStruct((length, width), BF),
            jax.ShapeDtypeStruct((tokens, width), F32),
        ],
        compiler_params=params(),
        cost_estimate=cost(2 * length * width * width, 22 << 20),
        name="out_project",
    )(me, *pieces, w_out, x_all, gain[None])


def roll_blocks(values, first):
    n = values.shape[0]
    return lax.dynamic_slice_in_dim(jnp.concatenate([values, values]), first, n, 0)


def columns_to_parts(values, me, count):
    part = values.shape[1] // count
    columns = lambda p: lax.dynamic_slice_in_dim(values, (me + p) % count * part, part, 1)
    got = [columns(0)] + [
        lax.ppermute(columns(p), "seq", [(i, (i + p) % count) for i in range(count)])
        for p in range(1, count)
    ]
    return jnp.concatenate([got[(count - q) % count] for q in range(count)], axis=0)


def build(dp_count, seq_count):
    assert seq_count == 4

    def shards(
        layer_input,
        segments,
        w_query,
        w_key,
        w_value,
        w_output,
        w_gate,
        w_up,
        w_down,
        query_gain,
        key_gain,
        attn_gain,
        ff_gain,
        cotangent,
    ):
        n = seq_count
        tokens, width = layer_input.shape[1:]
        shard_rows = w_query.shape[0]
        part = width // n
        ff_part = w_gate.shape[1] // n
        length = n * tokens
        devices = dp_count * n
        me = lax.axis_index("seq")
        me_ref = me[None].astype(jnp.int32)
        cot = cotangent[0]
        chunks = lambda v: [v[p * tokens : (p + 1) * tokens] for p in range(n)]
        by_part = lambda w: w.reshape(shard_rows, n, -1).transpose(1, 0, 2)
        rows_of = lambda blocks: blocks.reshape(n * shard_rows, -1)

        fence = lax.optimization_barrier
        qkv_blocks = jnp.concatenate([by_part(w) for w in (w_query, w_key, w_value)], axis=2)
        qkv_blocks = swap_blocks(qkv_blocks)
        w_qkv = gather_dp(rows_of(qkv_blocks))
        qkv_blocks, w_output, w_gate, w_down_t = fence((qkv_blocks, w_output, w_gate, w_down.T))
        out_blocks = gather_cyclic(w_output, n)
        gate_blocks = send_columns(w_gate, me, n)
        out_blocks, gate_blocks, x_own = fence((out_blocks, gate_blocks, layer_input[0]))
        out_blocks = out_blocks[:1] + out_blocks[:0:-1]
        w_first = place_blocks(out_blocks, me, 0, width + ff_part)
        w_first = gather_dp(place_blocks(gate_blocks, me, width, width + ff_part, w_first))
        x_chunks, w_up = fence((gather_cyclic(x_own, n), w_up))
        up_blocks = send_columns(w_up, me, n)
        x_all, qkv, squares = qkv_project(me_ref, x_chunks, w_qkv)
        squares, up_blocks = fence((squares, up_blocks))

        natural = jnp.arange(length, dtype=jnp.int32)
        positions = (natural + me * tokens) % length
        seg_row = segments[0]
        seg = lax.dynamic_slice_in_dim(
            jnp.concatenate([seg_row, seg_row]), me * tokens, length, 0
        )
        tables = rope_tables(positions.astype(F32))
        own_gain = lambda g: lax.dynamic_slice_in_dim(g, me * part, part, 0)
        q_gain = own_gain(query_gain)
        k_gain = own_gain(key_gain)

        squares = sum_stats(squares[:, 0].reshape(2, n, tokens), n).reshape(2, length)
        squares, w_down_t = fence((squares, w_down_t))
        down_blocks = send_columns(w_down_t, me, n)
        factors = lax.rsqrt(squares / width + EPSILON).T
        mixed, q_low, k_low, v_low = attend(me_ref, qkv, factors, q_gain, k_gain, tables, seg, n)

        mixed, down_blocks = fence((mixed, down_blocks))
        w_second = place_blocks(up_blocks, me, 0, 2 * ff_part)
        w_second = gather_dp(place_blocks(down_blocks, me, ff_part, 2 * ff_part, w_second))
        pieces = gather_cyclic(mixed, n)
        residual_all, attn_out = out_project(me_ref, pieces, w_first, x_all, attn_gain, n)
        attn_factor = inv_rms(attn_out)
        attn_normed = attn_out * attn_factor
        residual = x_own.astype(F32) + attn_normed * attn_gain

        *saved, after, before, far = ff_forward(
            residual_all, w_first, w_second, 0, (BF, BF, F32)
        )
        sent = scatter_start(after, before, n)
        residual_late, first_sent = fence((residual_all, sent[0]))
        gate, up, hidden, own = ff_forward(residual_late, w_first, w_second, 3, (F32,), saved)
        ff_out = scatter_end(own, sent[1:] + [scatter_far(far, first_sent, n)])
        ff_factor = inv_rms(ff_out)
        ff_normed = ff_out * ff_factor
        activation = (residual + ff_normed * ff_gain).astype(BF)
        grad_ff_gain = jnp.sum(cot.astype(F32) * ff_normed, axis=0)
        d_ff = rms_back(ff_normed, ff_factor, ff_gain, cot.astype(F32)).astype(BF)
        d_ffs = gather_cyclic(d_ff, n)
        d_both, own = ff_backward(d_ffs[0], w_first, w_second, gate, up, 3, (F32,))
        d_ffs, d_both = fence((d_ffs, d_both))
        d_ff_near = jnp.concatenate([d_ffs[1], d_ffs[3]], axis=0)
        d_both, after, before = ff_backward(
            d_ff_near, w_first, w_second, gate, up, 0, (BF, BF), (d_both,)
        )
        after, before, d_ffs, hidden = fence((after, before, d_ffs, hidden))
        sent = scatter_start(after, before, n)
        d_ff_all = jnp.concatenate([d_ff_near, d_ffs[2], d_ffs[0]], axis=0)
        down_grad = rows_product(d_ff_all, hidden).astype(BF)
        down_rows = scatter_dp(down_grad)
        d_ff_far, down_grad = fence((d_ffs[2], down_grad))
        d_both, far = ff_backward(d_ff_far, w_first, w_second, gate, up, 2, (F32,), (d_both,))
        d_both, far, sent[0] = fence((d_both, far, sent[0]))
        sent[0] = scatter_far(far, sent[0], n)
        joined = lambda g: g.transpose(1, 0, 2).reshape(shard_rows, -1).astype(F32)
        gate_up_grad = rows_product(residual_all, d_both).astype(BF)
        gate_up_grad, sent = fence((gate_up_grad, sent))
        gate_up_rows = scatter_dp(gate_up_grad)
        d_res = cot.astype(F32) + scatter_end(own, sent)

        grad_attn_gain = jnp.sum(d_res * attn_normed, axis=0)
        d_attn = rms_back(attn_normed, attn_factor, attn_gain, d_res).astype(BF)
        d_pieces = mixed_back(me_ref, d_attn, w_first, n)
        d_mixed = [d_pieces[0]] + [None] * (n - 1)
        for p in range(1, n):
            d_mixed[n - p] = lax.ppermute(
                d_pieces[p], "seq", [(i, (i + p) % n) for i in range(n)]
            )
        d_mixed, d_attn, down_rows = fence((d_mixed, d_attn, down_rows))
        d_attn_part = columns_to_parts(d_attn, me, n)
        d_query, d_key, d_v, inner, gain_sums = attend_back(
            me_ref, d_mixed, q_low, k_low, v_low, qkv, factors, q_gain, k_gain, tables, seg, n
        )
        inner, d_attn_part = fence((inner, d_attn_part))
        inner = sum_stats(inner[:, 0].reshape(2, n, tokens), n).reshape(2, length)
        inner, down_rows = fence((inner, down_rows))
        down_back = send_rows(down_rows, me, n)
        d_qkv, after, before, far, own = input_back(
            d_query, d_key, d_v, qkv, (inner / width).T, factors, w_qkv, n
        )
        after, before, far, own, d_qkv, down_back = fence(
            (after, before, far, own, d_qkv, down_back)
        )
        sent = scatter_start(after, before, n)
        qkv_grad = rows_product(x_all, d_qkv).astype(BF)
        sent, qkv_grad = fence((sent, qkv_grad))
        sent[0] = scatter_far(far, sent[0], n)
        out_grads = [
            rows_product(piece, jnp.roll(d_attn_part, -p * tokens, axis=0)).astype(BF)
            for p, piece in enumerate(pieces)
        ]
        out_grad = roll_blocks(jnp.stack(out_grads), (n - me) % n).reshape(width, part)
        attn_grads = jnp.concatenate([qkv_grad, out_grad], axis=1)
        attn_rows = scatter_dp(attn_grads)
        input_grad = d_res + scatter_end(own, sent)
        spread = lambda g: lax.dynamic_update_slice(jnp.zeros(width, F32), g, (me * part,))
        gains = jnp.stack(
            [spread(gain_sums[0, 0]), spread(gain_sums[1, 0]), grad_attn_gain, grad_ff_gain]
        )
        input_grad, gate_up_rows, gains = fence((input_grad, gate_up_rows, gains))
        gate_up_back = send_rows(gate_up_rows, me, n)
        gains = sum_everywhere(gains, dp_count, n)
        attn_rows, input_grad, gate_up_back, down_back, gains = fence(
            (attn_rows, input_grad, gate_up_back, down_back, gains)
        )
        attn_back = swap_blocks(attn_rows.reshape(n, shard_rows, -1))
        by_tile = [b.reshape(shard_rows, -1, 2, min(FF_TILE, ff_part)) for b in gate_up_back]
        grad_gate, grad_up = (
            join_columns([b[:, :, j].reshape(shard_rows, ff_part) for b in by_tile], me)
            for j in range(2)
        )
        grad_down = join_columns(down_back, me).T
        grad_query, grad_key, grad_value, grad_output = (
            joined(attn_back[:, :, j * part : (j + 1) * part]) for j in range(4)
        )

        share = width // devices
        gains = lax.dynamic_slice_in_dim(
            gains, (lax.axis_index("dp") * n + me) * share, share, 1
        )
        return (
            activation[None],
            input_grad.astype(BF)[None],
            grad_query,
            grad_key,
            grad_value,
            grad_output,
            grad_gate,
            grad_up,
            grad_down,
            gains[0],
            gains[1],
            gains[2],
            gains[3],
        )

    return shards


def solution(mesh):
    both = P(("dp", "seq"), None)
    tokens = P("dp", "seq", None)
    columns = P(None, ("dp", "seq"))
    gain = P(("dp", "seq"))
    return jax.shard_map(
        build(mesh.shape["dp"], mesh.shape["seq"]),
        mesh=mesh,
        in_specs=(tokens, P("dp", None)) + (both,) * 6 + (columns,) + (P(),) * 4 + (tokens,),
        out_specs=(tokens, tokens) + (both,) * 6 + (columns,) + (gain,) * 4,
        check_vma=False,
    )
```

time: 1160 us -> 933 us (0.80)
  Pallas kernels: 0 us -> 202 us
  matrix products: 232 us -> 51.3 us
  starting transfers between devices: 231 us -> 126 us
  blocking collectives: 103 us -> 26.5 us
  waiting for transfers between devices: 435 us -> 393 us
    pallas_call x0 -> x11, Pallas kernels: none -> 202 us  [the longest x3 58.2 us: ff_backward(): pl.pallas_call(functools.partial(ff_back_kernel, len(saved)), grid=(ff_pa...]
    dot_general x24 -> x0, matrix products: 174 us -> none  [the longest x5 78.1 us: project(): return jnp.dot(left, weight, preferred_element_type=F32)]
    all_to_all x3 -> x1, blocking collectives: 103 us -> 26.5 us  [swap_blocks(): lax.all_to_all(values, 'seq', split_axis=0, concat_axis=0, tiled=True)]
    ppermute x4, starting transfers between devices: 86.2 us -> 20.1 us  [gather_cyclic(): before = lax.ppermute(values, 'seq', [(i, i + 1) for i in range(3)])]
    ppermute x5, waiting for transfers between devices: 76.5 us -> 42.1 us  [sum_everywhere(): lax.ppermute(values, name, [(i, i ^ bit) for i in range(count)])]
    ppermute x4, waiting for transfers between devices: 103 us -> 133 us  [gather_cyclic(): far = lax.ppermute(values, 'seq', [(i ^ 2, i) for i in range(4)])]
    all_to_all x5 -> x1, starting transfers between devices: 28.2 us -> 3.73 us  [swap_blocks(): lax.all_to_all(values, 'seq', split_axis=0, concat_axis=0, tiled=True)]
    all_to_all x5 -> x1, waiting for transfers between devices: 17.3 us -> 0.01 us  [swap_blocks(): lax.all_to_all(values, 'seq', split_axis=0, concat_axis=0, tiled=True)]
  transfers between devices with their start and end apart: 60 -> 67, of which waited for: 29 -> 26; matrix products, arithmetic and copies ran while one was open for 25% -> 13% of each run, Pallas kernels for 0% -> 16%
where the time goes in v2:
time: 933 us; the launch traced here: 927 us
  waiting for transfers between devices  393 us (42%)
  Pallas kernels  202 us (22%)
  starting transfers between devices  126 us (14%)
  other arithmetic  65.9 us (7%)
  matrix products  51.3 us (5%)
  local copies, waits for them, and re-layouts  46.4 us (5%)
  blocking collectives  26.5 us (3%)
  between operations  16.2 us (2%)
    ppermute x4, waiting for transfers between devices, gather_cyclic(): far = lax.ppermute(values, 'seq', [(i ^ 2, i) for i in range(4)])  133 us
    ppermute x3, waiting for transfers between devices, scatter_far(): return lax.ppermute(far_sum, 'seq', [(i, i ^ 2) for i in range(count)])  84.7 us
    pallas_call x3, Pallas kernels, ff_backward(): pl.pallas_call(functools.partial(ff_back_kernel, len(saved)), grid=(ff_pa...  58.2 us
    ppermute x4, waiting for transfers between devices, gather_cyclic(): ends = lax.ppermute(far, 'seq', [(2, 3), (1, 0)])  53.9 us
    dot_general x7, matrix products, rows_product(): lax.dot_general(left, right, (((0,), (0,)), ((), ())), preferred_element_...  51.3 us
    pallas_call x2, Pallas kernels, ff_forward(): pl.pallas_call(functools.partial(ff_kernel, len(saved)), grid=(ff_part //...  46.6 us
    ppermute x3, waiting for transfers between devices, scatter_start(): lax.ppermute(jnp.where(me == 0, before, after), 'seq', [(0, 1), (count -...  44 us
    ppermute x5, waiting for transfers between devices, sum_everywhere(): lax.ppermute(values, name, [(i, i ^ bit) for i in range(count)])  42.1 us
  transfers between devices with their start and end apart: 67, of which 26 were waited for; matrix products, arithmetic and copies ran while one was open for 13% of the time, Pallas kernels for 16%

profile of v2, /device:TPU:0, one launch (start us, length us, event | category | flops | bytes accessed | tf_op | source)
XLA Modules:
  0.0 926.5 jit_solution(16719040057888158196)
XLA Ops:
  9.4 26.5 %all_to_all.10 = bf16[4,64,1536]{2,1,0:T(8,128)(2,1)} all-to-all(bf16[4,64,1536]{2,1,0:T(8,128)(2,1)S(1)} %pad_maximum_fusion.3), channel_id=1, replica_groups=mesh['dp'=8,'seq'=4] {'seq'}, dimensions={0} | all-to-all | bytes 1572864 | tf_op jit(solution)/shard_map/all_to_all | solution.py:106
  41.2 7.8 collective-permute-done
  56.7 9.9 %collective-permute-done.1 = bf16[64,2048]{1,0:T(8,128)(2,1)S(1)} collective-permute-done((bf16[64,2048]{1,0:T(8,128)(2,1)S(1)}, bf16[64,2048]{1,0:T(8,128)(2,1)S(1)}, u32[]{:S(2)}, u32[]{:S(2)}) %collective-permute-start.1) | collective-permute-done | bytes 262176 | tf_op jit(solution)/shard_map/ppermute | solution.py:62
  85.2 43.3 %collective-permute-done.7.refs_2_ = bf16[256,2048]{1,0:T(8,128)(2,1)} collective-permute-done((bf16[256,2048]{1,0:T(8,128)(2,1)}, bf16[256,2048]{1,0:T(8,128)(2,1)}, u32[]{:S(2)}, u32[]{:S(2)}) %collective-permute-start.7) | collective-permute-done | bytes 1048608 | tf_op jit(solution)/shard_map/ppermute | solution.py:59
  136.8 17.1 %collective-permute-done.8 = bf16[256,2048]{1,0:T(8,128)(2,1)S(1)} collective-permute-done((bf16[256,2048]{1,0:T(8,128)(2,1)}, bf16[256,2048]{1,0:T(8,128)(2,1)S(1)}, u32[]{:S(2)}, u32[]{:S(2)}) %collective-permute-start.8) | collective-permute-done | bytes 1048608 | tf_op jit(solution)/shard_map/ppermute | solution.py:62
  159.5 16.1 %qkv_project.1 = (bf16[1024,2048]{1,0:T(8,128)(2,1)}, f32[1024,1536]{1,0:T(8,128)}, f32[2,8,1024]{2,1,0:T(8,128)}) custom-call(s32[1]{0:T(128)} %bitcast.5.me_ref.refs_0_, bf16[256,2048]{1,0:T(8,128)(2,1)} %bitcast.4.refs_0_, bf16[256,2048]{1,0:T(8,128)(2,1)} %get-tuple-element.143.refs_1_, bf16[256,2048]{1,0:T(8,128)(2,1)} %collective-permute-done.7.refs_2_, ...), custom_call_target="tpu_custom_call" | custom-call | flops 6442450944 | bytes 20971520 | tf_op jit(solution)/shard_map/qkv_project/pallas_call | solution.py:435
  198.4 16.2 %attend.1 = (bf16[1024,512]{1,0:T(8,128)(2,1)}, bf16[1024,512]{1,0:T(8,128)(2,1)}, bf16[1024,512]{1,0:T(8,128)(2,1)}, bf16[1024,512]{1,0:T(8,128)(2,1)}) custom-call(s32[1]{0:T(128)} %bitcast.5.me_ref.refs_0_, f32[1024,1536]{1,0:T(8,128)} %get-tuple-element.146.q_ref.k_ref.v_ref.refs_7_.refs_8_.qp_ref.kp_ref, ...), custom_call_target="tpu_custom_call" | custom-call | flops 2147483648 | bytes 16777216 | tf_op jit(solution)/shard_map/attend/pallas_call | solution.py:279
  224.6 41.2 %collective-permute-done.20.refs_3_ = bf16[1024,512]{1,0:T(8,128)(2,1)S(1)} collective-permute-done((bf16[1024,512]{1,0:T(8,128)(2,1)S(1)}, bf16[1024,512]{1,0:T(8,128)(2,1)S(1)}, u32[]{:S(2)}, u32[]{:S(2)}) %collective-permute-start.20) | collective-permute-done | bytes 1048608 | tf_op jit(solution)/shard_map/ppermute | solution.py:59
  267.8 22.8 %collective-permute-done.21 = bf16[1024,512]{1,0:T(8,128)(2,1)S(1)} collective-permute-done((bf16[1024,512]{1,0:T(8,128)(2,1)S(1)}, bf16[1024,512]{1,0:T(8,128)(2,1)S(1)}, u32[]{:S(2)}, u32[]{:S(2)}) %collective-permute-start.21) | collective-permute-done | bytes 1048608 | tf_op jit(solution)/shard_map/ppermute | solution.py:62
  292.2 17.6 %out_project.1 = (bf16[1024,2048]{1,0:T(8,128)(2,1)}, f32[256,2048]{1,0:T(8,128)}) custom-call(s32[1]{0:T(128)} %bitcast.5.me_ref.refs_0_, bf16[1024,512]{1,0:T(8,128)(2,1)} %get-tuple-element.154.refs_1_, bf16[1024,512]{1,0:T(8,128)(2,1)} %get-tuple-element.307.refs_2_, bf16[1024,512]{1,0:T(8,128)(2,1)} %copy-done.47, ...), custom_call_target="tpu_custom_call" | custom-call | flops 8589934592 | bytes 23068672 | tf_op jit(solution)/shard_map/out_project/pallas_call | solution.py:591
  309.8 30.9 %ff_forward.2 = (f32[1024,2048]{1,0:T(8,128)}, f32[1024,2048]{1,0:T(8,128)}, bf16[1024,2048]{1,0:T(8,128)(2,1)}, bf16[256,2048]{1,0:T(8,128)(2,1)}, bf16[256,2048]{1,0:T(8,128)(2,1)}, /*index=5*/f32[256,2048]{1,0:T(8,128)}) custom-call(bf16[1024,2048]{1,0:T(8,128)(2,1)} %get-tuple-element.176.h_ref, ...), custom_call_target="tpu_custom_call" | custom-call | flops 19327352832 | bytes 41943040 | tf_op jit(solution)/shard_map/ff_forward/pallas_call | solution.py:521
  350.0 17.5 %collective-permute-done.24 = bf16[256,2048]{1,0:T(8,128)(2,1)S(1)} collective-permute-done((bf16[256,2048]{1,0:T(8,128)(2,1)S(1)}, bf16[256,2048]{1,0:T(8,128)(2,1)S(1)}, u32[]{:S(2)}, u32[]{:S(2)}) %collective-permute-start.24) | collective-permute-done | bytes 1048608 | tf_op jit(solution)/shard_map/ppermute | solution.py:68
  373.0 15.7 %ff_forward.3 = (f32[1024,2048]{1,0:T(8,128)}, f32[1024,2048]{1,0:T(8,128)}, bf16[1024,2048]{1,0:T(8,128)(2,1)}, f32[256,2048]{1,0:T(8,128)}) custom-call(bf16[1024,2048]{1,0:T(8,128)(2,1)} %get-tuple-element.176.h_ref, ...), custom_call_target="tpu_custom_call", output_to_operand_aliasing={{0}: (4, {}), {1}: (5, {}), {2}: (6, {})} | custom-call | flops 6442450944 | bytes 41943040 | tf_op jit(solution)/shard_map/ff_forward/pallas_call | solution.py:521
  392.1 23.2 %collective-permute-done.27 = bf16[256,2048]{1,0:T(8,128)(2,1)S(1)} collective-permute-done((bf16[256,2048]{1,0:T(8,128)(2,1)S(1)}, bf16[256,2048]{1,0:T(8,128)(2,1)S(1)}, u32[]{:S(2)}, u32[]{:S(2)}) %collective-permute-start.27) | collective-permute-done | bytes 1048608 | tf_op jit(solution)/shard_map/ppermute | solution.py:77
  419.5 7.5 collective-permute-start.31
  428.3 40.7 %collective-permute-done.28.d_ref = bf16[256,2048]{1,0:T(8,128)(2,1)S(1)} collective-permute-done((bf16[256,2048]{1,0:T(8,128)(2,1)S(1)}, bf16[256,2048]{1,0:T(8,128)(2,1)S(1)}, u32[]{:S(2)}, u32[]{:S(2)}) %collective-permute-start.28) | collective-permute-done | bytes 1048608 | tf_op jit(solution)/shard_map/ppermute | solution.py:59
  470.5 16.1 %ff_backward.3 = (bf16[1024,4096]{1,0:T(8,128)(2,1)}, f32[256,2048]{1,0:T(8,128)}) custom-call(bf16[256,2048]{1,0:T(8,128)(2,1)} %copy-done.7, bf16[2048,4096]{1,0:T(8,128)(2,1)} %all-gather.6.cloned.1.call-done.refs_5_.wg_ref.w_ref, bf16[2048,4096]{1,0:T(8,128)(2,1)} %all-gather.8.cloned.1.call-done.wu_ref.wd_ref, ...), custom_call_target="tpu_custom_call" | custom-call | flops 6442450944 | bytes 41943040 | tf_op jit(solution)/shard_map/ff_backward/pallas_call | solution.py:546
  496.0 23.6 %ff_backward.4 = (bf16[1024,4096]{1,0:T(8,128)(2,1)}, bf16[256,2048]{1,0:T(8,128)(2,1)}, bf16[256,2048]{1,0:T(8,128)(2,1)}) custom-call(bf16[512,2048]{1,0:T(8,128)(2,1)} %pad_maximum_fusion.1.d_ref, bf16[2048,4096]{1,0:T(8,128)(2,1)} %all-gather.6.cloned.1.call-done.refs_5_.wg_ref.w_ref, ...), custom_call_target="tpu_custom_call", output_to_operand_aliasing={{0}: (6, {})} | custom-call | flops 12884901888 | bytes 41943040 | tf_op jit(solution)/shard_map/ff_backward/pallas_call | solution.py:546
  519.7 13.4 %convolution_convert_fusion.2 = bf16[2048,2048]{1,0:T(8,128)(2,1)} fusion(bf16[1024,2048]{1,0:T(8,128)(2,1)} %get-tuple-element.197, bf16[256,2048]{1,0:T(8,128)(2,1)S(1)} %copy-done.8, bf16[256,2048]{1,0:T(8,128)(2,1)S(1)} %collective-permute-done.28.d_ref, bf16[256,2048]{1,0:T(8,128)(2,1)S(1)} %get-tuple-element.188, ...), kind=kOutput, calls=%fused_computation.3 | convolution fusion | flops 8610906112 | bytes 16777216 | tf_op jit(solution)/shard_map/dot_general | solution.py:30
  540.3 18.4 %ff_backward.5 = (bf16[1024,4096]{1,0:T(8,128)(2,1)}, f32[256,2048]{1,0:T(8,128)}) custom-call(bf16[256,2048]{1,0:T(8,128)(2,1)} %copy-done.18, bf16[2048,4096]{1,0:T(8,128)(2,1)} %all-gather.6.cloned.1.call-done.refs_5_.wg_ref.w_ref, bf16[2048,4096]{1,0:T(8,128)(2,1)} %all-gather.8.cloned.1.call-done.wu_ref.wd_ref, ...), custom_call_target="tpu_custom_call", output_to_operand_aliasing={{0}: (6, {})} | custom-call | flops 6442450944 | bytes 41943040 | tf_op jit(solution)/shard_map/ff_backward/pallas_call | solution.py:546
  567.6 24.0 %convolution_convert_fusion = bf16[2048,4096]{1,0:T(8,128)(2,1)} fusion(bf16[1024,2048]{1,0:T(8,128)(2,1)S(1)} %copy-done.9, bf16[1024,4096]{1,0:T(8,128)(2,1)} %get-tuple-element.204), kind=kOutput, calls=%fused_computation | convolution fusion | flops 17188257792 | bytes 29360128 | tf_op jit(solution)/shard_map/dot_general | solution.py:30
  591.6 19.4 %collective-permute-done.33 = bf16[256,2048]{1,0:T(8,128)(2,1)} collective-permute-done((bf16[256,2048]{1,0:T(8,128)(2,1)}, bf16[256,2048]{1,0:T(8,128)(2,1)}, u32[]{:S(2)}, u32[]{:S(2)}) %collective-permute-start.33) | collective-permute-done | bytes 1048608 | tf_op jit(solution)/shard_map/ppermute | solution.py:77
  621.4 8.2 mixed_back.1
  641.4 12.9 %collective-permute-done.37.refs_2_ = bf16[256,512]{1,0:T(8,128)(2,1)S(1)} collective-permute-done((bf16[256,512]{1,0:T(8,128)(2,1)}, bf16[256,512]{1,0:T(8,128)(2,1)S(1)}, u32[]{:S(2)}, u32[]{:S(2)}) %collective-permute-start.37) | collective-permute-done | bytes 262176 | tf_op jit(solution)/shard_map/ppermute | solution.py:740
  660.6 23.0 %attend_back.1 = (f32[1024,512]{1,0:T(8,128)}, f32[1024,512]{1,0:T(8,128)}, bf16[1024,512]{1,0:T(8,128)(2,1)}, f32[2,8,1024]{2,1,0:T(8,128)}, f32[2,8,512]{2,1,0:T(8,128)}) custom-call(s32[1]{0:T(128)} %bitcast.5.me_ref.refs_0_, bf16[256,512]{1,0:T(8,128)(2,1)} %get-tuple-element.214.refs_0_, bf16[256,512]{1,0:T(8,128)(2,1)} %copy-done.49, ...), custom_call_target="tpu_custom_call" | custom-call | flops 5368709120 | bytes 25165824 | tf_op jit(solution)/shard_map/attend_back/pallas_call | solution.py:302
  707.4 15.7 %input_back.1 = (bf16[1024,1536]{1,0:T(8,128)(2,1)}, bf16[256,2048]{1,0:T(8,128)(2,1)}, bf16[256,2048]{1,0:T(8,128)(2,1)}, f32[256,2048]{1,0:T(8,128)}, f32[256,2048]{1,0:T(8,128)}) custom-call(f32[1024,512]{1,0:T(8,128)} %get-tuple-element.221.q_ref, f32[1024,512]{1,0:T(8,128)} %get-tuple-element.222.k_ref, bf16[1024,512]{1,0:T(8,128)(2,1)} %get-tuple-element.223.v_ref, ...), custom_call_target="tpu_custom_call" | custom-call | flops 6442450944 | bytes 25165824 | tf_op jit(solution)/shard_map/input_back/pallas_call | solution.py:380
  736.7 11.0 %convolution_convert_fusion.1 = bf16[2048,1536]{1,0:T(8,128)(2,1)} fusion(bf16[1024,2048]{1,0:T(8,128)(2,1)} %get-tuple-element.163.refs_6_, bf16[1024,1536]{1,0:T(8,128)(2,1)S(1)} %copy-done.44), kind=kOutput, calls=%fused_computation.2 | convolution fusion | flops 6445596672 | bytes 13631488 | tf_op jit(solution)/shard_map/dot_general | solution.py:30
  747.7 25.4 %collective-permute-done.48 = bf16[256,2048]{1,0:T(8,128)(2,1)S(1)} collective-permute-done((bf16[256,2048]{1,0:T(8,128)(2,1)S(1)}, bf16[256,2048]{1,0:T(8,128)(2,1)S(1)}, u32[]{:S(2)}, u32[]{:S(2)}) %collective-permute-start.48) | collective-permute-done | bytes 1048608 | tf_op jit(solution)/shard_map/ppermute | solution.py:68
  773.2 7.5 pad_maximum_fusion
  787.4 42.2 %collective-permute-done.51 = bf16[256,2048]{1,0:T(8,128)(2,1)S(1)} collective-permute-done((bf16[256,2048]{1,0:T(8,128)(2,1)S(1)}, bf16[256,2048]{1,0:T(8,128)(2,1)S(1)}, u32[]{:S(2)}, u32[]{:S(2)}) %collective-permute-start.51) | collective-permute-done | bytes 1048608 | tf_op jit(solution)/shard_map/ppermute | solution.py:77
  850.4 22.2 %collective-permute-done.58 = f32[4,2048]{1,0:T(4,128)S(1)} collective-permute-done((f32[4,2048]{1,0:T(4,128)S(1)}, f32[4,2048]{1,0:T(4,128)S(1)}, u32[]{:S(2)}, u32[]{:S(2)}) %collective-permute-start.58) | collective-permute-done | bytes 32800 | tf_op jit(solution)/shard_map/ppermute | solution.py:100
  873.4 11.3 %collective-permute-done.59 = f32[4,2048]{1,0:T(4,128)S(1)} collective-permute-done((f32[4,2048]{1,0:T(4,128)S(1)}, f32[4,2048]{1,0:T(4,128)S(1)}, u32[]{:S(2)}, u32[]{:S(2)}) %collective-permute-start.59) | collective-permute-done | bytes 32800 | tf_op jit(solution)/shard_map/ppermute | solution.py:100
  (376 shorter events, 262.1 us)
Async XLA Ops:
  7.2 152.3 %all-gather.4.cloned.1.call-start = ((), (), s32[]{:S(2)}) async-start(), calls=%async_computation.5 | async-start | bytes 7077888 | tf_op jit(solution)/shard_map/all_gather | solution.py:147
  35.9 256.4 %all-gather.6.cloned.1.call-start = ((), (), s32[]{:S(2)}) async-start(), calls=%async_computation.6 | async-start | bytes 18874368 | tf_op jit(solution)/shard_map/all_gather | solution.py:147
  78.7 231.2 %all-gather.8.cloned.1.call-start = ((), (), s32[]{:S(2)}) async-start(), calls=%async_computation.7 | async-start | bytes 18874368 | tf_op jit(solution)/shard_map/all_gather | solution.py:147
  78.7 49.7 %collective-permute-start.7 = (bf16[256,2048]{1,0:T(8,128)(2,1)}, bf16[256,2048]{1,0:T(8,128)(2,1)}, u32[]{:S(2)}, u32[]{:S(2)}) collective-permute-start(bf16[256,2048]{1,0:T(8,128)(2,1)} %bitcast.4.refs_0_), channel_id=1, source_target_pairs={{2,0},{3,1},{0,2},{1,3},{6,4},{7,5},{4,6},{5,7},{10,8},{11,9},{8,1... | collective-permute-start | bytes 3145736 | tf_op jit(solution)/shard_map/ppermute | solution.py:59
  79.0 57.8 %collective-permute-start.10 = (bf16[256,2048]{1,0:T(8,128)(2,1)}, bf16[256,2048]{1,0:T(8,128)(2,1)S(1)}, u32[]{:S(2)}, u32[]{:S(2)}) collective-permute-start(bf16[256,2048]{1,0:T(8,128)(2,1)} %bitcast.4.refs_0_), channel_id=1, source_target_pairs={{0,1},{1,2},{2,3},{4,5},{5,6},{6,7},{8,9},{9,10},{10,11},{12,13},{... | collective-permute-start | bytes 3145736 | tf_op jit(solution)/shard_map/ppermute | solution.py:61
  83.9 53.0 %collective-permute-start.9 = (bf16[256,2048]{1,0:T(8,128)(2,1)}, bf16[256,2048]{1,0:T(8,128)(2,1)S(1)}, u32[]{:S(2)}, u32[]{:S(2)}) collective-permute-start(bf16[256,2048]{1,0:T(8,128)(2,1)} %bitcast.4.refs_0_), channel_id=1, source_target_pairs={{1,0},{2,1},{3,2},{5,4},{6,5},{7,6},{9,8},{10,9},{11,10},{13,12},{... | collective-permute-start | bytes 3145736 | tf_op jit(solution)/shard_map/ppermute | solution.py:60
  216.1 438.2 %reduce-scatter.4.cloned.1.call-start = ((), (), s32[]{:S(2)}) async-start(), calls=%async_computation.8 | async-start | bytes 9437184 | tf_op jit(solution)/shard_map/reduce_scatter | solution.py:151
  216.2 49.7 %collective-permute-start.20 = (bf16[1024,512]{1,0:T(8,128)(2,1)S(1)}, bf16[1024,512]{1,0:T(8,128)(2,1)S(1)}, u32[]{:S(2)}, u32[]{:S(2)}) collective-permute-start(bf16[1024,512]{1,0:T(8,128)(2,1)S(1)} %copy-done.45), channel_id=1, source_target_pairs={{2,0},{3,1},{0,2},{1,3},{6,4},{7,5},{4,6},{5,7},{10,8},{11,9},{8,1... | collective-permute-start | bytes 3145736 | tf_op jit(solution)/shard_map/ppermute | solution.py:59
  219.3 48.2 %collective-permute-start.23 = (bf16[1024,512]{1,0:T(8,128)(2,1)S(1)}, bf16[1024,512]{1,0:T(8,128)(2,1)S(1)}, u32[]{:S(2)}, u32[]{:S(2)}) collective-permute-start(bf16[1024,512]{1,0:T(8,128)(2,1)S(1)} %copy-done.45), channel_id=1, source_target_pairs={{0,1},{1,2},{2,3},{4,5},{5,6},{6,7},{8,9},{9,10},{10,11},{12,13},{... | collective-permute-start | bytes 3145736 | tf_op jit(solution)/shard_map/ppermute | solution.py:61
  223.3 44.5 %collective-permute-start.22 = (bf16[1024,512]{1,0:T(8,128)(2,1)S(1)}, bf16[1024,512]{1,0:T(8,128)(2,1)S(1)}, u32[]{:S(2)}, u32[]{:S(2)}) collective-permute-start(bf16[1024,512]{1,0:T(8,128)(2,1)S(1)} %copy-done.45), channel_id=1, source_target_pairs={{1,0},{2,1},{3,2},{5,4},{6,5},{7,6},{9,8},{10,9},{11,10},{13,12},{... | collective-permute-start | bytes 3145736 | tf_op jit(solution)/shard_map/ppermute | solution.py:60
  344.1 48.0 %collective-permute-start.26 = (bf16[256,2048]{1,0:T(8,128)(2,1)}, bf16[256,2048]{1,0:T(8,128)(2,1)S(1)}, u32[]{:S(2)}, u32[]{:S(2)}) collective-permute-start(bf16[256,2048]{1,0:T(8,128)(2,1)} %get-tuple-element.174), channel_id=1, source_target_pairs={{1,0},{2,1},{3,2},{5,4},{6,5},{7,6},{9,8},{10,9},{11,10},{13,12},{... | collective-permute-start | bytes 3145736 | tf_op jit(solution)/shard_map/ppermute | solution.py:71
  345.4 46.7 %collective-permute-start.25 = (bf16[256,2048]{1,0:T(8,128)(2,1)S(1)}, bf16[256,2048]{1,0:T(8,128)(2,1)S(1)}, u32[]{:S(2)}, u32[]{:S(2)}) collective-permute-start(bf16[256,2048]{1,0:T(8,128)(2,1)S(1)} %copy-done.23), channel_id=1, source_target_pairs={{0,1},{1,2},{2,3},{4,5},{5,6},{6,7},{8,9},{9,10},{10,11},{12,13},{... | collective-permute-start | bytes 3145736 | tf_op jit(solution)/shard_map/ppermute | solution.py:70
  367.9 47.4 %collective-permute-start.27 = (bf16[256,2048]{1,0:T(8,128)(2,1)S(1)}, bf16[256,2048]{1,0:T(8,128)(2,1)S(1)}, u32[]{:S(2)}, u32[]{:S(2)}) collective-permute-start(bf16[256,2048]{1,0:T(8,128)(2,1)S(1)} %add_convert_fusion.3), channel_id=1, source_target_pairs={{0,2},{1,3},{2,0},{3,1},{4,6},{5,7},{6,4},{7,5},{8,10},{9,11},{10,... | collective-permute-start | bytes 3145736 | tf_op jit(solution)/shard_map/ppermute | solution.py:77
  419.4 49.6 %collective-permute-start.28 = (bf16[256,2048]{1,0:T(8,128)(2,1)S(1)}, bf16[256,2048]{1,0:T(8,128)(2,1)S(1)}, u32[]{:S(2)}, u32[]{:S(2)}) collective-permute-start(bf16[256,2048]{1,0:T(8,128)(2,1)S(1)} %fusion.11.d_ref), channel_id=1, source_target_pairs={{2,0},{3,1},{0,2},{1,3},{6,4},{7,5},{4,6},{5,7},{10,8},{11,9},{8,1... | collective-permute-start | bytes 3145736 | tf_op jit(solution)/shard_map/ppermute | solution.py:59
  419.5 67.1 %collective-permute-start.31 = (bf16[256,2048]{1,0:T(8,128)(2,1)S(1)}, bf16[256,2048]{1,0:T(8,128)(2,1)S(1)}, u32[]{:S(2)}, u32[]{:S(2)}) collective-permute-start(bf16[256,2048]{1,0:T(8,128)(2,1)S(1)} %fusion.11.d_ref), channel_id=1, source_target_pairs={{0,1},{1,2},{2,3},{4,5},{5,6},{6,7},{8,9},{9,10},{10,11},{12,13},{... | collective-permute-start | bytes 3145736 | tf_op jit(solution)/shard_map/ppermute | solution.py:61
  427.0 59.6 %collective-permute-start.30 = (bf16[256,2048]{1,0:T(8,128)(2,1)S(1)}, bf16[256,2048]{1,0:T(8,128)(2,1)S(1)}, u32[]{:S(2)}, u32[]{:S(2)}) collective-permute-start(bf16[256,2048]{1,0:T(8,128)(2,1)S(1)} %fusion.11.d_ref), channel_id=1, source_target_pairs={{1,0},{2,1},{3,2},{5,4},{6,5},{7,6},{9,8},{10,9},{11,10},{13,12},{... | collective-permute-start | bytes 3145736 | tf_op jit(solution)/shard_map/ppermute | solution.py:60
  533.1 299.8 %reduce-scatter.8.cloned.1.call-start = ((), (), s32[]{:S(2)}) async-start(), calls=%async_computation.10 | async-start | bytes 18874368 | tf_op jit(solution)/shard_map/reduce_scatter | solution.py:151
  536.2 55.4 %collective-permute-start.34 = (bf16[256,2048]{1,0:T(8,128)(2,1)}, bf16[256,2048]{1,0:T(8,128)(2,1)}, u32[]{:S(2)}, u32[]{:S(2)}) collective-permute-start(bf16[256,2048]{1,0:T(8,128)(2,1)} %get-tuple-element.203), channel_id=1, source_target_pairs={{0,1},{1,2},{2,3},{4,5},{5,6},{6,7},{8,9},{9,10},{10,11},{12,13},{... | collective-permute-start | bytes 3145736 | tf_op jit(solution)/shard_map/ppermute | solution.py:70
  538.6 53.0 %collective-permute-start.35 = (bf16[256,2048]{1,0:T(8,128)(2,1)}, bf16[256,2048]{1,0:T(8,128)(2,1)}, u32[]{:S(2)}, u32[]{:S(2)}) collective-permute-start(bf16[256,2048]{1,0:T(8,128)(2,1)} %get-tuple-element.202), channel_id=1, source_target_pairs={{1,0},{2,1},{3,2},{5,4},{6,5},{7,6},{9,8},{10,9},{11,10},{13,12},{... | collective-permute-start | bytes 3145736 | tf_op jit(solution)/shard_map/ppermute | solution.py:71
  564.0 47.0 %collective-permute-start.33 = (bf16[256,2048]{1,0:T(8,128)(2,1)}, bf16[256,2048]{1,0:T(8,128)(2,1)}, u32[]{:S(2)}, u32[]{:S(2)}) collective-permute-start(bf16[256,2048]{1,0:T(8,128)(2,1)} %add_convert_fusion.1), channel_id=1, source_target_pairs={{0,2},{1,3},{2,0},{3,1},{4,6},{5,7},{6,4},{7,5},{8,10},{9,11},{10,... | collective-permute-start | bytes 3145736 | tf_op jit(solution)/shard_map/ppermute | solution.py:77
  611.0 273.7 %reduce-scatter.6.cloned.1.call-start = ((), (), s32[]{:S(2)}) async-start(), calls=%async_computation.9 | async-start | bytes 9437184 | tf_op jit(solution)/shard_map/reduce_scatter | solution.py:151
  654.4 29.1 %collective-permute-start.41 = (bf16[256,512]{1,0:T(8,128)(2,1)S(1)}, bf16[256,512]{1,0:T(8,128)(2,1)S(1)}, u32[]{:S(2)}, u32[]{:S(2)}) collective-permute-start(bf16[256,512]{1,0:T(8,128)(2,1)S(1)} %get-tuple-element.301), channel_id=1, source_target_pairs={{0,1},{1,2},{2,3},{3,0},{4,5},{5,6},{6,7},{7,4},{8,9},{9,10},{10,1... | collective-permute-start | bytes 786440 | tf_op jit(solution)/shard_map/ppermute | solution.py:620
  655.6 28.0 %collective-permute-start.40 = (bf16[256,512]{1,0:T(8,128)(2,1)S(1)}, bf16[256,512]{1,0:T(8,128)(2,1)S(1)}, u32[]{:S(2)}, u32[]{:S(2)}) collective-permute-start(bf16[256,512]{1,0:T(8,128)(2,1)S(1)} %get-tuple-element.302), channel_id=1, source_target_pairs={{0,2},{1,3},{2,0},{3,1},{4,6},{5,7},{6,4},{7,5},{8,10},{9,11},{10,... | collective-permute-start | bytes 786440 | tf_op jit(solution)/shard_map/ppermute | solution.py:620
  657.5 26.1 %collective-permute-start.39 = (bf16[256,512]{1,0:T(8,128)(2,1)S(1)}, bf16[256,512]{1,0:T(8,128)(2,1)S(1)}, u32[]{:S(2)}, u32[]{:S(2)}) collective-permute-start(bf16[256,512]{1,0:T(8,128)(2,1)S(1)} %get-tuple-element.303), channel_id=1, source_target_pairs={{0,3},{1,0},{2,1},{3,2},{4,7},{5,4},{6,5},{7,6},{8,11},{9,8},{10,9... | collective-permute-start | bytes 786440 | tf_op jit(solution)/shard_map/ppermute | solution.py:620
  723.2 50.0 %collective-permute-start.49 = (bf16[256,2048]{1,0:T(8,128)(2,1)}, bf16[256,2048]{1,0:T(8,128)(2,1)}, u32[]{:S(2)}, u32[]{:S(2)}) collective-permute-start(bf16[256,2048]{1,0:T(8,128)(2,1)} %get-tuple-element.236), channel_id=1, source_target_pairs={{0,1},{1,2},{2,3},{4,5},{5,6},{6,7},{8,9},{9,10},{10,11},{12,13},{... | collective-permute-start | bytes 3145736 | tf_op jit(solution)/shard_map/ppermute | solution.py:70
  729.4 43.7 %collective-permute-start.50 = (bf16[256,2048]{1,0:T(8,128)(2,1)}, bf16[256,2048]{1,0:T(8,128)(2,1)}, u32[]{:S(2)}, u32[]{:S(2)}) collective-permute-start(bf16[256,2048]{1,0:T(8,128)(2,1)} %get-tuple-element.235), channel_id=1, source_target_pairs={{1,0},{2,1},{3,2},{5,4},{6,5},{7,6},{9,8},{10,9},{11,10},{13,12},{... | collective-permute-start | bytes 3145736 | tf_op jit(solution)/shard_map/ppermute | solution.py:71
  732.1 41.1 %collective-permute-start.48 = (bf16[256,2048]{1,0:T(8,128)(2,1)S(1)}, bf16[256,2048]{1,0:T(8,128)(2,1)S(1)}, u32[]{:S(2)}, u32[]{:S(2)}) collective-permute-start(bf16[256,2048]{1,0:T(8,128)(2,1)S(1)} %broadcast_select_fusion.2), channel_id=1, source_target_pairs={{0,1},{3,2},{4,5},{7,6},{8,9},{11,10},{12,13},{15,14},{16,17},{19,... | collective-permute-start | bytes 3145736 | tf_op jit(solution)/shard_map/ppermute | solution.py:68
  782.5 47.0 %collective-permute-start.51 = (bf16[256,2048]{1,0:T(8,128)(2,1)S(1)}, bf16[256,2048]{1,0:T(8,128)(2,1)S(1)}, u32[]{:S(2)}, u32[]{:S(2)}) collective-permute-start(bf16[256,2048]{1,0:T(8,128)(2,1)S(1)} %add_convert_fusion), channel_id=1, source_target_pairs={{0,2},{1,3},{2,0},{3,1},{4,6},{5,7},{6,4},{7,5},{8,10},{9,11},{10,... | collective-permute-start | bytes 3145736 | tf_op jit(solution)/shard_map/ppermute | solution.py:77
  835.3 49.3 %collective-permute-start.52 = (bf16[64,4096]{1,0:T(8,128)(2,1)}, bf16[64,4096]{1,0:T(8,128)(2,1)S(1)}, u32[]{:S(2)}, u32[]{:S(2)}) collective-permute-start(bf16[64,4096]{1,0:T(8,128)(2,1)} %get-tuple-element.284), channel_id=1, source_target_pairs={{0,1},{1,2},{2,3},{3,0},{4,5},{5,6},{6,7},{7,4},{8,9},{9,10},{10,1... | collective-permute-start | bytes 1572872 | tf_op jit(solution)/shard_map/ppermute | solution.py:132
  835.4 49.4 %collective-permute-start.53 = (bf16[64,4096]{1,0:T(8,128)(2,1)S(1)}, bf16[64,4096]{1,0:T(8,128)(2,1)S(1)}, u32[]{:S(2)}, u32[]{:S(2)}) collective-permute-start(bf16[64,4096]{1,0:T(8,128)(2,1)S(1)} %get-tuple-element.283), channel_id=1, source_target_pairs={{0,2},{1,3},{2,0},{3,1},{4,6},{5,7},{6,4},{7,5},{8,10},{9,11},{10,... | collective-permute-start | bytes 1572872 | tf_op jit(solution)/shard_map/ppermute | solution.py:132
  837.7 47.1 %collective-permute-start.54 = (bf16[64,4096]{1,0:T(8,128)(2,1)S(1)}, bf16[64,4096]{1,0:T(8,128)(2,1)S(1)}, u32[]{:S(2)}, u32[]{:S(2)}) collective-permute-start(bf16[64,4096]{1,0:T(8,128)(2,1)S(1)} %get-tuple-element.282), channel_id=1, source_target_pairs={{0,3},{1,0},{2,1},{3,2},{4,7},{5,4},{6,5},{7,6},{8,11},{9,8},{10,9... | collective-permute-start | bytes 1572872 | tf_op jit(solution)/shard_map/ppermute | solution.py:132
  885.5 30.1 %all-to-all-start.1 = ((bf16[4,64,2048]{2,1,0:T(8,128)(2,1)}), bf16[4,64,2048]{2,1,0:T(8,128)(2,1)S(1)}, u32[]{:S(2)}, u32[]{:S(2)}) async-start(bf16[4,64,2048]{2,1,0:T(8,128)(2,1)} %bitcast.159), calls=%async_computation.4 | async-start | bytes 2097152 | tf_op jit(solution)/shard_map/all_to_all | solution.py:106
  (87 other events, 1213.0 us)
Sparse Core Ops, SparseCore 0:
  36.0 44.6 all-gather.3
  83.1 89.8 all-gather.5
  216.2 92.0 all-gather.7
  533.2 70.5 reduce-scatter.3
  611.1 117.2 reduce-scatter.7
  780.8 71.9 reduce-scatter.5

commit v3 on v2

--- a/solution.py
+++ b/solution.py
@@ -14,20 +14,6 @@
 LOG2E = 1.4426950408889634
 BF = jnp.bfloat16
 F32 = jnp.float32
-
-
-def project(left, weight):
-    return jnp.dot(left, weight, preferred_element_type=F32)
-
-
-def back_project(grad_in, weight):
-    return lax.dot_general(
-        grad_in, weight, (((grad_in.ndim - 1,), (1,)), ((), ())), preferred_element_type=F32
-    )
-
-
-def rows_product(left, right):
-    return lax.dot_general(left, right, (((0,), (0,)), ((), ())), preferred_element_type=F32)
 
 
 def inv_rms(values):
@@ -63,9 +49,8 @@
     return [values, jnp.where(me == 3, ends, after), far, jnp.where(me == 0, ends, before)]
 
 
-def scatter_start(after, before, count):
-    me = lax.axis_index("seq")
-    ends = lax.ppermute(jnp.where(me == 0, before, after), "seq", [(0, 1), (count - 1, count - 2)])
+def scatter_start(ends, after, before, count):
+    ends = lax.ppermute(ends, "seq", [(0, 1), (count - 1, count - 2)])
     step = [(i, i + 1) for i in range(count - 1)]
     after = lax.ppermute(after, "seq", step)
     before = lax.ppermute(before, "seq", [(j, i) for i, j in step])
@@ -355,7 +340,9 @@
     )(me, d_attn, w_first)
 
 
-def input_back_kernel(part, order, q_ref, k_ref, v_ref, qp_ref, kp_ref, in_ref, f_ref, w_ref, d_ref, *outs):
+def input_back_kernel(
+    part, me_ref, q_ref, k_ref, v_ref, qp_ref, kp_ref, in_ref, f_ref, w_ref, d_ref, ends_ref, *outs
+):
     for j, (grad, proj) in enumerate(((q_ref, qp_ref), (k_ref, kp_ref))):
         factor = f_ref[:, j : j + 1]
         normed = proj[...] * factor
@@ -369,27 +356,109 @@
         def _(out=out):
             out[...] = total.astype(out.dtype)
 
-
-def input_back(d_query, d_key, d_v, qkv, inner, factors, w_qkv, count):
+    @pl.when((pl.program_id(0) == 0) | ((pl.program_id(0) == 1) & (me_ref[0] == 0)))
+    def _():
+        ends_ref[...] = total.astype(BF)
+
+
+def input_back(me, d_query, d_key, d_v, qkv, inner, factors, w_qkv, count):
     length, part = d_query.shape
     width = w_qkv.shape[0]
     tokens = length // count
     place = lambda t: jnp.where(t == 0, 1, jnp.where(t == 1, 3, jnp.where(t == 2, 2, 0)))
-    rows = lambda columns, at=0: pl.BlockSpec((tokens, columns), lambda t: (place(t), at))
-    kinds = (BF, BF, F32, F32)
+    rows = lambda columns, at=0: pl.BlockSpec((tokens, columns), lambda t, me: (place(t), at))
+    kinds = (BF, BF, BF, F32, F32)
     return pl.pallas_call(
-        functools.partial(input_back_kernel, part, None),
-        grid=(count,),
-        in_specs=[rows(part)] * 3
-        + [rows(part), rows(part, 1), rows(2), rows(2)]
-        + [once((width, 3 * part), lambda t: (0, 0))],
-        out_specs=[rows(3 * part)] + [pl.BlockSpec((tokens, width), lambda t: (0, 0))] * count,
+        functools.partial(input_back_kernel, part),
+        grid_spec=pltpu.PrefetchScalarGridSpec(
+            num_scalar_prefetch=1,
+            grid=(count,),
+            in_specs=[rows(part)] * 3
+            + [rows(part), rows(part, 1), rows(2), rows(2)]
+            + [once((width, 3 * part), lambda t, me: (0, 0))],
+            out_specs=[rows(3 * part)]
+            + [pl.BlockSpec((tokens, width), lambda t, me: (0, 0))] * len(kinds),
+        ),
         out_shape=[jax.ShapeDtypeStruct((length, 3 * part), BF)]
         + [jax.ShapeDtypeStruct((tokens, width), kind) for kind in kinds],
         compiler_params=params(),
         cost_estimate=cost(6 * length * width * part, 24 << 20),
         name="input_back",
-    )(d_query, d_key, d_v, qkv, qkv, inner, factors, w_qkv)
+    )(me, d_query, d_key, d_v, qkv, qkv, inner, factors, w_qkv)
+
+
+def tn_dot(left, right):
+    return lax.dot_general(left, right, (((0,), (0,)), ((), ())), preferred_element_type=F32)
+
+
+def weight_grad_kernel(lefts, right_ref, out_ref):
+    total, at = None, 0
+    for left in lefts:
+        rows = left.shape[0]
+        product = tn_dot(left[...], right_ref[at : at + rows, :])
+        total = product if total is None else total + product
+        at += rows
+    out_ref[...] = total.astype(BF)
+
+
+def weight_grad(lefts, right):
+    width = lefts[0].shape[1]
+    length, columns = right.shape
+    tile, wide = 256, min(columns, 2048)
+    return pl.pallas_call(
+        lambda *refs: weight_grad_kernel(refs[:-2], *refs[-2:]),
+        grid=(columns // wide, width // tile),
+        in_specs=[pl.BlockSpec((left.shape[0], tile), lambda j, i: (0, i)) for left in lefts]
+        + [pl.BlockSpec((length, wide), lambda j, i: (0, j))],
+        out_specs=pl.BlockSpec((tile, wide), lambda j, i: (i, j)),
+        out_shape=jax.ShapeDtypeStruct((width, columns), BF),
+        compiler_params=params(),
+        cost_estimate=cost(2 * length * width * columns, 2 * (length + width) * columns),
+        name="weight_grad",
+    )(*lefts, right)
+
+
+def attn_grad_kernel(count, me_ref, x_ref, d_ref, *refs):
+    pieces, parts, out_ref = refs[:count], refs[count : 2 * count], refs[-1]
+    columns = d_ref.shape[1]
+    out_ref[:, :columns] = tn_dot(x_ref[...], d_ref[...]).astype(BF)
+    source = (pl.program_id(0) // (pl.num_programs(0) // count) + count - me_ref[0]) % count
+    for p, piece in enumerate(pieces):
+
+        @pl.when(source == p)
+        def _(p=p, piece=piece):
+            total, tokens = None, parts[0].shape[0]
+            for q in range(count):
+                rows = slice(q * tokens, (q + 1) * tokens)
+                product = tn_dot(piece[rows, :], parts[(q + p) % count][...])
+                total = product if total is None else total + product
+            out_ref[:, columns:] = total.astype(BF)
+
+
+def attn_grad(me, x_all, d_qkv, pieces, d_parts):
+    count = len(pieces)
+    length, width = x_all.shape
+    columns, part = d_qkv.shape[1], d_parts[0].shape[1]
+    tile = min(256, part)
+    per_part = part // tile
+    return pl.pallas_call(
+        functools.partial(attn_grad_kernel, count),
+        grid_spec=pltpu.PrefetchScalarGridSpec(
+            num_scalar_prefetch=1,
+            grid=(width // tile,),
+            in_specs=[
+                pl.BlockSpec((length, tile), lambda i, me: (0, i)),
+                once((length, columns), lambda i, me: (0, 0)),
+            ]
+            + [pl.BlockSpec((length, tile), lambda i, me: (0, i % per_part))] * count
+            + [once((length // count, part), lambda i, me: (0, 0))] * count,
+            out_specs=pl.BlockSpec((tile, columns + part), lambda i, me: (i, 0)),
+        ),
+        out_shape=jax.ShapeDtypeStruct((width, columns + part), BF),
+        compiler_params=params(),
+        cost_estimate=cost(2 * length * width * (columns + part), 20 << 20),
+        name="attn_grad",
+    )(me, x_all, d_qkv, *pieces, *d_parts)
 
 
 def cost(flops, moved, exps=0):
@@ -459,7 +528,7 @@
 FF_TILE = 512
 
 
-def ff_finish(step, product, acc, outs):
+def ff_finish(step, product, acc, me_ref, outs):
     @pl.when(step == 0)
     def _():
         acc[...] = product
@@ -470,12 +539,15 @@
 
     @pl.when(step == pl.num_programs(0) - 1)
     def _():
-        tokens = acc.shape[0] // len(outs)
-        for j, out in enumerate(outs):
+        tokens = outs[0].shape[0]
+        for j, out in enumerate(outs[:2]):
             out[...] = acc[j * tokens : (j + 1) * tokens].astype(out.dtype)
-
-
-def ff_kernel(saved, h_ref, wg_ref, wu_ref, wd_ref, *refs):
+        if len(outs) == 3:
+            at = pl.multiple_of(jnp.where(me_ref[0] == 0, tokens, 0), tokens)
+            outs[2][...] = acc[pl.ds(at, tokens), :].astype(BF)
+
+
+def ff_kernel(saved, me_ref, h_ref, wg_ref, wu_ref, wd_ref, *refs):
     gate_ref, up_ref, hid_ref = refs[saved : saved + 3]
     h = h_ref[...]
     gate = jnp.dot(h, wg_ref[...], preferred_element_type=F32)
@@ -484,13 +556,17 @@
     gate_ref[...] = gate
     up_ref[...] = up
     hid_ref[...] = hidden
-    ff_finish(pl.program_id(0), nt_dot(hidden, wd_ref[...]), refs[-1], refs[saved + 3 : -1])
-
-
-def ff_back_kernel(saved, d_ref, wg_ref, wu_ref, wd_ref, gate_ref, up_ref, *refs):
+    product = nt_dot(hidden, wd_ref[...])
+    ff_finish(pl.program_id(0), product, refs[-1], me_ref, refs[saved + 3 : -1])
+
+
+def ff_back_kernel(saved, groups, me_ref, *refs):
+    d_refs, (wg_ref, wu_ref, wd_ref, gate_ref, up_ref) = refs[:groups], refs[groups : groups + 5]
+    refs = refs[groups + 5 :]
     dgu_ref = refs[saved]
     tile = wg_ref.shape[1]
-    d_hidden = jnp.dot(d_ref[...], wd_ref[...], preferred_element_type=F32)
+    d_ff = d_refs[0][...] if groups == 1 else jnp.concatenate([d[...] for d in d_refs], axis=0)
+    d_hidden = jnp.dot(d_ff, wd_ref[...], preferred_element_type=F32)
     gate = gate_ref[...]
     sig = 1.0 / (1.0 + jnp.exp(-gate))
     d_gate = (d_hidden * up_ref[...] * sig * (1.0 + gate * (1.0 - sig))).astype(BF)
@@ -498,7 +574,7 @@
     dgu_ref[:, :tile] = d_gate
     dgu_ref[:, tile:] = d_up
     product = nt_dot(d_gate, wg_ref[...]) + nt_dot(d_up, wu_ref[...])
-    ff_finish(pl.program_id(0), product, refs[-1], refs[saved + 1 : -1])
+    ff_finish(pl.program_id(0), product, refs[-1], me_ref, refs[saved + 1 : -1])
 
 
 def ff_specs(width, tile, gate_at, down_at):
@@ -509,57 +585,61 @@
     ]
 
 
-def ff_forward(residual_all, w_first, w_second, place, kinds, saved=()):
+def ff_forward(me, residual_all, w_first, w_second, place, kinds, saved=()):
     length, width = residual_all.shape
     tokens = length // 4
-    rows = len(kinds) * tokens
+    group = min(len(kinds), 2)
+    rows = group * tokens
     ff_part = w_second.shape[1] // 2
     tile = min(FF_TILE, ff_part)
-    block = pl.BlockSpec((rows, tile), lambda t: (place // len(kinds), t))
+    block = pl.BlockSpec((rows, tile), lambda t: (place // group, t))
     whole = pl.BlockSpec((tokens, width), lambda t: (0, 0))
     shape = lambda kind: jax.ShapeDtypeStruct((length, ff_part), kind)
     return pl.pallas_call(
         functools.partial(ff_kernel, len(saved)),
         grid=(ff_part // tile,),
-        in_specs=[once((rows, width), lambda t: (place // len(kinds), 0))]
+        in_specs=[pl.BlockSpec(memory_space=pltpu.SMEM)]
+        + [once((rows, width), lambda t: (place // group, 0))]
         + ff_specs(width, tile, w_first.shape[1] - ff_part, ff_part)
         + [pl.BlockSpec(memory_space=pl.ANY)] * len(saved),
         out_specs=[block] * 3 + [whole] * len(kinds),
         out_shape=[shape(F32), shape(F32), shape(BF)]
         + [jax.ShapeDtypeStruct((tokens, width), kind) for kind in kinds],
         scratch_shapes=[pltpu.VMEM((rows, width), F32)],
-        input_output_aliases={4 + j: j for j in range(len(saved))},
+        input_output_aliases={5 + j: j for j in range(len(saved))},
         compiler_params=params(),
         cost_estimate=cost(6 * rows * width * ff_part, 40 << 20, rows * ff_part),
         name="ff_forward",
-    )(residual_all, w_first, w_second, w_second, *saved)
-
-
-def ff_backward(d_ff, w_first, w_second, gate, up, place, kinds, saved=()):
-    rows, width = d_ff.shape
+    )(me, residual_all, w_first, w_second, w_second, *saved)
+
+
+def ff_backward(me, d_ffs, w_first, w_second, gate, up, place, kinds, saved=()):
+    tokens, width = d_ffs[0].shape
+    group = len(d_ffs)
+    rows = group * tokens
     length = gate.shape[0]
-    tokens = length // 4
     ff_part = w_second.shape[1] // 2
     tile = min(FF_TILE, ff_part)
-    block = pl.BlockSpec((rows, tile), lambda t: (place // len(kinds), t))
+    block = pl.BlockSpec((rows, tile), lambda t: (place // group, t))
     whole = pl.BlockSpec((tokens, width), lambda t: (0, 0))
     return pl.pallas_call(
-        functools.partial(ff_back_kernel, len(saved)),
+        functools.partial(ff_back_kernel, len(saved), group),
         grid=(ff_part // tile,),
-        in_specs=[once((rows, width), lambda t: (0, 0))]
+        in_specs=[pl.BlockSpec(memory_space=pltpu.SMEM)]
+        + [once((tokens, width), lambda t: (0, 0))] * group
         + ff_specs(width, tile, w_first.shape[1] - ff_part, ff_part)
         + [block, block]
         + [pl.BlockSpec(memory_space=pl.ANY)] * len(saved),
-        out_specs=[pl.BlockSpec((rows, 2 * tile), lambda t: (place // len(kinds), t))]
+        out_specs=[pl.BlockSpec((rows, 2 * tile), lambda t: (place // group, t))]
         + [whole] * len(kinds),
         out_shape=[jax.ShapeDtypeStruct((length, 2 * ff_part), BF)]
         + [jax.ShapeDtypeStruct((tokens, width), kind) for kind in kinds],
         scratch_shapes=[pltpu.VMEM((rows, width), F32)],
-        input_output_aliases={6 + j: j for j in range(len(saved))},
+        input_output_aliases={6 + group + j: j for j in range(len(saved))},
         compiler_params=params(),
         cost_estimate=cost(6 * rows * width * ff_part, 40 << 20, rows * ff_part),
         name="ff_backward",
-    )(d_ff, w_first, w_second, w_second, gate, up, *saved)
+    )(me, *d_ffs, w_first, w_second, w_second, gate, up, *saved)
 
 
 def out_kernel(count, part, *refs):
@@ -608,11 +688,6 @@
     )(me, *pieces, w_out, x_all, gain[None])
 
 
-def roll_blocks(values, first):
-    n = values.shape[0]
-    return lax.dynamic_slice_in_dim(jnp.concatenate([values, values]), first, n, 0)
-
-
 def columns_to_parts(values, me, count):
     part = values.shape[1] // count
     columns = lambda p: lax.dynamic_slice_in_dim(values, (me + p) % count * part, part, 1)
@@ -620,7 +695,7 @@
         lax.ppermute(columns(p), "seq", [(i, (i + p) % count) for i in range(count)])
         for p in range(1, count)
     ]
-    return jnp.concatenate([got[(count - q) % count] for q in range(count)], axis=0)
+    return [got[(count - q) % count] for q in range(count)]
 
 
 def build(dp_count, seq_count):
@@ -652,7 +727,6 @@
         me = lax.axis_index("seq")
         me_ref = me[None].astype(jnp.int32)
         cot = cotangent[0]
-        chunks = lambda v: [v[p * tokens : (p + 1) * tokens] for p in range(n)]
         by_part = lambda w: w.reshape(shard_rows, n, -1).transpose(1, 0, 2)
         rows_of = lambda blocks: blocks.reshape(n * shard_rows, -1)
 
@@ -698,36 +772,40 @@
         attn_normed = attn_out * attn_factor
         residual = x_own.astype(F32) + attn_normed * attn_gain
 
-        *saved, after, before, far = ff_forward(
-            residual_all, w_first, w_second, 0, (BF, BF, F32)
-        )
-        sent = scatter_start(after, before, n)
-        residual_late, first_sent = fence((residual_all, sent[0]))
-        gate, up, hidden, own = ff_forward(residual_late, w_first, w_second, 3, (F32,), saved)
-        ff_out = scatter_end(own, sent[1:] + [scatter_far(far, first_sent, n)])
+        *saved, after, before, ends = ff_forward(
+            me_ref, residual_all, w_first, w_second, 0, (BF, BF, BF)
+        )
+        sent = scatter_start(ends, after, before, n)
+        *saved, far = ff_forward(me_ref, residual_all, w_first, w_second, 2, (F32,), saved)
+        far, sent[0], residual_late = fence((far, sent[0], residual_all))
+        sent[0] = scatter_far(far, sent[0], n)
+        gate, up, hidden, own = ff_forward(
+            me_ref, residual_late, w_first, w_second, 3, (F32,), saved
+        )
+        ff_out = scatter_end(own, sent)
         ff_factor = inv_rms(ff_out)
         ff_normed = ff_out * ff_factor
         activation = (residual + ff_normed * ff_gain).astype(BF)
         grad_ff_gain = jnp.sum(cot.astype(F32) * ff_normed, axis=0)
         d_ff = rms_back(ff_normed, ff_factor, ff_gain, cot.astype(F32)).astype(BF)
         d_ffs = gather_cyclic(d_ff, n)
-        d_both, own = ff_backward(d_ffs[0], w_first, w_second, gate, up, 3, (F32,))
+        d_both, own = ff_backward(me_ref, d_ffs[:1], w_first, w_second, gate, up, 3, (F32,))
         d_ffs, d_both = fence((d_ffs, d_both))
-        d_ff_near = jnp.concatenate([d_ffs[1], d_ffs[3]], axis=0)
-        d_both, after, before = ff_backward(
-            d_ff_near, w_first, w_second, gate, up, 0, (BF, BF), (d_both,)
-        )
-        after, before, d_ffs, hidden = fence((after, before, d_ffs, hidden))
-        sent = scatter_start(after, before, n)
-        d_ff_all = jnp.concatenate([d_ff_near, d_ffs[2], d_ffs[0]], axis=0)
-        down_grad = rows_product(d_ff_all, hidden).astype(BF)
+        d_both, after, before, ends = ff_backward(
+            me_ref, d_ffs[1::2], w_first, w_second, gate, up, 0, (BF, BF, BF), (d_both,)
+        )
+        after, before, ends, d_ffs, hidden = fence((after, before, ends, d_ffs, hidden))
+        sent = scatter_start(ends, after, before, n)
+        down_grad = weight_grad([d_ffs[1], d_ffs[3], d_ffs[2], d_ffs[0]], hidden)
         down_rows = scatter_dp(down_grad)
         d_ff_far, down_grad = fence((d_ffs[2], down_grad))
-        d_both, far = ff_backward(d_ff_far, w_first, w_second, gate, up, 2, (F32,), (d_both,))
+        d_both, far = ff_backward(
+            me_ref, [d_ff_far], w_first, w_second, gate, up, 2, (F32,), (d_both,)
+        )
         d_both, far, sent[0] = fence((d_both, far, sent[0]))
         sent[0] = scatter_far(far, sent[0], n)
         joined = lambda g: g.transpose(1, 0, 2).reshape(shard_rows, -1).astype(F32)
-        gate_up_grad = rows_product(residual_all, d_both).astype(BF)
+        gate_up_grad = weight_grad([residual_all], d_both)
         gate_up_grad, sent = fence((gate_up_grad, sent))
         gate_up_rows = scatter_dp(gate_up_grad)
         d_res = cot.astype(F32) + scatter_end(own, sent)
@@ -749,22 +827,16 @@
         inner = sum_stats(inner[:, 0].reshape(2, n, tokens), n).reshape(2, length)
         inner, down_rows = fence((inner, down_rows))
         down_back = send_rows(down_rows, me, n)
-        d_qkv, after, before, far, own = input_back(
-            d_query, d_key, d_v, qkv, (inner / width).T, factors, w_qkv, n
-        )
-        after, before, far, own, d_qkv, down_back = fence(
-            (after, before, far, own, d_qkv, down_back)
-        )
-        sent = scatter_start(after, before, n)
-        qkv_grad = rows_product(x_all, d_qkv).astype(BF)
-        sent, qkv_grad = fence((sent, qkv_grad))
+        d_qkv, ends, after, before, far, own = input_back(
+            me_ref, d_query, d_key, d_v, qkv, (inner / width).T, factors, w_qkv, n
+        )
+        ends, after, before, far, own, d_qkv, down_back = fence(
+            (ends, after, before, far, own, d_qkv, down_back)
+        )
+        sent = scatter_start(ends, after, before, n)
+        attn_grads = attn_grad(me_ref, x_all, d_qkv, pieces, d_attn_part)
+        sent, attn_grads = fence((sent, attn_grads))
         sent[0] = scatter_far(far, sent[0], n)
-        out_grads = [
-            rows_product(piece, jnp.roll(d_attn_part, -p * tokens, axis=0)).astype(BF)
-            for p, piece in enumerate(pieces)
-        ]
-        out_grad = roll_blocks(jnp.stack(out_grads), (n - me) % n).reshape(width, part)
-        attn_grads = jnp.concatenate([qkv_grad, out_grad], axis=1)
         attn_rows = scatter_dp(attn_grads)
         input_grad = d_res + scatter_end(own, sent)
         spread = lambda g: lax.dynamic_update_slice(jnp.zeros(width, F32), g, (me * part,))
@@ -784,6 +856,9 @@
             for j in range(2)
         )
         grad_down = join_columns(down_back, me).T
+        attn_back, grad_gate, grad_up, grad_down = fence(
+            (attn_back, grad_gate, grad_up, grad_down)
+        )
         grad_query, grad_key, grad_value, grad_output = (
             joined(attn_back[:, :, j * part : (j + 1) * part]) for j in range(4)
         )

time: 933 us -> 924 us (level)
  Pallas kernels: 202 us -> 269 us
  matrix products: 51.3 us -> 0 us
  starting transfers between devices: 126 us -> 111 us
  other arithmetic: 65.9 us -> 53 us
    pallas_call x4 -> x7, Pallas kernels: 73.9 us -> 134 us  [the longest x3 58.5 us: ff_backward(): pl.pallas_call(functools.partial(ff_back_kernel, len(saved), group), grid...]
    dot_general x7 -> x0, matrix products: 51.3 us -> none  [rows_product(): lax.dot_general(left, right, (((0,), (0,)), ((), ())), preferred_element_...]
    ppermute x3, waiting for transfers between devices: 44 us -> 8.32 us  [scatter_start(): ends = lax.ppermute(ends, 'seq', [(0, 1), (count - 1, count - 2)])]
    ppermute x3, waiting for transfers between devices: 0.01 us -> 20 us  [scatter_start(): after = lax.ppermute(after, 'seq', step)]
    all_to_all x1, waiting for transfers between devices: 0.01 us -> 17.3 us  [swap_blocks(): lax.all_to_all(values, 'seq', split_axis=0, concat_axis=0, tiled=True)]
    pallas_call x2 -> x3, Pallas kernels: 46.6 us -> 54.1 us  [ff_forward(): pl.pallas_call(functools.partial(ff_kernel, len(saved)), grid=(ff_part //...]
  transfers between devices with their start and end apart: 67 -> 67, of which waited for: 26 -> 30; matrix products, arithmetic and copies ran while one was open for 13% -> 6% of each run, Pallas kernels for 16% -> 23%
where the time goes in v3:
time: 924 us; the launch traced here: 918 us
  waiting for transfers between devices  397 us (43%)
  Pallas kernels  269 us (29%)
  starting transfers between devices  111 us (12%)
  other arithmetic  53 us (6%)
  local copies, waits for them, and re-layouts  45.2 us (5%)
  blocking collectives  26.5 us (3%)
  between operations  15.7 us (2%)
    ppermute x4, waiting for transfers between devices, gather_cyclic(): far = lax.ppermute(values, 'seq', [(i ^ 2, i) for i in range(4)])  127 us
    ppermute x3, waiting for transfers between devices, scatter_far(): return lax.ppermute(far_sum, 'seq', [(i, i ^ 2) for i in range(count)])  89.6 us
    pallas_call x3, Pallas kernels, ff_backward(): pl.pallas_call(functools.partial(ff_back_kernel, len(saved), group), grid...  58.5 us
    ppermute x4, waiting for transfers between devices, gather_cyclic(): ends = lax.ppermute(far, 'seq', [(2, 3), (1, 0)])  56.9 us
    pallas_call x3, Pallas kernels, ff_forward(): pl.pallas_call(functools.partial(ff_kernel, len(saved)), grid=(ff_part //...  54.1 us
    pallas_call x2, Pallas kernels, weight_grad(): pl.pallas_call(lambda *refs: weight_grad_kernel(refs[:-2], *refs[-2:]), g...  41.4 us
    ppermute x5, waiting for transfers between devices, sum_everywhere(): lax.ppermute(values, name, [(i, i ^ bit) for i in range(count)])  40.7 us
    all_to_all x1, blocking collectives, swap_blocks(): lax.all_to_all(values, 'seq', split_axis=0, concat_axis=0, tiled=True)  26.5 us
  transfers between devices with their start and end apart: 67, of which 30 were waited for; matrix products, arithmetic and copies ran while one was open for 6% of the time, Pallas kernels for 23%

profile of v3, /device:TPU:0, one launch (start us, length us, event | category | flops | bytes accessed | tf_op | source)
XLA Modules:
  0.0 917.5 jit_solution(3454671871313240271)
XLA Ops:
  9.4 26.5 %all_to_all.10 = bf16[4,64,1536]{2,1,0:T(8,128)(2,1)} all-to-all(bf16[4,64,1536]{2,1,0:T(8,128)(2,1)S(1)} %pad_maximum_fusion), channel_id=1, replica_groups=mesh['dp'=8,'seq'=4] {'seq'}, dimensions={0} | all-to-all | bytes 1572864 | tf_op jit(solution)/shard_map/all_to_all | solution.py:91
  42.0 7.0 collective-permute-done
  56.7 9.6 %collective-permute-done.1 = bf16[64,2048]{1,0:T(8,128)(2,1)S(1)} collective-permute-done((bf16[64,2048]{1,0:T(8,128)(2,1)S(1)}, bf16[64,2048]{1,0:T(8,128)(2,1)S(1)}, u32[]{:S(2)}, u32[]{:S(2)}) %collective-permute-start.1) | collective-permute-done | bytes 262176 | tf_op jit(solution)/shard_map/ppermute | solution.py:48
  85.2 42.5 %collective-permute-done.7.refs_2_ = bf16[256,2048]{1,0:T(8,128)(2,1)} collective-permute-done((bf16[256,2048]{1,0:T(8,128)(2,1)}, bf16[256,2048]{1,0:T(8,128)(2,1)}, u32[]{:S(2)}, u32[]{:S(2)}) %collective-permute-start.7) | collective-permute-done | bytes 1048608 | tf_op jit(solution)/shard_map/ppermute | solution.py:45
  136.0 15.5 %collective-permute-done.8 = bf16[256,2048]{1,0:T(8,128)(2,1)S(1)} collective-permute-done((bf16[256,2048]{1,0:T(8,128)(2,1)}, bf16[256,2048]{1,0:T(8,128)(2,1)S(1)}, u32[]{:S(2)}, u32[]{:S(2)}) %collective-permute-start.8) | collective-permute-done | bytes 1048608 | tf_op jit(solution)/shard_map/ppermute | solution.py:48
  158.8 16.1 %qkv_project.1 = (bf16[1024,2048]{1,0:T(8,128)(2,1)}, f32[1024,1536]{1,0:T(8,128)}, f32[2,8,1024]{2,1,0:T(8,128)}) custom-call(s32[1]{0:T(128)} %bitcast.5.me_ref.refs_0_, bf16[256,2048]{1,0:T(8,128)(2,1)} %bitcast.4.refs_0_, bf16[256,2048]{1,0:T(8,128)(2,1)} %get-tuple-element.161.refs_1_, bf16[256,2048]{1,0:T(8,128)(2,1)} %collective-permute-done.7.refs_2_, ...), custom_call_target="tpu_custom_call" | custom-call | flops 6442450944 | bytes 20971520 | tf_op jit(solution)/shard_map/qkv_project/pallas_call | solution.py:504
  199.6 16.1 %attend.1 = (bf16[1024,512]{1,0:T(8,128)(2,1)}, bf16[1024,512]{1,0:T(8,128)(2,1)}, bf16[1024,512]{1,0:T(8,128)(2,1)}, bf16[1024,512]{1,0:T(8,128)(2,1)}) custom-call(s32[1]{0:T(128)} %bitcast.5.me_ref.refs_0_, f32[1024,1536]{1,0:T(8,128)} %get-tuple-element.164.q_ref.k_ref.v_ref.refs_7_.refs_8_.qp_ref.kp_ref, ...), custom_call_target="tpu_custom_call" | custom-call | flops 2147483648 | bytes 16777216 | tf_op jit(solution)/shard_map/attend/pallas_call | solution.py:264
  226.4 40.7 %collective-permute-done.20.refs_3_.refs_2_ = bf16[1024,512]{1,0:T(8,128)(2,1)S(1)} collective-permute-done((bf16[1024,512]{1,0:T(8,128)(2,1)S(1)}, bf16[1024,512]{1,0:T(8,128)(2,1)S(1)}, u32[]{:S(2)}, u32[]{:S(2)}) %collective-permute-start.20) | collective-permute-done | bytes 1048608 | tf_op jit(solution)/shard_map/ppermute | solution.py:45
  268.8 22.1 %collective-permute-done.21 = bf16[1024,512]{1,0:T(8,128)(2,1)S(1)} collective-permute-done((bf16[1024,512]{1,0:T(8,128)(2,1)S(1)}, bf16[1024,512]{1,0:T(8,128)(2,1)S(1)}, u32[]{:S(2)}, u32[]{:S(2)}) %collective-permute-start.21) | collective-permute-done | bytes 1048608 | tf_op jit(solution)/shard_map/ppermute | solution.py:48
  292.4 17.3 %out_project.1 = (bf16[1024,2048]{1,0:T(8,128)(2,1)}, f32[256,2048]{1,0:T(8,128)}) custom-call(s32[1]{0:T(128)} %bitcast.5.me_ref.refs_0_, bf16[1024,512]{1,0:T(8,128)(2,1)} %get-tuple-element.172.refs_1_.refs_0_, bf16[1024,512]{1,0:T(8,128)(2,1)} %get-tuple-element.337.refs_2_.refs_1_, bf16[1024,512]{1,0:T(8,128)(2,1)} %copy-done.36, ...), custom_call_target="tpu_custom_call" | custom-call | flops 8589934592 | bytes 23068672 | tf_op jit(solution)/shard_map/out_project/pallas_call | solution.py:671
  309.8 22.6 %ff_forward.3 = (f32[1024,2048]{1,0:T(8,128)}, f32[1024,2048]{1,0:T(8,128)}, bf16[1024,2048]{1,0:T(8,128)(2,1)}, bf16[256,2048]{1,0:T(8,128)(2,1)}, bf16[256,204...) custom-call(s32[1]{0:T(128)} %bitcast.5.me_ref.refs_0_, bf16[1024,2048]{1,0:T(8,128)(2,1)} %get-tuple-element.197.h_ref.refs_0_, ...), custom_call_target="tpu_custom_call" | custom-call | flops 12884901888 | bytes 41943040 | tf_op jit(solution)/shard_map/ff_forward/pallas_call | solution.py:598
  337.7 15.8 %ff_forward.4 = (f32[1024,2048]{1,0:T(8,128)}, f32[1024,2048]{1,0:T(8,128)}, bf16[1024,2048]{1,0:T(8,128)(2,1)}, f32[256,2048]{1,0:T(8,128)}) custom-call(s32[1]{0:T(128)} %bitcast.5.me_ref.refs_0_, bf16[1024,2048]{1,0:T(8,128)(2,1)} %get-tuple-element.197.h_ref.refs_0_, ...), custom_call_target="tpu_custom_call", output_to_operand_aliasing={{0}: (5, {}), {1}: (6, {}), {2}: (7, {})} | custom-call | flops 6442450944 | bytes 41943040 | tf_op jit(solution)/shard_map/ff_forward/pallas_call | solution.py:598
  365.7 15.8 %ff_forward.5 = (f32[1024,2048]{1,0:T(8,128)}, f32[1024,2048]{1,0:T(8,128)}, bf16[1024,2048]{1,0:T(8,128)(2,1)}, f32[256,2048]{1,0:T(8,128)}) custom-call(s32[1]{0:T(128)} %bitcast.5.me_ref.refs_0_, bf16[1024,2048]{1,0:T(8,128)(2,1)} %get-tuple-element.197.h_ref.refs_0_, ...), custom_call_target="tpu_custom_call", output_to_operand_aliasing={{0}: (5, {}), {1}: (6, {}), {2}: (7, {})} | custom-call | flops 6442450944 | bytes 41943040 | tf_op jit(solution)/shard_map/ff_forward/pallas_call | solution.py:598
  381.5 28.8 %collective-permute-done.25 = bf16[256,2048]{1,0:T(8,128)(2,1)S(1)} collective-permute-done((bf16[256,2048]{1,0:T(8,128)(2,1)S(1)}, bf16[256,2048]{1,0:T(8,128)(2,1)S(1)}, u32[]{:S(2)}, u32[]{:S(2)}) %collective-permute-start.25) | collective-permute-done | bytes 1048608 | tf_op jit(solution)/shard_map/ppermute | solution.py:62
  419.9 36.6 %collective-permute-done.28.refs_2_.refs_0_ = bf16[256,2048]{1,0:T(8,128)(2,1)S(1)} collective-permute-done((bf16[256,2048]{1,0:T(8,128)(2,1)S(1)}, bf16[256,2048]{1,0:T(8,128)(2,1)S(1)}, u32[]{:S(2)}, u32[]{:S(2)}) %collective-permute-start.28) | collective-permute-done | bytes 1048608 | tf_op jit(solution)/shard_map/ppermute | solution.py:45
  457.9 16.1 %ff_backward.3 = (bf16[1024,4096]{1,0:T(8,128)(2,1)}, f32[256,2048]{1,0:T(8,128)}) custom-call(s32[1]{0:T(128)} %bitcast.5.me_ref.refs_0_, bf16[256,2048]{1,0:T(8,128)(2,1)} %copy-done.7, bf16[2048,4096]{1,0:T(8,128)(2,1)} %all-gather.6.cloned.1.call-done.refs_5_.wg_ref.refs_1_.refs_2_.w_ref, ...), custom_call_target="tpu_custom_call" | custom-call | flops 6442450944 | bytes 41943040 | tf_op jit(solution)/shard_map/ff_backward/pallas_call | solution.py:625
  474.1 9.7 %collective-permute-done.29 = bf16[256,2048]{1,0:T(8,128)(2,1)} collective-permute-done((bf16[256,2048]{1,0:T(8,128)(2,1)S(1)}, bf16[256,2048]{1,0:T(8,128)(2,1)}, u32[]{:S(2)}, u32[]{:S(2)}) %collective-permute-start.29) | collective-permute-done | bytes 1048608 | tf_op jit(solution)/shard_map/ppermute | solution.py:48
  486.4 24.0 %ff_backward.4 = (bf16[1024,4096]{1,0:T(8,128)(2,1)}, bf16[256,2048]{1,0:T(8,128)(2,1)}, bf16[256,2048]{1,0:T(8,128)(2,1)}, bf16[256,2048]{1,0:T(8,128)(2,1)}) custom-call(s32[1]{0:T(128)} %bitcast.5.me_ref.refs_0_, bf16[256,2048]{1,0:T(8,128)(2,1)} %get-tuple-element.220.refs_0_, ...), custom_call_target="tpu_custom_call", output_to_operand_aliasing={{0}: (8, {})} | custom-call | flops 12884901888 | bytes 41943040 | tf_op jit(solution)/shard_map/ff_backward/pallas_call | solution.py:625
  510.4 14.4 %weight_grad.2 = bf16[2048,2048]{1,0:T(8,128)(2,1)} custom-call(bf16[256,2048]{1,0:T(8,128)(2,1)} %get-tuple-element.220.refs_0_, bf16[256,2048]{1,0:T(8,128)(2,1)} %get-tuple-element.221.refs_1_, bf16[256,2048]{1,0:T(8,128)(2,1)} %copy-done.19, bf16[256,2048]{1,0:T(8,128)(2,1)} %copy-done.7, bf16[1024,2048]{1,0:T(8,128)(2,1)} %get-tuple-element.223.refs_4_), custom_call_target="tpu_custom_call" | custom-call | flops 8589934592 | bytes 12582912 | tf_op jit(solution)/shard_map/weight_grad/pallas_call | solution.py:408
  530.0 18.3 %ff_backward.5 = (bf16[1024,4096]{1,0:T(8,128)(2,1)}, f32[256,2048]{1,0:T(8,128)}) custom-call(s32[1]{0:T(128)} %bitcast.5.me_ref.refs_0_, bf16[256,2048]{1,0:T(8,128)(2,1)} %copy-done.19, bf16[2048,4096]{1,0:T(8,128)(2,1)} %all-gather.6.cloned.1.call-done.refs_5_.wg_ref.refs_1_.refs_2_.w_ref, ...), custom_call_target="tpu_custom_call", output_to_operand_aliasing={{0}: (7, {})} | custom-call | flops 6442450944 | bytes 41943040 | tf_op jit(solution)/shard_map/ff_backward/pallas_call | solution.py:625
  554.9 26.9 %weight_grad.3 = bf16[2048,4096]{1,0:T(8,128)(2,1)} custom-call(bf16[1024,2048]{1,0:T(8,128)(2,1)} %get-tuple-element.197.h_ref.refs_0_, bf16[1024,4096]{1,0:T(8,128)(2,1)} %get-tuple-element.229.refs_1_), custom_call_target="tpu_custom_call" | custom-call | flops 17179869184 | bytes 25165824 | tf_op jit(solution)/shard_map/weight_grad/pallas_call | solution.py:408
  581.8 17.8 %collective-permute-done.33 = bf16[256,2048]{1,0:T(8,128)(2,1)} collective-permute-done((bf16[256,2048]{1,0:T(8,128)(2,1)}, bf16[256,2048]{1,0:T(8,128)(2,1)}, u32[]{:S(2)}, u32[]{:S(2)}) %collective-permute-start.33) | collective-permute-done | bytes 1048608 | tf_op jit(solution)/shard_map/ppermute | solution.py:62
  610.5 8.3 mixed_back.1
  628.1 12.2 %collective-permute-done.37.refs_2_ = bf16[256,512]{1,0:T(8,128)(2,1)S(1)} collective-permute-done((bf16[256,512]{1,0:T(8,128)(2,1)}, bf16[256,512]{1,0:T(8,128)(2,1)S(1)}, u32[]{:S(2)}, u32[]{:S(2)}) %collective-permute-start.37) | collective-permute-done | bytes 262176 | tf_op jit(solution)/shard_map/ppermute | solution.py:818
  648.3 23.0 %attend_back.1 = (f32[1024,512]{1,0:T(8,128)}, f32[1024,512]{1,0:T(8,128)}, bf16[1024,512]{1,0:T(8,128)(2,1)}, f32[2,8,1024]{2,1,0:T(8,128)}, f32[2,8,512]{2,1,0:T(8,128)}) custom-call(s32[1]{0:T(128)} %bitcast.5.me_ref.refs_0_, bf16[256,512]{1,0:T(8,128)(2,1)} %get-tuple-element.241.refs_0_, bf16[256,512]{1,0:T(8,128)(2,1)} %copy-done.40, ...), custom_call_target="tpu_custom_call" | custom-call | flops 5368709120 | bytes 25165824 | tf_op jit(solution)/shard_map/attend_back/pallas_call | solution.py:287
  691.0 15.9 %input_back.1 = (bf16[1024,1536]{1,0:T(8,128)(2,1)}, bf16[256,2048]{1,0:T(8,128)(2,1)}, bf16[256,2048]{1,0:T(8,128)(2,1)}, bf16[256,2048]{1,0:T(8,128)(2,1)}, f32[256,2048]{1,0:T(8,128)}, /*index=5*/f32[256,2048]{1,0:T(8,128)}) custom-call(s32[1]{0:T(128)} %bitcast.5.me_ref.refs_0_, f32[1024,512]{1,0:T(8,128)} %get-tuple-element.248.q_ref, ...), custom_call_target="tpu_custom_call" | custom-call | flops 6442450944 | bytes 25165824 | tf_op jit(solution)/shard_map/input_back/pallas_call | solution.py:371
  715.1 18.2 %attn_grad.1 = bf16[2048,2048]{1,0:T(8,128)(2,1)} custom-call(s32[1]{0:T(128)} %bitcast.5.me_ref.refs_0_, bf16[1024,2048]{1,0:T(8,128)(2,1)} %get-tuple-element.181.refs_6_.x_ref, bf16[1024,1536]{1,0:T(8,128)(2,1)} %get-tuple-element.266.d_ref, bf16[1024,512]{1,0:T(8,128)(2,1)} %get-tuple-element.172.refs_1_.refs_0_, ...), custom_call_target="tpu_custom_call" | custom-call | flops 8589934592 | bytes 20971520 | tf_op jit(solution)/shard_map/attn_grad/pallas_call | solution.py:444
  734.4 20.0 %collective-permute-done.49 = bf16[256,2048]{1,0:T(8,128)(2,1)} collective-permute-done((bf16[256,2048]{1,0:T(8,128)(2,1)}, bf16[256,2048]{1,0:T(8,128)(2,1)}, u32[]{:S(2)}, u32[]{:S(2)}) %collective-permute-start.49) | collective-permute-done | bytes 1048608 | tf_op jit(solution)/shard_map/ppermute | solution.py:55
  758.8 43.0 %collective-permute-done.51 = bf16[256,2048]{1,0:T(8,128)(2,1)S(1)} collective-permute-done((bf16[256,2048]{1,0:T(8,128)(2,1)S(1)}, bf16[256,2048]{1,0:T(8,128)(2,1)S(1)}, u32[]{:S(2)}, u32[]{:S(2)}) %collective-permute-start.51) | collective-permute-done | bytes 1048608 | tf_op jit(solution)/shard_map/ppermute | solution.py:62
  822.9 21.7 %collective-permute-done.58 = f32[4,2048]{1,0:T(4,128)S(1)} collective-permute-done((f32[4,2048]{1,0:T(4,128)S(1)}, f32[4,2048]{1,0:T(4,128)S(1)}, u32[]{:S(2)}, u32[]{:S(2)}) %collective-permute-start.58) | collective-permute-done | bytes 32800 | tf_op jit(solution)/shard_map/ppermute | solution.py:85
  845.3 11.3 %collective-permute-done.59 = f32[4,2048]{1,0:T(4,128)S(1)} collective-permute-done((f32[4,2048]{1,0:T(4,128)S(1)}, f32[4,2048]{1,0:T(4,128)S(1)}, u32[]{:S(2)}, u32[]{:S(2)}) %collective-permute-start.59) | collective-permute-done | bytes 32800 | tf_op jit(solution)/shard_map/ppermute | solution.py:85
  889.5 17.3 %all-to-all-done.1 = bf16[4,64,2048]{2,1,0:T(8,128)(2,1)S(1)} async-done(((bf16[4,64,2048]{2,1,0:T(8,128)(2,1)}), bf16[4,64,2048]{2,1,0:T(8,128)(2,1)S(1)}, u32[]{:S(2)}, u32[]{:S(2)}) %all-to-all-start.1) | async-done | bytes 1048608 | tf_op jit(solution)/shard_map/all_to_all | solution.py:91
  (341 shorter events, 250.7 us)
Async XLA Ops:
  7.2 151.6 %all-gather.4.cloned.1.call-start = ((), (), s32[]{:S(2)}) async-start(), calls=%async_computation.5 | async-start | bytes 7077888 | tf_op jit(solution)/shard_map/all_gather | solution.py:132
  35.9 256.6 %all-gather.6.cloned.1.call-start = ((), (), s32[]{:S(2)}) async-start(), calls=%async_computation.6 | async-start | bytes 18874368 | tf_op jit(solution)/shard_map/all_gather | solution.py:132
  77.8 232.0 %all-gather.8.cloned.1.call-start = ((), (), s32[]{:S(2)}) async-start(), calls=%async_computation.7 | async-start | bytes 18874368 | tf_op jit(solution)/shard_map/all_gather | solution.py:132
  77.8 49.9 %collective-permute-start.7 = (bf16[256,2048]{1,0:T(8,128)(2,1)}, bf16[256,2048]{1,0:T(8,128)(2,1)}, u32[]{:S(2)}, u32[]{:S(2)}) collective-permute-start(bf16[256,2048]{1,0:T(8,128)(2,1)} %bitcast.4.refs_0_), channel_id=1, source_target_pairs={{2,0},{3,1},{0,2},{1,3},{6,4},{7,5},{4,6},{5,7},{10,8},{11,9},{8,1... | collective-permute-start | bytes 3145736 | tf_op jit(solution)/shard_map/ppermute | solution.py:45
  79.0 57.0 %collective-permute-start.10 = (bf16[256,2048]{1,0:T(8,128)(2,1)}, bf16[256,2048]{1,0:T(8,128)(2,1)S(1)}, u32[]{:S(2)}, u32[]{:S(2)}) collective-permute-start(bf16[256,2048]{1,0:T(8,128)(2,1)} %bitcast.4.refs_0_), channel_id=1, source_target_pairs={{0,1},{1,2},{2,3},{4,5},{5,6},{6,7},{8,9},{9,10},{10,11},{12,13},{... | collective-permute-start | bytes 3145736 | tf_op jit(solution)/shard_map/ppermute | solution.py:47
  83.9 52.2 %collective-permute-start.9 = (bf16[256,2048]{1,0:T(8,128)(2,1)}, bf16[256,2048]{1,0:T(8,128)(2,1)S(1)}, u32[]{:S(2)}, u32[]{:S(2)}) collective-permute-start(bf16[256,2048]{1,0:T(8,128)(2,1)} %bitcast.4.refs_0_), channel_id=1, source_target_pairs={{1,0},{2,1},{3,2},{5,4},{6,5},{7,6},{9,8},{10,9},{11,10},{13,12},{... | collective-permute-start | bytes 3145736 | tf_op jit(solution)/shard_map/ppermute | solution.py:46
  217.3 423.0 %reduce-scatter.4.cloned.1.call-start = ((), (), s32[]{:S(2)}) async-start(), calls=%async_computation.8 | async-start | bytes 9437184 | tf_op jit(solution)/shard_map/reduce_scatter | solution.py:136
  217.4 49.7 %collective-permute-start.20 = (bf16[1024,512]{1,0:T(8,128)(2,1)S(1)}, bf16[1024,512]{1,0:T(8,128)(2,1)S(1)}, u32[]{:S(2)}, u32[]{:S(2)}) collective-permute-start(bf16[1024,512]{1,0:T(8,128)(2,1)S(1)} %copy-done.35), channel_id=1, source_target_pairs={{2,0},{3,1},{0,2},{1,3},{6,4},{7,5},{4,6},{5,7},{10,8},{11,9},{8,1... | collective-permute-start | bytes 3145736 | tf_op jit(solution)/shard_map/ppermute | solution.py:45
  220.5 48.3 %collective-permute-start.22 = (bf16[1024,512]{1,0:T(8,128)(2,1)S(1)}, bf16[1024,512]{1,0:T(8,128)(2,1)S(1)}, u32[]{:S(2)}, u32[]{:S(2)}) collective-permute-start(bf16[1024,512]{1,0:T(8,128)(2,1)S(1)} %copy-done.35), channel_id=1, source_target_pairs={{1,0},{2,1},{3,2},{5,4},{6,5},{7,6},{9,8},{10,9},{11,10},{13,12},{... | collective-permute-start | bytes 3145736 | tf_op jit(solution)/shard_map/ppermute | solution.py:46
  221.8 47.0 %collective-permute-start.23 = (bf16[1024,512]{1,0:T(8,128)(2,1)S(1)}, bf16[1024,512]{1,0:T(8,128)(2,1)S(1)}, u32[]{:S(2)}, u32[]{:S(2)}) collective-permute-start(bf16[1024,512]{1,0:T(8,128)(2,1)S(1)} %copy-done.35), channel_id=1, source_target_pairs={{0,1},{1,2},{2,3},{4,5},{5,6},{6,7},{8,9},{9,10},{10,11},{12,13},{... | collective-permute-start | bytes 3145736 | tf_op jit(solution)/shard_map/ppermute | solution.py:47
  332.4 26.4 %collective-permute-start.24 = (bf16[256,2048]{1,0:T(8,128)(2,1)}, bf16[256,2048]{1,0:T(8,128)(2,1)S(1)}, u32[]{:S(2)}, u32[]{:S(2)}) collective-permute-start(bf16[256,2048]{1,0:T(8,128)(2,1)} %get-tuple-element.196), channel_id=1, source_target_pairs={{0,1},{3,2},{4,5},{7,6},{8,9},{11,10},{12,13},{15,14},{16,17},{19,... | collective-permute-start | bytes 3145736 | tf_op jit(solution)/shard_map/ppermute | solution.py:53
  335.1 46.4 %collective-permute-start.26 = (bf16[256,2048]{1,0:T(8,128)(2,1)}, bf16[256,2048]{1,0:T(8,128)(2,1)S(1)}, u32[]{:S(2)}, u32[]{:S(2)}) collective-permute-start(bf16[256,2048]{1,0:T(8,128)(2,1)} %get-tuple-element.204), channel_id=1, source_target_pairs={{0,1},{1,2},{2,3},{4,5},{5,6},{6,7},{8,9},{9,10},{10,11},{12,13},{... | collective-permute-start | bytes 3145736 | tf_op jit(solution)/shard_map/ppermute | solution.py:55
  336.4 45.0 %collective-permute-start.27 = (bf16[256,2048]{1,0:T(8,128)(2,1)}, bf16[256,2048]{1,0:T(8,128)(2,1)S(1)}, u32[]{:S(2)}, u32[]{:S(2)}) collective-permute-start(bf16[256,2048]{1,0:T(8,128)(2,1)} %get-tuple-element.205), channel_id=1, source_target_pairs={{1,0},{2,1},{3,2},{5,4},{6,5},{7,6},{9,8},{10,9},{11,10},{13,12},{... | collective-permute-start | bytes 3145736 | tf_op jit(solution)/shard_map/ppermute | solution.py:56
  360.7 49.6 %collective-permute-start.25 = (bf16[256,2048]{1,0:T(8,128)(2,1)S(1)}, bf16[256,2048]{1,0:T(8,128)(2,1)S(1)}, u32[]{:S(2)}, u32[]{:S(2)}) collective-permute-start(bf16[256,2048]{1,0:T(8,128)(2,1)S(1)} %add_convert_fusion.3), channel_id=1, source_target_pairs={{0,2},{1,3},{2,0},{3,1},{4,6},{5,7},{6,4},{7,5},{8,10},{9,11},{10,... | collective-permute-start | bytes 3145736 | tf_op jit(solution)/shard_map/ppermute | solution.py:62
  413.9 42.6 %collective-permute-start.28 = (bf16[256,2048]{1,0:T(8,128)(2,1)S(1)}, bf16[256,2048]{1,0:T(8,128)(2,1)S(1)}, u32[]{:S(2)}, u32[]{:S(2)}) collective-permute-start(bf16[256,2048]{1,0:T(8,128)(2,1)S(1)} %fusion.4.refs_0_.refs_3_), channel_id=1, source_target_pairs={{2,0},{3,1},{0,2},{1,3},{6,4},{7,5},{4,6},{5,7},{10,8},{11,9},{8,1... | collective-permute-start | bytes 3145736 | tf_op jit(solution)/shard_map/ppermute | solution.py:45
  413.9 60.1 %collective-permute-start.30 = (bf16[256,2048]{1,0:T(8,128)(2,1)S(1)}, bf16[256,2048]{1,0:T(8,128)(2,1)S(1)}, u32[]{:S(2)}, u32[]{:S(2)}) collective-permute-start(bf16[256,2048]{1,0:T(8,128)(2,1)S(1)} %fusion.4.refs_0_.refs_3_), channel_id=1, source_target_pairs={{1,0},{2,1},{3,2},{5,4},{6,5},{7,6},{9,8},{10,9},{11,10},{13,12},{... | collective-permute-start | bytes 3145736 | tf_op jit(solution)/shard_map/ppermute | solution.py:46
  415.2 58.8 %collective-permute-start.31 = (bf16[256,2048]{1,0:T(8,128)(2,1)S(1)}, bf16[256,2048]{1,0:T(8,128)(2,1)S(1)}, u32[]{:S(2)}, u32[]{:S(2)}) collective-permute-start(bf16[256,2048]{1,0:T(8,128)(2,1)S(1)} %fusion.4.refs_0_.refs_3_), channel_id=1, source_target_pairs={{0,1},{1,2},{2,3},{4,5},{5,6},{6,7},{8,9},{9,10},{10,11},{12,13},{... | collective-permute-start | bytes 3145736 | tf_op jit(solution)/shard_map/ppermute | solution.py:47
  456.4 27.3 %collective-permute-start.29 = (bf16[256,2048]{1,0:T(8,128)(2,1)S(1)}, bf16[256,2048]{1,0:T(8,128)(2,1)}, u32[]{:S(2)}, u32[]{:S(2)}) collective-permute-start(bf16[256,2048]{1,0:T(8,128)(2,1)S(1)} %collective-permute-done.28.refs_2_.refs_0_), channel_id=1, source_target_pairs={{2,3},{1,0},{6,7},{5,4},{10,11},{9,8},{14,15},{13,12},{18,19},{17,... | collective-permute-start | bytes 3145736 | tf_op jit(solution)/shard_map/ppermute | solution.py:48
  524.9 280.2 %reduce-scatter.8.cloned.1.call-start = ((), (), s32[]{:S(2)}) async-start(), calls=%async_computation.10 | async-start | bytes 18874368 | tf_op jit(solution)/shard_map/reduce_scatter | solution.py:136
  526.4 55.4 %collective-permute-start.34 = (bf16[256,2048]{1,0:T(8,128)(2,1)}, bf16[256,2048]{1,0:T(8,128)(2,1)}, u32[]{:S(2)}, u32[]{:S(2)}) collective-permute-start(bf16[256,2048]{1,0:T(8,128)(2,1)} %get-tuple-element.232), channel_id=1, source_target_pairs={{0,1},{1,2},{2,3},{4,5},{5,6},{6,7},{8,9},{9,10},{10,11},{12,13},{... | collective-permute-start | bytes 3145736 | tf_op jit(solution)/shard_map/ppermute | solution.py:55
  528.7 53.1 %collective-permute-start.35 = (bf16[256,2048]{1,0:T(8,128)(2,1)}, bf16[256,2048]{1,0:T(8,128)(2,1)}, u32[]{:S(2)}, u32[]{:S(2)}) collective-permute-start(bf16[256,2048]{1,0:T(8,128)(2,1)} %get-tuple-element.233), channel_id=1, source_target_pairs={{1,0},{2,1},{3,2},{5,4},{6,5},{7,6},{9,8},{10,9},{11,10},{13,12},{... | collective-permute-start | bytes 3145736 | tf_op jit(solution)/shard_map/ppermute | solution.py:56
  553.0 46.6 %collective-permute-start.33 = (bf16[256,2048]{1,0:T(8,128)(2,1)}, bf16[256,2048]{1,0:T(8,128)(2,1)}, u32[]{:S(2)}, u32[]{:S(2)}) collective-permute-start(bf16[256,2048]{1,0:T(8,128)(2,1)} %add_convert_fusion.1), channel_id=1, source_target_pairs={{0,2},{1,3},{2,0},{3,1},{4,6},{5,7},{6,4},{7,5},{8,10},{9,11},{10,... | collective-permute-start | bytes 3145736 | tf_op jit(solution)/shard_map/ppermute | solution.py:62
  599.6 257.0 %reduce-scatter.6.cloned.1.call-start = ((), (), s32[]{:S(2)}) async-start(), calls=%async_computation.9 | async-start | bytes 9437184 | tf_op jit(solution)/shard_map/reduce_scatter | solution.py:136
  641.2 30.1 %collective-permute-start.39 = (bf16[256,512]{1,0:T(8,128)(2,1)S(1)}, bf16[256,512]{1,0:T(8,128)(2,1)S(1)}, u32[]{:S(2)}, u32[]{:S(2)}) collective-permute-start(bf16[256,512]{1,0:T(8,128)(2,1)S(1)} %get-tuple-element.332), channel_id=1, source_target_pairs={{0,3},{1,0},{2,1},{3,2},{4,7},{5,4},{6,5},{7,6},{8,11},{9,8},{10,9... | collective-permute-start | bytes 786440 | tf_op jit(solution)/shard_map/ppermute | solution.py:695
  641.2 30.1 %collective-permute-start.40 = (bf16[256,512]{1,0:T(8,128)(2,1)S(1)}, bf16[256,512]{1,0:T(8,128)(2,1)S(1)}, u32[]{:S(2)}, u32[]{:S(2)}) collective-permute-start(bf16[256,512]{1,0:T(8,128)(2,1)S(1)} %get-tuple-element.331), channel_id=1, source_target_pairs={{0,2},{1,3},{2,0},{3,1},{4,6},{5,7},{6,4},{7,5},{8,10},{9,11},{10,... | collective-permute-start | bytes 786440 | tf_op jit(solution)/shard_map/ppermute | solution.py:695
  711.5 42.9 %collective-permute-start.49 = (bf16[256,2048]{1,0:T(8,128)(2,1)}, bf16[256,2048]{1,0:T(8,128)(2,1)}, u32[]{:S(2)}, u32[]{:S(2)}) collective-permute-start(bf16[256,2048]{1,0:T(8,128)(2,1)} %get-tuple-element.264), channel_id=1, source_target_pairs={{0,1},{1,2},{2,3},{4,5},{5,6},{6,7},{8,9},{9,10},{10,11},{12,13},{... | collective-permute-start | bytes 3145736 | tf_op jit(solution)/shard_map/ppermute | solution.py:55
  713.8 40.6 %collective-permute-start.50 = (bf16[256,2048]{1,0:T(8,128)(2,1)}, bf16[256,2048]{1,0:T(8,128)(2,1)}, u32[]{:S(2)}, u32[]{:S(2)}) collective-permute-start(bf16[256,2048]{1,0:T(8,128)(2,1)} %get-tuple-element.265), channel_id=1, source_target_pairs={{1,0},{2,1},{3,2},{5,4},{6,5},{7,6},{9,8},{10,9},{11,10},{13,12},{... | collective-permute-start | bytes 3145736 | tf_op jit(solution)/shard_map/ppermute | solution.py:56
  756.1 45.6 %collective-permute-start.51 = (bf16[256,2048]{1,0:T(8,128)(2,1)S(1)}, bf16[256,2048]{1,0:T(8,128)(2,1)S(1)}, u32[]{:S(2)}, u32[]{:S(2)}) collective-permute-start(bf16[256,2048]{1,0:T(8,128)(2,1)S(1)} %add_convert_fusion), channel_id=1, source_target_pairs={{0,2},{1,3},{2,0},{3,1},{4,6},{5,7},{6,4},{7,5},{8,10},{9,11},{10,... | collective-permute-start | bytes 3145736 | tf_op jit(solution)/shard_map/ppermute | solution.py:62
  807.6 49.0 %collective-permute-start.52 = (bf16[64,4096]{1,0:T(8,128)(2,1)}, bf16[64,4096]{1,0:T(8,128)(2,1)S(1)}, u32[]{:S(2)}, u32[]{:S(2)}) collective-permute-start(bf16[64,4096]{1,0:T(8,128)(2,1)} %get-tuple-element.320), channel_id=1, source_target_pairs={{0,1},{1,2},{2,3},{3,0},{4,5},{5,6},{6,7},{7,4},{8,9},{9,10},{10,1... | collective-permute-start | bytes 1572872 | tf_op jit(solution)/shard_map/ppermute | solution.py:117
  807.6 49.0 %collective-permute-start.53 = (bf16[64,4096]{1,0:T(8,128)(2,1)S(1)}, bf16[64,4096]{1,0:T(8,128)(2,1)S(1)}, u32[]{:S(2)}, u32[]{:S(2)}) collective-permute-start(bf16[64,4096]{1,0:T(8,128)(2,1)S(1)} %get-tuple-element.319), channel_id=1, source_target_pairs={{0,2},{1,3},{2,0},{3,1},{4,6},{5,7},{6,4},{7,5},{8,10},{9,11},{10,... | collective-permute-start | bytes 1572872 | tf_op jit(solution)/shard_map/ppermute | solution.py:117
  809.6 47.1 %collective-permute-start.54 = (bf16[64,4096]{1,0:T(8,128)(2,1)S(1)}, bf16[64,4096]{1,0:T(8,128)(2,1)S(1)}, u32[]{:S(2)}, u32[]{:S(2)}) collective-permute-start(bf16[64,4096]{1,0:T(8,128)(2,1)S(1)} %get-tuple-element.318), channel_id=1, source_target_pairs={{0,3},{1,0},{2,1},{3,2},{4,7},{5,4},{6,5},{7,6},{8,11},{9,8},{10,9... | collective-permute-start | bytes 1572872 | tf_op jit(solution)/shard_map/ppermute | solution.py:117
  877.1 29.7 %all-to-all-start.1 = ((bf16[4,64,2048]{2,1,0:T(8,128)(2,1)}), bf16[4,64,2048]{2,1,0:T(8,128)(2,1)S(1)}, u32[]{:S(2)}, u32[]{:S(2)}) async-start(bf16[4,64,2048]{2,1,0:T(8,128)(2,1)} %bitcast.139), calls=%async_computation.4 | async-start | bytes 2097152 | tf_op jit(solution)/shard_map/all_to_all | solution.py:91
  (78 other events, 1042.6 us)
Sparse Core Ops, SparseCore 0:
  36.0 44.6 all-gather.3
  83.1 89.8 all-gather.5
  217.4 91.5 all-gather.7
  525.0 69.8 reduce-scatter.3
  599.8 115.7 reduce-scatter.7
  754.5 71.8 reduce-scatter.5

commit v4 on v3

--- a/solution.py
+++ b/solution.py
@@ -110,22 +110,52 @@
     return total
 
 
-def send_rows(values, me, count):
+def row_blocks(values, me, count):
     size = values.shape[0] // count
-    rows = lambda p: lax.dynamic_slice_in_dim(values, (me + p) % count * size, size, 0)
-    return [rows(0)] + [
-        lax.ppermute(rows(p), "seq", [(i, (i + p) % count) for i in range(count)])
+    return [
+        lax.dynamic_slice_in_dim(values, (me + p) % count * size, size, 0) for p in range(count)
+    ]
+
+
+def send_blocks(blocks):
+    count = len(blocks)
+    return blocks[:1] + [
+        lax.ppermute(blocks[p], "seq", [(i, (i + p) % count) for i in range(count)])
         for p in range(1, count)
     ]
 
 
-def join_columns(blocks, me):
+def join_kernel(sides, me_ref, *refs):
+    blocks, outs = refs[:-sides], refs[-sides:]
+    for p, block in enumerate(blocks):
+
+        @pl.when(pl.program_id(0) == p)
+        def _(block=block):
+            for j, out in enumerate(outs):
+                tile = min(FF_TILE, out.shape[1])
+                for at in range(0, out.shape[1], tile):
+                    first = at * sides + j * tile
+                    out[:, at : at + tile] = block[:, first : first + tile].astype(F32)
+
+
+def join_columns(me, blocks, sides):
     count = len(blocks)
-    rows, part = blocks[0].shape
-    total = jnp.zeros((rows, count * part), F32)
-    for p, block in enumerate(blocks):
-        total = lax.dynamic_update_slice(total, block.astype(F32), (0, (me - p) % count * part))
-    return total
+    rows, columns = blocks[0].shape
+    part = columns // sides
+    out = pl.BlockSpec((rows, part), lambda p, me: (0, (me[0] + count - p) % count))
+    return pl.pallas_call(
+        functools.partial(join_kernel, sides),
+        grid_spec=pltpu.PrefetchScalarGridSpec(
+            num_scalar_prefetch=1,
+            grid=(count,),
+            in_specs=[once((rows, columns), lambda p, me: (0, 0))] * count,
+            out_specs=[out] * sides,
+        ),
+        out_shape=[jax.ShapeDtypeStruct((rows, count * part), F32)] * sides,
+        compiler_params=params(),
+        cost_estimate=cost(0, 0),
+        name="join_columns",
+    )(me, *blocks)
 
 
 def gather_dp(values):
@@ -273,7 +303,7 @@
         ),
         out_shape=[low] * 4,
         compiler_params=params(),
-        cost_estimate=cost(4 * length * length * part, 16 << 20, length * length * heads),
+        cost_estimate=cost(0, 0),
         name="attend",
     )(me, qkv, qkv, qkv, factors, q_gain[None], k_gain[None], *tables, seg[:, None], seg[None])
 
@@ -304,40 +334,63 @@
         out_shape=[jax.ShapeDtypeStruct((length, part), t) for t in (F32, F32, BF)]
         + [jax.ShapeDtypeStruct((2, 8, m), F32) for m in (length, part)],
         compiler_params=params(),
-        cost_estimate=cost(10 * length * length * part, 24 << 20, length * length * heads),
+        cost_estimate=cost(0, 0),
         name="attend_back",
     )(me, *pieces, query, key, value, qkv, qkv, factors, q_gain[None], k_gain[None], *tables,
       seg[:, None], seg[None])
 
 
-def mixed_back_kernel(me_ref, d_ref, w_ref, *refs):
-    for p, out in enumerate(refs):
-
-        @pl.when(pl.program_id(0) == p)
+def residual_back_kernel(
+    me_ref, own_ref, a_ref, b_ref, c_ref, cot_ref, attn_ref, gain_ref, w_ref, res_ref, d_ref, sum_ref, *outs
+):
+    step = pl.program_id(0)
+
+    @pl.when(step == 0)
+    def _():
+        grad = cot_ref[...].astype(F32) + own_ref[...]
+        for ref in (a_ref, b_ref, c_ref):
+            grad = grad + ref[...].astype(F32)
+        res_ref[...] = grad
+        attn = attn_ref[...]
+        factor = inv_rms(attn)
+        normed = attn * factor
+        sums = jnp.sum(grad * normed, axis=0, keepdims=True)
+        sum_ref[...] = jnp.broadcast_to(sums, sum_ref.shape)
+        d_ref[...] = rms_back(normed, factor, gain_ref[...], grad).astype(BF)
+
+    piece = nt_dot(d_ref[...], w_ref[...]).astype(BF)
+    for p, out in enumerate(outs):
+
+        @pl.when(step == p)
         def _(out=out):
-            out[...] = nt_dot(d_ref[...], w_ref[...]).astype(BF)
-
-
-def mixed_back(me, d_attn, w_first, count):
-    tokens, width = d_attn.shape
+            out[...] = piece
+
+
+def residual_back(me, own, got, cot, attn_out, gain, w_first, count):
+    tokens, width = own.shape
     part = width // count
     piece = pl.BlockSpec((tokens, part), lambda p, me: (0, 0))
-    return pl.pallas_call(
-        mixed_back_kernel,
+    full = once((tokens, width), lambda p, me: (0, 0))
+    whole = lambda rows: pl.BlockSpec((rows, width), lambda p, me: (0, 0))
+    return pl.pallas_call(
+        residual_back_kernel,
         grid_spec=pltpu.PrefetchScalarGridSpec(
             num_scalar_prefetch=1,
             grid=(count,),
-            in_specs=[
-                pl.BlockSpec((tokens, width), lambda p, me: (0, 0)),
-                pl.BlockSpec((part, width), lambda p, me: ((me[0] + p) % count, 0)),
-            ],
-            out_specs=[piece] * count,
+            in_specs=[full] * 6
+            + [whole(1), pl.BlockSpec((part, width), lambda p, me: ((me[0] + p) % count, 0))],
+            out_specs=[whole(tokens), whole(tokens), whole(8)] + [piece] * count,
         ),
-        out_shape=[jax.ShapeDtypeStruct((tokens, part), BF)] * count,
-        compiler_params=params(),
-        cost_estimate=cost(2 * tokens * width * width, 10 << 20),
-        name="mixed_back",
-    )(me, d_attn, w_first)
+        out_shape=[
+            jax.ShapeDtypeStruct((tokens, width), F32),
+            jax.ShapeDtypeStruct((tokens, width), BF),
+            jax.ShapeDtypeStruct((8, width), F32),
+        ]
+        + [jax.ShapeDtypeStruct((tokens, part), BF)] * count,
+        compiler_params=params(),
+        cost_estimate=cost(LATE_COST, 0),
+        name="residual_back",
+    )(me, own, *got, cot, attn_out, gain[None], w_first)
 
 
 def input_back_kernel(
@@ -350,29 +403,30 @@
         d_ref[:, j * part : (j + 1) * part] = low
     d_ref[:, 2 * part :] = v_ref[...]
     total = nt_dot(d_ref[...], w_ref[...])
-    for step, out in enumerate(outs):
-
-        @pl.when(pl.program_id(0) == step)
+    step = pl.program_id(0)
+    for j, out in enumerate(outs):
+
+        @pl.when(step == j)
         def _(out=out):
             out[...] = total.astype(out.dtype)
 
-    @pl.when((pl.program_id(0) == 0) | ((pl.program_id(0) == 1) & (me_ref[0] == 0)))
+    @pl.when((step == 0) | ((step == 1) & (me_ref[0] == 0)))
     def _():
         ends_ref[...] = total.astype(BF)
 
 
-def input_back(me, d_query, d_key, d_v, qkv, inner, factors, w_qkv, count):
+def input_back(me, d_query, d_key, d_v, qkv, inner, factors, w_qkv):
     length, part = d_query.shape
     width = w_qkv.shape[0]
-    tokens = length // count
+    tokens = length // 4
     place = lambda t: jnp.where(t == 0, 1, jnp.where(t == 1, 3, jnp.where(t == 2, 2, 0)))
     rows = lambda columns, at=0: pl.BlockSpec((tokens, columns), lambda t, me: (place(t), at))
-    kinds = (BF, BF, BF, F32, F32)
+    kinds = (BF, BF, BF, BF, F32)
     return pl.pallas_call(
         functools.partial(input_back_kernel, part),
         grid_spec=pltpu.PrefetchScalarGridSpec(
             num_scalar_prefetch=1,
-            grid=(count,),
+            grid=(4,),
             in_specs=[rows(part)] * 3
             + [rows(part), rows(part, 1), rows(2), rows(2)]
             + [once((width, 3 * part), lambda t, me: (0, 0))],
@@ -382,9 +436,32 @@
         out_shape=[jax.ShapeDtypeStruct((length, 3 * part), BF)]
         + [jax.ShapeDtypeStruct((tokens, width), kind) for kind in kinds],
         compiler_params=params(),
-        cost_estimate=cost(6 * length * width * part, 24 << 20),
+        cost_estimate=cost(0, 0),
         name="input_back",
     )(me, d_query, d_key, d_v, qkv, qkv, inner, factors, w_qkv)
+
+
+def add_up_kernel(*refs):
+    total = refs[0][...]
+    for ref in refs[1:-1]:
+        total = total + ref[...].astype(F32)
+    refs[-1][...] = total.astype(BF)
+
+
+def add_up(parts):
+    tokens, width = parts[0].shape
+    tile = tokens // 4
+    block = pl.BlockSpec((tile, width), lambda i: (i, 0))
+    return pl.pallas_call(
+        add_up_kernel,
+        grid=(4,),
+        in_specs=[block] * len(parts),
+        out_specs=block,
+        out_shape=jax.ShapeDtypeStruct((tokens, width), BF),
+        compiler_params=params(),
+        cost_estimate=cost(LATE_COST, 0),
+        name="add_up",
+    )(*parts)
 
 
 def tn_dot(left, right):
@@ -413,7 +490,7 @@
         out_specs=pl.BlockSpec((tile, wide), lambda j, i: (i, j)),
         out_shape=jax.ShapeDtypeStruct((width, columns), BF),
         compiler_params=params(),
-        cost_estimate=cost(2 * length * width * columns, 2 * (length + width) * columns),
+        cost_estimate=cost(0, 0),
         name="weight_grad",
     )(*lefts, right)
 
@@ -456,7 +533,7 @@
         ),
         out_shape=jax.ShapeDtypeStruct((width, columns + part), BF),
         compiler_params=params(),
-        cost_estimate=cost(2 * length * width * (columns + part), 20 << 20),
+        cost_estimate=cost(SIDE_COST, 0),
         name="attn_grad",
     )(me, x_all, d_qkv, *pieces, *d_parts)
 
@@ -479,21 +556,21 @@
 
 def qkv_kernel(count, part, me_ref, *refs):
     chunks, (w_ref, x_ref, qkv_ref, sq_ref) = refs[:-4], refs[-4:]
-    ones = jnp.ones((8, part), F32)
     for q in range(count):
 
         @pl.when(pl.program_id(0) == q)
         def _(q=q):
-            x = chunks[q][...]
-            x_ref[...] = x
-            qkv = jnp.dot(x, w_ref[...], preferred_element_type=F32)
-            qkv_ref[...] = qkv
-            for j in range(2):
-                values = qkv[:, j * part : (j + 1) * part]
-                sq_ref[j] = lax.dot_general(
-                    ones, values * values, (((1,), (1,)), ((), ())),
-                    precision=lax.Precision.HIGHEST, preferred_element_type=F32,
-                )
+            x_ref[...] = chunks[q][...]
+
+    qkv = jnp.dot(x_ref[...], w_ref[...], preferred_element_type=F32)
+    qkv_ref[...] = qkv
+    ones = jnp.ones((8, part), F32)
+    for j in range(2):
+        values = qkv[:, j * part : (j + 1) * part]
+        sq_ref[j] = lax.dot_general(
+            ones, values * values, (((1,), (1,)), ((), ())),
+            precision=lax.Precision.HIGHEST, preferred_element_type=F32,
+        )
 
 
 def qkv_project(me, chunks, w_qkv):
@@ -520,12 +597,14 @@
             jax.ShapeDtypeStruct((2, 8, length), F32),
         ],
         compiler_params=params(),
-        cost_estimate=cost(2 * length * width * columns, 20 << 20),
+        cost_estimate=cost(0, 0),
         name="qkv_project",
     )(me, *chunks, w_qkv)
 
 
 FF_TILE = 512
+LATE_COST = 10**12
+SIDE_COST = 10**11
 
 
 def ff_finish(step, product, acc, me_ref, outs):
@@ -608,7 +687,7 @@
         scratch_shapes=[pltpu.VMEM((rows, width), F32)],
         input_output_aliases={5 + j: j for j in range(len(saved))},
         compiler_params=params(),
-        cost_estimate=cost(6 * rows * width * ff_part, 40 << 20, rows * ff_part),
+        cost_estimate=cost(0, 0),
         name="ff_forward",
     )(me, residual_all, w_first, w_second, w_second, *saved)
 
@@ -637,7 +716,7 @@
         scratch_shapes=[pltpu.VMEM((rows, width), F32)],
         input_output_aliases={6 + group + j: j for j in range(len(saved))},
         compiler_params=params(),
-        cost_estimate=cost(6 * rows * width * ff_part, 40 << 20, rows * ff_part),
+        cost_estimate=cost(SIDE_COST, 0),
         name="ff_backward",
     )(me, *d_ffs, w_first, w_second, w_second, gate, up, *saved)
 
@@ -683,7 +762,7 @@
             jax.ShapeDtypeStruct((tokens, width), F32),
         ],
         compiler_params=params(),
-        cost_estimate=cost(2 * length * width * width, 22 << 20),
+        cost_estimate=cost(0, 0),
         name="out_project",
     )(me, *pieces, w_out, x_all, gain[None])
 
@@ -794,31 +873,28 @@
         d_both, after, before, ends = ff_backward(
             me_ref, d_ffs[1::2], w_first, w_second, gate, up, 0, (BF, BF, BF), (d_both,)
         )
-        after, before, ends, d_ffs, hidden = fence((after, before, ends, d_ffs, hidden))
         sent = scatter_start(ends, after, before, n)
+        d_both, far = ff_backward(
+            me_ref, d_ffs[2:3], w_first, w_second, gate, up, 2, (F32,), (d_both,)
+        )
+        d_both, far, sent[0], d_ffs, hidden = fence((d_both, far, sent[0], d_ffs, hidden))
+        sent[0] = scatter_far(far, sent[0], n)
+        joined = lambda g: g.transpose(1, 0, 2).reshape(shard_rows, -1).astype(F32)
         down_grad = weight_grad([d_ffs[1], d_ffs[3], d_ffs[2], d_ffs[0]], hidden)
         down_rows = scatter_dp(down_grad)
-        d_ff_far, down_grad = fence((d_ffs[2], down_grad))
-        d_both, far = ff_backward(
-            me_ref, [d_ff_far], w_first, w_second, gate, up, 2, (F32,), (d_both,)
-        )
-        d_both, far, sent[0] = fence((d_both, far, sent[0]))
-        sent[0] = scatter_far(far, sent[0], n)
-        joined = lambda g: g.transpose(1, 0, 2).reshape(shard_rows, -1).astype(F32)
-        gate_up_grad = weight_grad([residual_all], d_both)
-        gate_up_grad, sent = fence((gate_up_grad, sent))
-        gate_up_rows = scatter_dp(gate_up_grad)
-        d_res = cot.astype(F32) + scatter_end(own, sent)
-
-        grad_attn_gain = jnp.sum(d_res * attn_normed, axis=0)
-        d_attn = rms_back(attn_normed, attn_factor, attn_gain, d_res).astype(BF)
-        d_pieces = mixed_back(me_ref, d_attn, w_first, n)
+        down_grad, sent = fence((down_grad, sent))
+        d_res, d_attn, grad_attn_gain, *d_pieces = residual_back(
+            me_ref, own, sent, cot, attn_out, attn_gain, w_first, n
+        )
         d_mixed = [d_pieces[0]] + [None] * (n - 1)
         for p in range(1, n):
             d_mixed[n - p] = lax.ppermute(
                 d_pieces[p], "seq", [(i, (i + p) % n) for i in range(n)]
             )
-        d_mixed, d_attn, down_rows = fence((d_mixed, d_attn, down_rows))
+        residual_all, d_both, _ = fence((residual_all, d_both, d_pieces[0]))
+        gate_up_grad = weight_grad([residual_all], d_both)
+        d_mixed, d_attn, gate_up_grad = fence((d_mixed, d_attn, gate_up_grad))
+        gate_up_rows = scatter_dp(gate_up_grad)
         d_attn_part = columns_to_parts(d_attn, me, n)
         d_query, d_key, d_v, inner, gain_sums = attend_back(
             me_ref, d_mixed, q_low, k_low, v_low, qkv, factors, q_gain, k_gain, tables, seg, n
@@ -826,36 +902,34 @@
         inner, d_attn_part = fence((inner, d_attn_part))
         inner = sum_stats(inner[:, 0].reshape(2, n, tokens), n).reshape(2, length)
         inner, down_rows = fence((inner, down_rows))
-        down_back = send_rows(down_rows, me, n)
+        down_back = send_blocks(row_blocks(down_rows, me, n))
         d_qkv, ends, after, before, far, own = input_back(
-            me_ref, d_query, d_key, d_v, qkv, (inner / width).T, factors, w_qkv, n
-        )
-        ends, after, before, far, own, d_qkv, down_back = fence(
-            (ends, after, before, far, own, d_qkv, down_back)
-        )
-        sent = scatter_start(ends, after, before, n)
+            me_ref, d_query, d_key, d_v, qkv, (inner / width).T, factors, w_qkv
+        )
+        d_qkv, ends, after, before, far, own, down_back = fence(
+            (d_qkv, ends, after, before, far, own, down_back)
+        )
+        ends, *sent = scatter_start(ends, after, before, n)
+        sent.append(lax.ppermute(far, "seq", [(0, 2), (3, 1)]))
         attn_grads = attn_grad(me_ref, x_all, d_qkv, pieces, d_attn_part)
-        sent, attn_grads = fence((sent, attn_grads))
-        sent[0] = scatter_far(far, sent[0], n)
+        ends, attn_grads = fence((ends, attn_grads))
         attn_rows = scatter_dp(attn_grads)
-        input_grad = d_res + scatter_end(own, sent)
+        far = (far.astype(F32) + ends.astype(F32)).astype(BF)
+        sent.append(lax.ppermute(far, "seq", [(1, 3), (2, 0)]))
+        input_grad = add_up([d_res, own] + sent)
         spread = lambda g: lax.dynamic_update_slice(jnp.zeros(width, F32), g, (me * part,))
         gains = jnp.stack(
-            [spread(gain_sums[0, 0]), spread(gain_sums[1, 0]), grad_attn_gain, grad_ff_gain]
+            [spread(gain_sums[0, 0]), spread(gain_sums[1, 0]), grad_attn_gain[0], grad_ff_gain]
         )
         input_grad, gate_up_rows, gains = fence((input_grad, gate_up_rows, gains))
-        gate_up_back = send_rows(gate_up_rows, me, n)
+        gate_up_back = send_blocks(row_blocks(gate_up_rows, me, n))
         gains = sum_everywhere(gains, dp_count, n)
         attn_rows, input_grad, gate_up_back, down_back, gains = fence(
             (attn_rows, input_grad, gate_up_back, down_back, gains)
         )
         attn_back = swap_blocks(attn_rows.reshape(n, shard_rows, -1))
-        by_tile = [b.reshape(shard_rows, -1, 2, min(FF_TILE, ff_part)) for b in gate_up_back]
-        grad_gate, grad_up = (
-            join_columns([b[:, :, j].reshape(shard_rows, ff_part) for b in by_tile], me)
-            for j in range(2)
-        )
-        grad_down = join_columns(down_back, me).T
+        grad_gate, grad_up = join_columns(me_ref, gate_up_back, 2)
+        grad_down = join_columns(me_ref, down_back, 1)[0].T
         attn_back, grad_gate, grad_up, grad_down = fence(
             (attn_back, grad_gate, grad_up, grad_down)
         )
@@ -869,7 +943,7 @@
         )
         return (
             activation[None],
-            input_grad.astype(BF)[None],
+            input_grad[None],
             grad_query,
             grad_key,
             grad_value,

time: 924 us -> 883 us (0.956)
  other arithmetic: 53 us -> 25.2 us
  waiting for transfers between devices: 397 us -> 370 us
  Pallas kernels: 269 us -> 284 us
    ppermute x3 -> x2, waiting for transfers between devices: 89.6 us -> 54.5 us  [scatter_far(): return lax.ppermute(far_sum, 'seq', [(i, i ^ 2) for i in range(count)])]
    ppermute x6 -> x8, waiting for transfers between devices: 0.02 us -> 27.8 us  [the longest x1 19.6 us: shards(): sent.append(lax.ppermute(far, 'seq', [(0, 2), (3, 1)]))]
    ppermute x3, waiting for transfers between devices: 18.8 us -> 0.01 us  [shards(): lax.ppermute(d_pieces[p], 'seq', [(i, (i + p) % n) for i in range(n)])]
    pallas_call x1 -> x4, Pallas kernels: 8.27 us -> 24.5 us  [the longest x1 12.4 us: residual_back(): pl.pallas_call(residual_back_kernel, grid_spec=pltpu.PrefetchScalarGridSp...]
    convert_element_type x5 -> x1, other arithmetic: 16.5 us -> 0.39 us  [shards(): far = (far.astype(F32) + ends.astype(F32)).astype(BF)]
  transfers between devices with their start and end apart: 67 -> 68, of which waited for: 30 -> 29; matrix products, arithmetic and copies ran while one was open for 6% -> 5% of each run, Pallas kernels for 23% -> 27%
where the time goes in v4:
time: 883 us; the launch traced here: 873 us
  waiting for transfers between devices  370 us (42%)
  Pallas kernels  284 us (32%)
  starting transfers between devices  114 us (13%)
  local copies, waits for them, and re-layouts  38.3 us (4%)
  blocking collectives  26.5 us (3%)
  other arithmetic  25.2 us (3%)
  between operations  15.9 us (2%)
    ppermute x4, waiting for transfers between devices, gather_cyclic(): far = lax.ppermute(values, 'seq', [(i ^ 2, i) for i in range(4)])  134 us
    ppermute x4, waiting for transfers between devices, gather_cyclic(): ends = lax.ppermute(far, 'seq', [(2, 3), (1, 0)])  60.9 us
    pallas_call x3, Pallas kernels, ff_backward(): pl.pallas_call(functools.partial(ff_back_kernel, len(saved), group), grid...  56.3 us
    ppermute x2, waiting for transfers between devices, scatter_far(): return lax.ppermute(far_sum, 'seq', [(i, i ^ 2) for i in range(count)])  54.5 us
    pallas_call x3, Pallas kernels, ff_forward(): pl.pallas_call(functools.partial(ff_kernel, len(saved)), grid=(ff_part //...  54.1 us
    pallas_call x2, Pallas kernels, weight_grad(): pl.pallas_call(lambda *refs: weight_grad_kernel(refs[:-2], *refs[-2:]), g...  41.3 us
    ppermute x5, waiting for transfers between devices, sum_everywhere(): lax.ppermute(values, name, [(i, i ^ bit) for i in range(count)])  37.6 us
    all_to_all x1, blocking collectives, swap_blocks(): lax.all_to_all(values, 'seq', split_axis=0, concat_axis=0, tiled=True)  26.5 us
  transfers between devices with their start and end apart: 68, of which 29 were waited for; matrix products, arithmetic and copies ran while one was open for 5% of the time, Pallas kernels for 27%

profile of v4, /device:TPU:0, one launch (start us, length us, event | category | flops | bytes accessed | tf_op | source)
XLA Modules:
  0.0 873.4 jit_solution(14673199241108884036)
XLA Ops:
  9.4 26.5 %all_to_all.10 = bf16[4,64,1536]{2,1,0:T(8,128)(2,1)} all-to-all(bf16[4,64,1536]{2,1,0:T(8,128)(2,1)S(1)} %pad_maximum_fusion), channel_id=1, replica_groups=mesh['dp'=8,'seq'=4] {'seq'}, dimensions={0} | all-to-all | bytes 1572864 | tf_op jit(solution)/shard_map/all_to_all | solution.py:91
  41.2 7.8 collective-permute-done
  56.7 9.9 %collective-permute-done.1 = bf16[64,2048]{1,0:T(8,128)(2,1)S(1)} collective-permute-done((bf16[64,2048]{1,0:T(8,128)(2,1)S(1)}, bf16[64,2048]{1,0:T(8,128)(2,1)S(1)}, u32[]{:S(2)}, u32[]{:S(2)}) %collective-permute-start.1) | collective-permute-done | bytes 262176 | tf_op jit(solution)/shard_map/ppermute | solution.py:48
  85.8 43.1 %collective-permute-done.7.refs_2_ = bf16[256,2048]{1,0:T(8,128)(2,1)} collective-permute-done((bf16[256,2048]{1,0:T(8,128)(2,1)S(1)}, bf16[256,2048]{1,0:T(8,128)(2,1)}, u32[]{:S(2)}, u32[]{:S(2)}) %collective-permute-start.7) | collective-permute-done | bytes 1048608 | tf_op jit(solution)/shard_map/ppermute | solution.py:45
  131.3 23.1 %collective-permute-done.8 = bf16[256,2048]{1,0:T(8,128)(2,1)} collective-permute-done((bf16[256,2048]{1,0:T(8,128)(2,1)}, bf16[256,2048]{1,0:T(8,128)(2,1)}, u32[]{:S(2)}, u32[]{:S(2)}) %collective-permute-start.8) | collective-permute-done | bytes 1048608 | tf_op jit(solution)/shard_map/ppermute | solution.py:48
  168.4 15.6 %qkv_project.1 = (bf16[1024,2048]{1,0:T(8,128)(2,1)}, f32[1024,1536]{1,0:T(8,128)}, f32[2,8,1024]{2,1,0:T(8,128)}) custom-call(s32[1]{0:T(128)} %bitcast.5.me_ref.refs_0_, bf16[256,2048]{1,0:T(8,128)(2,1)} %bitcast.98, bf16[256,2048]{1,0:T(8,128)(2,1)} %get-tuple-element.161.refs_1_, bf16[256,2048]{1,0:T(8,128)(2,1)} %collective-permute-done.7.refs_2_, ...), custom_call_target="tpu_custom_call" | custom-call | tf_op jit(solution)/shard_map/qkv_project/pallas_call | solution.py:581
  203.9 16.2 %attend.1 = (bf16[1024,512]{1,0:T(8,128)(2,1)}, bf16[1024,512]{1,0:T(8,128)(2,1)}, bf16[1024,512]{1,0:T(8,128)(2,1)}, bf16[1024,512]{1,0:T(8,128)(2,1)}) custom-call(s32[1]{0:T(128)} %bitcast.5.me_ref.refs_0_, f32[1024,1536]{1,0:T(8,128)} %get-tuple-element.164.q_ref.k_ref.v_ref.refs_7_.refs_8_.qp_ref.kp_ref, ...), custom_call_target="tpu_custom_call" | custom-call | tf_op jit(solution)/shard_map/attend/pallas_call | solution.py:294
  227.0 43.7 %collective-permute-done.20.refs_3_.refs_2_ = bf16[1024,512]{1,0:T(8,128)(2,1)S(1)} collective-permute-done((bf16[1024,512]{1,0:T(8,128)(2,1)S(1)}, bf16[1024,512]{1,0:T(8,128)(2,1)S(1)}, u32[]{:S(2)}, u32[]{:S(2)}) %collective-permute-start.20) | collective-permute-done | bytes 1048608 | tf_op jit(solution)/shard_map/ppermute | solution.py:45
  272.0 21.0 %collective-permute-done.21 = bf16[1024,512]{1,0:T(8,128)(2,1)S(1)} collective-permute-done((bf16[1024,512]{1,0:T(8,128)(2,1)S(1)}, bf16[1024,512]{1,0:T(8,128)(2,1)S(1)}, u32[]{:S(2)}, u32[]{:S(2)}) %collective-permute-start.21) | collective-permute-done | bytes 1048608 | tf_op jit(solution)/shard_map/ppermute | solution.py:48
  294.6 17.3 %out_project.1 = (bf16[1024,2048]{1,0:T(8,128)(2,1)}, f32[256,2048]{1,0:T(8,128)}) custom-call(s32[1]{0:T(128)} %bitcast.5.me_ref.refs_0_, bf16[1024,512]{1,0:T(8,128)(2,1)} %get-tuple-element.172.refs_1_.refs_0_, bf16[1024,512]{1,0:T(8,128)(2,1)} %get-tuple-element.326.refs_2_.refs_1_, bf16[1024,512]{1,0:T(8,128)(2,1)} %copy-done.8, ...), custom_call_target="tpu_custom_call" | custom-call | tf_op jit(solution)/shard_map/out_project/pallas_call | solution.py:750
  311.9 22.6 %ff_forward.3 = (f32[1024,2048]{1,0:T(8,128)}, f32[1024,2048]{1,0:T(8,128)}, bf16[1024,2048]{1,0:T(8,128)(2,1)}, bf16[256,2048]{1,0:T(8,128)(2,1)}, bf16[256,204...) custom-call(s32[1]{0:T(128)} %bitcast.5.me_ref.refs_0_, bf16[1024,2048]{1,0:T(8,128)(2,1)} %get-tuple-element.238.h_ref.refs_0_, ...), custom_call_target="tpu_custom_call" | custom-call | tf_op jit(solution)/shard_map/ff_forward/pallas_call | solution.py:677
  343.6 15.8 %ff_forward.4 = (f32[1024,2048]{1,0:T(8,128)}, f32[1024,2048]{1,0:T(8,128)}, bf16[1024,2048]{1,0:T(8,128)(2,1)}, f32[256,2048]{1,0:T(8,128)}) custom-call(s32[1]{0:T(128)} %bitcast.5.me_ref.refs_0_, bf16[1024,2048]{1,0:T(8,128)(2,1)} %get-tuple-element.238.h_ref.refs_0_, ...), custom_call_target="tpu_custom_call", output_to_operand_aliasing={{0}: (5, {}), {1}: (6, {}), {2}: (7, {})} | custom-call | tf_op jit(solution)/shard_map/ff_forward/pallas_call | solution.py:677
  367.8 15.8 %ff_forward.5 = (f32[1024,2048]{1,0:T(8,128)}, f32[1024,2048]{1,0:T(8,128)}, bf16[1024,2048]{1,0:T(8,128)(2,1)}, f32[256,2048]{1,0:T(8,128)}) custom-call(s32[1]{0:T(128)} %bitcast.5.me_ref.refs_0_, bf16[1024,2048]{1,0:T(8,128)(2,1)} %get-tuple-element.238.h_ref.refs_0_, ...), custom_call_target="tpu_custom_call", output_to_operand_aliasing={{0}: (5, {}), {1}: (6, {}), {2}: (7, {})} | custom-call | tf_op jit(solution)/shard_map/ff_forward/pallas_call | solution.py:677
  383.7 26.7 %collective-permute-done.25 = bf16[256,2048]{1,0:T(8,128)(2,1)S(1)} collective-permute-done((bf16[256,2048]{1,0:T(8,128)(2,1)S(1)}, bf16[256,2048]{1,0:T(8,128)(2,1)S(1)}, u32[]{:S(2)}, u32[]{:S(2)}) %collective-permute-start.25) | collective-permute-done | bytes 1048608 | tf_op jit(solution)/shard_map/ppermute | solution.py:62
  423.2 39.8 %collective-permute-done.28.refs_0_.refs_2_ = bf16[256,2048]{1,0:T(8,128)(2,1)S(1)} collective-permute-done((bf16[256,2048]{1,0:T(8,128)(2,1)S(1)}, bf16[256,2048]{1,0:T(8,128)(2,1)S(1)}, u32[]{:S(2)}, u32[]{:S(2)}) %collective-permute-start.28) | collective-permute-done | bytes 1048608 | tf_op jit(solution)/shard_map/ppermute | solution.py:45
  464.5 16.1 %ff_backward.3 = (bf16[1024,4096]{1,0:T(8,128)(2,1)}, f32[256,2048]{1,0:T(8,128)}) custom-call(s32[1]{0:T(128)} %bitcast.5.me_ref.refs_0_, bf16[256,2048]{1,0:T(8,128)(2,1)} %copy-done.3, bf16[2048,4096]{1,0:T(8,128)(2,1)} %all-gather.6.cloned.1.call-done.refs_5_.wg_ref.refs_1_.refs_2_.w_ref, ...), custom_call_target="tpu_custom_call" | custom-call | flops 99999997952 | tf_op jit(solution)/shard_map/ff_backward/pallas_call | solution.py:704
  480.6 6.9 collective-permute-done.29
  489.1 24.0 %ff_backward.4 = (bf16[1024,4096]{1,0:T(8,128)(2,1)}, bf16[256,2048]{1,0:T(8,128)(2,1)}, bf16[256,2048]{1,0:T(8,128)(2,1)}, bf16[256,2048]{1,0:T(8,128)(2,1)}) custom-call(s32[1]{0:T(128)} %bitcast.5.me_ref.refs_0_, bf16[256,2048]{1,0:T(8,128)(2,1)} %get-tuple-element.220.refs_0_, ...), custom_call_target="tpu_custom_call", output_to_operand_aliasing={{0}: (8, {})} | custom-call | flops 99999997952 | tf_op jit(solution)/shard_map/ff_backward/pallas_call | solution.py:704
  517.3 16.1 %ff_backward.5 = (bf16[1024,4096]{1,0:T(8,128)(2,1)}, f32[256,2048]{1,0:T(8,128)}) custom-call(s32[1]{0:T(128)} %bitcast.5.me_ref.refs_0_, bf16[256,2048]{1,0:T(8,128)(2,1)} %copy-done.10, bf16[2048,4096]{1,0:T(8,128)(2,1)} %all-gather.6.cloned.1.call-done.refs_5_.wg_ref.refs_1_.refs_2_.w_ref, ...), custom_call_target="tpu_custom_call", output_to_operand_aliasing={{0}: (7, {})} | custom-call | flops 99999997952 | tf_op jit(solution)/shard_map/ff_backward/pallas_call | solution.py:704
  543.9 14.4 %weight_grad.2 = bf16[2048,2048]{1,0:T(8,128)(2,1)} custom-call(bf16[256,2048]{1,0:T(8,128)(2,1)} %get-tuple-element.220.refs_0_, bf16[256,2048]{1,0:T(8,128)(2,1)} %get-tuple-element.221.refs_1_, bf16[256,2048]{1,0:T(8,128)(2,1)} %copy-done.10, bf16[256,2048]{1,0:T(8,128)(2,1)} %copy-done.3, bf16[1024,2048]{1,0:T(8,128)(2,1)} %get-tuple-element.224.refs_4_), custom_call_target="tpu_custom_call" | custom-call | tf_op jit(solution)/shard_map/weight_grad/pallas_call | solution.py:485
  560.9 27.8 %collective-permute-done.33.a_ref = bf16[256,2048]{1,0:T(8,128)(2,1)} collective-permute-done((bf16[256,2048]{1,0:T(8,128)(2,1)S(1)}, bf16[256,2048]{1,0:T(8,128)(2,1)}, u32[]{:S(2)}, u32[]{:S(2)}) %collective-permute-start.33) | collective-permute-done | bytes 1048608 | tf_op jit(solution)/shard_map/ppermute | solution.py:62
  588.8 12.4 %residual_back.1 = (f32[256,2048]{1,0:T(8,128)}, bf16[256,2048]{1,0:T(8,128)(2,1)}, f32[8,2048]{1,0:T(8,128)}, bf16[256,512]{1,0:T(8,128)(2,1)}, bf16[256,512]{1...) custom-call(s32[1]{0:T(128)} %bitcast.5.me_ref.refs_0_, f32[256,2048]{1,0:T(8,128)} %get-tuple-element.208.own_ref, ...), custom_call_target="tpu_custom_call" | custom-call | flops 999999995904 | tf_op jit(solution)/shard_map/residual_back/pallas_call | solution.py:375
  603.2 26.9 %weight_grad.3 = bf16[2048,4096]{1,0:T(8,128)(2,1)} custom-call(bf16[1024,2048]{1,0:T(8,128)(2,1)} %get-tuple-element.238.h_ref.refs_0_, bf16[1024,4096]{1,0:T(8,128)(2,1)} %get-tuple-element.239.refs_1_), custom_call_target="tpu_custom_call" | custom-call | tf_op jit(solution)/shard_map/weight_grad/pallas_call | solution.py:485
  637.4 23.6 %attend_back.1 = (f32[1024,512]{1,0:T(8,128)}, f32[1024,512]{1,0:T(8,128)}, bf16[1024,512]{1,0:T(8,128)(2,1)}, f32[2,8,1024]{2,1,0:T(8,128)}, f32[2,8,512]{2,1,0:T(8,128)}) custom-call(s32[1]{0:T(128)} %bitcast.5.me_ref.refs_0_, bf16[256,512]{1,0:T(8,128)(2,1)} %get-tuple-element.240.refs_0_, bf16[256,512]{1,0:T(8,128)(2,1)} %copy-done.18, ...), custom_call_target="tpu_custom_call" | custom-call | tf_op jit(solution)/shard_map/attend_back/pallas_call | solution.py:317
  682.4 15.9 %input_back.1 = (bf16[1024,1536]{1,0:T(8,128)(2,1)}, bf16[256,2048]{1,0:T(8,128)(2,1)}, bf16[256,2048]{1,0:T(8,128)(2,1)}, bf16[256,2048]{1,0:T(8,128)(2,1)}, bf...) custom-call(s32[1]{0:T(128)} %bitcast.5.me_ref.refs_0_, f32[1024,512]{1,0:T(8,128)} %get-tuple-element.247.q_ref, ...), custom_call_target="tpu_custom_call" | custom-call | tf_op jit(solution)/shard_map/input_back/pallas_call | solution.py:425
  711.6 18.8 %attn_grad.1 = bf16[2048,2048]{1,0:T(8,128)(2,1)} custom-call(s32[1]{0:T(128)} %bitcast.5.me_ref.refs_0_, bf16[1024,2048]{1,0:T(8,128)(2,1)} %get-tuple-element.181.refs_6_.x_ref, bf16[1024,1536]{1,0:T(8,128)(2,1)} %get-tuple-element.262.d_ref, bf16[1024,512]{1,0:T(8,128)(2,1)} %get-tuple-element.172.refs_1_.refs_0_, ...), custom_call_target="tpu_custom_call" | custom-call | flops 99999997952 | tf_op jit(solution)/shard_map/attn_grad/pallas_call | solution.py:521
  735.2 13.7 %collective-permute-done.49.refs_2_ = bf16[256,2048]{1,0:T(8,128)(2,1)} collective-permute-done((bf16[256,2048]{1,0:T(8,128)(2,1)}, bf16[256,2048]{1,0:T(8,128)(2,1)}, u32[]{:S(2)}, u32[]{:S(2)}) %collective-permute-start.49) | collective-permute-done | bytes 1048608 | tf_op jit(solution)/shard_map/ppermute | solution.py:55
  748.9 19.6 %collective-permute-done.51.refs_4_ = bf16[256,2048]{1,0:T(8,128)(2,1)} collective-permute-done((bf16[256,2048]{1,0:T(8,128)(2,1)}, bf16[256,2048]{1,0:T(8,128)(2,1)}, u32[]{:S(2)}, u32[]{:S(2)}) %collective-permute-start.51) | collective-permute-done | bytes 1048608 | tf_op jit(solution)/shard_map/ppermute | solution.py:913
  768.4 8.3 collective-permute-done.52.refs_5_
  802.1 18.6 %collective-permute-done.59 = f32[4,2048]{1,0:T(4,128)S(1)} collective-permute-done((f32[4,2048]{1,0:T(4,128)S(1)}, f32[4,2048]{1,0:T(4,128)S(1)}, u32[]{:S(2)}, u32[]{:S(2)}) %collective-permute-start.59) | collective-permute-done | bytes 32800 | tf_op jit(solution)/shard_map/ppermute | solution.py:85
  821.4 11.3 %collective-permute-done.60 = f32[4,2048]{1,0:T(4,128)S(1)} collective-permute-done((f32[4,2048]{1,0:T(4,128)S(1)}, f32[4,2048]{1,0:T(4,128)S(1)}, u32[]{:S(2)}, u32[]{:S(2)}) %collective-permute-start.60) | collective-permute-done | bytes 32800 | tf_op jit(solution)/shard_map/ppermute | solution.py:85
  844.1 18.4 %all-to-all-done.1 = bf16[4,64,2048]{2,1,0:T(8,128)(2,1)S(1)} async-done(((bf16[4,64,2048]{2,1,0:T(8,128)(2,1)}), bf16[4,64,2048]{2,1,0:T(8,128)(2,1)S(1)}, u32[]{:S(2)}, u32[]{:S(2)}) %all-to-all-start.1) | async-done | bytes 1048608 | tf_op jit(solution)/shard_map/all_to_all | solution.py:91
  (312 shorter events, 219.8 us)
Async XLA Ops:
  7.2 161.2 %all-gather.4.cloned.1.call-start = ((), (), s32[]{:S(2)}) async-start(), calls=%async_computation.5 | async-start | bytes 7077888 | tf_op jit(solution)/shard_map/all_gather | solution.py:162
  35.9 258.7 %all-gather.6.cloned.1.call-start = ((), (), s32[]{:S(2)}) async-start(), calls=%async_computation.6 | async-start | bytes 18874368 | tf_op jit(solution)/shard_map/all_gather | solution.py:162
  79.3 232.6 %all-gather.8.cloned.1.call-start = ((), (), s32[]{:S(2)}) async-start(), calls=%async_computation.7 | async-start | bytes 18874368 | tf_op jit(solution)/shard_map/all_gather | solution.py:162
  79.4 49.5 %collective-permute-start.7 = (bf16[256,2048]{1,0:T(8,128)(2,1)S(1)}, bf16[256,2048]{1,0:T(8,128)(2,1)}, u32[]{:S(2)}, u32[]{:S(2)}) collective-permute-start(bf16[256,2048]{1,0:T(8,128)(2,1)S(1)} %bitcast.99), channel_id=1, source_target_pairs={{2,0},{3,1},{0,2},{1,3},{6,4},{7,5},{4,6},{5,7},{10,8},{11,9},{8,1... | collective-permute-start | bytes 3145736 | tf_op jit(solution)/shard_map/ppermute | solution.py:45
  79.7 50.6 %collective-permute-start.10 = (bf16[256,2048]{1,0:T(8,128)(2,1)S(1)}, bf16[256,2048]{1,0:T(8,128)(2,1)S(1)}, u32[]{:S(2)}, u32[]{:S(2)}) collective-permute-start(bf16[256,2048]{1,0:T(8,128)(2,1)S(1)} %bitcast.100), channel_id=1, source_target_pairs={{0,1},{1,2},{2,3},{4,5},{5,6},{6,7},{8,9},{9,10},{10,11},{12,13},{... | collective-permute-start | bytes 3145736 | tf_op jit(solution)/shard_map/ppermute | solution.py:47
  84.5 46.8 %collective-permute-start.9 = (bf16[256,2048]{1,0:T(8,128)(2,1)S(1)}, bf16[256,2048]{1,0:T(8,128)(2,1)}, u32[]{:S(2)}, u32[]{:S(2)}) collective-permute-start(bf16[256,2048]{1,0:T(8,128)(2,1)S(1)} %bitcast.101), channel_id=1, source_target_pairs={{1,0},{2,1},{3,2},{5,4},{6,5},{7,6},{9,8},{10,9},{11,10},{13,12},{... | collective-permute-start | bytes 3145736 | tf_op jit(solution)/shard_map/ppermute | solution.py:46
  221.6 453.4 %reduce-scatter.4.cloned.1.call-start = ((), (), s32[]{:S(2)}) async-start(), calls=%async_computation.8 | async-start | bytes 9437184 | tf_op jit(solution)/shard_map/reduce_scatter | solution.py:166
  221.7 49.0 %collective-permute-start.20 = (bf16[1024,512]{1,0:T(8,128)(2,1)S(1)}, bf16[1024,512]{1,0:T(8,128)(2,1)S(1)}, u32[]{:S(2)}, u32[]{:S(2)}) collective-permute-start(bf16[1024,512]{1,0:T(8,128)(2,1)S(1)} %copy-done.7), channel_id=1, source_target_pairs={{2,0},{3,1},{0,2},{1,3},{6,4},{7,5},{4,6},{5,7},{10,8},{11,9},{8,1... | collective-permute-start | bytes 3145736 | tf_op jit(solution)/shard_map/ppermute | solution.py:45
  223.2 48.8 %collective-permute-start.23 = (bf16[1024,512]{1,0:T(8,128)(2,1)S(1)}, bf16[1024,512]{1,0:T(8,128)(2,1)S(1)}, u32[]{:S(2)}, u32[]{:S(2)}) collective-permute-start(bf16[1024,512]{1,0:T(8,128)(2,1)S(1)} %copy-done.7), channel_id=1, source_target_pairs={{0,1},{1,2},{2,3},{4,5},{5,6},{6,7},{8,9},{9,10},{10,11},{12,13},{... | collective-permute-start | bytes 3145736 | tf_op jit(solution)/shard_map/ppermute | solution.py:47
  225.7 46.3 %collective-permute-start.22 = (bf16[1024,512]{1,0:T(8,128)(2,1)S(1)}, bf16[1024,512]{1,0:T(8,128)(2,1)S(1)}, u32[]{:S(2)}, u32[]{:S(2)}) collective-permute-start(bf16[1024,512]{1,0:T(8,128)(2,1)S(1)} %copy-done.7), channel_id=1, source_target_pairs={{1,0},{2,1},{3,2},{5,4},{6,5},{7,6},{9,8},{10,9},{11,10},{13,12},{... | collective-permute-start | bytes 3145736 | tf_op jit(solution)/shard_map/ppermute | solution.py:46
  337.3 46.3 %collective-permute-start.27 = (bf16[256,2048]{1,0:T(8,128)(2,1)}, bf16[256,2048]{1,0:T(8,128)(2,1)S(1)}, u32[]{:S(2)}, u32[]{:S(2)}) collective-permute-start(bf16[256,2048]{1,0:T(8,128)(2,1)} %get-tuple-element.205), channel_id=1, source_target_pairs={{1,0},{2,1},{3,2},{5,4},{6,5},{7,6},{9,8},{10,9},{11,10},{13,12},{... | collective-permute-start | bytes 3145736 | tf_op jit(solution)/shard_map/ppermute | solution.py:56
  338.6 45.0 %collective-permute-start.26 = (bf16[256,2048]{1,0:T(8,128)(2,1)}, bf16[256,2048]{1,0:T(8,128)(2,1)S(1)}, u32[]{:S(2)}, u32[]{:S(2)}) collective-permute-start(bf16[256,2048]{1,0:T(8,128)(2,1)} %get-tuple-element.204), channel_id=1, source_target_pairs={{0,1},{1,2},{2,3},{4,5},{5,6},{6,7},{8,9},{9,10},{10,11},{12,13},{... | collective-permute-start | bytes 3145736 | tf_op jit(solution)/shard_map/ppermute | solution.py:55
  363.1 47.3 %collective-permute-start.25 = (bf16[256,2048]{1,0:T(8,128)(2,1)S(1)}, bf16[256,2048]{1,0:T(8,128)(2,1)S(1)}, u32[]{:S(2)}, u32[]{:S(2)}) collective-permute-start(bf16[256,2048]{1,0:T(8,128)(2,1)S(1)} %add_convert_fusion.3), channel_id=1, source_target_pairs={{0,2},{1,3},{2,0},{3,1},{4,6},{5,7},{6,4},{7,5},{8,10},{9,11},{10,... | collective-permute-start | bytes 3145736 | tf_op jit(solution)/shard_map/ppermute | solution.py:62
  416.0 47.0 %collective-permute-start.28 = (bf16[256,2048]{1,0:T(8,128)(2,1)S(1)}, bf16[256,2048]{1,0:T(8,128)(2,1)S(1)}, u32[]{:S(2)}, u32[]{:S(2)}) collective-permute-start(bf16[256,2048]{1,0:T(8,128)(2,1)S(1)} %get-tuple-element.223.refs_0_.refs_3_), channel_id=1, source_target_pairs={{2,0},{3,1},{0,2},{1,3},{6,4},{7,5},{4,6},{5,7},{10,8},{11,9},{8,1... | collective-permute-start | bytes 3145736 | tf_op jit(solution)/shard_map/ppermute | solution.py:45
  416.0 64.6 %collective-permute-start.31 = (bf16[256,2048]{1,0:T(8,128)(2,1)S(1)}, bf16[256,2048]{1,0:T(8,128)(2,1)S(1)}, u32[]{:S(2)}, u32[]{:S(2)}) collective-permute-start(bf16[256,2048]{1,0:T(8,128)(2,1)S(1)} %get-tuple-element.223.refs_0_.refs_3_), channel_id=1, source_target_pairs={{0,1},{1,2},{2,3},{4,5},{5,6},{6,7},{8,9},{9,10},{10,11},{12,13},{... | collective-permute-start | bytes 3145736 | tf_op jit(solution)/shard_map/ppermute | solution.py:47
  421.9 58.7 %collective-permute-start.30 = (bf16[256,2048]{1,0:T(8,128)(2,1)S(1)}, bf16[256,2048]{1,0:T(8,128)(2,1)S(1)}, u32[]{:S(2)}, u32[]{:S(2)}) collective-permute-start(bf16[256,2048]{1,0:T(8,128)(2,1)S(1)} %get-tuple-element.223.refs_0_.refs_3_), channel_id=1, source_target_pairs={{1,0},{2,1},{3,2},{5,4},{6,5},{7,6},{9,8},{10,9},{11,10},{13,12},{... | collective-permute-start | bytes 3145736 | tf_op jit(solution)/shard_map/ppermute | solution.py:46
  514.6 46.3 %collective-permute-start.34 = (bf16[256,2048]{1,0:T(8,128)(2,1)}, bf16[256,2048]{1,0:T(8,128)(2,1)S(1)}, u32[]{:S(2)}, u32[]{:S(2)}) collective-permute-start(bf16[256,2048]{1,0:T(8,128)(2,1)} %get-tuple-element.227), channel_id=1, source_target_pairs={{0,1},{1,2},{2,3},{4,5},{5,6},{6,7},{8,9},{9,10},{10,11},{12,13},{... | collective-permute-start | bytes 3145736 | tf_op jit(solution)/shard_map/ppermute | solution.py:55
  516.0 45.0 %collective-permute-start.35 = (bf16[256,2048]{1,0:T(8,128)(2,1)}, bf16[256,2048]{1,0:T(8,128)(2,1)S(1)}, u32[]{:S(2)}, u32[]{:S(2)}) collective-permute-start(bf16[256,2048]{1,0:T(8,128)(2,1)} %get-tuple-element.228), channel_id=1, source_target_pairs={{1,0},{2,1},{3,2},{5,4},{6,5},{7,6},{9,8},{10,9},{11,10},{13,12},{... | collective-permute-start | bytes 3145736 | tf_op jit(solution)/shard_map/ppermute | solution.py:56
  540.3 48.4 %collective-permute-start.33 = (bf16[256,2048]{1,0:T(8,128)(2,1)S(1)}, bf16[256,2048]{1,0:T(8,128)(2,1)}, u32[]{:S(2)}, u32[]{:S(2)}) collective-permute-start(bf16[256,2048]{1,0:T(8,128)(2,1)S(1)} %add_convert_fusion.1), channel_id=1, source_target_pairs={{0,2},{1,3},{2,0},{3,1},{4,6},{5,7},{6,4},{7,5},{8,10},{9,11},{10,... | collective-permute-start | bytes 3145736 | tf_op jit(solution)/shard_map/ppermute | solution.py:62
  558.3 224.4 %reduce-scatter.8.cloned.1.call-start = ((), (), s32[]{:S(2)}) async-start(), calls=%async_computation.10 | async-start | bytes 18874368 | tf_op jit(solution)/shard_map/reduce_scatter | solution.py:166
  601.2 29.0 %collective-permute-start.36 = (bf16[256,512]{1,0:T(8,128)(2,1)}, bf16[256,512]{1,0:T(8,128)(2,1)S(1)}, u32[]{:S(2)}, u32[]{:S(2)}) collective-permute-start(bf16[256,512]{1,0:T(8,128)(2,1)} %get-tuple-element.233), channel_id=1, source_target_pairs={{0,3},{1,0},{2,1},{3,2},{4,7},{5,4},{6,5},{7,6},{8,11},{9,8},{10,9... | collective-permute-start | bytes 786440 | tf_op jit(solution)/shard_map/ppermute | solution.py:891
  601.2 29.0 %collective-permute-start.37 = (bf16[256,512]{1,0:T(8,128)(2,1)}, bf16[256,512]{1,0:T(8,128)(2,1)S(1)}, u32[]{:S(2)}, u32[]{:S(2)}) collective-permute-start(bf16[256,512]{1,0:T(8,128)(2,1)} %get-tuple-element.234), channel_id=1, source_target_pairs={{0,2},{1,3},{2,0},{3,1},{4,6},{5,7},{6,4},{7,5},{8,10},{9,11},{10,... | collective-permute-start | bytes 786440 | tf_op jit(solution)/shard_map/ppermute | solution.py:891
  631.0 201.7 %reduce-scatter.6.cloned.1.call-start = ((), (), s32[]{:S(2)}) async-start(), calls=%async_computation.9 | async-start | bytes 9437184 | tf_op jit(solution)/shard_map/reduce_scatter | solution.py:166
  699.1 31.3 %collective-permute-start.48 = (bf16[256,2048]{1,0:T(8,128)(2,1)}, bf16[256,2048]{1,0:T(8,128)(2,1)S(1)}, u32[]{:S(2)}, u32[]{:S(2)}) collective-permute-start(bf16[256,2048]{1,0:T(8,128)(2,1)} %get-tuple-element.261), channel_id=1, source_target_pairs={{0,1},{3,2},{4,5},{7,6},{8,9},{11,10},{12,13},{15,14},{16,17},{19,... | collective-permute-start | bytes 3145736 | tf_op jit(solution)/shard_map/ppermute | solution.py:53
  702.6 46.3 %collective-permute-start.49 = (bf16[256,2048]{1,0:T(8,128)(2,1)}, bf16[256,2048]{1,0:T(8,128)(2,1)}, u32[]{:S(2)}, u32[]{:S(2)}) collective-permute-start(bf16[256,2048]{1,0:T(8,128)(2,1)} %get-tuple-element.270), channel_id=1, source_target_pairs={{0,1},{1,2},{2,3},{4,5},{5,6},{6,7},{8,9},{9,10},{10,11},{12,13},{... | collective-permute-start | bytes 3145736 | tf_op jit(solution)/shard_map/ppermute | solution.py:55
  704.9 44.0 %collective-permute-start.50 = (bf16[256,2048]{1,0:T(8,128)(2,1)}, bf16[256,2048]{1,0:T(8,128)(2,1)}, u32[]{:S(2)}, u32[]{:S(2)}) collective-permute-start(bf16[256,2048]{1,0:T(8,128)(2,1)} %get-tuple-element.271), channel_id=1, source_target_pairs={{1,0},{2,1},{3,2},{5,4},{6,5},{7,6},{9,8},{10,9},{11,10},{13,12},{... | collective-permute-start | bytes 3145736 | tf_op jit(solution)/shard_map/ppermute | solution.py:56
  706.2 62.2 %collective-permute-start.51 = (bf16[256,2048]{1,0:T(8,128)(2,1)}, bf16[256,2048]{1,0:T(8,128)(2,1)}, u32[]{:S(2)}, u32[]{:S(2)}) collective-permute-start(bf16[256,2048]{1,0:T(8,128)(2,1)} %get-tuple-element.272), channel_id=1, source_target_pairs={{0,2},{3,1},{4,6},{7,5},{8,10},{11,9},{12,14},{15,13},{16,18},{19,... | collective-permute-start | bytes 3145736 | tf_op jit(solution)/shard_map/ppermute | solution.py:913
  730.9 45.8 %collective-permute-start.52 = (bf16[256,2048]{1,0:T(8,128)(2,1)S(1)}, bf16[256,2048]{1,0:T(8,128)(2,1)S(1)}, u32[]{:S(2)}, u32[]{:S(2)}) collective-permute-start(bf16[256,2048]{1,0:T(8,128)(2,1)S(1)} %add_convert_fusion), channel_id=1, source_target_pairs={{1,3},{2,0},{5,7},{6,4},{9,11},{10,8},{13,15},{14,12},{17,19},{18,... | collective-permute-start | bytes 3145736 | tf_op jit(solution)/shard_map/ppermute | solution.py:918
  785.2 47.6 %collective-permute-start.53 = (bf16[64,4096]{1,0:T(8,128)(2,1)S(1)}, bf16[64,4096]{1,0:T(8,128)(2,1)S(1)}, u32[]{:S(2)}, u32[]{:S(2)}) collective-permute-start(bf16[64,4096]{1,0:T(8,128)(2,1)S(1)} %get-tuple-element.309), channel_id=1, source_target_pairs={{0,1},{1,2},{2,3},{3,0},{4,5},{5,6},{6,7},{7,4},{8,9},{9,10},{10,1... | collective-permute-start | bytes 1572872 | tf_op jit(solution)/shard_map/ppermute | solution.py:123
  786.3 46.5 %collective-permute-start.54 = (bf16[64,4096]{1,0:T(8,128)(2,1)S(1)}, bf16[64,4096]{1,0:T(8,128)(2,1)S(1)}, u32[]{:S(2)}, u32[]{:S(2)}) collective-permute-start(bf16[64,4096]{1,0:T(8,128)(2,1)S(1)} %get-tuple-element.308), channel_id=1, source_target_pairs={{0,2},{1,3},{2,0},{3,1},{4,6},{5,7},{6,4},{7,5},{8,10},{9,11},{10,... | collective-permute-start | bytes 1572872 | tf_op jit(solution)/shard_map/ppermute | solution.py:123
  789.4 43.4 %collective-permute-start.55 = (bf16[64,4096]{1,0:T(8,128)(2,1)S(1)}, bf16[64,4096]{1,0:T(8,128)(2,1)S(1)}, u32[]{:S(2)}, u32[]{:S(2)}) collective-permute-start(bf16[64,4096]{1,0:T(8,128)(2,1)S(1)} %get-tuple-element.307), channel_id=1, source_target_pairs={{0,3},{1,0},{2,1},{3,2},{4,7},{5,4},{6,5},{7,6},{8,11},{9,8},{10,9... | collective-permute-start | bytes 1572872 | tf_op jit(solution)/shard_map/ppermute | solution.py:123
  832.8 29.7 %all-to-all-start.1 = ((bf16[4,64,2048]{2,1,0:T(8,128)(2,1)}), bf16[4,64,2048]{2,1,0:T(8,128)(2,1)S(1)}, u32[]{:S(2)}, u32[]{:S(2)}) async-start(bf16[4,64,2048]{2,1,0:T(8,128)(2,1)} %bitcast.108), calls=%async_computation.4 | async-start | bytes 2097152 | tf_op jit(solution)/shard_map/all_to_all | solution.py:91
  (79 other events, 1028.9 us)
Sparse Core Ops, SparseCore 0:
  36.0 44.6 all-gather.3
  83.1 89.8 all-gather.5
  221.7 89.5 all-gather.7
  558.4 69.1 reduce-scatter.3
  631.5 115.9 reduce-scatter.7
  751.2 71.9 reduce-scatter.5

commit v5 on v4

--- a/solution.py
+++ b/solution.py
@@ -38,15 +38,19 @@
     return lax.ppermute(values, "seq", [((i + step) % count, i) for i in range(count)])
 
 
+def gather_raw(values, count):
+    far = lax.ppermute(values, "seq", [(i ^ 2, i) for i in range(count)])
+    after = lax.ppermute(values, "seq", [(i + 1, i) for i in range(count - 1)])
+    before = lax.ppermute(values, "seq", [(i, i + 1) for i in range(count - 1)])
+    ends = lax.ppermute(far, "seq", [(2, 3), (1, 0)])
+    return [values, after, far, before, ends]
+
+
 def gather_cyclic(values, count):
-    if count != 4:
-        return [values] + [shift(values, count, p) for p in range(1, count)]
+    own, after, far, before, ends = gather_raw(values, count)
     me = lax.axis_index("seq")
-    far = lax.ppermute(values, "seq", [(i ^ 2, i) for i in range(4)])
-    after = lax.ppermute(values, "seq", [(i + 1, i) for i in range(3)])
-    before = lax.ppermute(values, "seq", [(i, i + 1) for i in range(3)])
-    ends = lax.ppermute(far, "seq", [(2, 3), (1, 0)])
-    return [values, jnp.where(me == 3, ends, after), far, jnp.where(me == 0, ends, before)]
+    after = jnp.where(me == count - 1, ends, after)
+    return [own, after, far, jnp.where(me == 0, ends, before)]
 
 
 def scatter_start(ends, after, before, count):
@@ -71,8 +75,12 @@
 def sum_stats(stats, count):
     total = stats
     for p in range(1, count):
-        total = total + jnp.roll(shift(stats, count, p), p, axis=1)
+        total = total + jnp.roll(shift(stats, count, p), p, axis=0)
     return total
+
+
+def stat_columns(stats):
+    return stats[:, :2].transpose(0, 2, 1).reshape(-1, 2)
 
 
 def sum_everywhere(values, dp_count, seq_count):
@@ -91,12 +99,10 @@
     return lax.all_to_all(values, "seq", split_axis=0, concat_axis=0, tiled=True)
 
 
-def send_columns(values, me, count):
+def part_columns(values, me, count):
     part = values.shape[1] // count
-    columns = lambda p: lax.dynamic_slice_in_dim(values, (me + p) % count * part, part, 1)
-    return [columns(0)] + [
-        lax.ppermute(columns(p), "seq", [(i, (i + p) % count) for i in range(count)])
-        for p in range(1, count)
+    return [
+        lax.dynamic_slice_in_dim(values, (me + p) % count * part, part, 1) for p in range(count)
     ]
 
 
@@ -258,8 +264,8 @@
                 ds, q, (((0,), (0,)), ((), ())), preferred_element_type=F32
             )
         dq_ref[rows, :] = dq
-    ones = jnp.ones((8, HD), F32)
     first = pl.program_id(0) == 0
+    sums = []
     sides = ((dq_ref, dq_ref, qp_ref, qg_ref), (dk_sum, dk_ref, kp_ref, kg_ref))
     for j, (raw_ref, out_ref, proj_ref, g_ref) in enumerate(sides):
         raw = (raw_ref[...] * scale).astype(BF).astype(F32)
@@ -268,11 +274,11 @@
         gain_ref[j] = jnp.broadcast_to(jnp.sum(back * normed, axis=0, keepdims=True), (8, HD))
         back = back * g_ref[...]
         out_ref[...] = back
-        sums = lax.dot_general(
-            ones, back * normed, (((1,), (1,)), ((), ())),
-            precision=lax.Precision.HIGHEST, preferred_element_type=F32,
-        )
-        inner_ref[j] = jnp.where(first, sums, inner_ref[j] + sums)
+        sums.append(feature_sums(back * normed))
+    sums = two_rows(*sums)
+    for place in range(count):
+        part = sums[:, place * tokens : (place + 1) * tokens]
+        inner_ref[place] = jnp.where(first, part, inner_ref[place] + part)
     dv_ref[...] = dv_sum[...].astype(BF)
 
 
@@ -326,13 +332,13 @@
             + [whole(length, 1), whole(1, length)],
             out_specs=[head(0)] * 3
             + [
-                pl.BlockSpec((2, 8, length), lambda h, me: (0, 0, 0)),
+                pl.BlockSpec((count, 8, tokens), lambda h, me: (0, 0, 0)),
                 pl.BlockSpec((2, 8, HD), lambda h, me: (0, 0, h)),
             ],
             scratch_shapes=[pltpu.VMEM((length, HD), F32)] * 2,
         ),
         out_shape=[jax.ShapeDtypeStruct((length, part), t) for t in (F32, F32, BF)]
-        + [jax.ShapeDtypeStruct((2, 8, m), F32) for m in (length, part)],
+        + [jax.ShapeDtypeStruct(m, F32) for m in ((count, 8, tokens), (2, 8, part))],
         compiler_params=params(),
         cost_estimate=cost(0, 0),
         name="attend_back",
@@ -554,52 +560,69 @@
     return lax.dot_general(left, right, (((1,), (1,)), ((), ())), preferred_element_type=F32)
 
 
-def qkv_kernel(count, part, me_ref, *refs):
-    chunks, (w_ref, x_ref, qkv_ref, sq_ref) = refs[:-4], refs[-4:]
-    for q in range(count):
-
-        @pl.when(pl.program_id(0) == q)
+def feature_sums(values):
+    ones = jnp.ones((8, values.shape[1]), BF)
+    total = None
+    for _ in range(3):
+        term = values.astype(BF)
+        values = values - term.astype(F32)
+        total = nt_dot(ones, term) if total is None else total + nt_dot(ones, term)
+    return total
+
+
+def two_rows(first, second):
+    return jnp.where(lax.broadcasted_iota(jnp.int32, first.shape, 0) == 0, first, second)
+
+
+def qkv_kernel(part, saved, me_ref, *refs):
+    chunks, w_ref, (x_ref, qkv_ref, sq_ref) = refs[: -4 - saved], refs[-4 - saved], refs[-3:]
+    step, me = pl.program_id(0), me_ref[0]
+    at_end = (step == 0) & (me == 3) | (step == 1) & (me == 0) if len(chunks) == 3 else step < 0
+    for q in range(2):
+
+        @pl.when((step == q) & jnp.logical_not(at_end))
         def _(q=q):
             x_ref[...] = chunks[q][...]
 
+    @pl.when(at_end)
+    def _():
+        x_ref[...] = chunks[-1][...]
+
     qkv = jnp.dot(x_ref[...], w_ref[...], preferred_element_type=F32)
     qkv_ref[...] = qkv
-    ones = jnp.ones((8, part), F32)
-    for j in range(2):
-        values = qkv[:, j * part : (j + 1) * part]
-        sq_ref[j] = lax.dot_general(
-            ones, values * values, (((1,), (1,)), ((), ())),
-            precision=lax.Precision.HIGHEST, preferred_element_type=F32,
-        )
-
-
-def qkv_project(me, chunks, w_qkv):
-    count = len(chunks)
+    q, k = (qkv[:, j * part : (j + 1) * part] for j in range(2))
+    sq_ref[0] = two_rows(feature_sums(q * q), feature_sums(k * k))
+
+
+def qkv_project(me, first, chunks, w_qkv, saved=()):
     tokens, width = chunks[0].shape
     columns = w_qkv.shape[1]
-    length = count * tokens
-    return pl.pallas_call(
-        functools.partial(qkv_kernel, count, columns // 3),
+    length = 4 * tokens
+    place = lambda q: 2 * q + first
+    return pl.pallas_call(
+        functools.partial(qkv_kernel, columns // 3, len(saved)),
         grid_spec=pltpu.PrefetchScalarGridSpec(
             num_scalar_prefetch=1,
-            grid=(count,),
-            in_specs=[once((tokens, width), lambda q, me: (0, 0))] * count
-            + [once((width, columns), lambda q, me: (0, 0))],
+            grid=(2,),
+            in_specs=[once((tokens, width), lambda q, me: (0, 0))] * len(chunks)
+            + [once((width, columns), lambda q, me: (0, 0))]
+            + [pl.BlockSpec(memory_space=pl.ANY)] * len(saved),
             out_specs=[
-                pl.BlockSpec((tokens, width), lambda q, me: (q, 0)),
-                pl.BlockSpec((tokens, columns), lambda q, me: (q, 0)),
-                pl.BlockSpec((2, 8, tokens), lambda q, me: (0, 0, q)),
+                pl.BlockSpec((tokens, width), lambda q, me: (place(q), 0)),
+                pl.BlockSpec((tokens, columns), lambda q, me: (place(q), 0)),
+                pl.BlockSpec((1, 8, tokens), lambda q, me: (place(q), 0, 0)),
             ],
         ),
         out_shape=[
             jax.ShapeDtypeStruct((length, width), BF),
             jax.ShapeDtypeStruct((length, columns), F32),
-            jax.ShapeDtypeStruct((2, 8, length), F32),
+            jax.ShapeDtypeStruct((4, 8, tokens), F32),
         ],
+        input_output_aliases={2 + len(chunks) + j: j for j in range(len(saved))},
         compiler_params=params(),
         cost_estimate=cost(0, 0),
         name="qkv_project",
-    )(me, *chunks, w_qkv)
+    )(me, *chunks, w_qkv, *saved)
 
 
 FF_TILE = 512
@@ -813,18 +836,6 @@
         qkv_blocks = jnp.concatenate([by_part(w) for w in (w_query, w_key, w_value)], axis=2)
         qkv_blocks = swap_blocks(qkv_blocks)
         w_qkv = gather_dp(rows_of(qkv_blocks))
-        qkv_blocks, w_output, w_gate, w_down_t = fence((qkv_blocks, w_output, w_gate, w_down.T))
-        out_blocks = gather_cyclic(w_output, n)
-        gate_blocks = send_columns(w_gate, me, n)
-        out_blocks, gate_blocks, x_own = fence((out_blocks, gate_blocks, layer_input[0]))
-        out_blocks = out_blocks[:1] + out_blocks[:0:-1]
-        w_first = place_blocks(out_blocks, me, 0, width + ff_part)
-        w_first = gather_dp(place_blocks(gate_blocks, me, width, width + ff_part, w_first))
-        x_chunks, w_up = fence((gather_cyclic(x_own, n), w_up))
-        up_blocks = send_columns(w_up, me, n)
-        x_all, qkv, squares = qkv_project(me_ref, x_chunks, w_qkv)
-        squares, up_blocks = fence((squares, up_blocks))
-
         natural = jnp.arange(length, dtype=jnp.int32)
         positions = (natural + me * tokens) % length
         seg_row = segments[0]
@@ -836,10 +847,29 @@
         q_gain = own_gain(query_gain)
         k_gain = own_gain(key_gain)
 
-        squares = sum_stats(squares[:, 0].reshape(2, n, tokens), n).reshape(2, length)
-        squares, w_down_t = fence((squares, w_down_t))
-        down_blocks = send_columns(w_down_t, me, n)
-        factors = lax.rsqrt(squares / width + EPSILON).T
+        up_columns, down_columns = (part_columns(w, me, n) for w in (w_up, w_down.T))
+        ready = (seg, tables, q_gain, k_gain, up_columns, down_columns)
+        qkv_blocks, w_output, w_gate = fence((qkv_blocks, w_output, w_gate))
+        out_blocks = gather_cyclic(w_output, n)
+        gate_blocks = send_blocks(part_columns(w_gate, me, n))
+        out_blocks, gate_blocks, x_own, ready = fence(
+            (out_blocks, gate_blocks, layer_input[0], ready)
+        )
+        seg, tables, q_gain, k_gain, up_columns, down_columns = ready
+        out_blocks = out_blocks[:1] + out_blocks[:0:-1]
+        w_first = place_blocks(out_blocks, me, 0, width + ff_part)
+        w_first = gather_dp(place_blocks(gate_blocks, me, width, width + ff_part, w_first))
+        x_own, x_after, x_far, x_before, x_ends = gather_raw(x_own, n)
+        saved = qkv_project(me_ref, 0, [x_own, x_far], w_qkv)
+        x_sides, saved, up_columns = fence(([x_after, x_before, x_ends], saved, up_columns))
+        up_blocks = send_blocks(up_columns)
+        x_all, qkv, squares = qkv_project(me_ref, 1, x_sides, w_qkv, saved)
+        squares, up_blocks = fence((squares, up_blocks))
+
+        squares = sum_stats(squares, n)
+        squares, down_columns = fence((squares, down_columns))
+        down_blocks = send_blocks(down_columns)
+        factors = lax.rsqrt(stat_columns(squares) / width + EPSILON)
         mixed, q_low, k_low, v_low = attend(me_ref, qkv, factors, q_gain, k_gain, tables, seg, n)
 
         mixed, down_blocks = fence((mixed, down_blocks))
@@ -899,12 +929,14 @@
         d_query, d_key, d_v, inner, gain_sums = attend_back(
             me_ref, d_mixed, q_low, k_low, v_low, qkv, factors, q_gain, k_gain, tables, seg, n
         )
-        inner, d_attn_part = fence((inner, d_attn_part))
-        inner = sum_stats(inner[:, 0].reshape(2, n, tokens), n).reshape(2, length)
-        inner, down_rows = fence((inner, down_rows))
-        down_back = send_blocks(row_blocks(down_rows, me, n))
+        inner, d_attn_part, down_back = fence(
+            (inner, d_attn_part, row_blocks(down_rows, me, n))
+        )
+        inner = sum_stats(inner, n)
+        inner, down_back = fence((inner, down_back))
+        down_back = send_blocks(down_back)
         d_qkv, ends, after, before, far, own = input_back(
-            me_ref, d_query, d_key, d_v, qkv, (inner / width).T, factors, w_qkv
+            me_ref, d_query, d_key, d_v, qkv, stat_columns(inner) / width, factors, w_qkv
         )
         d_qkv, ends, after, before, far, own, down_back = fence(
             (d_qkv, ends, after, before, far, own, down_back)
@@ -916,13 +948,15 @@
         attn_rows = scatter_dp(attn_grads)
         far = (far.astype(F32) + ends.astype(F32)).astype(BF)
         sent.append(lax.ppermute(far, "seq", [(1, 3), (2, 0)]))
+        gate_up_back = row_blocks(gate_up_rows, me, n)
+        sent, gate_up_back = fence((sent, gate_up_back))
         input_grad = add_up([d_res, own] + sent)
         spread = lambda g: lax.dynamic_update_slice(jnp.zeros(width, F32), g, (me * part,))
         gains = jnp.stack(
             [spread(gain_sums[0, 0]), spread(gain_sums[1, 0]), grad_attn_gain[0], grad_ff_gain]
         )
-        input_grad, gate_up_rows, gains = fence((input_grad, gate_up_rows, gains))
-        gate_up_back = send_blocks(row_blocks(gate_up_rows, me, n))
+        input_grad, gains = fence((input_grad, gains))
+        gate_up_back = send_blocks(gate_up_back)
         gains = sum_everywhere(gains, dp_count, n)
         attn_rows, input_grad, gate_up_back, down_back, gains = fence(
             (attn_rows, input_grad, gate_up_back, down_back, gains)

time: 883 us -> 873 us (0.989)
  starting transfers between devices: 114 us -> 124 us
  waiting for transfers between devices: 370 us -> 361 us
    ppermute x25 -> x16, waiting for transfers between devices: 207 us -> 179 us  [the longest x4 128 us: gather_raw(): far = lax.ppermute(values, 'seq', [(i ^ 2, i) for i in range(count)])]
    reduce_scatter x3, waiting for transfers between devices: 0.05 us -> 21.3 us  [scatter_dp(): return lax.psum_scatter(values, 'dp', scatter_dimension=0, tiled=True)]
    ppermute x6 -> x15, starting transfers between devices: 8.75 us -> 26.2 us  [send_blocks(): lax.ppermute(blocks[p], 'seq', [(i, (i + p) % count) for i in range(count)])]
    ppermute x6 -> x15, waiting for transfers between devices: 0.02 us -> 16.7 us  [send_blocks(): lax.ppermute(blocks[p], 'seq', [(i, (i + p) % count) for i in range(count)])]
    ppermute x3, waiting for transfers between devices: 16.1 us -> 2.37 us  [scatter_start(): after = lax.ppermute(after, 'seq', step)]
    ppermute x25 -> x16, starting transfers between devices: 44.5 us -> 33.6 us  [the longest x4 18.1 us: gather_raw(): before = lax.ppermute(values, 'seq', [(i, i + 1) for i in range(count - 1)])]
    pallas_call x1 -> x2, Pallas kernels: 15.6 us -> 18.4 us  [qkv_project(): pl.pallas_call(functools.partial(qkv_kernel, columns // 3, len(saved)), g...]
  transfers between devices with their start and end apart: 68 -> 68, of which waited for: 29 -> 29; matrix products, arithmetic and copies ran while one was open for 5% -> 4% of each run, Pallas kernels for 27% -> 28%
where the time goes in v5:
time: 873 us; the launch traced here: 863 us
  waiting for transfers between devices  361 us (41%)
  Pallas kernels  286 us (33%)
  starting transfers between devices  124 us (14%)
  local copies, waits for them, and re-layouts  32.7 us (4%)
  blocking collectives  26.5 us (3%)
  other arithmetic  17.7 us (2%)
  between operations  15.8 us (2%)
    ppermute x4, waiting for transfers between devices, gather_raw(): far = lax.ppermute(values, 'seq', [(i ^ 2, i) for i in range(count)])  128 us
    pallas_call x3, Pallas kernels, ff_backward(): pl.pallas_call(functools.partial(ff_back_kernel, len(saved), group), grid...  56.3 us
    pallas_call x3, Pallas kernels, ff_forward(): pl.pallas_call(functools.partial(ff_kernel, len(saved)), grid=(ff_part //...  54.1 us
    ppermute x2, waiting for transfers between devices, scatter_far(): return lax.ppermute(far_sum, 'seq', [(i, i ^ 2) for i in range(count)])  54 us
    ppermute x4, waiting for transfers between devices, gather_raw(): ends = lax.ppermute(far, 'seq', [(2, 3), (1, 0)])  50.9 us
    pallas_call x2, Pallas kernels, weight_grad(): pl.pallas_call(lambda *refs: weight_grad_kernel(refs[:-2], *refs[-2:]), g...  41.3 us
    ppermute x5, waiting for transfers between devices, sum_everywhere(): lax.ppermute(values, name, [(i, i ^ bit) for i in range(count)])  30.9 us
    all_to_all x1, blocking collectives, swap_blocks(): lax.all_to_all(values, 'seq', split_axis=0, concat_axis=0, tiled=True)  26.5 us
  transfers between devices with their start and end apart: 68, of which 29 were waited for; matrix products, arithmetic and copies ran while one was open for 4% of the time, Pallas kernels for 28%

profile of v5, /device:TPU:0, one launch (start us, length us, event | category | flops | bytes accessed | tf_op | source)
XLA Modules:
  0.0 863.2 jit_solution(13449223074108791925)
XLA Ops:
  9.4 26.5 %all_to_all.10 = bf16[4,64,1536]{2,1,0:T(8,128)(2,1)} all-to-all(bf16[4,64,1536]{2,1,0:T(8,128)(2,1)S(1)} %pad_maximum_fusion), channel_id=1, replica_groups=mesh['dp'=8,'seq'=4] {'seq'}, dimensions={0} | all-to-all | bytes 1572864 | tf_op jit(solution)/shard_map/all_to_all | solution.py:99
  69.0 8.6 %collective-permute-done.5 = bf16[64,2048]{1,0:T(8,128)(2,1)S(1)} collective-permute-done((bf16[64,2048]{1,0:T(8,128)(2,1)S(1)}, bf16[64,2048]{1,0:T(8,128)(2,1)S(1)}, u32[]{:S(2)}, u32[]{:S(2)}) %collective-permute-start.5) | collective-permute-done | bytes 262176 | tf_op jit(solution)/shard_map/ppermute | solution.py:129
  92.1 40.0 %collective-permute-done.9.refs_1_ = bf16[256,2048]{1,0:T(8,128)(2,1)} collective-permute-done((bf16[256,2048]{1,0:T(8,128)(2,1)S(1)}, bf16[256,2048]{1,0:T(8,128)(2,1)}, u32[]{:S(2)}, u32[]{:S(2)}) %collective-permute-start.9) | collective-permute-done | bytes 1048608 | tf_op jit(solution)/shard_map/ppermute | solution.py:42
  133.4 9.1 %qkv_project.2 = (bf16[1024,2048]{1,0:T(8,128)(2,1)}, f32[1024,1536]{1,0:T(8,128)}, f32[4,8,256]{2,1,0:T(8,128)}) custom-call(s32[1]{0:T(128)} %bitcast.9.me_ref.refs_0_, bf16[256,2048]{1,0:T(8,128)(2,1)} %bitcast.81, bf16[256,2048]{1,0:T(8,128)(2,1)} %collective-permute-done.9.refs_1_, bf16[2048,1536]{1,0:T(8,128)(2,1)} %all-gather.4.cloned.1.call-done.refs_2_.refs_3_.w_ref), custom_call_target="tpu_custom_call" | custom-call | tf_op jit(solution)/shard_map/qkv_project/pallas_call | solution.py:602
  142.6 15.3 %collective-permute-done.10.refs_2_ = bf16[256,2048]{1,0:T(8,128)(2,1)} collective-permute-done((bf16[256,2048]{1,0:T(8,128)(2,1)}, bf16[256,2048]{1,0:T(8,128)(2,1)}, u32[]{:S(2)}, u32[]{:S(2)}) %collective-permute-start.10) | collective-permute-done | bytes 1048608 | tf_op jit(solution)/shard_map/ppermute | solution.py:45
  164.2 9.4 %qkv_project.3 = (bf16[1024,2048]{1,0:T(8,128)(2,1)}, f32[1024,1536]{1,0:T(8,128)}, f32[4,8,256]{2,1,0:T(8,128)}) custom-call(s32[1]{0:T(128)} %bitcast.9.me_ref.refs_0_, bf16[256,2048]{1,0:T(8,128)(2,1)} %copy-done.11, bf16[256,2048]{1,0:T(8,128)(2,1)} %copy-done.12, ...), custom_call_target="tpu_custom_call", output_to_operand_aliasing={{0}: (5, {}), {1}: (6, {}), {2}: (7, {})} | custom-call | tf_op jit(solution)/shard_map/qkv_project/pallas_call | solution.py:602
  198.1 16.1 %attend.1 = (bf16[1024,512]{1,0:T(8,128)(2,1)}, bf16[1024,512]{1,0:T(8,128)(2,1)}, bf16[1024,512]{1,0:T(8,128)(2,1)}, bf16[1024,512]{1,0:T(8,128)(2,1)}) custom-call(s32[1]{0:T(128)} %bitcast.9.me_ref.refs_0_, f32[1024,1536]{1,0:T(8,128)} %get-tuple-element.210.q_ref.k_ref.v_ref.refs_7_.refs_8_.qp_ref.kp_ref, ...), custom_call_target="tpu_custom_call" | custom-call | tf_op jit(solution)/shard_map/attend/pallas_call | solution.py:300
  225.8 43.2 %collective-permute-done.20.refs_3_.refs_2_ = bf16[1024,512]{1,0:T(8,128)(2,1)S(1)} collective-permute-done((bf16[1024,512]{1,0:T(8,128)(2,1)S(1)}, bf16[1024,512]{1,0:T(8,128)(2,1)S(1)}, u32[]{:S(2)}, u32[]{:S(2)}) %collective-permute-start.20) | collective-permute-done | bytes 1048608 | tf_op jit(solution)/shard_map/ppermute | solution.py:42
  270.3 21.7 %collective-permute-done.21 = bf16[1024,512]{1,0:T(8,128)(2,1)S(1)} collective-permute-done((bf16[1024,512]{1,0:T(8,128)(2,1)S(1)}, bf16[1024,512]{1,0:T(8,128)(2,1)S(1)}, u32[]{:S(2)}, u32[]{:S(2)}) %collective-permute-start.21) | collective-permute-done | bytes 1048608 | tf_op jit(solution)/shard_map/ppermute | solution.py:45
  293.5 17.3 %out_project.1 = (bf16[1024,2048]{1,0:T(8,128)(2,1)}, f32[256,2048]{1,0:T(8,128)}) custom-call(s32[1]{0:T(128)} %bitcast.9.me_ref.refs_0_, bf16[1024,512]{1,0:T(8,128)(2,1)} %get-tuple-element.232.refs_1_.refs_0_, bf16[1024,512]{1,0:T(8,128)(2,1)} %get-tuple-element.400.refs_2_.refs_1_, bf16[1024,512]{1,0:T(8,128)(2,1)} %copy-done.8, ...), custom_call_target="tpu_custom_call" | custom-call | tf_op jit(solution)/shard_map/out_project/pallas_call | solution.py:773
  310.8 22.6 %ff_forward.3 = (f32[1024,2048]{1,0:T(8,128)}, f32[1024,2048]{1,0:T(8,128)}, bf16[1024,2048]{1,0:T(8,128)(2,1)}, bf16[256,2048]{1,0:T(8,128)(2,1)}, bf16[256,204...) custom-call(s32[1]{0:T(128)} %bitcast.9.me_ref.refs_0_, bf16[1024,2048]{1,0:T(8,128)(2,1)} %get-tuple-element.298.h_ref.refs_0_, ...), custom_call_target="tpu_custom_call" | custom-call | tf_op jit(solution)/shard_map/ff_forward/pallas_call | solution.py:700
  342.4 15.8 %ff_forward.4 = (f32[1024,2048]{1,0:T(8,128)}, f32[1024,2048]{1,0:T(8,128)}, bf16[1024,2048]{1,0:T(8,128)(2,1)}, f32[256,2048]{1,0:T(8,128)}) custom-call(s32[1]{0:T(128)} %bitcast.9.me_ref.refs_0_, bf16[1024,2048]{1,0:T(8,128)(2,1)} %get-tuple-element.298.h_ref.refs_0_, ...), custom_call_target="tpu_custom_call", output_to_operand_aliasing={{0}: (5, {}), {1}: (6, {}), {2}: (7, {})} | custom-call | tf_op jit(solution)/shard_map/ff_forward/pallas_call | solution.py:700
  367.1 15.8 %ff_forward.5 = (f32[1024,2048]{1,0:T(8,128)}, f32[1024,2048]{1,0:T(8,128)}, bf16[1024,2048]{1,0:T(8,128)(2,1)}, f32[256,2048]{1,0:T(8,128)}) custom-call(s32[1]{0:T(128)} %bitcast.9.me_ref.refs_0_, bf16[1024,2048]{1,0:T(8,128)(2,1)} %get-tuple-element.298.h_ref.refs_0_, ...), custom_call_target="tpu_custom_call", output_to_operand_aliasing={{0}: (5, {}), {1}: (6, {}), {2}: (7, {})} | custom-call | tf_op jit(solution)/shard_map/ff_forward/pallas_call | solution.py:700
  382.9 26.2 %collective-permute-done.25 = bf16[256,2048]{1,0:T(8,128)(2,1)S(1)} collective-permute-done((bf16[256,2048]{1,0:T(8,128)(2,1)S(1)}, bf16[256,2048]{1,0:T(8,128)(2,1)S(1)}, u32[]{:S(2)}, u32[]{:S(2)}) %collective-permute-start.25) | collective-permute-done | bytes 1048608 | tf_op jit(solution)/shard_map/ppermute | solution.py:66
  421.9 39.3 %collective-permute-done.28.refs_0_.refs_2_ = bf16[256,2048]{1,0:T(8,128)(2,1)S(1)} collective-permute-done((bf16[256,2048]{1,0:T(8,128)(2,1)S(1)}, bf16[256,2048]{1,0:T(8,128)(2,1)S(1)}, u32[]{:S(2)}, u32[]{:S(2)}) %collective-permute-start.28) | collective-permute-done | bytes 1048608 | tf_op jit(solution)/shard_map/ppermute | solution.py:42
  462.7 16.1 %ff_backward.3 = (bf16[1024,4096]{1,0:T(8,128)(2,1)}, f32[256,2048]{1,0:T(8,128)}) custom-call(s32[1]{0:T(128)} %bitcast.9.me_ref.refs_0_, bf16[256,2048]{1,0:T(8,128)(2,1)} %copy-done.5, bf16[2048,4096]{1,0:T(8,128)(2,1)} %all-gather.6.cloned.1.call-done.refs_5_.wg_ref.refs_1_.refs_2_.w_ref, ...), custom_call_target="tpu_custom_call" | custom-call | flops 99999997952 | tf_op jit(solution)/shard_map/ff_backward/pallas_call | solution.py:727
  478.9 7.4 collective-permute-done.29
  487.8 24.1 %ff_backward.4 = (bf16[1024,4096]{1,0:T(8,128)(2,1)}, bf16[256,2048]{1,0:T(8,128)(2,1)}, bf16[256,2048]{1,0:T(8,128)(2,1)}, bf16[256,2048]{1,0:T(8,128)(2,1)}) custom-call(s32[1]{0:T(128)} %bitcast.9.me_ref.refs_0_, bf16[256,2048]{1,0:T(8,128)(2,1)} %get-tuple-element.280.refs_0_, ...), custom_call_target="tpu_custom_call", output_to_operand_aliasing={{0}: (8, {})} | custom-call | flops 99999997952 | tf_op jit(solution)/shard_map/ff_backward/pallas_call | solution.py:727
  516.1 16.1 %ff_backward.5 = (bf16[1024,4096]{1,0:T(8,128)(2,1)}, f32[256,2048]{1,0:T(8,128)}) custom-call(s32[1]{0:T(128)} %bitcast.9.me_ref.refs_0_, bf16[256,2048]{1,0:T(8,128)(2,1)} %copy-done.10, bf16[2048,4096]{1,0:T(8,128)(2,1)} %all-gather.6.cloned.1.call-done.refs_5_.wg_ref.refs_1_.refs_2_.w_ref, ...), custom_call_target="tpu_custom_call", output_to_operand_aliasing={{0}: (7, {})} | custom-call | flops 99999997952 | tf_op jit(solution)/shard_map/ff_backward/pallas_call | solution.py:727
  542.7 14.4 %weight_grad.2 = bf16[2048,2048]{1,0:T(8,128)(2,1)} custom-call(bf16[256,2048]{1,0:T(8,128)(2,1)} %get-tuple-element.280.refs_0_, bf16[256,2048]{1,0:T(8,128)(2,1)} %get-tuple-element.281.refs_1_, bf16[256,2048]{1,0:T(8,128)(2,1)} %copy-done.10, bf16[256,2048]{1,0:T(8,128)(2,1)} %copy-done.5, bf16[1024,2048]{1,0:T(8,128)(2,1)} %get-tuple-element.284.refs_4_), custom_call_target="tpu_custom_call" | custom-call | tf_op jit(solution)/shard_map/weight_grad/pallas_call | solution.py:491
  559.7 27.8 %collective-permute-done.33.a_ref = bf16[256,2048]{1,0:T(8,128)(2,1)} collective-permute-done((bf16[256,2048]{1,0:T(8,128)(2,1)S(1)}, bf16[256,2048]{1,0:T(8,128)(2,1)}, u32[]{:S(2)}, u32[]{:S(2)}) %collective-permute-start.33) | collective-permute-done | bytes 1048608 | tf_op jit(solution)/shard_map/ppermute | solution.py:66
  587.6 12.4 %residual_back.1 = (f32[256,2048]{1,0:T(8,128)}, bf16[256,2048]{1,0:T(8,128)(2,1)}, f32[8,2048]{1,0:T(8,128)}, bf16[256,512]{1,0:T(8,128)(2,1)}, bf16[256,512]{1...) custom-call(s32[1]{0:T(128)} %bitcast.9.me_ref.refs_0_, f32[256,2048]{1,0:T(8,128)} %get-tuple-element.268.own_ref, ...), custom_call_target="tpu_custom_call" | custom-call | flops 999999995904 | tf_op jit(solution)/shard_map/residual_back/pallas_call | solution.py:381
  602.0 26.9 %weight_grad.3 = bf16[2048,4096]{1,0:T(8,128)(2,1)} custom-call(bf16[1024,2048]{1,0:T(8,128)(2,1)} %get-tuple-element.298.h_ref.refs_0_, bf16[1024,4096]{1,0:T(8,128)(2,1)} %get-tuple-element.299.refs_1_), custom_call_target="tpu_custom_call" | custom-call | tf_op jit(solution)/shard_map/weight_grad/pallas_call | solution.py:491
  636.2 23.0 %attend_back.1 = (f32[1024,512]{1,0:T(8,128)}, f32[1024,512]{1,0:T(8,128)}, bf16[1024,512]{1,0:T(8,128)(2,1)}, f32[4,8,256]{2,1,0:T(8,128)}, f32[2,8,512]{2,1,0:T(8,128)}) custom-call(s32[1]{0:T(128)} %bitcast.9.me_ref.refs_0_, bf16[256,512]{1,0:T(8,128)(2,1)} %get-tuple-element.300.refs_0_, bf16[256,512]{1,0:T(8,128)(2,1)} %copy-done.18, ...), custom_call_target="tpu_custom_call" | custom-call | tf_op jit(solution)/shard_map/attend_back/pallas_call | solution.py:323
  675.5 15.9 %input_back.1 = (bf16[1024,1536]{1,0:T(8,128)(2,1)}, bf16[256,2048]{1,0:T(8,128)(2,1)}, bf16[256,2048]{1,0:T(8,128)(2,1)}, bf16[256,2048]{1,0:T(8,128)(2,1)}, bf...) custom-call(s32[1]{0:T(128)} %bitcast.9.me_ref.refs_0_, f32[1024,512]{1,0:T(8,128)} %get-tuple-element.307.q_ref, ...), custom_call_target="tpu_custom_call" | custom-call | tf_op jit(solution)/shard_map/input_back/pallas_call | solution.py:431
  705.3 18.8 %attn_grad.1 = bf16[2048,2048]{1,0:T(8,128)(2,1)} custom-call(s32[1]{0:T(128)} %bitcast.9.me_ref.refs_0_, bf16[1024,2048]{1,0:T(8,128)(2,1)} %get-tuple-element.241.refs_6_.x_ref, bf16[1024,1536]{1,0:T(8,128)(2,1)} %get-tuple-element.329.d_ref, bf16[1024,512]{1,0:T(8,128)(2,1)} %get-tuple-element.232.refs_1_.refs_0_, ...), custom_call_target="tpu_custom_call" | custom-call | flops 99999997952 | tf_op jit(solution)/shard_map/attn_grad/pallas_call | solution.py:527
  728.0 18.2 %reduce-scatter.8.cloned.1.call-done = bf16[256,4096]{1,0:T(8,128)(2,1)} async-done(((bf16[2048,4096]{1,0:T(8,128)(2,1)}), bf16[256,4096]{1,0:T(8,128)(2,1)}) %reduce-scatter.8.cloned.1.call-update) | async-done | bytes 2097168 | tf_op jit(solution)/shard_map/reduce_scatter | solution.py:172
  749.1 13.3 %collective-permute-done.51.refs_4_ = bf16[256,2048]{1,0:T(8,128)(2,1)} collective-permute-done((bf16[256,2048]{1,0:T(8,128)(2,1)}, bf16[256,2048]{1,0:T(8,128)(2,1)}, u32[]{:S(2)}, u32[]{:S(2)}) %collective-permute-start.51) | collective-permute-done | bytes 1048608 | tf_op jit(solution)/shard_map/ppermute | solution.py:945
  762.4 8.4 collective-permute-done.52.refs_5_
  795.2 11.7 %collective-permute-done.59 = f32[4,2048]{1,0:T(4,128)S(1)} collective-permute-done((f32[4,2048]{1,0:T(4,128)S(1)}, f32[4,2048]{1,0:T(4,128)S(1)}, u32[]{:S(2)}, u32[]{:S(2)}) %collective-permute-start.59) | collective-permute-done | bytes 32800 | tf_op jit(solution)/shard_map/ppermute | solution.py:93
  808.0 10.9 %collective-permute-done.60 = f32[4,2048]{1,0:T(4,128)S(1)} collective-permute-done((f32[4,2048]{1,0:T(4,128)S(1)}, f32[4,2048]{1,0:T(4,128)S(1)}, u32[]{:S(2)}, u32[]{:S(2)}) %collective-permute-start.60) | collective-permute-done | bytes 32800 | tf_op jit(solution)/shard_map/ppermute | solution.py:93
  834.2 18.1 %all-to-all-done.1 = bf16[4,64,2048]{2,1,0:T(8,128)(2,1)S(1)} async-done(((bf16[4,64,2048]{2,1,0:T(8,128)(2,1)}), bf16[4,64,2048]{2,1,0:T(8,128)(2,1)S(1)}, u32[]{:S(2)}, u32[]{:S(2)}) %all-to-all-start.1) | async-done | bytes 1048608 | tf_op jit(solution)/shard_map/all_to_all | solution.py:99
  (316 shorter events, 237.1 us)
Async XLA Ops:
  7.2 126.3 %all-gather.4.cloned.1.call-start = ((), (), s32[]{:S(2)}) async-start(), calls=%async_computation.5 | async-start | bytes 7077888 | tf_op jit(solution)/shard_map/all_gather | solution.py:168
  35.9 257.6 %all-gather.6.cloned.1.call-start = ((), (), s32[]{:S(2)}) async-start(), calls=%async_computation.6 | async-start | bytes 18874368 | tf_op jit(solution)/shard_map/all_gather | solution.py:168
  82.5 228.3 %all-gather.8.cloned.1.call-start = ((), (), s32[]{:S(2)}) async-start(), calls=%async_computation.7 | async-start | bytes 18874368 | tf_op jit(solution)/shard_map/all_gather | solution.py:168
  82.6 49.5 %collective-permute-start.9 = (bf16[256,2048]{1,0:T(8,128)(2,1)S(1)}, bf16[256,2048]{1,0:T(8,128)(2,1)}, u32[]{:S(2)}, u32[]{:S(2)}) collective-permute-start(bf16[256,2048]{1,0:T(8,128)(2,1)S(1)} %bitcast.82), channel_id=1, source_target_pairs={{2,0},{3,1},{0,2},{1,3},{6,4},{7,5},{4,6},{5,7},{10,8},{11,9},{8,1... | collective-permute-start | bytes 3145736 | tf_op jit(solution)/shard_map/ppermute | solution.py:42
  85.3 57.2 %collective-permute-start.7 = (bf16[256,2048]{1,0:T(8,128)(2,1)S(1)}, bf16[256,2048]{1,0:T(8,128)(2,1)S(1)}, u32[]{:S(2)}, u32[]{:S(2)}) collective-permute-start(bf16[256,2048]{1,0:T(8,128)(2,1)S(1)} %bitcast.83), channel_id=1, source_target_pairs={{1,0},{2,1},{3,2},{5,4},{6,5},{7,6},{9,8},{10,9},{11,10},{13,12},{... | collective-permute-start | bytes 3145736 | tf_op jit(solution)/shard_map/ppermute | solution.py:43
  86.6 55.9 %collective-permute-start.8 = (bf16[256,2048]{1,0:T(8,128)(2,1)S(1)}, bf16[256,2048]{1,0:T(8,128)(2,1)S(1)}, u32[]{:S(2)}, u32[]{:S(2)}) collective-permute-start(bf16[256,2048]{1,0:T(8,128)(2,1)S(1)} %bitcast.84), channel_id=1, source_target_pairs={{0,1},{1,2},{2,3},{4,5},{5,6},{6,7},{8,9},{9,10},{10,11},{12,13},{... | collective-permute-start | bytes 3145736 | tf_op jit(solution)/shard_map/ppermute | solution.py:44
  219.3 439.8 %reduce-scatter.4.cloned.1.call-start = ((), (), s32[]{:S(2)}) async-start(), calls=%async_computation.8 | async-start | bytes 9437184 | tf_op jit(solution)/shard_map/reduce_scatter | solution.py:172
  219.4 49.6 %collective-permute-start.20 = (bf16[1024,512]{1,0:T(8,128)(2,1)S(1)}, bf16[1024,512]{1,0:T(8,128)(2,1)S(1)}, u32[]{:S(2)}, u32[]{:S(2)}) collective-permute-start(bf16[1024,512]{1,0:T(8,128)(2,1)S(1)} %copy-done.7), channel_id=1, source_target_pairs={{2,0},{3,1},{0,2},{1,3},{6,4},{7,5},{4,6},{5,7},{10,8},{11,9},{8,1... | collective-permute-start | bytes 3145736 | tf_op jit(solution)/shard_map/ppermute | solution.py:42
  221.4 48.8 %collective-permute-start.23 = (bf16[1024,512]{1,0:T(8,128)(2,1)S(1)}, bf16[1024,512]{1,0:T(8,128)(2,1)S(1)}, u32[]{:S(2)}, u32[]{:S(2)}) collective-permute-start(bf16[1024,512]{1,0:T(8,128)(2,1)S(1)} %copy-done.7), channel_id=1, source_target_pairs={{0,1},{1,2},{2,3},{4,5},{5,6},{6,7},{8,9},{9,10},{10,11},{12,13},{... | collective-permute-start | bytes 3145736 | tf_op jit(solution)/shard_map/ppermute | solution.py:44
  224.5 45.8 %collective-permute-start.22 = (bf16[1024,512]{1,0:T(8,128)(2,1)S(1)}, bf16[1024,512]{1,0:T(8,128)(2,1)S(1)}, u32[]{:S(2)}, u32[]{:S(2)}) collective-permute-start(bf16[1024,512]{1,0:T(8,128)(2,1)S(1)} %copy-done.7), channel_id=1, source_target_pairs={{1,0},{2,1},{3,2},{5,4},{6,5},{7,6},{9,8},{10,9},{11,10},{13,12},{... | collective-permute-start | bytes 3145736 | tf_op jit(solution)/shard_map/ppermute | solution.py:43
  336.0 46.8 %collective-permute-start.27 = (bf16[256,2048]{1,0:T(8,128)(2,1)}, bf16[256,2048]{1,0:T(8,128)(2,1)S(1)}, u32[]{:S(2)}, u32[]{:S(2)}) collective-permute-start(bf16[256,2048]{1,0:T(8,128)(2,1)} %get-tuple-element.265), channel_id=1, source_target_pairs={{1,0},{2,1},{3,2},{5,4},{6,5},{7,6},{9,8},{10,9},{11,10},{13,12},{... | collective-permute-start | bytes 3145736 | tf_op jit(solution)/shard_map/ppermute | solution.py:60
  337.3 45.5 %collective-permute-start.26 = (bf16[256,2048]{1,0:T(8,128)(2,1)}, bf16[256,2048]{1,0:T(8,128)(2,1)S(1)}, u32[]{:S(2)}, u32[]{:S(2)}) collective-permute-start(bf16[256,2048]{1,0:T(8,128)(2,1)} %get-tuple-element.264), channel_id=1, source_target_pairs={{0,1},{1,2},{2,3},{4,5},{5,6},{6,7},{8,9},{9,10},{10,11},{12,13},{... | collective-permute-start | bytes 3145736 | tf_op jit(solution)/shard_map/ppermute | solution.py:59
  361.8 47.3 %collective-permute-start.25 = (bf16[256,2048]{1,0:T(8,128)(2,1)S(1)}, bf16[256,2048]{1,0:T(8,128)(2,1)S(1)}, u32[]{:S(2)}, u32[]{:S(2)}) collective-permute-start(bf16[256,2048]{1,0:T(8,128)(2,1)S(1)} %add_convert_fusion.3), channel_id=1, source_target_pairs={{0,2},{1,3},{2,0},{3,1},{4,6},{5,7},{6,4},{7,5},{8,10},{9,11},{10,... | collective-permute-start | bytes 3145736 | tf_op jit(solution)/shard_map/ppermute | solution.py:66
  414.8 46.5 %collective-permute-start.28 = (bf16[256,2048]{1,0:T(8,128)(2,1)S(1)}, bf16[256,2048]{1,0:T(8,128)(2,1)S(1)}, u32[]{:S(2)}, u32[]{:S(2)}) collective-permute-start(bf16[256,2048]{1,0:T(8,128)(2,1)S(1)} %get-tuple-element.283.refs_0_.refs_3_), channel_id=1, source_target_pairs={{2,0},{3,1},{0,2},{1,3},{6,4},{7,5},{4,6},{5,7},{10,8},{11,9},{8,1... | collective-permute-start | bytes 3145736 | tf_op jit(solution)/shard_map/ppermute | solution.py:42
  414.8 64.1 %collective-permute-start.31 = (bf16[256,2048]{1,0:T(8,128)(2,1)S(1)}, bf16[256,2048]{1,0:T(8,128)(2,1)S(1)}, u32[]{:S(2)}, u32[]{:S(2)}) collective-permute-start(bf16[256,2048]{1,0:T(8,128)(2,1)S(1)} %get-tuple-element.283.refs_0_.refs_3_), channel_id=1, source_target_pairs={{0,1},{1,2},{2,3},{4,5},{5,6},{6,7},{8,9},{9,10},{10,11},{12,13},{... | collective-permute-start | bytes 3145736 | tf_op jit(solution)/shard_map/ppermute | solution.py:44
  420.6 58.2 %collective-permute-start.30 = (bf16[256,2048]{1,0:T(8,128)(2,1)S(1)}, bf16[256,2048]{1,0:T(8,128)(2,1)S(1)}, u32[]{:S(2)}, u32[]{:S(2)}) collective-permute-start(bf16[256,2048]{1,0:T(8,128)(2,1)S(1)} %get-tuple-element.283.refs_0_.refs_3_), channel_id=1, source_target_pairs={{1,0},{2,1},{3,2},{5,4},{6,5},{7,6},{9,8},{10,9},{11,10},{13,12},{... | collective-permute-start | bytes 3145736 | tf_op jit(solution)/shard_map/ppermute | solution.py:43
  513.4 46.3 %collective-permute-start.34 = (bf16[256,2048]{1,0:T(8,128)(2,1)}, bf16[256,2048]{1,0:T(8,128)(2,1)S(1)}, u32[]{:S(2)}, u32[]{:S(2)}) collective-permute-start(bf16[256,2048]{1,0:T(8,128)(2,1)} %get-tuple-element.287), channel_id=1, source_target_pairs={{0,1},{1,2},{2,3},{4,5},{5,6},{6,7},{8,9},{9,10},{10,11},{12,13},{... | collective-permute-start | bytes 3145736 | tf_op jit(solution)/shard_map/ppermute | solution.py:59
  514.8 45.0 %collective-permute-start.35 = (bf16[256,2048]{1,0:T(8,128)(2,1)}, bf16[256,2048]{1,0:T(8,128)(2,1)S(1)}, u32[]{:S(2)}, u32[]{:S(2)}) collective-permute-start(bf16[256,2048]{1,0:T(8,128)(2,1)} %get-tuple-element.288), channel_id=1, source_target_pairs={{1,0},{2,1},{3,2},{5,4},{6,5},{7,6},{9,8},{10,9},{11,10},{13,12},{... | collective-permute-start | bytes 3145736 | tf_op jit(solution)/shard_map/ppermute | solution.py:60
  539.1 48.4 %collective-permute-start.33 = (bf16[256,2048]{1,0:T(8,128)(2,1)S(1)}, bf16[256,2048]{1,0:T(8,128)(2,1)}, u32[]{:S(2)}, u32[]{:S(2)}) collective-permute-start(bf16[256,2048]{1,0:T(8,128)(2,1)S(1)} %add_convert_fusion.1), channel_id=1, source_target_pairs={{0,2},{1,3},{2,0},{3,1},{4,6},{5,7},{6,4},{7,5},{8,10},{9,11},{10,... | collective-permute-start | bytes 3145736 | tf_op jit(solution)/shard_map/ppermute | solution.py:66
  557.1 189.2 %reduce-scatter.8.cloned.1.call-start = ((), (), s32[]{:S(2)}) async-start(), calls=%async_computation.10 | async-start | bytes 18874368 | tf_op jit(solution)/shard_map/reduce_scatter | solution.py:172
  600.0 28.9 %collective-permute-start.37 = (bf16[256,512]{1,0:T(8,128)(2,1)}, bf16[256,512]{1,0:T(8,128)(2,1)S(1)}, u32[]{:S(2)}, u32[]{:S(2)}) collective-permute-start(bf16[256,512]{1,0:T(8,128)(2,1)} %get-tuple-element.294), channel_id=1, source_target_pairs={{0,2},{1,3},{2,0},{3,1},{4,6},{5,7},{6,4},{7,5},{8,10},{9,11},{10,... | collective-permute-start | bytes 786440 | tf_op jit(solution)/shard_map/ppermute | solution.py:921
  629.8 192.1 %reduce-scatter.6.cloned.1.call-start = ((), (), s32[]{:S(2)}) async-start(), calls=%async_computation.9 | async-start | bytes 9437184 | tf_op jit(solution)/shard_map/reduce_scatter | solution.py:172
  631.2 29.9 %collective-permute-start.39 = (bf16[256,512]{1,0:T(8,128)(2,1)S(1)}, bf16[256,512]{1,0:T(8,128)(2,1)S(1)}, u32[]{:S(2)}, u32[]{:S(2)}) collective-permute-start(bf16[256,512]{1,0:T(8,128)(2,1)S(1)} %get-tuple-element.395), channel_id=1, source_target_pairs={{0,3},{1,0},{2,1},{3,2},{4,7},{5,4},{6,5},{7,6},{8,11},{9,8},{10,9... | collective-permute-start | bytes 786440 | tf_op jit(solution)/shard_map/ppermute | solution.py:797
  692.3 31.8 %collective-permute-start.48 = (bf16[256,2048]{1,0:T(8,128)(2,1)}, bf16[256,2048]{1,0:T(8,128)(2,1)S(1)}, u32[]{:S(2)}, u32[]{:S(2)}) collective-permute-start(bf16[256,2048]{1,0:T(8,128)(2,1)} %get-tuple-element.328), channel_id=1, source_target_pairs={{0,1},{3,2},{4,5},{7,6},{8,9},{11,10},{12,13},{15,14},{16,17},{19,... | collective-permute-start | bytes 3145736 | tf_op jit(solution)/shard_map/ppermute | solution.py:57
  696.0 53.1 %collective-permute-start.49 = (bf16[256,2048]{1,0:T(8,128)(2,1)}, bf16[256,2048]{1,0:T(8,128)(2,1)}, u32[]{:S(2)}, u32[]{:S(2)}) collective-permute-start(bf16[256,2048]{1,0:T(8,128)(2,1)} %get-tuple-element.337), channel_id=1, source_target_pairs={{0,1},{1,2},{2,3},{4,5},{5,6},{6,7},{8,9},{9,10},{10,11},{12,13},{... | collective-permute-start | bytes 3145736 | tf_op jit(solution)/shard_map/ppermute | solution.py:59
  698.3 50.8 %collective-permute-start.50 = (bf16[256,2048]{1,0:T(8,128)(2,1)}, bf16[256,2048]{1,0:T(8,128)(2,1)}, u32[]{:S(2)}, u32[]{:S(2)}) collective-permute-start(bf16[256,2048]{1,0:T(8,128)(2,1)} %get-tuple-element.338), channel_id=1, source_target_pairs={{1,0},{2,1},{3,2},{5,4},{6,5},{7,6},{9,8},{10,9},{11,10},{13,12},{... | collective-permute-start | bytes 3145736 | tf_op jit(solution)/shard_map/ppermute | solution.py:60
  699.6 62.8 %collective-permute-start.51 = (bf16[256,2048]{1,0:T(8,128)(2,1)}, bf16[256,2048]{1,0:T(8,128)(2,1)}, u32[]{:S(2)}, u32[]{:S(2)}) collective-permute-start(bf16[256,2048]{1,0:T(8,128)(2,1)} %get-tuple-element.339), channel_id=1, source_target_pairs={{0,2},{3,1},{4,6},{7,5},{8,10},{11,9},{12,14},{15,13},{16,18},{19,... | collective-permute-start | bytes 3145736 | tf_op jit(solution)/shard_map/ppermute | solution.py:945
  724.6 46.2 %collective-permute-start.52 = (bf16[256,2048]{1,0:T(8,128)(2,1)S(1)}, bf16[256,2048]{1,0:T(8,128)(2,1)S(1)}, u32[]{:S(2)}, u32[]{:S(2)}) collective-permute-start(bf16[256,2048]{1,0:T(8,128)(2,1)S(1)} %add_convert_fusion), channel_id=1, source_target_pairs={{1,3},{2,0},{5,7},{6,4},{9,11},{10,8},{13,15},{14,12},{17,19},{18,... | collective-permute-start | bytes 3145736 | tf_op jit(solution)/shard_map/ppermute | solution.py:950
  770.8 51.2 %collective-permute-start.53 = (bf16[64,4096]{1,0:T(8,128)(2,1)}, bf16[64,4096]{1,0:T(8,128)(2,1)}, u32[]{:S(2)}, u32[]{:S(2)}) collective-permute-start(bf16[64,4096]{1,0:T(8,128)(2,1)} %get-tuple-element.350), channel_id=1, source_target_pairs={{0,1},{1,2},{2,3},{3,0},{4,5},{5,6},{6,7},{7,4},{8,9},{9,10},{10,1... | collective-permute-start | bytes 1572872 | tf_op jit(solution)/shard_map/ppermute | solution.py:129
  774.0 48.0 %collective-permute-start.54 = (bf16[64,4096]{1,0:T(8,128)(2,1)}, bf16[64,4096]{1,0:T(8,128)(2,1)}, u32[]{:S(2)}, u32[]{:S(2)}) collective-permute-start(bf16[64,4096]{1,0:T(8,128)(2,1)} %get-tuple-element.351), channel_id=1, source_target_pairs={{0,2},{1,3},{2,0},{3,1},{4,6},{5,7},{6,4},{7,5},{8,10},{9,11},{10,... | collective-permute-start | bytes 1572872 | tf_op jit(solution)/shard_map/ppermute | solution.py:129
  777.3 44.6 %collective-permute-start.55 = (bf16[64,4096]{1,0:T(8,128)(2,1)}, bf16[64,4096]{1,0:T(8,128)(2,1)}, u32[]{:S(2)}, u32[]{:S(2)}) collective-permute-start(bf16[64,4096]{1,0:T(8,128)(2,1)} %get-tuple-element.352), channel_id=1, source_target_pairs={{0,3},{1,0},{2,1},{3,2},{4,7},{5,4},{6,5},{7,6},{8,11},{9,8},{10,9... | collective-permute-start | bytes 1572872 | tf_op jit(solution)/shard_map/ppermute | solution.py:129
  822.0 30.3 %all-to-all-start.1 = ((bf16[4,64,2048]{2,1,0:T(8,128)(2,1)}), bf16[4,64,2048]{2,1,0:T(8,128)(2,1)S(1)}, u32[]{:S(2)}, u32[]{:S(2)}) async-start(bf16[4,64,2048]{2,1,0:T(8,128)(2,1)} %bitcast.90), calls=%async_computation.4 | async-start | bytes 2097152 | tf_op jit(solution)/shard_map/all_to_all | solution.py:99
  (88 other events, 1357.4 us)
Sparse Core Ops, SparseCore 0:
  36.0 44.6 all-gather.3
  83.1 92.0 all-gather.5
  219.4 90.5 all-gather.7
  557.2 69.1 reduce-scatter.3
  630.3 115.9 reduce-scatter.7
  750.0 71.9 reduce-scatter.5

commit v6 on v5

--- a/solution.py
+++ b/solution.py
@@ -679,20 +679,17 @@
     ff_finish(pl.program_id(0), product, refs[-1], me_ref, refs[saved + 1 : -1])
 
 
-def ff_specs(width, tile, gate_at, down_at):
-    return [
-        pl.BlockSpec((width, tile), lambda t: (0, gate_at // tile + t)),
-        pl.BlockSpec((width, tile), lambda t: (0, t)),
-        pl.BlockSpec((width, tile), lambda t: (0, down_at // tile + t)),
-    ]
-
-
-def ff_forward(me, residual_all, w_first, w_second, place, kinds, saved=()):
+def ff_specs(width, tile, gate_at):
+    rest = pl.BlockSpec((width, tile), lambda t: (0, t))
+    return [pl.BlockSpec((width, tile), lambda t: (0, gate_at // tile + t)), rest, rest]
+
+
+def ff_forward(me, residual_all, w_first, w_up, w_down, place, kinds, saved=()):
     length, width = residual_all.shape
     tokens = length // 4
     group = min(len(kinds), 2)
     rows = group * tokens
-    ff_part = w_second.shape[1] // 2
+    ff_part = w_up.shape[1]
     tile = min(FF_TILE, ff_part)
     block = pl.BlockSpec((rows, tile), lambda t: (place // group, t))
     whole = pl.BlockSpec((tokens, width), lambda t: (0, 0))
@@ -702,7 +699,7 @@
         grid=(ff_part // tile,),
         in_specs=[pl.BlockSpec(memory_space=pltpu.SMEM)]
         + [once((rows, width), lambda t: (place // group, 0))]
-        + ff_specs(width, tile, w_first.shape[1] - ff_part, ff_part)
+        + ff_specs(width, tile, w_first.shape[1] - ff_part)
         + [pl.BlockSpec(memory_space=pl.ANY)] * len(saved),
         out_specs=[block] * 3 + [whole] * len(kinds),
         out_shape=[shape(F32), shape(F32), shape(BF)]
@@ -712,15 +709,15 @@
         compiler_params=params(),
         cost_estimate=cost(0, 0),
         name="ff_forward",
-    )(me, residual_all, w_first, w_second, w_second, *saved)
-
-
-def ff_backward(me, d_ffs, w_first, w_second, gate, up, place, kinds, saved=()):
+    )(me, residual_all, w_first, w_up, w_down, *saved)
+
+
+def ff_backward(me, d_ffs, w_first, w_up, w_down, gate, up, place, kinds, saved=()):
     tokens, width = d_ffs[0].shape
     group = len(d_ffs)
     rows = group * tokens
     length = gate.shape[0]
-    ff_part = w_second.shape[1] // 2
+    ff_part = w_up.shape[1]
     tile = min(FF_TILE, ff_part)
     block = pl.BlockSpec((rows, tile), lambda t: (place // group, t))
     whole = pl.BlockSpec((tokens, width), lambda t: (0, 0))
@@ -729,7 +726,7 @@
         grid=(ff_part // tile,),
         in_specs=[pl.BlockSpec(memory_space=pltpu.SMEM)]
         + [once((tokens, width), lambda t: (0, 0))] * group
-        + ff_specs(width, tile, w_first.shape[1] - ff_part, ff_part)
+        + ff_specs(width, tile, w_first.shape[1] - ff_part)
         + [block, block]
         + [pl.BlockSpec(memory_space=pl.ANY)] * len(saved),
         out_specs=[pl.BlockSpec((rows, 2 * tile), lambda t: (place // group, t))]
@@ -741,53 +738,56 @@
         compiler_params=params(),
         cost_estimate=cost(SIDE_COST, 0),
         name="ff_backward",
-    )(me, *d_ffs, w_first, w_second, w_second, gate, up, *saved)
-
-
-def out_kernel(count, part, *refs):
-    me_ref, pieces, (w_ref, x_ref, g_ref, res_ref, own_ref) = refs[0], refs[1:-5], refs[-5:]
+    )(me, *d_ffs, w_first, w_up, w_down, gate, up, *saved)
+
+
+def out_kernel(count, part, saved, me_ref, *refs):
+    pieces, (w_ref, x_ref, g_ref), outs = refs[:count], refs[count : count + 3], refs[count + 3 + saved :]
     total = None
     for p, piece in enumerate(pieces):
         rows = pl.ds(pl.multiple_of((me_ref[0] + p) % count * part, part), part)
         product = jnp.dot(piece[...], w_ref[rows, :], preferred_element_type=F32)
         total = product if total is None else total + product
     normed = total * inv_rms(total)
-    res_ref[...] = (x_ref[...].astype(F32) + normed * g_ref[...]).astype(BF)
-
-    @pl.when(pl.program_id(0) == 0)
-    def _():
-        own_ref[...] = total
+    outs[0][...] = (x_ref[...].astype(F32) + normed * g_ref[...]).astype(BF)
+    if saved:
+
+        @pl.when(pl.program_id(0) == 1)
+        def _():
+            outs[1][...] = total
 
 
 def ff_place(q):
     return jnp.where(q == 0, 3, jnp.where(q == 3, 1, jnp.where(q == 2, 2, 0)))
 
 
-def out_project(me, pieces, w_out, x_all, gain, count):
+def out_project(me, pieces, w_out, x_all, gain, count, saved=()):
     length, width = x_all.shape
     tokens = length // count
     part = pieces[0].shape[1]
-    rolled = lambda p: pl.BlockSpec((tokens, part), lambda q, me: ((q + count - p) % count, 0))
-    chunk = pl.BlockSpec((tokens, width), lambda q, me: (q, 0))
-    moved = pl.BlockSpec((tokens, width), lambda q, me: (ff_place(q), 0))
-    return pl.pallas_call(
-        functools.partial(out_kernel, count, part),
+    place = lambda t: 2 - 2 * t if saved else 2 * t + 1
+    rolled = lambda p: pl.BlockSpec((tokens, part), lambda t, me: ((place(t) + count - p) % count, 0))
+    chunk = pl.BlockSpec((tokens, width), lambda t, me: (place(t), 0))
+    moved = pl.BlockSpec((tokens, width), lambda t, me: (ff_place(place(t)), 0))
+    own = pl.BlockSpec((tokens, width), lambda t, me: (0, 0))
+    return pl.pallas_call(
+        functools.partial(out_kernel, count, part, len(saved)),
         grid_spec=pltpu.PrefetchScalarGridSpec(
             num_scalar_prefetch=1,
-            grid=(count,),
+            grid=(2,),
             in_specs=[rolled(p) for p in range(count)]
-            + [pl.BlockSpec((width, width), lambda q, me: (0, 0), pipeline_mode=pl.Buffered(1))]
-            + [chunk, pl.BlockSpec((1, width), lambda q, me: (0, 0))],
-            out_specs=[moved, pl.BlockSpec((tokens, width), lambda q, me: (0, 0))],
+            + [once((width, width), lambda t, me: (0, 0))]
+            + [chunk, pl.BlockSpec((1, width), lambda t, me: (0, 0))]
+            + [pl.BlockSpec(memory_space=pl.ANY)] * len(saved),
+            out_specs=[moved] + [own] * len(saved),
         ),
-        out_shape=[
-            jax.ShapeDtypeStruct((length, width), BF),
-            jax.ShapeDtypeStruct((tokens, width), F32),
-        ],
+        out_shape=[jax.ShapeDtypeStruct((length, width), BF)]
+        + [jax.ShapeDtypeStruct((tokens, width), F32)] * len(saved),
+        input_output_aliases={4 + count + j: j for j in range(len(saved))},
         compiler_params=params(),
         cost_estimate=cost(0, 0),
         name="out_project",
-    )(me, *pieces, w_out, x_all, gain[None])
+    )(me, *pieces, w_out, x_all, gain[None], *saved)
 
 
 def columns_to_parts(values, me, count):
@@ -865,6 +865,7 @@
         up_blocks = send_blocks(up_columns)
         x_all, qkv, squares = qkv_project(me_ref, 1, x_sides, w_qkv, saved)
         squares, up_blocks = fence((squares, up_blocks))
+        w_up_all = gather_dp(place_blocks(up_blocks, me, 0, ff_part))
 
         squares = sum_stats(squares, n)
         squares, down_columns = fence((squares, down_columns))
@@ -873,23 +874,26 @@
         mixed, q_low, k_low, v_low = attend(me_ref, qkv, factors, q_gain, k_gain, tables, seg, n)
 
         mixed, down_blocks = fence((mixed, down_blocks))
-        w_second = place_blocks(up_blocks, me, 0, 2 * ff_part)
-        w_second = gather_dp(place_blocks(down_blocks, me, ff_part, 2 * ff_part, w_second))
+        w_down_all = gather_dp(place_blocks(down_blocks, me, 0, ff_part))
         pieces = gather_cyclic(mixed, n)
-        residual_all, attn_out = out_project(me_ref, pieces, w_first, x_all, attn_gain, n)
+        operands = (w_first, x_all, attn_gain, n)
+        saved_residual = out_project(me_ref, pieces, *operands)
+        *saved, after, before, ends = ff_forward(
+            me_ref, saved_residual[0], w_first, w_up_all, w_down_all, 0, (BF, BF, BF)
+        )
+        sent = scatter_start(ends, after, before, n)
+        saved_residual, after = fence((saved_residual, after))
+        residual_all, attn_out = out_project(me_ref, pieces, *operands, saved_residual)
         attn_factor = inv_rms(attn_out)
         attn_normed = attn_out * attn_factor
         residual = x_own.astype(F32) + attn_normed * attn_gain
-
-        *saved, after, before, ends = ff_forward(
-            me_ref, residual_all, w_first, w_second, 0, (BF, BF, BF)
-        )
-        sent = scatter_start(ends, after, before, n)
-        *saved, far = ff_forward(me_ref, residual_all, w_first, w_second, 2, (F32,), saved)
+        *saved, far = ff_forward(
+            me_ref, residual_all, w_first, w_up_all, w_down_all, 2, (F32,), saved
+        )
         far, sent[0], residual_late = fence((far, sent[0], residual_all))
         sent[0] = scatter_far(far, sent[0], n)
         gate, up, hidden, own = ff_forward(
-            me_ref, residual_late, w_first, w_second, 3, (F32,), saved
+            me_ref, residual_late, w_first, w_up_all, w_down_all, 3, (F32,), saved
         )
         ff_out = scatter_end(own, sent)
         ff_factor = inv_rms(ff_out)
@@ -898,14 +902,14 @@
         grad_ff_gain = jnp.sum(cot.astype(F32) * ff_normed, axis=0)
         d_ff = rms_back(ff_normed, ff_factor, ff_gain, cot.astype(F32)).astype(BF)
         d_ffs = gather_cyclic(d_ff, n)
-        d_both, own = ff_backward(me_ref, d_ffs[:1], w_first, w_second, gate, up, 3, (F32,))
+        d_both, own = ff_backward(me_ref, d_ffs[:1], w_first, w_up_all, w_down_all, gate, up, 3, (F32,))
         d_ffs, d_both = fence((d_ffs, d_both))
         d_both, after, before, ends = ff_backward(
-            me_ref, d_ffs[1::2], w_first, w_second, gate, up, 0, (BF, BF, BF), (d_both,)
+            me_ref, d_ffs[1::2], w_first, w_up_all, w_down_all, gate, up, 0, (BF, BF, BF), (d_both,)
         )
         sent = scatter_start(ends, after, before, n)
         d_both, far = ff_backward(
-            me_ref, d_ffs[2:3], w_first, w_second, gate, up, 2, (F32,), (d_both,)
+            me_ref, d_ffs[2:3], w_first, w_up_all, w_down_all, gate, up, 2, (F32,), (d_both,)
         )
         d_both, far, sent[0], d_ffs, hidden = fence((d_both, far, sent[0], d_ffs, hidden))
         sent[0] = scatter_far(far, sent[0], n)

time: 873 us -> 877 us (level)
    ppermute x5, waiting for transfers between devices: 30.9 us -> 12.1 us  [sum_everywhere(): lax.ppermute(values, name, [(i, i ^ bit) for i in range(count)])]
    ppermute x1, waiting for transfers between devices: 8.37 us -> 25.5 us  [shards(): sent.append(lax.ppermute(far, 'seq', [(1, 3), (2, 0)]))]
    reduce_scatter x3, waiting for transfers between devices: 21.3 us -> 31.2 us  [scatter_dp(): return lax.psum_scatter(values, 'dp', scatter_dimension=0, tiled=True)]
    ppermute x1, waiting for transfers between devices: 13.3 us -> 4.22 us  [shards(): sent.append(lax.ppermute(far, 'seq', [(0, 2), (3, 1)]))]
    pallas_call x1 -> x2, Pallas kernels: 17.3 us -> 22.6 us  [out_project(): pl.pallas_call(functools.partial(out_kernel, count, part, len(saved)), gr...]
  transfers between devices with their start and end apart: 68 -> 69, of which waited for: 29 -> 31; matrix products, arithmetic and copies ran while one was open for 4% -> 3% of each run, Pallas kernels for 28% -> 28%
where the time goes in v6:
time: 877 us; the launch traced here: 868 us
  waiting for transfers between devices  369 us (42%)
  Pallas kernels  291 us (33%)
  starting transfers between devices  119 us (14%)
  local copies, waits for them, and re-layouts  29.2 us (3%)
  blocking collectives  26.5 us (3%)
  other arithmetic  17.7 us (2%)
  between operations  15.8 us (2%)
    ppermute x4, waiting for transfers between devices, gather_raw(): far = lax.ppermute(values, 'seq', [(i ^ 2, i) for i in range(count)])  128 us
    pallas_call x3, Pallas kernels, ff_backward(): pl.pallas_call(functools.partial(ff_back_kernel, len(saved), group), grid...  56.2 us
    pallas_call x3, Pallas kernels, ff_forward(): pl.pallas_call(functools.partial(ff_kernel, len(saved)), grid=(ff_part //...  54 us
    ppermute x2, waiting for transfers between devices, scatter_far(): return lax.ppermute(far_sum, 'seq', [(i, i ^ 2) for i in range(count)])  53.9 us
    ppermute x4, waiting for transfers between devices, gather_raw(): ends = lax.ppermute(far, 'seq', [(2, 3), (1, 0)])  53.2 us
    pallas_call x2, Pallas kernels, weight_grad(): pl.pallas_call(lambda *refs: weight_grad_kernel(refs[:-2], *refs[-2:]), g...  41.6 us
    reduce_scatter x3, waiting for transfers between devices, scatter_dp(): return lax.psum_scatter(values, 'dp', scatter_dimension=0, tiled=True)  31.2 us
    all_to_all x1, blocking collectives, swap_blocks(): lax.all_to_all(values, 'seq', split_axis=0, concat_axis=0, tiled=True)  26.5 us
  transfers between devices with their start and end apart: 69, of which 31 were waited for; matrix products, arithmetic and copies ran while one was open for 3% of the time, Pallas kernels for 28%

profile of v6, /device:TPU:0, one launch (start us, length us, event | category | flops | bytes accessed | tf_op | source)
XLA Modules:
  0.0 868.0 jit_solution(6499187689832180559)
XLA Ops:
  9.4 26.5 %all_to_all.10 = bf16[4,64,1536]{2,1,0:T(8,128)(2,1)} all-to-all(bf16[4,64,1536]{2,1,0:T(8,128)(2,1)S(1)} %pad_maximum_fusion), channel_id=1, replica_groups=mesh['dp'=8,'seq'=4] {'seq'}, dimensions={0} | all-to-all | bytes 1572864 | tf_op jit(solution)/shard_map/all_to_all | solution.py:99
  69.0 8.6 collective-permute-done.5
  92.1 40.0 %collective-permute-done.9.refs_1_ = bf16[256,2048]{1,0:T(8,128)(2,1)} collective-permute-done((bf16[256,2048]{1,0:T(8,128)(2,1)S(1)}, bf16[256,2048]{1,0:T(8,128)(2,1)}, u32[]{:S(2)}, u32[]{:S(2)}) %collective-permute-start.9) | collective-permute-done | bytes 1048608 | tf_op jit(solution)/shard_map/ppermute | solution.py:42
  133.5 9.1 %qkv_project.2 = (bf16[1024,2048]{1,0:T(8,128)(2,1)}, f32[1024,1536]{1,0:T(8,128)}, f32[4,8,256]{2,1,0:T(8,128)}) custom-call(s32[1]{0:T(128)} %bitcast.9.me_ref, bf16[256,2048]{1,0:T(8,128)(2,1)} %bitcast.81, bf16[256,2048]{1,0:T(8,128)(2,1)} %collective-permute-done.9.refs_1_, bf16[2048,1536]{1,0:T(8,128)(2,1)} %all-gather.5.cloned.1.call-done.refs_2_.refs_3_.w_ref), custom_call_target="tpu_custom_call" | custom-call | tf_op jit(solution)/shard_map/qkv_project/pallas_call | solution.py:602
  142.7 15.2 %collective-permute-done.10.refs_2_ = bf16[256,2048]{1,0:T(8,128)(2,1)} collective-permute-done((bf16[256,2048]{1,0:T(8,128)(2,1)}, bf16[256,2048]{1,0:T(8,128)(2,1)}, u32[]{:S(2)}, u32[]{:S(2)}) %collective-permute-start.10) | collective-permute-done | bytes 1048608 | tf_op jit(solution)/shard_map/ppermute | solution.py:45
  163.2 9.4 %qkv_project.3 = (bf16[1024,2048]{1,0:T(8,128)(2,1)}, f32[1024,1536]{1,0:T(8,128)}, f32[4,8,256]{2,1,0:T(8,128)}) custom-call(s32[1]{0:T(128)} %bitcast.9.me_ref, bf16[256,2048]{1,0:T(8,128)(2,1)} %copy-done.12, bf16[256,2048]{1,0:T(8,128)(2,1)} %copy-done.13, ...), custom_call_target="tpu_custom_call", output_to_operand_aliasing={{0}: (5, {}), {1}: (6, {}), {2}: (7, {})} | custom-call | tf_op jit(solution)/shard_map/qkv_project/pallas_call | solution.py:602
  198.6 16.2 %attend.1 = (bf16[1024,512]{1,0:T(8,128)(2,1)}, bf16[1024,512]{1,0:T(8,128)(2,1)}, bf16[1024,512]{1,0:T(8,128)(2,1)}, bf16[1024,512]{1,0:T(8,128)(2,1)}) custom-call(s32[1]{0:T(128)} %bitcast.9.me_ref, f32[1024,1536]{1,0:T(8,128)} %get-tuple-element.211.q_ref.k_ref.v_ref.refs_7_.refs_8_.qp_ref.kp_ref, ...), custom_call_target="tpu_custom_call" | custom-call | tf_op jit(solution)/shard_map/attend/pallas_call | solution.py:300
  223.0 42.7 %collective-permute-done.20.refs_2_ = bf16[1024,512]{1,0:T(8,128)(2,1)S(1)} collective-permute-done((bf16[1024,512]{1,0:T(8,128)(2,1)S(1)}, bf16[1024,512]{1,0:T(8,128)(2,1)S(1)}, u32[]{:S(2)}, u32[]{:S(2)}) %collective-permute-start.20) | collective-permute-done | bytes 1048608 | tf_op jit(solution)/shard_map/ppermute | solution.py:42
  267.2 22.2 %collective-permute-done.21 = bf16[1024,512]{1,0:T(8,128)(2,1)S(1)} collective-permute-done((bf16[1024,512]{1,0:T(8,128)(2,1)S(1)}, bf16[1024,512]{1,0:T(8,128)(2,1)S(1)}, u32[]{:S(2)}, u32[]{:S(2)}) %collective-permute-start.21) | collective-permute-done | bytes 1048608 | tf_op jit(solution)/shard_map/ppermute | solution.py:45
  290.9 11.0 %out_project.2.h_ref.refs_7_ = bf16[1024,2048]{1,0:T(8,128)(2,1)} custom-call(s32[1]{0:T(128)} %bitcast.9.me_ref, bf16[1024,512]{1,0:T(8,128)(2,1)} %get-tuple-element.233.refs_0_, bf16[1024,512]{1,0:T(8,128)(2,1)} %get-tuple-element.402.refs_1_, bf16[1024,512]{1,0:T(8,128)(2,1)} %copy-done.5, bf16[1024,512]{1,0:T(8,128)(2,1)} %get-tuple-element.401.refs_3_, ...), custom_call_target="tpu_custom_call" | custom-call | tf_op jit(solution)/shard_map/out_project/pallas_call | solution.py:773
  301.9 22.6 %ff_forward.3 = (f32[1024,2048]{1,0:T(8,128)}, f32[1024,2048]{1,0:T(8,128)}, bf16[1024,2048]{1,0:T(8,128)(2,1)}, bf16[256,2048]{1,0:T(8,128)(2,1)}, bf16[256,204...) custom-call(s32[1]{0:T(128)} %bitcast.9.me_ref, bf16[1024,2048]{1,0:T(8,128)(2,1)} %out_project.2.h_ref.refs_7_, ...), custom_call_target="tpu_custom_call" | custom-call | tf_op jit(solution)/shard_map/ff_forward/pallas_call | solution.py:697
  329.0 11.6 %out_project.3 = (bf16[1024,2048]{1,0:T(8,128)(2,1)}, f32[256,2048]{1,0:T(8,128)}) custom-call(s32[1]{0:T(128)} %bitcast.9.me_ref, bf16[1024,512]{1,0:T(8,128)(2,1)} %get-tuple-element.233.refs_0_, bf16[1024,512]{1,0:T(8,128)(2,1)} %get-tuple-element.402.refs_1_, bf16[1024,512]{1,0:T(8,128)(2,1)} %copy-done.5, ...), custom_call_target="tpu_custom_call", output_to_operand_aliasing={{0}: (8, {})} | custom-call | tf_op jit(solution)/shard_map/out_project/pallas_call | solution.py:773
  340.6 15.7 %ff_forward.4 = (f32[1024,2048]{1,0:T(8,128)}, f32[1024,2048]{1,0:T(8,128)}, bf16[1024,2048]{1,0:T(8,128)(2,1)}, f32[256,2048]{1,0:T(8,128)}) custom-call(s32[1]{0:T(128)} %bitcast.9.me_ref, bf16[1024,2048]{1,0:T(8,128)(2,1)} %get-tuple-element.300.h_ref.refs_0_, ...), custom_call_target="tpu_custom_call", output_to_operand_aliasing={{0}: (5, {}), {1}: (6, {}), {2}: (7, {})} | custom-call | tf_op jit(solution)/shard_map/ff_forward/pallas_call | solution.py:697
  358.4 6.7 collective-permute-start.25
  365.3 15.7 %ff_forward.5 = (f32[1024,2048]{1,0:T(8,128)}, f32[1024,2048]{1,0:T(8,128)}, bf16[1024,2048]{1,0:T(8,128)(2,1)}, f32[256,2048]{1,0:T(8,128)}) custom-call(s32[1]{0:T(128)} %bitcast.9.me_ref, bf16[1024,2048]{1,0:T(8,128)(2,1)} %get-tuple-element.300.h_ref.refs_0_, ...), custom_call_target="tpu_custom_call", output_to_operand_aliasing={{0}: (5, {}), {1}: (6, {}), {2}: (7, {})} | custom-call | tf_op jit(solution)/shard_map/ff_forward/pallas_call | solution.py:697
  381.1 28.4 %collective-permute-done.25 = bf16[256,2048]{1,0:T(8,128)(2,1)S(1)} collective-permute-done((bf16[256,2048]{1,0:T(8,128)(2,1)S(1)}, bf16[256,2048]{1,0:T(8,128)(2,1)S(1)}, u32[]{:S(2)}, u32[]{:S(2)}) %collective-permute-start.25) | collective-permute-done | bytes 1048608 | tf_op jit(solution)/shard_map/ppermute | solution.py:66
  422.9 39.9 %collective-permute-done.28.refs_0_.refs_2_ = bf16[256,2048]{1,0:T(8,128)(2,1)S(1)} collective-permute-done((bf16[256,2048]{1,0:T(8,128)(2,1)S(1)}, bf16[256,2048]{1,0:T(8,128)(2,1)S(1)}, u32[]{:S(2)}, u32[]{:S(2)}) %collective-permute-start.28) | collective-permute-done | bytes 1048608 | tf_op jit(solution)/shard_map/ppermute | solution.py:42
  464.2 16.1 %ff_backward.3 = (bf16[1024,4096]{1,0:T(8,128)(2,1)}, f32[256,2048]{1,0:T(8,128)}) custom-call(s32[1]{0:T(128)} %bitcast.9.me_ref, bf16[256,2048]{1,0:T(8,128)(2,1)} %copy-done.6, bf16[2048,4096]{1,0:T(8,128)(2,1)} %all-gather.7.cloned.1.call-done.refs_4_.wg_ref.refs_1_.refs_2_.w_ref, bf16[2048,2048]{1,0:T(8,128)(2,1)} %all-gather.9.cloned.1.call-done.wu_ref.refs_2_.refs_3_, ...), custom_call_target="tpu_custom_call" | custom-call | flops 99999997952 | tf_op jit(solution)/shard_map/ff_backward/pallas_call | solution.py:724
  480.3 9.2 %collective-permute-done.29 = bf16[256,2048]{1,0:T(8,128)(2,1)S(1)} collective-permute-done((bf16[256,2048]{1,0:T(8,128)(2,1)S(1)}, bf16[256,2048]{1,0:T(8,128)(2,1)S(1)}, u32[]{:S(2)}, u32[]{:S(2)}) %collective-permute-start.29) | collective-permute-done | bytes 1048608 | tf_op jit(solution)/shard_map/ppermute | solution.py:45
  491.1 24.1 %ff_backward.4 = (bf16[1024,4096]{1,0:T(8,128)(2,1)}, bf16[256,2048]{1,0:T(8,128)(2,1)}, bf16[256,2048]{1,0:T(8,128)(2,1)}, bf16[256,2048]{1,0:T(8,128)(2,1)}) custom-call(s32[1]{0:T(128)} %bitcast.9.me_ref, bf16[256,2048]{1,0:T(8,128)(2,1)} %get-tuple-element.282.refs_0_, ...), custom_call_target="tpu_custom_call", output_to_operand_aliasing={{0}: (8, {})} | custom-call | flops 99999997952 | tf_op jit(solution)/shard_map/ff_backward/pallas_call | solution.py:724
  519.3 16.1 %ff_backward.5 = (bf16[1024,4096]{1,0:T(8,128)(2,1)}, f32[256,2048]{1,0:T(8,128)}) custom-call(s32[1]{0:T(128)} %bitcast.9.me_ref, bf16[256,2048]{1,0:T(8,128)(2,1)} %copy-done.11, bf16[2048,4096]{1,0:T(8,128)(2,1)} %all-gather.7.cloned.1.call-done.refs_4_.wg_ref.refs_1_.refs_2_.w_ref, ...), custom_call_target="tpu_custom_call", output_to_operand_aliasing={{0}: (7, {})} | custom-call | flops 99999997952 | tf_op jit(solution)/shard_map/ff_backward/pallas_call | solution.py:724
  543.6 14.4 %weight_grad.2 = bf16[2048,2048]{1,0:T(8,128)(2,1)} custom-call(bf16[256,2048]{1,0:T(8,128)(2,1)} %get-tuple-element.282.refs_0_, bf16[256,2048]{1,0:T(8,128)(2,1)} %get-tuple-element.283.refs_1_, bf16[256,2048]{1,0:T(8,128)(2,1)} %copy-done.11, bf16[256,2048]{1,0:T(8,128)(2,1)} %copy-done.6, bf16[1024,2048]{1,0:T(8,128)(2,1)} %get-tuple-element.286.refs_4_), custom_call_target="tpu_custom_call" | custom-call | tf_op jit(solution)/shard_map/weight_grad/pallas_call | solution.py:491
  563.0 25.5 %collective-permute-done.33.a_ref = bf16[256,2048]{1,0:T(8,128)(2,1)} collective-permute-done((bf16[256,2048]{1,0:T(8,128)(2,1)S(1)}, bf16[256,2048]{1,0:T(8,128)(2,1)}, u32[]{:S(2)}, u32[]{:S(2)}) %collective-permute-start.33) | collective-permute-done | bytes 1048608 | tf_op jit(solution)/shard_map/ppermute | solution.py:66
  588.5 12.6 %residual_back.1 = (f32[256,2048]{1,0:T(8,128)}, bf16[256,2048]{1,0:T(8,128)(2,1)}, f32[8,2048]{1,0:T(8,128)}, bf16[256,512]{1,0:T(8,128)(2,1)}, bf16[256,512]{1...) custom-call(s32[1]{0:T(128)} %bitcast.9.me_ref, f32[256,2048]{1,0:T(8,128)} %get-tuple-element.270.own_ref, ...), custom_call_target="tpu_custom_call" | custom-call | flops 999999995904 | tf_op jit(solution)/shard_map/residual_back/pallas_call | solution.py:381
  603.1 27.2 %weight_grad.3 = bf16[2048,4096]{1,0:T(8,128)(2,1)} custom-call(bf16[1024,2048]{1,0:T(8,128)(2,1)} %get-tuple-element.300.h_ref.refs_0_, bf16[1024,4096]{1,0:T(8,128)(2,1)} %get-tuple-element.301.refs_1_), custom_call_target="tpu_custom_call" | custom-call | tf_op jit(solution)/shard_map/weight_grad/pallas_call | solution.py:491
  637.6 22.4 %attend_back.1 = (f32[1024,512]{1,0:T(8,128)}, f32[1024,512]{1,0:T(8,128)}, bf16[1024,512]{1,0:T(8,128)(2,1)}, f32[4,8,256]{2,1,0:T(8,128)}, f32[2,8,512]{2,1,0:T(8,128)}) custom-call(s32[1]{0:T(128)} %bitcast.9.me_ref, bf16[256,512]{1,0:T(8,128)(2,1)} %get-tuple-element.302.refs_0_, bf16[256,512]{1,0:T(8,128)(2,1)} %copy-done.19, ...), custom_call_target="tpu_custom_call" | custom-call | tf_op jit(solution)/shard_map/attend_back/pallas_call | solution.py:323
  681.6 16.0 %input_back.1 = (bf16[1024,1536]{1,0:T(8,128)(2,1)}, bf16[256,2048]{1,0:T(8,128)(2,1)}, bf16[256,2048]{1,0:T(8,128)(2,1)}, bf16[256,2048]{1,0:T(8,128)(2,1)}, bf...) custom-call(s32[1]{0:T(128)} %bitcast.9.me_ref, f32[1024,512]{1,0:T(8,128)} %get-tuple-element.309.q_ref, ...), custom_call_target="tpu_custom_call" | custom-call | tf_op jit(solution)/shard_map/input_back/pallas_call | solution.py:431
  710.7 18.4 %attn_grad.1 = bf16[2048,2048]{1,0:T(8,128)(2,1)} custom-call(s32[1]{0:T(128)} %bitcast.9.me_ref, bf16[1024,2048]{1,0:T(8,128)(2,1)} %get-tuple-element.242.refs_5_.x_ref, bf16[1024,1536]{1,0:T(8,128)(2,1)} %get-tuple-element.331.d_ref, bf16[1024,512]{1,0:T(8,128)(2,1)} %get-tuple-element.233.refs_0_, bf16[1024,512]{1,0:T(8,128)(2,1)} %get-tuple-element.402.refs_1_, ...), custom_call_target="tpu_custom_call" | custom-call | flops 99999997952 | tf_op jit(solution)/shard_map/attn_grad/pallas_call | solution.py:527
  733.0 17.9 %reduce-scatter.8.cloned.1.call-done = bf16[256,4096]{1,0:T(8,128)(2,1)} async-done(((bf16[2048,4096]{1,0:T(8,128)(2,1)}), bf16[256,4096]{1,0:T(8,128)(2,1)}) %reduce-scatter.8.cloned.1.call-update) | async-done | bytes 2097168 | tf_op jit(solution)/shard_map/reduce_scatter | solution.py:172
  758.0 25.5 %collective-permute-done.52.refs_5_ = bf16[256,2048]{1,0:T(8,128)(2,1)S(1)} collective-permute-done((bf16[256,2048]{1,0:T(8,128)(2,1)S(1)}, bf16[256,2048]{1,0:T(8,128)(2,1)S(1)}, u32[]{:S(2)}, u32[]{:S(2)}) %collective-permute-start.52) | collective-permute-done | bytes 1048608 | tf_op jit(solution)/shard_map/ppermute | solution.py:954
  813.4 13.3 %reduce-scatter.6.cloned.1.call-done = bf16[256,2048]{1,0:T(8,128)(2,1)} async-done(((bf16[2048,2048]{1,0:T(8,128)(2,1)}), bf16[256,2048]{1,0:T(8,128)(2,1)}) %reduce-scatter.6.cloned.1.call-update) | async-done | bytes 1048592 | tf_op jit(solution)/shard_map/reduce_scatter | solution.py:172
  838.9 18.1 %all-to-all-done.1 = bf16[4,64,2048]{2,1,0:T(8,128)(2,1)S(1)} async-done(((bf16[4,64,2048]{2,1,0:T(8,128)(2,1)}), bf16[4,64,2048]{2,1,0:T(8,128)(2,1)S(1)}, u32[]{:S(2)}, u32[]{:S(2)}) %all-to-all-start.1) | async-done | bytes 1048608 | tf_op jit(solution)/shard_map/all_to_all | solution.py:99
  (315 shorter events, 234.2 us)
Async XLA Ops:
  7.2 126.3 %all-gather.5.cloned.1.call-start = ((), (), s32[]{:S(2)}) async-start(), calls=%async_computation.5 | async-start | bytes 7077888 | tf_op jit(solution)/shard_map/all_gather | solution.py:168
  35.9 255.1 %all-gather.7.cloned.1.call-start = ((), (), s32[]{:S(2)}) async-start(), calls=%async_computation.6 | async-start | bytes 18874368 | tf_op jit(solution)/shard_map/all_gather | solution.py:168
  82.5 219.4 %all-gather.9.cloned.1.call-start = ((), (), s32[]{:S(2)}) async-start(), calls=%async_computation.7 | async-start | bytes 9437184 | tf_op jit(solution)/shard_map/all_gather | solution.py:168
  82.6 49.5 %collective-permute-start.9 = (bf16[256,2048]{1,0:T(8,128)(2,1)S(1)}, bf16[256,2048]{1,0:T(8,128)(2,1)}, u32[]{:S(2)}, u32[]{:S(2)}) collective-permute-start(bf16[256,2048]{1,0:T(8,128)(2,1)S(1)} %bitcast.82), channel_id=1, source_target_pairs={{2,0},{3,1},{0,2},{1,3},{6,4},{7,5},{4,6},{5,7},{10,8},{11,9},{8,1... | collective-permute-start | bytes 3145736 | tf_op jit(solution)/shard_map/ppermute | solution.py:42
  85.3 57.3 %collective-permute-start.7 = (bf16[256,2048]{1,0:T(8,128)(2,1)S(1)}, bf16[256,2048]{1,0:T(8,128)(2,1)S(1)}, u32[]{:S(2)}, u32[]{:S(2)}) collective-permute-start(bf16[256,2048]{1,0:T(8,128)(2,1)S(1)} %bitcast.83), channel_id=1, source_target_pairs={{1,0},{2,1},{3,2},{5,4},{6,5},{7,6},{9,8},{10,9},{11,10},{13,12},{... | collective-permute-start | bytes 3145736 | tf_op jit(solution)/shard_map/ppermute | solution.py:43
  86.6 56.0 %collective-permute-start.8 = (bf16[256,2048]{1,0:T(8,128)(2,1)S(1)}, bf16[256,2048]{1,0:T(8,128)(2,1)S(1)}, u32[]{:S(2)}, u32[]{:S(2)}) collective-permute-start(bf16[256,2048]{1,0:T(8,128)(2,1)S(1)} %bitcast.84), channel_id=1, source_target_pairs={{0,1},{1,2},{2,3},{4,5},{5,6},{6,7},{8,9},{9,10},{10,11},{12,13},{... | collective-permute-start | bytes 3145736 | tf_op jit(solution)/shard_map/ppermute | solution.py:44
  180.3 121.6 %all-gather.11.cloned.1.call-start = ((), (), s32[]{:S(2)}) async-start(), calls=%async_computation.8 | async-start | bytes 9437184 | tf_op jit(solution)/shard_map/all_gather | solution.py:168
  216.1 444.0 %reduce-scatter.4.cloned.1.call-start = ((), (), s32[]{:S(2)}) async-start(), calls=%async_computation.9 | async-start | bytes 9437184 | tf_op jit(solution)/shard_map/reduce_scatter | solution.py:172
  216.1 49.6 %collective-permute-start.20 = (bf16[1024,512]{1,0:T(8,128)(2,1)S(1)}, bf16[1024,512]{1,0:T(8,128)(2,1)S(1)}, u32[]{:S(2)}, u32[]{:S(2)}) collective-permute-start(bf16[1024,512]{1,0:T(8,128)(2,1)S(1)} %copy-done.4), channel_id=1, source_target_pairs={{2,0},{3,1},{0,2},{1,3},{6,4},{7,5},{4,6},{5,7},{10,8},{11,9},{8,1... | collective-permute-start | bytes 3145736 | tf_op jit(solution)/shard_map/ppermute | solution.py:42
  218.1 48.9 %collective-permute-start.23 = (bf16[1024,512]{1,0:T(8,128)(2,1)S(1)}, bf16[1024,512]{1,0:T(8,128)(2,1)S(1)}, u32[]{:S(2)}, u32[]{:S(2)}) collective-permute-start(bf16[1024,512]{1,0:T(8,128)(2,1)S(1)} %copy-done.4), channel_id=1, source_target_pairs={{0,1},{1,2},{2,3},{4,5},{5,6},{6,7},{8,9},{9,10},{10,11},{12,13},{... | collective-permute-start | bytes 3145736 | tf_op jit(solution)/shard_map/ppermute | solution.py:44
  221.7 45.5 %collective-permute-start.22 = (bf16[1024,512]{1,0:T(8,128)(2,1)S(1)}, bf16[1024,512]{1,0:T(8,128)(2,1)S(1)}, u32[]{:S(2)}, u32[]{:S(2)}) collective-permute-start(bf16[1024,512]{1,0:T(8,128)(2,1)S(1)} %copy-done.4), channel_id=1, source_target_pairs={{1,0},{2,1},{3,2},{5,4},{6,5},{7,6},{9,8},{10,9},{11,10},{13,12},{... | collective-permute-start | bytes 3145736 | tf_op jit(solution)/shard_map/ppermute | solution.py:43
  324.5 31.8 %collective-permute-start.24 = (bf16[256,2048]{1,0:T(8,128)(2,1)}, bf16[256,2048]{1,0:T(8,128)(2,1)S(1)}, u32[]{:S(2)}, u32[]{:S(2)}) collective-permute-start(bf16[256,2048]{1,0:T(8,128)(2,1)} %get-tuple-element.259), channel_id=1, source_target_pairs={{0,1},{3,2},{4,5},{7,6},{8,9},{11,10},{12,13},{15,14},{16,17},{19,... | collective-permute-start | bytes 3145736 | tf_op jit(solution)/shard_map/ppermute | solution.py:57
  325.9 55.2 %collective-permute-start.26 = (bf16[256,2048]{1,0:T(8,128)(2,1)}, bf16[256,2048]{1,0:T(8,128)(2,1)S(1)}, u32[]{:S(2)}, u32[]{:S(2)}) collective-permute-start(bf16[256,2048]{1,0:T(8,128)(2,1)} %get-tuple-element.251), channel_id=1, source_target_pairs={{0,1},{1,2},{2,3},{4,5},{5,6},{6,7},{8,9},{9,10},{10,11},{12,13},{... | collective-permute-start | bytes 3145736 | tf_op jit(solution)/shard_map/ppermute | solution.py:59
  327.3 53.8 %collective-permute-start.27 = (bf16[256,2048]{1,0:T(8,128)(2,1)}, bf16[256,2048]{1,0:T(8,128)(2,1)S(1)}, u32[]{:S(2)}, u32[]{:S(2)}) collective-permute-start(bf16[256,2048]{1,0:T(8,128)(2,1)} %get-tuple-element.267), channel_id=1, source_target_pairs={{1,0},{2,1},{3,2},{5,4},{6,5},{7,6},{9,8},{10,9},{11,10},{13,12},{... | collective-permute-start | bytes 3145736 | tf_op jit(solution)/shard_map/ppermute | solution.py:60
  358.4 51.1 %collective-permute-start.25 = (bf16[256,2048]{1,0:T(8,128)(2,1)S(1)}, bf16[256,2048]{1,0:T(8,128)(2,1)S(1)}, u32[]{:S(2)}, u32[]{:S(2)}) collective-permute-start(bf16[256,2048]{1,0:T(8,128)(2,1)S(1)} %add_convert_fusion.3), channel_id=1, source_target_pairs={{0,2},{1,3},{2,0},{3,1},{4,6},{5,7},{6,4},{7,5},{8,10},{9,11},{10,... | collective-permute-start | bytes 3145736 | tf_op jit(solution)/shard_map/ppermute | solution.py:66
  415.2 47.6 %collective-permute-start.28 = (bf16[256,2048]{1,0:T(8,128)(2,1)S(1)}, bf16[256,2048]{1,0:T(8,128)(2,1)S(1)}, u32[]{:S(2)}, u32[]{:S(2)}) collective-permute-start(bf16[256,2048]{1,0:T(8,128)(2,1)S(1)} %get-tuple-element.285.refs_0_.refs_3_), channel_id=1, source_target_pairs={{2,0},{3,1},{0,2},{1,3},{6,4},{7,5},{4,6},{5,7},{10,8},{11,9},{8,1... | collective-permute-start | bytes 3145736 | tf_op jit(solution)/shard_map/ppermute | solution.py:42
  415.2 65.1 %collective-permute-start.31 = (bf16[256,2048]{1,0:T(8,128)(2,1)S(1)}, bf16[256,2048]{1,0:T(8,128)(2,1)S(1)}, u32[]{:S(2)}, u32[]{:S(2)}) collective-permute-start(bf16[256,2048]{1,0:T(8,128)(2,1)S(1)} %get-tuple-element.285.refs_0_.refs_3_), channel_id=1, source_target_pairs={{0,1},{1,2},{2,3},{4,5},{5,6},{6,7},{8,9},{9,10},{10,11},{12,13},{... | collective-permute-start | bytes 3145736 | tf_op jit(solution)/shard_map/ppermute | solution.py:44
  421.6 58.7 %collective-permute-start.30 = (bf16[256,2048]{1,0:T(8,128)(2,1)S(1)}, bf16[256,2048]{1,0:T(8,128)(2,1)S(1)}, u32[]{:S(2)}, u32[]{:S(2)}) collective-permute-start(bf16[256,2048]{1,0:T(8,128)(2,1)S(1)} %get-tuple-element.285.refs_0_.refs_3_), channel_id=1, source_target_pairs={{1,0},{2,1},{3,2},{5,4},{6,5},{7,6},{9,8},{10,9},{11,10},{13,12},{... | collective-permute-start | bytes 3145736 | tf_op jit(solution)/shard_map/ppermute | solution.py:43
  516.7 46.3 %collective-permute-start.34 = (bf16[256,2048]{1,0:T(8,128)(2,1)}, bf16[256,2048]{1,0:T(8,128)(2,1)S(1)}, u32[]{:S(2)}, u32[]{:S(2)}) collective-permute-start(bf16[256,2048]{1,0:T(8,128)(2,1)} %get-tuple-element.289), channel_id=1, source_target_pairs={{0,1},{1,2},{2,3},{4,5},{5,6},{6,7},{8,9},{9,10},{10,11},{12,13},{... | collective-permute-start | bytes 3145736 | tf_op jit(solution)/shard_map/ppermute | solution.py:59
  518.0 45.0 %collective-permute-start.35 = (bf16[256,2048]{1,0:T(8,128)(2,1)}, bf16[256,2048]{1,0:T(8,128)(2,1)S(1)}, u32[]{:S(2)}, u32[]{:S(2)}) collective-permute-start(bf16[256,2048]{1,0:T(8,128)(2,1)} %get-tuple-element.290), channel_id=1, source_target_pairs={{1,0},{2,1},{3,2},{5,4},{6,5},{7,6},{9,8},{10,9},{11,10},{13,12},{... | collective-permute-start | bytes 3145736 | tf_op jit(solution)/shard_map/ppermute | solution.py:60
  542.4 46.1 %collective-permute-start.33 = (bf16[256,2048]{1,0:T(8,128)(2,1)S(1)}, bf16[256,2048]{1,0:T(8,128)(2,1)}, u32[]{:S(2)}, u32[]{:S(2)}) collective-permute-start(bf16[256,2048]{1,0:T(8,128)(2,1)S(1)} %add_convert_fusion.1), channel_id=1, source_target_pairs={{0,2},{1,3},{2,0},{3,1},{4,6},{5,7},{6,4},{7,5},{8,10},{9,11},{10,... | collective-permute-start | bytes 3145736 | tf_op jit(solution)/shard_map/ppermute | solution.py:66
  558.0 192.9 %reduce-scatter.8.cloned.1.call-start = ((), (), s32[]{:S(2)}) async-start(), calls=%async_computation.11 | async-start | bytes 18874368 | tf_op jit(solution)/shard_map/reduce_scatter | solution.py:172
  631.2 195.5 %reduce-scatter.6.cloned.1.call-start = ((), (), s32[]{:S(2)}) async-start(), calls=%async_computation.10 | async-start | bytes 9437184 | tf_op jit(solution)/shard_map/reduce_scatter | solution.py:172
  698.5 30.6 %collective-permute-start.48 = (bf16[256,2048]{1,0:T(8,128)(2,1)}, bf16[256,2048]{1,0:T(8,128)(2,1)S(1)}, u32[]{:S(2)}, u32[]{:S(2)}) collective-permute-start(bf16[256,2048]{1,0:T(8,128)(2,1)} %get-tuple-element.330), channel_id=1, source_target_pairs={{0,1},{3,2},{4,5},{7,6},{8,9},{11,10},{12,13},{15,14},{16,17},{19,... | collective-permute-start | bytes 3145736 | tf_op jit(solution)/shard_map/ppermute | solution.py:57
  702.6 51.1 %collective-permute-start.49 = (bf16[256,2048]{1,0:T(8,128)(2,1)}, bf16[256,2048]{1,0:T(8,128)(2,1)}, u32[]{:S(2)}, u32[]{:S(2)}) collective-permute-start(bf16[256,2048]{1,0:T(8,128)(2,1)} %get-tuple-element.339), channel_id=1, source_target_pairs={{0,1},{1,2},{2,3},{4,5},{5,6},{6,7},{8,9},{9,10},{10,11},{12,13},{... | collective-permute-start | bytes 3145736 | tf_op jit(solution)/shard_map/ppermute | solution.py:59
  704.9 48.8 %collective-permute-start.50 = (bf16[256,2048]{1,0:T(8,128)(2,1)}, bf16[256,2048]{1,0:T(8,128)(2,1)}, u32[]{:S(2)}, u32[]{:S(2)}) collective-permute-start(bf16[256,2048]{1,0:T(8,128)(2,1)} %get-tuple-element.340), channel_id=1, source_target_pairs={{1,0},{2,1},{3,2},{5,4},{6,5},{7,6},{9,8},{10,9},{11,10},{13,12},{... | collective-permute-start | bytes 3145736 | tf_op jit(solution)/shard_map/ppermute | solution.py:60
  706.2 51.8 %collective-permute-start.51 = (bf16[256,2048]{1,0:T(8,128)(2,1)}, bf16[256,2048]{1,0:T(8,128)(2,1)}, u32[]{:S(2)}, u32[]{:S(2)}) collective-permute-start(bf16[256,2048]{1,0:T(8,128)(2,1)} %get-tuple-element.341), channel_id=1, source_target_pairs={{0,2},{3,1},{4,6},{7,5},{8,10},{11,9},{12,14},{15,13},{16,18},{19,... | collective-permute-start | bytes 3145736 | tf_op jit(solution)/shard_map/ppermute | solution.py:949
  729.5 53.9 %collective-permute-start.52 = (bf16[256,2048]{1,0:T(8,128)(2,1)S(1)}, bf16[256,2048]{1,0:T(8,128)(2,1)S(1)}, u32[]{:S(2)}, u32[]{:S(2)}) collective-permute-start(bf16[256,2048]{1,0:T(8,128)(2,1)S(1)} %add_convert_fusion), channel_id=1, source_target_pairs={{1,3},{2,0},{5,7},{6,4},{9,11},{10,8},{13,15},{14,12},{17,19},{18,... | collective-permute-start | bytes 3145736 | tf_op jit(solution)/shard_map/ppermute | solution.py:954
  783.4 43.3 %collective-permute-start.53 = (bf16[64,4096]{1,0:T(8,128)(2,1)}, bf16[64,4096]{1,0:T(8,128)(2,1)}, u32[]{:S(2)}, u32[]{:S(2)}) collective-permute-start(bf16[64,4096]{1,0:T(8,128)(2,1)} %get-tuple-element.352), channel_id=1, source_target_pairs={{0,1},{1,2},{2,3},{3,0},{4,5},{5,6},{6,7},{7,4},{8,9},{9,10},{10,1... | collective-permute-start | bytes 1572872 | tf_op jit(solution)/shard_map/ppermute | solution.py:129
  785.0 41.7 %collective-permute-start.54 = (bf16[64,4096]{1,0:T(8,128)(2,1)}, bf16[64,4096]{1,0:T(8,128)(2,1)}, u32[]{:S(2)}, u32[]{:S(2)}) collective-permute-start(bf16[64,4096]{1,0:T(8,128)(2,1)} %get-tuple-element.353), channel_id=1, source_target_pairs={{0,2},{1,3},{2,0},{3,1},{4,6},{5,7},{6,4},{7,5},{8,10},{9,11},{10,... | collective-permute-start | bytes 1572872 | tf_op jit(solution)/shard_map/ppermute | solution.py:129
  788.4 38.3 %collective-permute-start.55 = (bf16[64,4096]{1,0:T(8,128)(2,1)}, bf16[64,4096]{1,0:T(8,128)(2,1)}, u32[]{:S(2)}, u32[]{:S(2)}) collective-permute-start(bf16[64,4096]{1,0:T(8,128)(2,1)} %get-tuple-element.354), channel_id=1, source_target_pairs={{0,3},{1,0},{2,1},{3,2},{4,7},{5,4},{6,5},{7,6},{8,11},{9,8},{10,9... | collective-permute-start | bytes 1572872 | tf_op jit(solution)/shard_map/ppermute | solution.py:129
  826.7 30.3 %all-to-all-start.1 = ((bf16[4,64,2048]{2,1,0:T(8,128)(2,1)}), bf16[4,64,2048]{2,1,0:T(8,128)(2,1)S(1)}, u32[]{:S(2)}, u32[]{:S(2)}) async-start(bf16[4,64,2048]{2,1,0:T(8,128)(2,1)} %bitcast.90), calls=%async_computation.4 | async-start | bytes 2097152 | tf_op jit(solution)/shard_map/all_to_all | solution.py:99
  (86 other events, 1428.4 us)
Sparse Core Ops, SparseCore 0:
  36.0 44.6 all-gather.4
  83.1 92.0 all-gather.6
  180.4 58.2 all-gather.8
  241.0 54.3 all-gather.10
  558.1 72.8 reduce-scatter.3
  634.9 115.9 reduce-scatter.7
  754.7 71.9 reduce-scatter.5

commit v7 on v5

--- a/solution.py
+++ b/solution.py
@@ -61,9 +61,9 @@
     return [ends, after, before]
 
 
-def scatter_far(far, ends, count):
-    far_sum = (far + ends.astype(F32)).astype(BF)
-    return lax.ppermute(far_sum, "seq", [(i, i ^ 2) for i in range(count)])
+def scatter_far(far, ends):
+    far = (far.astype(F32) + ends.astype(F32)).astype(BF)
+    return lax.ppermute(far, "seq", [(1, 3), (2, 0)])
 
 
 def scatter_end(own, got):
@@ -347,14 +347,14 @@
 
 
 def residual_back_kernel(
-    me_ref, own_ref, a_ref, b_ref, c_ref, cot_ref, attn_ref, gain_ref, w_ref, res_ref, d_ref, sum_ref, *outs
+    me_ref, own_ref, a_ref, b_ref, c_ref, e_ref, cot_ref, attn_ref, gain_ref, w_ref, res_ref, d_ref, sum_ref, *outs
 ):
     step = pl.program_id(0)
 
     @pl.when(step == 0)
     def _():
         grad = cot_ref[...].astype(F32) + own_ref[...]
-        for ref in (a_ref, b_ref, c_ref):
+        for ref in (a_ref, b_ref, c_ref, e_ref):
             grad = grad + ref[...].astype(F32)
         res_ref[...] = grad
         attn = attn_ref[...]
@@ -383,7 +383,7 @@
         grid_spec=pltpu.PrefetchScalarGridSpec(
             num_scalar_prefetch=1,
             grid=(count,),
-            in_specs=[full] * 6
+            in_specs=[full] * 7
             + [whole(1), pl.BlockSpec((part, width), lambda p, me: ((me[0] + p) % count, 0))],
             out_specs=[whole(tokens), whole(tokens), whole(8)] + [piece] * count,
         ),
@@ -484,7 +484,7 @@
     out_ref[...] = total.astype(BF)
 
 
-def weight_grad(lefts, right):
+def weight_grad(lefts, right, declared=0):
     width = lefts[0].shape[1]
     length, columns = right.shape
     tile, wide = 256, min(columns, 2048)
@@ -496,7 +496,7 @@
         out_specs=pl.BlockSpec((tile, wide), lambda j, i: (i, j)),
         out_shape=jax.ShapeDtypeStruct((width, columns), BF),
         compiler_params=params(),
-        cost_estimate=cost(0, 0),
+        cost_estimate=cost(declared, 0),
         name="weight_grad",
     )(*lefts, right)
 
@@ -679,20 +679,17 @@
     ff_finish(pl.program_id(0), product, refs[-1], me_ref, refs[saved + 1 : -1])
 
 
-def ff_specs(width, tile, gate_at, down_at):
-    return [
-        pl.BlockSpec((width, tile), lambda t: (0, gate_at // tile + t)),
-        pl.BlockSpec((width, tile), lambda t: (0, t)),
-        pl.BlockSpec((width, tile), lambda t: (0, down_at // tile + t)),
-    ]
-
-
-def ff_forward(me, residual_all, w_first, w_second, place, kinds, saved=()):
+def ff_specs(width, tile, gate_at):
+    rest = pl.BlockSpec((width, tile), lambda t: (0, t))
+    return [pl.BlockSpec((width, tile), lambda t: (0, gate_at // tile + t)), rest, rest]
+
+
+def ff_forward(me, residual_all, w_first, w_up, w_down, place, kinds, saved=()):
     length, width = residual_all.shape
     tokens = length // 4
     group = min(len(kinds), 2)
     rows = group * tokens
-    ff_part = w_second.shape[1] // 2
+    ff_part = w_up.shape[1]
     tile = min(FF_TILE, ff_part)
     block = pl.BlockSpec((rows, tile), lambda t: (place // group, t))
     whole = pl.BlockSpec((tokens, width), lambda t: (0, 0))
@@ -702,7 +699,7 @@
         grid=(ff_part // tile,),
         in_specs=[pl.BlockSpec(memory_space=pltpu.SMEM)]
         + [once((rows, width), lambda t: (place // group, 0))]
-        + ff_specs(width, tile, w_first.shape[1] - ff_part, ff_part)
+        + ff_specs(width, tile, w_first.shape[1] - ff_part)
         + [pl.BlockSpec(memory_space=pl.ANY)] * len(saved),
         out_specs=[block] * 3 + [whole] * len(kinds),
         out_shape=[shape(F32), shape(F32), shape(BF)]
@@ -712,15 +709,15 @@
         compiler_params=params(),
         cost_estimate=cost(0, 0),
         name="ff_forward",
-    )(me, residual_all, w_first, w_second, w_second, *saved)
-
-
-def ff_backward(me, d_ffs, w_first, w_second, gate, up, place, kinds, saved=()):
+    )(me, residual_all, w_first, w_up, w_down, *saved)
+
+
+def ff_backward(me, d_ffs, w_first, w_up, w_down, gate, up, place, kinds, saved=()):
     tokens, width = d_ffs[0].shape
     group = len(d_ffs)
     rows = group * tokens
     length = gate.shape[0]
-    ff_part = w_second.shape[1] // 2
+    ff_part = w_up.shape[1]
     tile = min(FF_TILE, ff_part)
     block = pl.BlockSpec((rows, tile), lambda t: (place // group, t))
     whole = pl.BlockSpec((tokens, width), lambda t: (0, 0))
@@ -729,7 +726,7 @@
         grid=(ff_part // tile,),
         in_specs=[pl.BlockSpec(memory_space=pltpu.SMEM)]
         + [once((tokens, width), lambda t: (0, 0))] * group
-        + ff_specs(width, tile, w_first.shape[1] - ff_part, ff_part)
+        + ff_specs(width, tile, w_first.shape[1] - ff_part)
         + [block, block]
         + [pl.BlockSpec(memory_space=pl.ANY)] * len(saved),
         out_specs=[pl.BlockSpec((rows, 2 * tile), lambda t: (place // group, t))]
@@ -741,7 +738,7 @@
         compiler_params=params(),
         cost_estimate=cost(SIDE_COST, 0),
         name="ff_backward",
-    )(me, *d_ffs, w_first, w_second, w_second, gate, up, *saved)
+    )(me, *d_ffs, w_first, w_up, w_down, gate, up, *saved)
 
 
 def out_kernel(count, part, *refs):
@@ -865,6 +862,7 @@
         up_blocks = send_blocks(up_columns)
         x_all, qkv, squares = qkv_project(me_ref, 1, x_sides, w_qkv, saved)
         squares, up_blocks = fence((squares, up_blocks))
+        w_up_all = gather_dp(place_blocks(up_blocks, me, 0, ff_part))
 
         squares = sum_stats(squares, n)
         squares, down_columns = fence((squares, down_columns))
@@ -873,48 +871,54 @@
         mixed, q_low, k_low, v_low = attend(me_ref, qkv, factors, q_gain, k_gain, tables, seg, n)
 
         mixed, down_blocks = fence((mixed, down_blocks))
-        w_second = place_blocks(up_blocks, me, 0, 2 * ff_part)
-        w_second = gather_dp(place_blocks(down_blocks, me, ff_part, 2 * ff_part, w_second))
+        w_down_all = gather_dp(place_blocks(down_blocks, me, 0, ff_part))
         pieces = gather_cyclic(mixed, n)
         residual_all, attn_out = out_project(me_ref, pieces, w_first, x_all, attn_gain, n)
         attn_factor = inv_rms(attn_out)
         attn_normed = attn_out * attn_factor
         residual = x_own.astype(F32) + attn_normed * attn_gain
 
+        *saved, far = ff_forward(me_ref, residual_all, w_first, w_up_all, w_down_all, 2, (BF,))
+        across = lax.ppermute(far, "seq", [(0, 2), (3, 1)])
         *saved, after, before, ends = ff_forward(
-            me_ref, residual_all, w_first, w_second, 0, (BF, BF, BF)
+            me_ref, residual_all, w_first, w_up_all, w_down_all, 0, (BF, BF, BF), saved
+        )
+        after, before, ends, across, residual_late = fence(
+            (after, before, ends, across, residual_all)
         )
         sent = scatter_start(ends, after, before, n)
-        *saved, far = ff_forward(me_ref, residual_all, w_first, w_second, 2, (F32,), saved)
-        far, sent[0], residual_late = fence((far, sent[0], residual_all))
-        sent[0] = scatter_far(far, sent[0], n)
         gate, up, hidden, own = ff_forward(
-            me_ref, residual_late, w_first, w_second, 3, (F32,), saved
-        )
-        ff_out = scatter_end(own, sent)
+            me_ref, residual_late, w_first, w_up_all, w_down_all, 3, (F32,), saved
+        )
+        own, sent[0] = fence((own, sent[0]))
+        sent[0] = scatter_far(far, sent[0])
+        ff_out = scatter_end(own, sent + [across])
         ff_factor = inv_rms(ff_out)
         ff_normed = ff_out * ff_factor
         activation = (residual + ff_normed * ff_gain).astype(BF)
         grad_ff_gain = jnp.sum(cot.astype(F32) * ff_normed, axis=0)
         d_ff = rms_back(ff_normed, ff_factor, ff_gain, cot.astype(F32)).astype(BF)
         d_ffs = gather_cyclic(d_ff, n)
-        d_both, own = ff_backward(me_ref, d_ffs[:1], w_first, w_second, gate, up, 3, (F32,))
-        d_ffs, d_both = fence((d_ffs, d_both))
+        d_both, own = ff_backward(me_ref, d_ffs[:1], w_first, w_up_all, w_down_all, gate, up, 3, (F32,))
+        d_both, far = ff_backward(
+            me_ref, d_ffs[2:3], w_first, w_up_all, w_down_all, gate, up, 2, (BF,), (d_both,)
+        )
+        d_ffs, d_both, far = fence((d_ffs, d_both, far))
+        across = lax.ppermute(far, "seq", [(0, 2), (3, 1)])
         d_both, after, before, ends = ff_backward(
-            me_ref, d_ffs[1::2], w_first, w_second, gate, up, 0, (BF, BF, BF), (d_both,)
-        )
-        sent = scatter_start(ends, after, before, n)
-        d_both, far = ff_backward(
-            me_ref, d_ffs[2:3], w_first, w_second, gate, up, 2, (F32,), (d_both,)
-        )
-        d_both, far, sent[0], d_ffs, hidden = fence((d_both, far, sent[0], d_ffs, hidden))
-        sent[0] = scatter_far(far, sent[0], n)
+            me_ref, d_ffs[1::2], w_first, w_up_all, w_down_all, gate, up, 0, (BF, BF, BF), (d_both,)
+        )
+        after, before, ends, across, d_ffs, hidden = fence(
+            (after, before, ends, across, d_ffs, hidden)
+        )
+        ends, *sent = scatter_start(ends, after, before, n)
         joined = lambda g: g.transpose(1, 0, 2).reshape(shard_rows, -1).astype(F32)
-        down_grad = weight_grad([d_ffs[1], d_ffs[3], d_ffs[2], d_ffs[0]], hidden)
+        down_grad = weight_grad([d_ffs[1], d_ffs[3], d_ffs[2], d_ffs[0]], hidden, SIDE_COST)
+        ends, down_grad = fence((ends, down_grad))
         down_rows = scatter_dp(down_grad)
-        down_grad, sent = fence((down_grad, sent))
+        sent = [scatter_far(far, ends)] + sent
         d_res, d_attn, grad_attn_gain, *d_pieces = residual_back(
-            me_ref, own, sent, cot, attn_out, attn_gain, w_first, n
+            me_ref, own, sent + [across], cot, attn_out, attn_gain, w_first, n
         )
         d_mixed = [d_pieces[0]] + [None] * (n - 1)
         for p in range(1, n):
@@ -946,8 +950,7 @@
         attn_grads = attn_grad(me_ref, x_all, d_qkv, pieces, d_attn_part)
         ends, attn_grads = fence((ends, attn_grads))
         attn_rows = scatter_dp(attn_grads)
-        far = (far.astype(F32) + ends.astype(F32)).astype(BF)
-        sent.append(lax.ppermute(far, "seq", [(1, 3), (2, 0)]))
+        sent.append(scatter_far(far, ends))
         gate_up_back = row_blocks(gate_up_rows, me, n)
         sent, gate_up_back = fence((sent, gate_up_back))
         input_grad = add_up([d_res, own] + sent)

time: 873 us -> 856 us (0.981)
  waiting for transfers between devices: 361 us -> 341 us
    ppermute x3 -> x5, waiting for transfers between devices: 62.4 us -> 26.6 us  [the longest x3 26.6 us: scatter_far(): return lax.ppermute(far, 'seq', [(1, 3), (2, 0)])]
    ppermute x3, waiting for transfers between devices: 2.37 us -> 35.7 us  [scatter_start(): after = lax.ppermute(after, 'seq', step)]
    ppermute x5, waiting for transfers between devices: 30.9 us -> 10.8 us  [sum_everywhere(): lax.ppermute(values, name, [(i, i ^ bit) for i in range(count)])]
    reduce_scatter x3, waiting for transfers between devices: 21.3 us -> 40.7 us  [scatter_dp(): return lax.psum_scatter(values, 'dp', scatter_dimension=0, tiled=True)]
    ppermute x4, waiting for transfers between devices: 128 us -> 111 us  [gather_raw(): far = lax.ppermute(values, 'seq', [(i ^ 2, i) for i in range(count)])]
    ppermute x1, waiting for transfers between devices: 13.3 us -> 0.01 us  [shards(): sent.append(lax.ppermute(far, 'seq', [(0, 2), (3, 1)]))]
  transfers between devices with their start and end apart: 68 -> 71, of which waited for: 29 -> 31; matrix products, arithmetic and copies ran while one was open for 4% -> 3% of each run, Pallas kernels for 28% -> 32%
where the time goes in v7:
time: 856 us; the launch traced here: 846 us
  waiting for transfers between devices  341 us (40%)
  Pallas kernels  286 us (33%)
  starting transfers between devices  132 us (15%)
  local copies, waits for them, and re-layouts  31.2 us (4%)
  blocking collectives  26.5 us (3%)
  between operations  15.6 us (2%)
  other arithmetic  14.6 us (2%)
    ppermute x4, waiting for transfers between devices, gather_raw(): far = lax.ppermute(values, 'seq', [(i ^ 2, i) for i in range(count)])  111 us
    pallas_call x3, Pallas kernels, ff_backward(): pl.pallas_call(functools.partial(ff_back_kernel, len(saved), group), grid...  56 us
    pallas_call x3, Pallas kernels, ff_forward(): pl.pallas_call(functools.partial(ff_kernel, len(saved)), grid=(ff_part //...  53.8 us
    ppermute x4, waiting for transfers between devices, gather_raw(): ends = lax.ppermute(far, 'seq', [(2, 3), (1, 0)])  51.5 us
    pallas_call x2, Pallas kernels, weight_grad(): pl.pallas_call(lambda *refs: weight_grad_kernel(refs[:-2], *refs[-2:]), g...  41.6 us
    reduce_scatter x3, waiting for transfers between devices, scatter_dp(): return lax.psum_scatter(values, 'dp', scatter_dimension=0, tiled=True)  40.7 us
    ppermute x3, waiting for transfers between devices, scatter_start(): after = lax.ppermute(after, 'seq', step)  35.7 us
    ppermute x3, waiting for transfers between devices, scatter_far(): return lax.ppermute(far, 'seq', [(1, 3), (2, 0)])  26.6 us
  transfers between devices with their start and end apart: 71, of which 31 were waited for; matrix products, arithmetic and copies ran while one was open for 3% of the time, Pallas kernels for 32%

profile of v7, /device:TPU:0, one launch (start us, length us, event | category | flops | bytes accessed | tf_op | source)
XLA Modules:
  0.0 846.2 jit_solution(4282594796038643746)
XLA Ops:
  9.4 26.5 %all_to_all.10 = bf16[4,64,1536]{2,1,0:T(8,128)(2,1)} all-to-all(bf16[4,64,1536]{2,1,0:T(8,128)(2,1)S(1)} %pad_maximum_fusion), channel_id=1, replica_groups=mesh['dp'=8,'seq'=4] {'seq'}, dimensions={0} | all-to-all | bytes 1572864 | tf_op jit(solution)/shard_map/all_to_all | solution.py:99
  62.3 6.6 collective-permute-done.1
  69.0 8.6 %collective-permute-done.5 = bf16[64,2048]{1,0:T(8,128)(2,1)S(1)} collective-permute-done((bf16[64,2048]{1,0:T(8,128)(2,1)S(1)}, bf16[64,2048]{1,0:T(8,128)(2,1)S(1)}, u32[]{:S(2)}, u32[]{:S(2)}) %collective-permute-start.5) | collective-permute-done | bytes 262176 | tf_op jit(solution)/shard_map/ppermute | solution.py:129
  92.1 40.1 %collective-permute-done.9.refs_1_ = bf16[256,2048]{1,0:T(8,128)(2,1)} collective-permute-done((bf16[256,2048]{1,0:T(8,128)(2,1)S(1)}, bf16[256,2048]{1,0:T(8,128)(2,1)}, u32[]{:S(2)}, u32[]{:S(2)}) %collective-permute-start.9) | collective-permute-done | bytes 1048608 | tf_op jit(solution)/shard_map/ppermute | solution.py:42
  133.5 9.1 %qkv_project.2 = (bf16[1024,2048]{1,0:T(8,128)(2,1)}, f32[1024,1536]{1,0:T(8,128)}, f32[4,8,256]{2,1,0:T(8,128)}) custom-call(s32[1]{0:T(128)} %bitcast.9.me_ref.refs_0_, bf16[256,2048]{1,0:T(8,128)(2,1)} %bitcast.81, bf16[256,2048]{1,0:T(8,128)(2,1)} %collective-permute-done.9.refs_1_, bf16[2048,1536]{1,0:T(8,128)(2,1)} %all-gather.5.cloned.1.call-done.refs_2_.refs_3_.w_ref), custom_call_target="tpu_custom_call" | custom-call | tf_op jit(solution)/shard_map/qkv_project/pallas_call | solution.py:602
  142.6 15.1 %collective-permute-done.10.refs_2_ = bf16[256,2048]{1,0:T(8,128)(2,1)} collective-permute-done((bf16[256,2048]{1,0:T(8,128)(2,1)}, bf16[256,2048]{1,0:T(8,128)(2,1)}, u32[]{:S(2)}, u32[]{:S(2)}) %collective-permute-start.10) | collective-permute-done | bytes 1048608 | tf_op jit(solution)/shard_map/ppermute | solution.py:45
  163.1 9.4 %qkv_project.3 = (bf16[1024,2048]{1,0:T(8,128)(2,1)}, f32[1024,1536]{1,0:T(8,128)}, f32[4,8,256]{2,1,0:T(8,128)}) custom-call(s32[1]{0:T(128)} %bitcast.9.me_ref.refs_0_, bf16[256,2048]{1,0:T(8,128)(2,1)} %copy-done.13, bf16[256,2048]{1,0:T(8,128)(2,1)} %copy-done.15, ...), custom_call_target="tpu_custom_call", output_to_operand_aliasing={{0}: (5, {}), {1}: (6, {}), {2}: (7, {})} | custom-call | tf_op jit(solution)/shard_map/qkv_project/pallas_call | solution.py:602
  198.9 16.1 %attend.1 = (bf16[1024,512]{1,0:T(8,128)(2,1)}, bf16[1024,512]{1,0:T(8,128)(2,1)}, bf16[1024,512]{1,0:T(8,128)(2,1)}, bf16[1024,512]{1,0:T(8,128)(2,1)}) custom-call(s32[1]{0:T(128)} %bitcast.9.me_ref.refs_0_, f32[1024,1536]{1,0:T(8,128)} %get-tuple-element.215.q_ref.k_ref.v_ref.refs_7_.refs_8_.qp_ref.kp_ref, ...), custom_call_target="tpu_custom_call" | custom-call | tf_op jit(solution)/shard_map/attend/pallas_call | solution.py:300
  222.9 43.1 %collective-permute-done.20.refs_3_.refs_2_ = bf16[1024,512]{1,0:T(8,128)(2,1)S(1)} collective-permute-done((bf16[1024,512]{1,0:T(8,128)(2,1)S(1)}, bf16[1024,512]{1,0:T(8,128)(2,1)S(1)}, u32[]{:S(2)}, u32[]{:S(2)}) %collective-permute-start.20) | collective-permute-done | bytes 1048608 | tf_op jit(solution)/shard_map/ppermute | solution.py:42
  267.3 22.1 %collective-permute-done.21 = bf16[1024,512]{1,0:T(8,128)(2,1)S(1)} collective-permute-done((bf16[1024,512]{1,0:T(8,128)(2,1)S(1)}, bf16[1024,512]{1,0:T(8,128)(2,1)S(1)}, u32[]{:S(2)}, u32[]{:S(2)}) %collective-permute-start.21) | collective-permute-done | bytes 1048608 | tf_op jit(solution)/shard_map/ppermute | solution.py:45
  290.9 17.5 %out_project.1 = (bf16[1024,2048]{1,0:T(8,128)(2,1)}, f32[256,2048]{1,0:T(8,128)}) custom-call(s32[1]{0:T(128)} %bitcast.9.me_ref.refs_0_, bf16[1024,512]{1,0:T(8,128)(2,1)} %get-tuple-element.237.refs_1_.refs_0_, bf16[1024,512]{1,0:T(8,128)(2,1)} %get-tuple-element.410.refs_2_.refs_1_, bf16[1024,512]{1,0:T(8,128)(2,1)} %copy-done.9, ...), custom_call_target="tpu_custom_call" | custom-call | tf_op jit(solution)/shard_map/out_project/pallas_call | solution.py:770
  308.4 15.4 %ff_forward.3 = (f32[1024,2048]{1,0:T(8,128)}, f32[1024,2048]{1,0:T(8,128)}, bf16[1024,2048]{1,0:T(8,128)(2,1)}, bf16[256,2048]{1,0:T(8,128)(2,1)}) custom-call(s32[1]{0:T(128)} %bitcast.9.me_ref.refs_0_, bf16[1024,2048]{1,0:T(8,128)(2,1)} %get-tuple-element.307.h_ref.refs_0_, ...), custom_call_target="tpu_custom_call" | custom-call | tf_op jit(solution)/shard_map/ff_forward/pallas_call | solution.py:697
  328.8 22.6 %ff_forward.4 = (f32[1024,2048]{1,0:T(8,128)}, f32[1024,2048]{1,0:T(8,128)}, bf16[1024,2048]{1,0:T(8,128)(2,1)}, bf16[256,2048]{1,0:T(8,128)(2,1)}, bf16[256,204...) custom-call(s32[1]{0:T(128)} %bitcast.9.me_ref.refs_0_, ...), custom_call_target="tpu_custom_call", output_to_operand_aliasing={{0}: (5, {}), {1}: (6, {}), {2}: (7, {})} | custom-call | tf_op jit(solution)/shard_map/ff_forward/pallas_call | solution.py:697
  360.8 15.8 %ff_forward.5 = (f32[1024,2048]{1,0:T(8,128)}, f32[1024,2048]{1,0:T(8,128)}, bf16[1024,2048]{1,0:T(8,128)(2,1)}, f32[256,2048]{1,0:T(8,128)}) custom-call(s32[1]{0:T(128)} %bitcast.9.me_ref.refs_0_, bf16[1024,2048]{1,0:T(8,128)(2,1)} %get-tuple-element.307.h_ref.refs_0_, ...), custom_call_target="tpu_custom_call", output_to_operand_aliasing={{0}: (5, {}), {1}: (6, {}), {2}: (7, {})} | custom-call | tf_op jit(solution)/shard_map/ff_forward/pallas_call | solution.py:697
  380.9 17.7 %collective-permute-done.27 = bf16[256,2048]{1,0:T(8,128)(2,1)S(1)} collective-permute-done((bf16[256,2048]{1,0:T(8,128)(2,1)}, bf16[256,2048]{1,0:T(8,128)(2,1)S(1)}, u32[]{:S(2)}, u32[]{:S(2)}) %collective-permute-start.27) | collective-permute-done | bytes 1048608 | tf_op jit(solution)/shard_map/ppermute | solution.py:59
  407.3 7.7 collective-permute-start.32
  416.3 16.1 %ff_backward.3 = (bf16[1024,4096]{1,0:T(8,128)(2,1)}, f32[256,2048]{1,0:T(8,128)}) custom-call(s32[1]{0:T(128)} %bitcast.9.me_ref.refs_0_, bf16[256,2048]{1,0:T(8,128)(2,1)} %get-tuple-element.295.refs_0_.refs_3_, bf16[2048,4096]{1,0:T(8,128)(2,1)} %all-gather.7.cloned.1.call-done.refs_5_.wg_ref.refs_1_.refs_2_.w_ref, ...), custom_call_target="tpu_custom_call" | custom-call | flops 99999997952 | tf_op jit(solution)/shard_map/ff_backward/pallas_call | solution.py:724
  432.4 22.2 %collective-permute-done.29.refs_0_.refs_2_ = bf16[256,2048]{1,0:T(8,128)(2,1)S(1)} collective-permute-done((bf16[256,2048]{1,0:T(8,128)(2,1)}, bf16[256,2048]{1,0:T(8,128)(2,1)S(1)}, u32[]{:S(2)}, u32[]{:S(2)}) %collective-permute-start.29) | collective-permute-done | bytes 1048608 | tf_op jit(solution)/shard_map/ppermute | solution.py:42
  456.1 15.8 %ff_backward.4 = (bf16[1024,4096]{1,0:T(8,128)(2,1)}, bf16[256,2048]{1,0:T(8,128)(2,1)}) custom-call(s32[1]{0:T(128)} %bitcast.9.me_ref.refs_0_, bf16[256,2048]{1,0:T(8,128)(2,1)} %copy-done.46, bf16[2048,4096]{1,0:T(8,128)(2,1)} %all-gather.7.cloned.1.call-done.refs_5_.wg_ref.refs_1_.refs_2_.w_ref, ...), custom_call_target="tpu_custom_call", output_to_operand_aliasing={{0}: (7, {})} | custom-call | flops 99999997952 | tf_op jit(solution)/shard_map/ff_backward/pallas_call | solution.py:724
  471.9 7.7 collective-permute-done.30
  483.7 24.1 %ff_backward.5 = (bf16[1024,4096]{1,0:T(8,128)(2,1)}, bf16[256,2048]{1,0:T(8,128)(2,1)}, bf16[256,2048]{1,0:T(8,128)(2,1)}, bf16[256,2048]{1,0:T(8,128)(2,1)}) custom-call(s32[1]{0:T(128)} %bitcast.9.me_ref.refs_0_, bf16[256,2048]{1,0:T(8,128)(2,1)} %get-tuple-element.292.refs_0_, ...), custom_call_target="tpu_custom_call", output_to_operand_aliasing={{0}: (8, {})} | custom-call | flops 99999997952 | tf_op jit(solution)/shard_map/ff_backward/pallas_call | solution.py:724
  514.4 14.4 %weight_grad.2 = bf16[2048,2048]{1,0:T(8,128)(2,1)} custom-call(bf16[256,2048]{1,0:T(8,128)(2,1)} %get-tuple-element.292.refs_0_, bf16[256,2048]{1,0:T(8,128)(2,1)} %get-tuple-element.293.refs_1_, bf16[256,2048]{1,0:T(8,128)(2,1)} %copy-done.46, bf16[256,2048]{1,0:T(8,128)(2,1)} %get-tuple-element.295.refs_0_.refs_3_, ...), custom_call_target="tpu_custom_call" | custom-call | flops 99999997952 | tf_op jit(solution)/shard_map/weight_grad/pallas_call | solution.py:491
  536.4 18.0 %collective-permute-done.36.b_ref = bf16[256,2048]{1,0:T(8,128)(2,1)} collective-permute-done((bf16[256,2048]{1,0:T(8,128)(2,1)}, bf16[256,2048]{1,0:T(8,128)(2,1)}, u32[]{:S(2)}, u32[]{:S(2)}) %collective-permute-start.36) | collective-permute-done | bytes 1048608 | tf_op jit(solution)/shard_map/ppermute | solution.py:59
  561.9 13.3 %residual_back.1 = (f32[256,2048]{1,0:T(8,128)}, bf16[256,2048]{1,0:T(8,128)(2,1)}, f32[8,2048]{1,0:T(8,128)}, bf16[256,512]{1,0:T(8,128)(2,1)}, bf16[256,512]{1...) custom-call(s32[1]{0:T(128)} %bitcast.9.me_ref.refs_0_, f32[256,2048]{1,0:T(8,128)} %get-tuple-element.277.own_ref, ...), custom_call_target="tpu_custom_call" | custom-call | flops 999999995904 | tf_op jit(solution)/shard_map/residual_back/pallas_call | solution.py:381
  577.5 27.1 %weight_grad.3 = bf16[2048,4096]{1,0:T(8,128)(2,1)} custom-call(bf16[1024,2048]{1,0:T(8,128)(2,1)} %get-tuple-element.307.h_ref.refs_0_, bf16[1024,4096]{1,0:T(8,128)(2,1)} %get-tuple-element.308.refs_1_), custom_call_target="tpu_custom_call" | custom-call | tf_op jit(solution)/shard_map/weight_grad/pallas_call | solution.py:491
  611.8 22.4 %attend_back.1 = (f32[1024,512]{1,0:T(8,128)}, f32[1024,512]{1,0:T(8,128)}, bf16[1024,512]{1,0:T(8,128)(2,1)}, f32[4,8,256]{2,1,0:T(8,128)}, f32[2,8,512]{2,1,0:T(8,128)}) custom-call(s32[1]{0:T(128)} %bitcast.9.me_ref.refs_0_, bf16[256,512]{1,0:T(8,128)(2,1)} %get-tuple-element.309.refs_0_, bf16[256,512]{1,0:T(8,128)(2,1)} %copy-done.21, ...), custom_call_target="tpu_custom_call" | custom-call | tf_op jit(solution)/shard_map/attend_back/pallas_call | solution.py:323
  655.4 16.2 %input_back.1 = (bf16[1024,1536]{1,0:T(8,128)(2,1)}, bf16[256,2048]{1,0:T(8,128)(2,1)}, bf16[256,2048]{1,0:T(8,128)(2,1)}, bf16[256,2048]{1,0:T(8,128)(2,1)}, bf...) custom-call(s32[1]{0:T(128)} %bitcast.9.me_ref.refs_0_, f32[1024,512]{1,0:T(8,128)} %get-tuple-element.316.q_ref, ...), custom_call_target="tpu_custom_call" | custom-call | tf_op jit(solution)/shard_map/input_back/pallas_call | solution.py:431
  684.7 18.5 %attn_grad.1 = bf16[2048,2048]{1,0:T(8,128)(2,1)} custom-call(s32[1]{0:T(128)} %bitcast.9.me_ref.refs_0_, bf16[1024,2048]{1,0:T(8,128)(2,1)} %get-tuple-element.246.refs_6_.x_ref, bf16[1024,1536]{1,0:T(8,128)(2,1)} %get-tuple-element.339.d_ref, bf16[1024,512]{1,0:T(8,128)(2,1)} %get-tuple-element.237.refs_1_.refs_0_, ...), custom_call_target="tpu_custom_call" | custom-call | flops 99999997952 | tf_op jit(solution)/shard_map/attn_grad/pallas_call | solution.py:527
  707.3 22.2 %reduce-scatter.8.cloned.1.call-done = bf16[256,4096]{1,0:T(8,128)(2,1)} async-done(((bf16[2048,4096]{1,0:T(8,128)(2,1)}), bf16[256,4096]{1,0:T(8,128)(2,1)}) %reduce-scatter.8.cloned.1.call-update) | async-done | bytes 2097168 | tf_op jit(solution)/shard_map/reduce_scatter | solution.py:172
  732.3 22.4 %collective-permute-done.54.refs_5_ = bf16[256,2048]{1,0:T(8,128)(2,1)S(1)} collective-permute-done((bf16[256,2048]{1,0:T(8,128)(2,1)S(1)}, bf16[256,2048]{1,0:T(8,128)(2,1)S(1)}, u32[]{:S(2)}, u32[]{:S(2)}) %collective-permute-start.54) | collective-permute-done | bytes 1048608 | tf_op jit(solution)/shard_map/ppermute | solution.py:66
  786.7 18.5 %reduce-scatter.6.cloned.1.call-done = bf16[256,2048]{1,0:T(8,128)(2,1)} async-done(((bf16[2048,2048]{1,0:T(8,128)(2,1)}), bf16[256,2048]{1,0:T(8,128)(2,1)}) %reduce-scatter.6.cloned.1.call-update) | async-done | bytes 1048592 | tf_op jit(solution)/shard_map/reduce_scatter | solution.py:172
  817.4 18.1 %all-to-all-done.1 = bf16[4,64,2048]{2,1,0:T(8,128)(2,1)S(1)} async-done(((bf16[4,64,2048]{2,1,0:T(8,128)(2,1)}), bf16[4,64,2048]{2,1,0:T(8,128)(2,1)S(1)}, u32[]{:S(2)}, u32[]{:S(2)}) %all-to-all-start.1) | async-done | bytes 1048608 | tf_op jit(solution)/shard_map/all_to_all | solution.py:99
  (324 shorter events, 240.3 us)
Async XLA Ops:
  7.2 126.3 %all-gather.5.cloned.1.call-start = ((), (), s32[]{:S(2)}) async-start(), calls=%async_computation.5 | async-start | bytes 7077888 | tf_op jit(solution)/shard_map/all_gather | solution.py:168
  35.9 255.0 %all-gather.7.cloned.1.call-start = ((), (), s32[]{:S(2)}) async-start(), calls=%async_computation.6 | async-start | bytes 18874368 | tf_op jit(solution)/shard_map/all_gather | solution.py:168
  82.5 225.9 %all-gather.9.cloned.1.call-start = ((), (), s32[]{:S(2)}) async-start(), calls=%async_computation.7 | async-start | bytes 9437184 | tf_op jit(solution)/shard_map/all_gather | solution.py:168
  82.6 49.5 %collective-permute-start.9 = (bf16[256,2048]{1,0:T(8,128)(2,1)S(1)}, bf16[256,2048]{1,0:T(8,128)(2,1)}, u32[]{:S(2)}, u32[]{:S(2)}) collective-permute-start(bf16[256,2048]{1,0:T(8,128)(2,1)S(1)} %bitcast.82), channel_id=1, source_target_pairs={{2,0},{3,1},{0,2},{1,3},{6,4},{7,5},{4,6},{5,7},{10,8},{11,9},{8,1... | collective-permute-start | bytes 3145736 | tf_op jit(solution)/shard_map/ppermute | solution.py:42
  85.3 57.3 %collective-permute-start.7 = (bf16[256,2048]{1,0:T(8,128)(2,1)S(1)}, bf16[256,2048]{1,0:T(8,128)(2,1)S(1)}, u32[]{:S(2)}, u32[]{:S(2)}) collective-permute-start(bf16[256,2048]{1,0:T(8,128)(2,1)S(1)} %bitcast.83), channel_id=1, source_target_pairs={{1,0},{2,1},{3,2},{5,4},{6,5},{7,6},{9,8},{10,9},{11,10},{13,12},{... | collective-permute-start | bytes 3145736 | tf_op jit(solution)/shard_map/ppermute | solution.py:43
  86.6 56.0 %collective-permute-start.8 = (bf16[256,2048]{1,0:T(8,128)(2,1)S(1)}, bf16[256,2048]{1,0:T(8,128)(2,1)S(1)}, u32[]{:S(2)}, u32[]{:S(2)}) collective-permute-start(bf16[256,2048]{1,0:T(8,128)(2,1)S(1)} %bitcast.84), channel_id=1, source_target_pairs={{0,1},{1,2},{2,3},{4,5},{5,6},{6,7},{8,9},{9,10},{10,11},{12,13},{... | collective-permute-start | bytes 3145736 | tf_op jit(solution)/shard_map/ppermute | solution.py:44
  180.2 128.2 %all-gather.11.cloned.1.call-start = ((), (), s32[]{:S(2)}) async-start(), calls=%async_computation.8 | async-start | bytes 9437184 | tf_op jit(solution)/shard_map/all_gather | solution.py:168
  216.3 417.9 %reduce-scatter.4.cloned.1.call-start = ((), (), s32[]{:S(2)}) async-start(), calls=%async_computation.9 | async-start | bytes 9437184 | tf_op jit(solution)/shard_map/reduce_scatter | solution.py:172
  216.4 49.6 %collective-permute-start.20 = (bf16[1024,512]{1,0:T(8,128)(2,1)S(1)}, bf16[1024,512]{1,0:T(8,128)(2,1)S(1)}, u32[]{:S(2)}, u32[]{:S(2)}) collective-permute-start(bf16[1024,512]{1,0:T(8,128)(2,1)S(1)} %copy-done.8), channel_id=1, source_target_pairs={{2,0},{3,1},{0,2},{1,3},{6,4},{7,5},{4,6},{5,7},{10,8},{11,9},{8,1... | collective-permute-start | bytes 3145736 | tf_op jit(solution)/shard_map/ppermute | solution.py:42
  218.4 48.9 %collective-permute-start.23 = (bf16[1024,512]{1,0:T(8,128)(2,1)S(1)}, bf16[1024,512]{1,0:T(8,128)(2,1)S(1)}, u32[]{:S(2)}, u32[]{:S(2)}) collective-permute-start(bf16[1024,512]{1,0:T(8,128)(2,1)S(1)} %copy-done.8), channel_id=1, source_target_pairs={{0,1},{1,2},{2,3},{4,5},{5,6},{6,7},{8,9},{9,10},{10,11},{12,13},{... | collective-permute-start | bytes 3145736 | tf_op jit(solution)/shard_map/ppermute | solution.py:44
  221.6 45.7 %collective-permute-start.22 = (bf16[1024,512]{1,0:T(8,128)(2,1)S(1)}, bf16[1024,512]{1,0:T(8,128)(2,1)S(1)}, u32[]{:S(2)}, u32[]{:S(2)}) collective-permute-start(bf16[1024,512]{1,0:T(8,128)(2,1)S(1)} %copy-done.8), channel_id=1, source_target_pairs={{1,0},{2,1},{3,2},{5,4},{6,5},{7,6},{9,8},{10,9},{11,10},{13,12},{... | collective-permute-start | bytes 3145736 | tf_op jit(solution)/shard_map/ppermute | solution.py:43
  356.2 42.4 %collective-permute-start.27 = (bf16[256,2048]{1,0:T(8,128)(2,1)}, bf16[256,2048]{1,0:T(8,128)(2,1)S(1)}, u32[]{:S(2)}, u32[]{:S(2)}) collective-permute-start(bf16[256,2048]{1,0:T(8,128)(2,1)} %get-tuple-element.272), channel_id=1, source_target_pairs={{0,1},{1,2},{2,3},{4,5},{5,6},{6,7},{8,9},{9,10},{10,11},{12,13},{... | collective-permute-start | bytes 3145736 | tf_op jit(solution)/shard_map/ppermute | solution.py:59
  407.3 47.2 %collective-permute-start.29 = (bf16[256,2048]{1,0:T(8,128)(2,1)}, bf16[256,2048]{1,0:T(8,128)(2,1)S(1)}, u32[]{:S(2)}, u32[]{:S(2)}) collective-permute-start(bf16[256,2048]{1,0:T(8,128)(2,1)} %get-tuple-element.295.refs_0_.refs_3_), channel_id=1, source_target_pairs={{2,0},{3,1},{0,2},{1,3},{6,4},{7,5},{4,6},{5,7},{10,8},{11,9},{8,1... | collective-permute-start | bytes 3145736 | tf_op jit(solution)/shard_map/ppermute | solution.py:42
  407.3 64.6 %collective-permute-start.32 = (bf16[256,2048]{1,0:T(8,128)(2,1)}, bf16[256,2048]{1,0:T(8,128)(2,1)}, u32[]{:S(2)}, u32[]{:S(2)}) collective-permute-start(bf16[256,2048]{1,0:T(8,128)(2,1)} %get-tuple-element.295.refs_0_.refs_3_), channel_id=1, source_target_pairs={{0,1},{1,2},{2,3},{4,5},{5,6},{6,7},{8,9},{9,10},{10,11},{12,13},{... | collective-permute-start | bytes 3145736 | tf_op jit(solution)/shard_map/ppermute | solution.py:44
  415.0 56.9 %collective-permute-start.31 = (bf16[256,2048]{1,0:T(8,128)(2,1)}, bf16[256,2048]{1,0:T(8,128)(2,1)}, u32[]{:S(2)}, u32[]{:S(2)}) collective-permute-start(bf16[256,2048]{1,0:T(8,128)(2,1)} %get-tuple-element.295.refs_0_.refs_3_), channel_id=1, source_target_pairs={{1,0},{2,1},{3,2},{5,4},{6,5},{7,6},{9,8},{10,9},{11,10},{13,12},{... | collective-permute-start | bytes 3145736 | tf_op jit(solution)/shard_map/ppermute | solution.py:43
  510.8 43.6 %collective-permute-start.36 = (bf16[256,2048]{1,0:T(8,128)(2,1)}, bf16[256,2048]{1,0:T(8,128)(2,1)}, u32[]{:S(2)}, u32[]{:S(2)}) collective-permute-start(bf16[256,2048]{1,0:T(8,128)(2,1)} %get-tuple-element.298), channel_id=1, source_target_pairs={{0,1},{1,2},{2,3},{4,5},{5,6},{6,7},{8,9},{9,10},{10,11},{12,13},{... | collective-permute-start | bytes 3145736 | tf_op jit(solution)/shard_map/ppermute | solution.py:59
  513.1 47.8 %collective-permute-start.37 = (bf16[256,2048]{1,0:T(8,128)(2,1)}, bf16[256,2048]{1,0:T(8,128)(2,1)}, u32[]{:S(2)}, u32[]{:S(2)}) collective-permute-start(bf16[256,2048]{1,0:T(8,128)(2,1)} %get-tuple-element.299), channel_id=1, source_target_pairs={{1,0},{2,1},{3,2},{5,4},{6,5},{7,6},{9,8},{10,9},{11,10},{13,12},{... | collective-permute-start | bytes 3145736 | tf_op jit(solution)/shard_map/ppermute | solution.py:60
  536.4 193.1 %reduce-scatter.8.cloned.1.call-start = ((), (), s32[]{:S(2)}) async-start(), calls=%async_computation.11 | async-start | bytes 18874368 | tf_op jit(solution)/shard_map/reduce_scatter | solution.py:172
  575.1 29.5 %collective-permute-start.38 = (bf16[256,512]{1,0:T(8,128)(2,1)}, bf16[256,512]{1,0:T(8,128)(2,1)S(1)}, u32[]{:S(2)}, u32[]{:S(2)}) collective-permute-start(bf16[256,512]{1,0:T(8,128)(2,1)} %get-tuple-element.302), channel_id=1, source_target_pairs={{0,3},{1,0},{2,1},{3,2},{4,7},{5,4},{6,5},{7,6},{8,11},{9,8},{10,9... | collective-permute-start | bytes 786440 | tf_op jit(solution)/shard_map/ppermute | solution.py:925
  575.1 29.5 %collective-permute-start.39 = (bf16[256,512]{1,0:T(8,128)(2,1)}, bf16[256,512]{1,0:T(8,128)(2,1)S(1)}, u32[]{:S(2)}, u32[]{:S(2)}) collective-permute-start(bf16[256,512]{1,0:T(8,128)(2,1)} %get-tuple-element.303), channel_id=1, source_target_pairs={{0,2},{1,3},{2,0},{3,1},{4,6},{5,7},{6,4},{7,5},{8,10},{9,11},{10,... | collective-permute-start | bytes 786440 | tf_op jit(solution)/shard_map/ppermute | solution.py:925
  575.2 29.5 %collective-permute-start.40 = (bf16[256,512]{1,0:T(8,128)(2,1)}, bf16[256,512]{1,0:T(8,128)(2,1)S(1)}, u32[]{:S(2)}, u32[]{:S(2)}) collective-permute-start(bf16[256,512]{1,0:T(8,128)(2,1)} %get-tuple-element.304), channel_id=1, source_target_pairs={{0,1},{1,2},{2,3},{3,0},{4,5},{5,6},{6,7},{7,4},{8,9},{9,10},{10,1... | collective-permute-start | bytes 786440 | tf_op jit(solution)/shard_map/ppermute | solution.py:925
  605.6 199.6 %reduce-scatter.6.cloned.1.call-start = ((), (), s32[]{:S(2)}) async-start(), calls=%async_computation.10 | async-start | bytes 9437184 | tf_op jit(solution)/shard_map/reduce_scatter | solution.py:172
  607.0 29.4 %collective-permute-start.41 = (bf16[256,512]{1,0:T(8,128)(2,1)S(1)}, bf16[256,512]{1,0:T(8,128)(2,1)S(1)}, u32[]{:S(2)}, u32[]{:S(2)}) collective-permute-start(bf16[256,512]{1,0:T(8,128)(2,1)S(1)} %get-tuple-element.405), channel_id=1, source_target_pairs={{0,3},{1,0},{2,1},{3,2},{4,7},{5,4},{6,5},{7,6},{8,11},{9,8},{10,9... | collective-permute-start | bytes 786440 | tf_op jit(solution)/shard_map/ppermute | solution.py:794
  672.5 30.7 %collective-permute-start.50 = (bf16[256,2048]{1,0:T(8,128)(2,1)}, bf16[256,2048]{1,0:T(8,128)(2,1)S(1)}, u32[]{:S(2)}, u32[]{:S(2)}) collective-permute-start(bf16[256,2048]{1,0:T(8,128)(2,1)} %get-tuple-element.338), channel_id=1, source_target_pairs={{0,1},{3,2},{4,5},{7,6},{8,9},{11,10},{12,13},{15,14},{16,17},{19,... | collective-permute-start | bytes 3145736 | tf_op jit(solution)/shard_map/ppermute | solution.py:57
  676.4 55.9 %collective-permute-start.51 = (bf16[256,2048]{1,0:T(8,128)(2,1)}, bf16[256,2048]{1,0:T(8,128)(2,1)}, u32[]{:S(2)}, u32[]{:S(2)}) collective-permute-start(bf16[256,2048]{1,0:T(8,128)(2,1)} %get-tuple-element.347), channel_id=1, source_target_pairs={{0,1},{1,2},{2,3},{4,5},{5,6},{6,7},{8,9},{9,10},{10,11},{12,13},{... | collective-permute-start | bytes 3145736 | tf_op jit(solution)/shard_map/ppermute | solution.py:59
  678.7 53.6 %collective-permute-start.52 = (bf16[256,2048]{1,0:T(8,128)(2,1)}, bf16[256,2048]{1,0:T(8,128)(2,1)}, u32[]{:S(2)}, u32[]{:S(2)}) collective-permute-start(bf16[256,2048]{1,0:T(8,128)(2,1)} %get-tuple-element.348), channel_id=1, source_target_pairs={{1,0},{2,1},{3,2},{5,4},{6,5},{7,6},{9,8},{10,9},{11,10},{13,12},{... | collective-permute-start | bytes 3145736 | tf_op jit(solution)/shard_map/ppermute | solution.py:60
  680.0 52.3 %collective-permute-start.53 = (bf16[256,2048]{1,0:T(8,128)(2,1)}, bf16[256,2048]{1,0:T(8,128)(2,1)}, u32[]{:S(2)}, u32[]{:S(2)}) collective-permute-start(bf16[256,2048]{1,0:T(8,128)(2,1)} %get-tuple-element.349), channel_id=1, source_target_pairs={{0,2},{3,1},{4,6},{7,5},{8,10},{11,9},{12,14},{15,13},{16,18},{19,... | collective-permute-start | bytes 3145736 | tf_op jit(solution)/shard_map/ppermute | solution.py:949
  703.6 51.1 %collective-permute-start.54 = (bf16[256,2048]{1,0:T(8,128)(2,1)S(1)}, bf16[256,2048]{1,0:T(8,128)(2,1)S(1)}, u32[]{:S(2)}, u32[]{:S(2)}) collective-permute-start(bf16[256,2048]{1,0:T(8,128)(2,1)S(1)} %add_convert_fusion), channel_id=1, source_target_pairs={{1,3},{2,0},{5,7},{6,4},{9,11},{10,8},{13,15},{14,12},{17,19},{18,... | collective-permute-start | bytes 3145736 | tf_op jit(solution)/shard_map/ppermute | solution.py:66
  754.7 50.5 %collective-permute-start.55 = (bf16[64,4096]{1,0:T(8,128)(2,1)}, bf16[64,4096]{1,0:T(8,128)(2,1)}, u32[]{:S(2)}, u32[]{:S(2)}) collective-permute-start(bf16[64,4096]{1,0:T(8,128)(2,1)} %get-tuple-element.360), channel_id=1, source_target_pairs={{0,1},{1,2},{2,3},{3,0},{4,5},{5,6},{6,7},{7,4},{8,9},{9,10},{10,1... | collective-permute-start | bytes 1572872 | tf_op jit(solution)/shard_map/ppermute | solution.py:129
  754.7 50.5 %collective-permute-start.56 = (bf16[64,4096]{1,0:T(8,128)(2,1)}, bf16[64,4096]{1,0:T(8,128)(2,1)}, u32[]{:S(2)}, u32[]{:S(2)}) collective-permute-start(bf16[64,4096]{1,0:T(8,128)(2,1)} %get-tuple-element.361), channel_id=1, source_target_pairs={{0,2},{1,3},{2,0},{3,1},{4,6},{5,7},{6,4},{7,5},{8,10},{9,11},{10,... | collective-permute-start | bytes 1572872 | tf_op jit(solution)/shard_map/ppermute | solution.py:129
  757.2 48.0 %collective-permute-start.57 = (bf16[64,4096]{1,0:T(8,128)(2,1)}, bf16[64,4096]{1,0:T(8,128)(2,1)}, u32[]{:S(2)}, u32[]{:S(2)}) collective-permute-start(bf16[64,4096]{1,0:T(8,128)(2,1)} %get-tuple-element.362), channel_id=1, source_target_pairs={{0,3},{1,0},{2,1},{3,2},{4,7},{5,4},{6,5},{7,6},{8,11},{9,8},{10,9... | collective-permute-start | bytes 1572872 | tf_op jit(solution)/shard_map/ppermute | solution.py:129
  805.2 30.3 %all-to-all-start.1 = ((bf16[4,64,2048]{2,1,0:T(8,128)(2,1)}), bf16[4,64,2048]{2,1,0:T(8,128)(2,1)S(1)}, u32[]{:S(2)}, u32[]{:S(2)}) async-start(bf16[4,64,2048]{2,1,0:T(8,128)(2,1)} %bitcast.90), calls=%async_computation.4 | async-start | bytes 2097152 | tf_op jit(solution)/shard_map/all_to_all | solution.py:99
  (91 other events, 1467.4 us)
Sparse Core Ops, SparseCore 0:
  36.0 44.6 all-gather.4
  83.1 91.9 all-gather.6
  180.4 58.2 all-gather.8
  241.0 54.3 all-gather.10
  536.5 73.0 reduce-scatter.3
  613.4 115.9 reduce-scatter.7
  733.3 71.8 reduce-scatter.5

commit v8 on v7

--- a/solution.py
+++ b/solution.py
@@ -912,7 +912,6 @@
             (after, before, ends, across, d_ffs, hidden)
         )
         ends, *sent = scatter_start(ends, after, before, n)
-        joined = lambda g: g.transpose(1, 0, 2).reshape(shard_rows, -1).astype(F32)
         down_grad = weight_grad([d_ffs[1], d_ffs[3], d_ffs[2], d_ffs[0]], hidden, SIDE_COST)
         ends, down_grad = fence((ends, down_grad))
         down_rows = scatter_dp(down_grad)
@@ -952,7 +951,7 @@
         attn_rows = scatter_dp(attn_grads)
         sent.append(scatter_far(far, ends))
         gate_up_back = row_blocks(gate_up_rows, me, n)
-        sent, gate_up_back = fence((sent, gate_up_back))
+        sent[0], gate_up_back = fence((sent[0], gate_up_back))
         input_grad = add_up([d_res, own] + sent)
         spread = lambda g: lax.dynamic_update_slice(jnp.zeros(width, F32), g, (me * part,))
         gains = jnp.stack(
@@ -964,15 +963,13 @@
         attn_rows, input_grad, gate_up_back, down_back, gains = fence(
             (attn_rows, input_grad, gate_up_back, down_back, gains)
         )
-        attn_back = swap_blocks(attn_rows.reshape(n, shard_rows, -1))
+        attn_back = send_blocks(row_blocks(attn_rows, me, n))
         grad_gate, grad_up = join_columns(me_ref, gate_up_back, 2)
         grad_down = join_columns(me_ref, down_back, 1)[0].T
         attn_back, grad_gate, grad_up, grad_down = fence(
             (attn_back, grad_gate, grad_up, grad_down)
         )
-        grad_query, grad_key, grad_value, grad_output = (
-            joined(attn_back[:, :, j * part : (j + 1) * part]) for j in range(4)
-        )
+        grad_query, grad_key, grad_value, grad_output = join_columns(me_ref, attn_back, 4)
 
         share = width // devices
         gains = lax.dynamic_slice_in_dim(

time: 856 us -> 852 us (level)
    all_to_all x1 -> x0, waiting for transfers between devices: 18.1 us -> none  [swap_blocks(): lax.all_to_all(values, 'seq', split_axis=0, concat_axis=0, tiled=True)]
    ppermute x3, waiting for transfers between devices: 26.6 us -> 39 us  [scatter_far(): return lax.ppermute(far, 'seq', [(1, 3), (2, 0)])]
    ppermute x15 -> x18, waiting for transfers between devices: 17.5 us -> 25.8 us  [send_blocks(): lax.ppermute(blocks[p], 'seq', [(i, (i + p) % count) for i in range(count)])]
    ppermute x15 -> x18, starting transfers between devices: 24.4 us -> 31.2 us  [send_blocks(): lax.ppermute(blocks[p], 'seq', [(i, (i + p) % count) for i in range(count)])]
  transfers between devices with their start and end apart: 71 -> 73, of which waited for: 31 -> 31; matrix products, arithmetic and copies ran while one was open for 3% -> 3% of each run, Pallas kernels for 32% -> 32%
where the time goes in v8:
time: 852 us; the launch traced here: 839 us
  waiting for transfers between devices  333 us (39%)
  Pallas kernels  289 us (34%)
  starting transfers between devices  130 us (15%)
  local copies, waits for them, and re-layouts  31.7 us (4%)
  blocking collectives  26.5 us (3%)
  between operations  15.6 us (2%)
  other arithmetic  14.3 us (2%)
    ppermute x4, waiting for transfers between devices, gather_raw(): far = lax.ppermute(values, 'seq', [(i ^ 2, i) for i in range(count)])  111 us
    pallas_call x3, Pallas kernels, ff_backward(): pl.pallas_call(functools.partial(ff_back_kernel, len(saved), group), grid...  55.9 us
    pallas_call x3, Pallas kernels, ff_forward(): pl.pallas_call(functools.partial(ff_kernel, len(saved)), grid=(ff_part //...  53.8 us
    ppermute x4, waiting for transfers between devices, gather_raw(): ends = lax.ppermute(far, 'seq', [(2, 3), (1, 0)])  51.5 us
    pallas_call x2, Pallas kernels, weight_grad(): pl.pallas_call(lambda *refs: weight_grad_kernel(refs[:-2], *refs[-2:]), g...  41.5 us
    ppermute x3, waiting for transfers between devices, scatter_far(): return lax.ppermute(far, 'seq', [(1, 3), (2, 0)])  39 us
    ppermute x3, waiting for transfers between devices, scatter_start(): after = lax.ppermute(after, 'seq', step)  35.7 us
    reduce_scatter x3, waiting for transfers between devices, scatter_dp(): return lax.psum_scatter(values, 'dp', scatter_dimension=0, tiled=True)  33.2 us
  transfers between devices with their start and end apart: 73, of which 31 were waited for; matrix products, arithmetic and copies ran while one was open for 3% of the time, Pallas kernels for 32%

profile of v8, /device:TPU:0, one launch (start us, length us, event | category | flops | bytes accessed | tf_op | source)
XLA Modules:
  0.0 839.3 jit_solution(17674848961793235602)
XLA Ops:
  9.4 26.5 %all_to_all.5 = bf16[4,64,1536]{2,1,0:T(8,128)(2,1)} all-to-all(bf16[4,64,1536]{2,1,0:T(8,128)(2,1)S(1)} %pad_maximum_fusion), channel_id=1, replica_groups=mesh['dp'=8,'seq'=4] {'seq'}, dimensions={0} | all-to-all | bytes 1572864 | tf_op jit(solution)/shard_map/all_to_all | solution.py:99
  62.3 6.6 collective-permute-done.1
  69.0 8.6 %collective-permute-done.5 = bf16[64,2048]{1,0:T(8,128)(2,1)S(1)} collective-permute-done((bf16[64,2048]{1,0:T(8,128)(2,1)S(1)}, bf16[64,2048]{1,0:T(8,128)(2,1)S(1)}, u32[]{:S(2)}, u32[]{:S(2)}) %collective-permute-start.5) | collective-permute-done | bytes 262176 | tf_op jit(solution)/shard_map/ppermute | solution.py:129
  92.1 40.1 %collective-permute-done.9.refs_1_ = bf16[256,2048]{1,0:T(8,128)(2,1)} collective-permute-done((bf16[256,2048]{1,0:T(8,128)(2,1)S(1)}, bf16[256,2048]{1,0:T(8,128)(2,1)}, u32[]{:S(2)}, u32[]{:S(2)}) %collective-permute-start.9) | collective-permute-done | bytes 1048608 | tf_op jit(solution)/shard_map/ppermute | solution.py:42
  133.5 9.1 %qkv_project.2 = (bf16[1024,2048]{1,0:T(8,128)(2,1)}, f32[1024,1536]{1,0:T(8,128)}, f32[4,8,256]{2,1,0:T(8,128)}) custom-call(s32[1]{0:T(128)} %bitcast.9.me_ref.refs_0_, bf16[256,2048]{1,0:T(8,128)(2,1)} %bitcast.64, bf16[256,2048]{1,0:T(8,128)(2,1)} %collective-permute-done.9.refs_1_, bf16[2048,1536]{1,0:T(8,128)(2,1)} %all-gather.5.cloned.1.call-done.refs_2_.refs_3_.w_ref), custom_call_target="tpu_custom_call" | custom-call | tf_op jit(solution)/shard_map/qkv_project/pallas_call | solution.py:602
  142.6 15.1 %collective-permute-done.10.refs_2_ = bf16[256,2048]{1,0:T(8,128)(2,1)} collective-permute-done((bf16[256,2048]{1,0:T(8,128)(2,1)}, bf16[256,2048]{1,0:T(8,128)(2,1)}, u32[]{:S(2)}, u32[]{:S(2)}) %collective-permute-start.10) | collective-permute-done | bytes 1048608 | tf_op jit(solution)/shard_map/ppermute | solution.py:45
  163.1 9.3 %qkv_project.3 = (bf16[1024,2048]{1,0:T(8,128)(2,1)}, f32[1024,1536]{1,0:T(8,128)}, f32[4,8,256]{2,1,0:T(8,128)}) custom-call(s32[1]{0:T(128)} %bitcast.9.me_ref.refs_0_, bf16[256,2048]{1,0:T(8,128)(2,1)} %copy-done.13, bf16[256,2048]{1,0:T(8,128)(2,1)} %copy-done.15, ...), custom_call_target="tpu_custom_call", output_to_operand_aliasing={{0}: (5, {}), {1}: (6, {}), {2}: (7, {})} | custom-call | tf_op jit(solution)/shard_map/qkv_project/pallas_call | solution.py:602
  198.9 16.1 %attend.1 = (bf16[1024,512]{1,0:T(8,128)(2,1)}, bf16[1024,512]{1,0:T(8,128)(2,1)}, bf16[1024,512]{1,0:T(8,128)(2,1)}, bf16[1024,512]{1,0:T(8,128)(2,1)}) custom-call(s32[1]{0:T(128)} %bitcast.9.me_ref.refs_0_, f32[1024,1536]{1,0:T(8,128)} %get-tuple-element.219.q_ref.k_ref.v_ref.refs_7_.refs_8_.qp_ref.kp_ref, ...), custom_call_target="tpu_custom_call" | custom-call | tf_op jit(solution)/shard_map/attend/pallas_call | solution.py:300
  222.9 43.1 %collective-permute-done.20.refs_3_.refs_2_ = bf16[1024,512]{1,0:T(8,128)(2,1)S(1)} collective-permute-done((bf16[1024,512]{1,0:T(8,128)(2,1)S(1)}, bf16[1024,512]{1,0:T(8,128)(2,1)S(1)}, u32[]{:S(2)}, u32[]{:S(2)}) %collective-permute-start.20) | collective-permute-done | bytes 1048608 | tf_op jit(solution)/shard_map/ppermute | solution.py:42
  267.3 22.1 %collective-permute-done.21 = bf16[1024,512]{1,0:T(8,128)(2,1)S(1)} collective-permute-done((bf16[1024,512]{1,0:T(8,128)(2,1)S(1)}, bf16[1024,512]{1,0:T(8,128)(2,1)S(1)}, u32[]{:S(2)}, u32[]{:S(2)}) %collective-permute-start.21) | collective-permute-done | bytes 1048608 | tf_op jit(solution)/shard_map/ppermute | solution.py:45
  290.8 17.5 %out_project.1 = (bf16[1024,2048]{1,0:T(8,128)(2,1)}, f32[256,2048]{1,0:T(8,128)}) custom-call(s32[1]{0:T(128)} %bitcast.9.me_ref.refs_0_, bf16[1024,512]{1,0:T(8,128)(2,1)} %get-tuple-element.241.refs_1_.refs_0_, bf16[1024,512]{1,0:T(8,128)(2,1)} %get-tuple-element.418.refs_2_.refs_1_, bf16[1024,512]{1,0:T(8,128)(2,1)} %copy-done.9, ...), custom_call_target="tpu_custom_call" | custom-call | tf_op jit(solution)/shard_map/out_project/pallas_call | solution.py:770
  308.4 15.3 %ff_forward.3 = (f32[1024,2048]{1,0:T(8,128)}, f32[1024,2048]{1,0:T(8,128)}, bf16[1024,2048]{1,0:T(8,128)(2,1)}, bf16[256,2048]{1,0:T(8,128)(2,1)}) custom-call(s32[1]{0:T(128)} %bitcast.9.me_ref.refs_0_, bf16[1024,2048]{1,0:T(8,128)(2,1)} %get-tuple-element.311.h_ref.refs_0_, ...), custom_call_target="tpu_custom_call" | custom-call | tf_op jit(solution)/shard_map/ff_forward/pallas_call | solution.py:697
  328.8 22.6 %ff_forward.4 = (f32[1024,2048]{1,0:T(8,128)}, f32[1024,2048]{1,0:T(8,128)}, bf16[1024,2048]{1,0:T(8,128)(2,1)}, bf16[256,2048]{1,0:T(8,128)(2,1)}, bf16[256,204...) custom-call(s32[1]{0:T(128)} %bitcast.9.me_ref.refs_0_, ...), custom_call_target="tpu_custom_call", output_to_operand_aliasing={{0}: (5, {}), {1}: (6, {}), {2}: (7, {})} | custom-call | tf_op jit(solution)/shard_map/ff_forward/pallas_call | solution.py:697
  360.8 15.8 %ff_forward.5 = (f32[1024,2048]{1,0:T(8,128)}, f32[1024,2048]{1,0:T(8,128)}, bf16[1024,2048]{1,0:T(8,128)(2,1)}, f32[256,2048]{1,0:T(8,128)}) custom-call(s32[1]{0:T(128)} %bitcast.9.me_ref.refs_0_, bf16[1024,2048]{1,0:T(8,128)(2,1)} %get-tuple-element.311.h_ref.refs_0_, ...), custom_call_target="tpu_custom_call", output_to_operand_aliasing={{0}: (5, {}), {1}: (6, {}), {2}: (7, {})} | custom-call | tf_op jit(solution)/shard_map/ff_forward/pallas_call | solution.py:697
  380.8 17.7 %collective-permute-done.27 = bf16[256,2048]{1,0:T(8,128)(2,1)S(1)} collective-permute-done((bf16[256,2048]{1,0:T(8,128)(2,1)}, bf16[256,2048]{1,0:T(8,128)(2,1)S(1)}, u32[]{:S(2)}, u32[]{:S(2)}) %collective-permute-start.27) | collective-permute-done | bytes 1048608 | tf_op jit(solution)/shard_map/ppermute | solution.py:59
  407.3 7.7 collective-permute-start.32
  416.3 16.1 %ff_backward.3 = (bf16[1024,4096]{1,0:T(8,128)(2,1)}, f32[256,2048]{1,0:T(8,128)}) custom-call(s32[1]{0:T(128)} %bitcast.9.me_ref.refs_0_, bf16[256,2048]{1,0:T(8,128)(2,1)} %get-tuple-element.299.refs_0_.refs_3_, bf16[2048,4096]{1,0:T(8,128)(2,1)} %all-gather.7.cloned.1.call-done.refs_5_.wg_ref.refs_1_.refs_2_.w_ref, ...), custom_call_target="tpu_custom_call" | custom-call | flops 99999997952 | tf_op jit(solution)/shard_map/ff_backward/pallas_call | solution.py:724
  432.4 22.2 %collective-permute-done.29.refs_0_.refs_2_ = bf16[256,2048]{1,0:T(8,128)(2,1)S(1)} collective-permute-done((bf16[256,2048]{1,0:T(8,128)(2,1)}, bf16[256,2048]{1,0:T(8,128)(2,1)S(1)}, u32[]{:S(2)}, u32[]{:S(2)}) %collective-permute-start.29) | collective-permute-done | bytes 1048608 | tf_op jit(solution)/shard_map/ppermute | solution.py:42
  456.0 15.8 %ff_backward.4 = (bf16[1024,4096]{1,0:T(8,128)(2,1)}, bf16[256,2048]{1,0:T(8,128)(2,1)}) custom-call(s32[1]{0:T(128)} %bitcast.9.me_ref.refs_0_, bf16[256,2048]{1,0:T(8,128)(2,1)} %copy-done.49, bf16[2048,4096]{1,0:T(8,128)(2,1)} %all-gather.7.cloned.1.call-done.refs_5_.wg_ref.refs_1_.refs_2_.w_ref, ...), custom_call_target="tpu_custom_call", output_to_operand_aliasing={{0}: (7, {})} | custom-call | flops 99999997952 | tf_op jit(solution)/shard_map/ff_backward/pallas_call | solution.py:724
  471.9 7.7 collective-permute-done.30
  483.7 24.0 %ff_backward.5 = (bf16[1024,4096]{1,0:T(8,128)(2,1)}, bf16[256,2048]{1,0:T(8,128)(2,1)}, bf16[256,2048]{1,0:T(8,128)(2,1)}, bf16[256,2048]{1,0:T(8,128)(2,1)}) custom-call(s32[1]{0:T(128)} %bitcast.9.me_ref.refs_0_, bf16[256,2048]{1,0:T(8,128)(2,1)} %get-tuple-element.296.refs_0_, ...), custom_call_target="tpu_custom_call", output_to_operand_aliasing={{0}: (8, {})} | custom-call | flops 99999997952 | tf_op jit(solution)/shard_map/ff_backward/pallas_call | solution.py:724
  514.2 14.4 %weight_grad.2 = bf16[2048,2048]{1,0:T(8,128)(2,1)} custom-call(bf16[256,2048]{1,0:T(8,128)(2,1)} %get-tuple-element.296.refs_0_, bf16[256,2048]{1,0:T(8,128)(2,1)} %get-tuple-element.297.refs_1_, bf16[256,2048]{1,0:T(8,128)(2,1)} %copy-done.49, bf16[256,2048]{1,0:T(8,128)(2,1)} %get-tuple-element.299.refs_0_.refs_3_, ...), custom_call_target="tpu_custom_call" | custom-call | flops 99999997952 | tf_op jit(solution)/shard_map/weight_grad/pallas_call | solution.py:491
  536.3 18.0 %collective-permute-done.36.b_ref = bf16[256,2048]{1,0:T(8,128)(2,1)} collective-permute-done((bf16[256,2048]{1,0:T(8,128)(2,1)}, bf16[256,2048]{1,0:T(8,128)(2,1)}, u32[]{:S(2)}, u32[]{:S(2)}) %collective-permute-start.36) | collective-permute-done | bytes 1048608 | tf_op jit(solution)/shard_map/ppermute | solution.py:59
  561.6 13.3 %residual_back.1 = (f32[256,2048]{1,0:T(8,128)}, bf16[256,2048]{1,0:T(8,128)(2,1)}, f32[8,2048]{1,0:T(8,128)}, bf16[256,512]{1,0:T(8,128)(2,1)}, bf16[256,512]{1...) custom-call(s32[1]{0:T(128)} %bitcast.9.me_ref.refs_0_, f32[256,2048]{1,0:T(8,128)} %get-tuple-element.281.own_ref, ...), custom_call_target="tpu_custom_call" | custom-call | flops 999999995904 | tf_op jit(solution)/shard_map/residual_back/pallas_call | solution.py:381
  577.3 27.0 %weight_grad.3 = bf16[2048,4096]{1,0:T(8,128)(2,1)} custom-call(bf16[1024,2048]{1,0:T(8,128)(2,1)} %get-tuple-element.311.h_ref.refs_0_, bf16[1024,4096]{1,0:T(8,128)(2,1)} %get-tuple-element.312.refs_1_), custom_call_target="tpu_custom_call" | custom-call | tf_op jit(solution)/shard_map/weight_grad/pallas_call | solution.py:491
  611.5 22.4 %attend_back.1 = (f32[1024,512]{1,0:T(8,128)}, f32[1024,512]{1,0:T(8,128)}, bf16[1024,512]{1,0:T(8,128)(2,1)}, f32[4,8,256]{2,1,0:T(8,128)}, f32[2,8,512]{2,1,0:T(8,128)}) custom-call(s32[1]{0:T(128)} %bitcast.9.me_ref.refs_0_, bf16[256,512]{1,0:T(8,128)(2,1)} %get-tuple-element.313.refs_0_, bf16[256,512]{1,0:T(8,128)(2,1)} %copy-done.21, ...), custom_call_target="tpu_custom_call" | custom-call | tf_op jit(solution)/shard_map/attend_back/pallas_call | solution.py:323
  655.3 16.2 %input_back.1 = (bf16[1024,1536]{1,0:T(8,128)(2,1)}, bf16[256,2048]{1,0:T(8,128)(2,1)}, bf16[256,2048]{1,0:T(8,128)(2,1)}, bf16[256,2048]{1,0:T(8,128)(2,1)}, bf...) custom-call(s32[1]{0:T(128)} %bitcast.9.me_ref.refs_0_, f32[1024,512]{1,0:T(8,128)} %get-tuple-element.320.q_ref, ...), custom_call_target="tpu_custom_call" | custom-call | tf_op jit(solution)/shard_map/input_back/pallas_call | solution.py:431
  684.6 18.5 %attn_grad.1 = bf16[2048,2048]{1,0:T(8,128)(2,1)} custom-call(s32[1]{0:T(128)} %bitcast.9.me_ref.refs_0_, bf16[1024,2048]{1,0:T(8,128)(2,1)} %get-tuple-element.250.refs_6_.x_ref, bf16[1024,1536]{1,0:T(8,128)(2,1)} %get-tuple-element.343.d_ref, bf16[1024,512]{1,0:T(8,128)(2,1)} %get-tuple-element.241.refs_1_.refs_0_, ...), custom_call_target="tpu_custom_call" | custom-call | flops 99999997952 | tf_op jit(solution)/shard_map/attn_grad/pallas_call | solution.py:527
  707.1 22.2 %reduce-scatter.8.cloned.1.call-done = bf16[256,4096]{1,0:T(8,128)(2,1)} async-done(((bf16[2048,4096]{1,0:T(8,128)(2,1)}), bf16[256,4096]{1,0:T(8,128)(2,1)}) %reduce-scatter.8.cloned.1.call-update) | async-done | bytes 2097168 | tf_op jit(solution)/shard_map/reduce_scatter | solution.py:172
  737.6 28.5 %collective-permute-done.54.refs_5_ = bf16[256,2048]{1,0:T(8,128)(2,1)S(1)} collective-permute-done((bf16[256,2048]{1,0:T(8,128)(2,1)S(1)}, bf16[256,2048]{1,0:T(8,128)(2,1)S(1)}, u32[]{:S(2)}, u32[]{:S(2)}) %collective-permute-start.54) | collective-permute-done | bytes 1048608 | tf_op jit(solution)/shard_map/ppermute | solution.py:66
  794.2 10.9 %reduce-scatter.6.cloned.1.call-done = bf16[256,2048]{1,0:T(8,128)(2,1)} async-done(((bf16[2048,2048]{1,0:T(8,128)(2,1)}), bf16[256,2048]{1,0:T(8,128)(2,1)}) %reduce-scatter.6.cloned.1.call-update) | async-done | bytes 1048592 | tf_op jit(solution)/shard_map/reduce_scatter | solution.py:172
  820.1 8.3 collective-permute-done.64.refs_2_
  (331 shorter events, 244.8 us)
Async XLA Ops:
  7.2 126.3 %all-gather.5.cloned.1.call-start = ((), (), s32[]{:S(2)}) async-start(), calls=%async_computation.4 | async-start | bytes 7077888 | tf_op jit(solution)/shard_map/all_gather | solution.py:168
  35.9 255.0 %all-gather.7.cloned.1.call-start = ((), (), s32[]{:S(2)}) async-start(), calls=%async_computation.5 | async-start | bytes 18874368 | tf_op jit(solution)/shard_map/all_gather | solution.py:168
  82.5 225.9 %all-gather.9.cloned.1.call-start = ((), (), s32[]{:S(2)}) async-start(), calls=%async_computation.6 | async-start | bytes 9437184 | tf_op jit(solution)/shard_map/all_gather | solution.py:168
  82.6 49.5 %collective-permute-start.9 = (bf16[256,2048]{1,0:T(8,128)(2,1)S(1)}, bf16[256,2048]{1,0:T(8,128)(2,1)}, u32[]{:S(2)}, u32[]{:S(2)}) collective-permute-start(bf16[256,2048]{1,0:T(8,128)(2,1)S(1)} %bitcast.65), channel_id=1, source_target_pairs={{2,0},{3,1},{0,2},{1,3},{6,4},{7,5},{4,6},{5,7},{10,8},{11,9},{8,1... | collective-permute-start | bytes 3145736 | tf_op jit(solution)/shard_map/ppermute | solution.py:42
  85.3 57.3 %collective-permute-start.7 = (bf16[256,2048]{1,0:T(8,128)(2,1)S(1)}, bf16[256,2048]{1,0:T(8,128)(2,1)S(1)}, u32[]{:S(2)}, u32[]{:S(2)}) collective-permute-start(bf16[256,2048]{1,0:T(8,128)(2,1)S(1)} %bitcast.66), channel_id=1, source_target_pairs={{1,0},{2,1},{3,2},{5,4},{6,5},{7,6},{9,8},{10,9},{11,10},{13,12},{... | collective-permute-start | bytes 3145736 | tf_op jit(solution)/shard_map/ppermute | solution.py:43
  86.6 56.0 %collective-permute-start.8 = (bf16[256,2048]{1,0:T(8,128)(2,1)S(1)}, bf16[256,2048]{1,0:T(8,128)(2,1)S(1)}, u32[]{:S(2)}, u32[]{:S(2)}) collective-permute-start(bf16[256,2048]{1,0:T(8,128)(2,1)S(1)} %bitcast.67), channel_id=1, source_target_pairs={{0,1},{1,2},{2,3},{4,5},{5,6},{6,7},{8,9},{9,10},{10,11},{12,13},{... | collective-permute-start | bytes 3145736 | tf_op jit(solution)/shard_map/ppermute | solution.py:44
  180.2 128.1 %all-gather.11.cloned.1.call-start = ((), (), s32[]{:S(2)}) async-start(), calls=%async_computation.7 | async-start | bytes 9437184 | tf_op jit(solution)/shard_map/all_gather | solution.py:168
  216.3 417.6 %reduce-scatter.4.cloned.1.call-start = ((), (), s32[]{:S(2)}) async-start(), calls=%async_computation.8 | async-start | bytes 9437184 | tf_op jit(solution)/shard_map/reduce_scatter | solution.py:172
  216.4 49.6 %collective-permute-start.20 = (bf16[1024,512]{1,0:T(8,128)(2,1)S(1)}, bf16[1024,512]{1,0:T(8,128)(2,1)S(1)}, u32[]{:S(2)}, u32[]{:S(2)}) collective-permute-start(bf16[1024,512]{1,0:T(8,128)(2,1)S(1)} %copy-done.8), channel_id=1, source_target_pairs={{2,0},{3,1},{0,2},{1,3},{6,4},{7,5},{4,6},{5,7},{10,8},{11,9},{8,1... | collective-permute-start | bytes 3145736 | tf_op jit(solution)/shard_map/ppermute | solution.py:42
  218.4 48.8 %collective-permute-start.23 = (bf16[1024,512]{1,0:T(8,128)(2,1)S(1)}, bf16[1024,512]{1,0:T(8,128)(2,1)S(1)}, u32[]{:S(2)}, u32[]{:S(2)}) collective-permute-start(bf16[1024,512]{1,0:T(8,128)(2,1)S(1)} %copy-done.8), channel_id=1, source_target_pairs={{0,1},{1,2},{2,3},{4,5},{5,6},{6,7},{8,9},{9,10},{10,11},{12,13},{... | collective-permute-start | bytes 3145736 | tf_op jit(solution)/shard_map/ppermute | solution.py:44
  221.6 45.7 %collective-permute-start.22 = (bf16[1024,512]{1,0:T(8,128)(2,1)S(1)}, bf16[1024,512]{1,0:T(8,128)(2,1)S(1)}, u32[]{:S(2)}, u32[]{:S(2)}) collective-permute-start(bf16[1024,512]{1,0:T(8,128)(2,1)S(1)} %copy-done.8), channel_id=1, source_target_pairs={{1,0},{2,1},{3,2},{5,4},{6,5},{7,6},{9,8},{10,9},{11,10},{13,12},{... | collective-permute-start | bytes 3145736 | tf_op jit(solution)/shard_map/ppermute | solution.py:43
  323.7 27.6 %collective-permute-start.24 = (bf16[256,2048]{1,0:T(8,128)(2,1)}, bf16[256,2048]{1,0:T(8,128)(2,1)S(1)}, u32[]{:S(2)}, u32[]{:S(2)}) collective-permute-start(bf16[256,2048]{1,0:T(8,128)(2,1)} %get-tuple-element.267), channel_id=1, source_target_pairs={{0,2},{3,1},{4,6},{7,5},{8,10},{11,9},{12,14},{15,13},{16,18},{19,... | collective-permute-start | bytes 3145736 | tf_op jit(solution)/shard_map/ppermute | solution.py:882
  356.2 42.4 %collective-permute-start.27 = (bf16[256,2048]{1,0:T(8,128)(2,1)}, bf16[256,2048]{1,0:T(8,128)(2,1)S(1)}, u32[]{:S(2)}, u32[]{:S(2)}) collective-permute-start(bf16[256,2048]{1,0:T(8,128)(2,1)} %get-tuple-element.276), channel_id=1, source_target_pairs={{0,1},{1,2},{2,3},{4,5},{5,6},{6,7},{8,9},{9,10},{10,11},{12,13},{... | collective-permute-start | bytes 3145736 | tf_op jit(solution)/shard_map/ppermute | solution.py:59
  407.3 47.2 %collective-permute-start.29 = (bf16[256,2048]{1,0:T(8,128)(2,1)}, bf16[256,2048]{1,0:T(8,128)(2,1)S(1)}, u32[]{:S(2)}, u32[]{:S(2)}) collective-permute-start(bf16[256,2048]{1,0:T(8,128)(2,1)} %get-tuple-element.299.refs_0_.refs_3_), channel_id=1, source_target_pairs={{2,0},{3,1},{0,2},{1,3},{6,4},{7,5},{4,6},{5,7},{10,8},{11,9},{8,1... | collective-permute-start | bytes 3145736 | tf_op jit(solution)/shard_map/ppermute | solution.py:42
  407.3 64.6 %collective-permute-start.32 = (bf16[256,2048]{1,0:T(8,128)(2,1)}, bf16[256,2048]{1,0:T(8,128)(2,1)}, u32[]{:S(2)}, u32[]{:S(2)}) collective-permute-start(bf16[256,2048]{1,0:T(8,128)(2,1)} %get-tuple-element.299.refs_0_.refs_3_), channel_id=1, source_target_pairs={{0,1},{1,2},{2,3},{4,5},{5,6},{6,7},{8,9},{9,10},{10,11},{12,13},{... | collective-permute-start | bytes 3145736 | tf_op jit(solution)/shard_map/ppermute | solution.py:44
  415.0 56.9 %collective-permute-start.31 = (bf16[256,2048]{1,0:T(8,128)(2,1)}, bf16[256,2048]{1,0:T(8,128)(2,1)}, u32[]{:S(2)}, u32[]{:S(2)}) collective-permute-start(bf16[256,2048]{1,0:T(8,128)(2,1)} %get-tuple-element.299.refs_0_.refs_3_), channel_id=1, source_target_pairs={{1,0},{2,1},{3,2},{5,4},{6,5},{7,6},{9,8},{10,9},{11,10},{13,12},{... | collective-permute-start | bytes 3145736 | tf_op jit(solution)/shard_map/ppermute | solution.py:43
  510.6 43.6 %collective-permute-start.36 = (bf16[256,2048]{1,0:T(8,128)(2,1)}, bf16[256,2048]{1,0:T(8,128)(2,1)}, u32[]{:S(2)}, u32[]{:S(2)}) collective-permute-start(bf16[256,2048]{1,0:T(8,128)(2,1)} %get-tuple-element.302), channel_id=1, source_target_pairs={{0,1},{1,2},{2,3},{4,5},{5,6},{6,7},{8,9},{9,10},{10,11},{12,13},{... | collective-permute-start | bytes 3145736 | tf_op jit(solution)/shard_map/ppermute | solution.py:59
  512.9 41.3 %collective-permute-start.37 = (bf16[256,2048]{1,0:T(8,128)(2,1)}, bf16[256,2048]{1,0:T(8,128)(2,1)}, u32[]{:S(2)}, u32[]{:S(2)}) collective-permute-start(bf16[256,2048]{1,0:T(8,128)(2,1)} %get-tuple-element.303), channel_id=1, source_target_pairs={{1,0},{2,1},{3,2},{5,4},{6,5},{7,6},{9,8},{10,9},{11,10},{13,12},{... | collective-permute-start | bytes 3145736 | tf_op jit(solution)/shard_map/ppermute | solution.py:60
  536.2 193.2 %reduce-scatter.8.cloned.1.call-start = ((), (), s32[]{:S(2)}) async-start(), calls=%async_computation.10 | async-start | bytes 18874368 | tf_op jit(solution)/shard_map/reduce_scatter | solution.py:172
  574.9 29.5 %collective-permute-start.38 = (bf16[256,512]{1,0:T(8,128)(2,1)}, bf16[256,512]{1,0:T(8,128)(2,1)S(1)}, u32[]{:S(2)}, u32[]{:S(2)}) collective-permute-start(bf16[256,512]{1,0:T(8,128)(2,1)} %get-tuple-element.306), channel_id=1, source_target_pairs={{0,3},{1,0},{2,1},{3,2},{4,7},{5,4},{6,5},{7,6},{8,11},{9,8},{10,9... | collective-permute-start | bytes 786440 | tf_op jit(solution)/shard_map/ppermute | solution.py:924
  574.9 29.5 %collective-permute-start.39 = (bf16[256,512]{1,0:T(8,128)(2,1)}, bf16[256,512]{1,0:T(8,128)(2,1)S(1)}, u32[]{:S(2)}, u32[]{:S(2)}) collective-permute-start(bf16[256,512]{1,0:T(8,128)(2,1)} %get-tuple-element.307), channel_id=1, source_target_pairs={{0,2},{1,3},{2,0},{3,1},{4,6},{5,7},{6,4},{7,5},{8,10},{9,11},{10,... | collective-permute-start | bytes 786440 | tf_op jit(solution)/shard_map/ppermute | solution.py:924
  574.9 29.4 %collective-permute-start.40 = (bf16[256,512]{1,0:T(8,128)(2,1)}, bf16[256,512]{1,0:T(8,128)(2,1)S(1)}, u32[]{:S(2)}, u32[]{:S(2)}) collective-permute-start(bf16[256,512]{1,0:T(8,128)(2,1)} %get-tuple-element.308), channel_id=1, source_target_pairs={{0,1},{1,2},{2,3},{3,0},{4,5},{5,6},{6,7},{7,4},{8,9},{9,10},{10,1... | collective-permute-start | bytes 786440 | tf_op jit(solution)/shard_map/ppermute | solution.py:924
  605.2 199.9 %reduce-scatter.6.cloned.1.call-start = ((), (), s32[]{:S(2)}) async-start(), calls=%async_computation.9 | async-start | bytes 9437184 | tf_op jit(solution)/shard_map/reduce_scatter | solution.py:172
  606.7 29.5 %collective-permute-start.41 = (bf16[256,512]{1,0:T(8,128)(2,1)S(1)}, bf16[256,512]{1,0:T(8,128)(2,1)S(1)}, u32[]{:S(2)}, u32[]{:S(2)}) collective-permute-start(bf16[256,512]{1,0:T(8,128)(2,1)S(1)} %get-tuple-element.413), channel_id=1, source_target_pairs={{0,3},{1,0},{2,1},{3,2},{4,7},{5,4},{6,5},{7,6},{8,11},{9,8},{10,9... | collective-permute-start | bytes 786440 | tf_op jit(solution)/shard_map/ppermute | solution.py:794
  672.5 30.6 %collective-permute-start.50 = (bf16[256,2048]{1,0:T(8,128)(2,1)}, bf16[256,2048]{1,0:T(8,128)(2,1)S(1)}, u32[]{:S(2)}, u32[]{:S(2)}) collective-permute-start(bf16[256,2048]{1,0:T(8,128)(2,1)} %get-tuple-element.342), channel_id=1, source_target_pairs={{0,1},{3,2},{4,5},{7,6},{8,9},{11,10},{12,13},{15,14},{16,17},{19,... | collective-permute-start | bytes 3145736 | tf_op jit(solution)/shard_map/ppermute | solution.py:57
  676.3 55.9 %collective-permute-start.51 = (bf16[256,2048]{1,0:T(8,128)(2,1)}, bf16[256,2048]{1,0:T(8,128)(2,1)}, u32[]{:S(2)}, u32[]{:S(2)}) collective-permute-start(bf16[256,2048]{1,0:T(8,128)(2,1)} %get-tuple-element.351), channel_id=1, source_target_pairs={{0,1},{1,2},{2,3},{4,5},{5,6},{6,7},{8,9},{9,10},{10,11},{12,13},{... | collective-permute-start | bytes 3145736 | tf_op jit(solution)/shard_map/ppermute | solution.py:59
  678.6 57.5 %collective-permute-start.52 = (bf16[256,2048]{1,0:T(8,128)(2,1)}, bf16[256,2048]{1,0:T(8,128)(2,1)}, u32[]{:S(2)}, u32[]{:S(2)}) collective-permute-start(bf16[256,2048]{1,0:T(8,128)(2,1)} %get-tuple-element.354), channel_id=1, source_target_pairs={{1,0},{2,1},{3,2},{5,4},{6,5},{7,6},{9,8},{10,9},{11,10},{13,12},{... | collective-permute-start | bytes 3145736 | tf_op jit(solution)/shard_map/ppermute | solution.py:60
  679.9 57.6 %collective-permute-start.53 = (bf16[256,2048]{1,0:T(8,128)(2,1)}, bf16[256,2048]{1,0:T(8,128)(2,1)}, u32[]{:S(2)}, u32[]{:S(2)}) collective-permute-start(bf16[256,2048]{1,0:T(8,128)(2,1)} %get-tuple-element.355), channel_id=1, source_target_pairs={{0,2},{3,1},{4,6},{7,5},{8,10},{11,9},{12,14},{15,13},{16,18},{19,... | collective-permute-start | bytes 3145736 | tf_op jit(solution)/shard_map/ppermute | solution.py:948
  703.5 62.6 %collective-permute-start.54 = (bf16[256,2048]{1,0:T(8,128)(2,1)S(1)}, bf16[256,2048]{1,0:T(8,128)(2,1)S(1)}, u32[]{:S(2)}, u32[]{:S(2)}) collective-permute-start(bf16[256,2048]{1,0:T(8,128)(2,1)S(1)} %add_convert_fusion), channel_id=1, source_target_pairs={{1,3},{2,0},{5,7},{6,4},{9,11},{10,8},{13,15},{14,12},{17,19},{18,... | collective-permute-start | bytes 3145736 | tf_op jit(solution)/shard_map/ppermute | solution.py:66
  732.2 72.9 %collective-permute-start.55 = (bf16[64,4096]{1,0:T(8,128)(2,1)}, bf16[64,4096]{1,0:T(8,128)(2,1)}, u32[]{:S(2)}, u32[]{:S(2)}) collective-permute-start(bf16[64,4096]{1,0:T(8,128)(2,1)} %get-tuple-element.361), channel_id=1, source_target_pairs={{0,1},{1,2},{2,3},{3,0},{4,5},{5,6},{6,7},{7,4},{8,9},{9,10},{10,1... | collective-permute-start | bytes 1572872 | tf_op jit(solution)/shard_map/ppermute | solution.py:129
  733.7 71.4 %collective-permute-start.56 = (bf16[64,4096]{1,0:T(8,128)(2,1)}, bf16[64,4096]{1,0:T(8,128)(2,1)}, u32[]{:S(2)}, u32[]{:S(2)}) collective-permute-start(bf16[64,4096]{1,0:T(8,128)(2,1)} %get-tuple-element.362), channel_id=1, source_target_pairs={{0,2},{1,3},{2,0},{3,1},{4,6},{5,7},{6,4},{7,5},{8,10},{9,11},{10,... | collective-permute-start | bytes 1572872 | tf_op jit(solution)/shard_map/ppermute | solution.py:129
  736.1 69.0 %collective-permute-start.57 = (bf16[64,4096]{1,0:T(8,128)(2,1)}, bf16[64,4096]{1,0:T(8,128)(2,1)}, u32[]{:S(2)}, u32[]{:S(2)}) collective-permute-start(bf16[64,4096]{1,0:T(8,128)(2,1)} %get-tuple-element.363), channel_id=1, source_target_pairs={{0,3},{1,0},{2,1},{3,2},{4,7},{5,4},{6,5},{7,6},{8,11},{9,8},{10,9... | collective-permute-start | bytes 1572872 | tf_op jit(solution)/shard_map/ppermute | solution.py:129
  (96 other events, 1496.2 us)
Sparse Core Ops, SparseCore 0:
  36.0 44.6 all-gather.4
  83.1 92.0 all-gather.6
  180.4 58.2 all-gather.8
  241.0 54.3 all-gather.10
  536.3 73.2 reduce-scatter.3
  613.4 115.8 reduce-scatter.7
  733.2 71.8 reduce-scatter.5

commit v9 on v8

--- a/solution.py
+++ b/solution.py
@@ -916,6 +916,9 @@
         ends, down_grad = fence((ends, down_grad))
         down_rows = scatter_dp(down_grad)
         sent = [scatter_far(far, ends)] + sent
+        gate_up_grad = weight_grad([residual_all], d_both)
+        sent, across, gate_up_grad = fence((sent, across, gate_up_grad))
+        gate_up_rows = scatter_dp(gate_up_grad)
         d_res, d_attn, grad_attn_gain, *d_pieces = residual_back(
             me_ref, own, sent + [across], cot, attn_out, attn_gain, w_first, n
         )
@@ -924,10 +927,7 @@
             d_mixed[n - p] = lax.ppermute(
                 d_pieces[p], "seq", [(i, (i + p) % n) for i in range(n)]
             )
-        residual_all, d_both, _ = fence((residual_all, d_both, d_pieces[0]))
-        gate_up_grad = weight_grad([residual_all], d_both)
-        d_mixed, d_attn, gate_up_grad = fence((d_mixed, d_attn, gate_up_grad))
-        gate_up_rows = scatter_dp(gate_up_grad)
+        d_mixed, d_attn = fence((d_mixed, d_attn))
         d_attn_part = columns_to_parts(d_attn, me, n)
         d_query, d_key, d_v, inner, gain_sums = attend_back(
             me_ref, d_mixed, q_low, k_low, v_low, qkv, factors, q_gain, k_gain, tables, seg, n

time: 852 us -> 859 us (level)
    reduce_scatter x3, waiting for transfers between devices: 33.2 us -> 9.65 us  [scatter_dp(): return lax.psum_scatter(values, 'dp', scatter_dimension=0, tiled=True)]
    ppermute x1, waiting for transfers between devices: 0.01 us -> 17.7 us  [shards(): sent.append(lax.ppermute(far, 'seq', [(0, 2), (3, 1)]))]
    ppermute x3, waiting for transfers between devices: 0.01 us -> 16 us  [shards(): lax.ppermute(d_pieces[p], 'seq', [(i, (i + p) % n) for i in range(n)])]
    ppermute x3, waiting for transfers between devices: 0.01 us -> 16 us  [scatter_start(): before = lax.ppermute(before, 'seq', [(j, i) for i, j in step])]
    ppermute x3, waiting for transfers between devices: 35.7 us -> 20.8 us  [scatter_start(): after = lax.ppermute(after, 'seq', step)]
  transfers between devices with their start and end apart: 73 -> 73, of which waited for: 31 -> 32; matrix products, arithmetic and copies ran while one was open for 3% -> 3% of each run, Pallas kernels for 32% -> 32%
where the time goes in v9:
time: 859 us; the launch traced here: 845 us
  waiting for transfers between devices  337 us (39%)
  Pallas kernels  290 us (34%)
  starting transfers between devices  129 us (15%)
  local copies, waits for them, and re-layouts  31.7 us (4%)
  blocking collectives  26.5 us (3%)
  between operations  15.6 us (2%)
  other arithmetic  14.3 us (2%)
    ppermute x4, waiting for transfers between devices, gather_raw(): far = lax.ppermute(values, 'seq', [(i ^ 2, i) for i in range(count)])  111 us
    pallas_call x3, Pallas kernels, ff_backward(): pl.pallas_call(functools.partial(ff_back_kernel, len(saved), group), grid...  55.8 us
    pallas_call x3, Pallas kernels, ff_forward(): pl.pallas_call(functools.partial(ff_kernel, len(saved)), grid=(ff_part //...  53.8 us
    ppermute x4, waiting for transfers between devices, gather_raw(): ends = lax.ppermute(far, 'seq', [(2, 3), (1, 0)])  51.4 us
    pallas_call x2, Pallas kernels, weight_grad(): pl.pallas_call(lambda *refs: weight_grad_kernel(refs[:-2], *refs[-2:]), g...  42.5 us
    ppermute x3, waiting for transfers between devices, scatter_far(): return lax.ppermute(far, 'seq', [(1, 3), (2, 0)])  36.5 us
    ppermute x18, starting transfers between devices, send_blocks(): lax.ppermute(blocks[p], 'seq', [(i, (i + p) % count) for i in range(count)])  28.5 us
    all_to_all x1, blocking collectives, swap_blocks(): lax.all_to_all(values, 'seq', split_axis=0, concat_axis=0, tiled=True)  26.5 us
  transfers between devices with their start and end apart: 73, of which 32 were waited for; matrix products, arithmetic and copies ran while one was open for 3% of the time, Pallas kernels for 32%

profile of v9, /device:TPU:0, one launch (start us, length us, event | category | flops | bytes accessed | tf_op | source)
XLA Modules:
  0.0 844.7 jit_solution(18321689745359165659)
XLA Ops:
  9.4 26.5 %all_to_all.5 = bf16[4,64,1536]{2,1,0:T(8,128)(2,1)} all-to-all(bf16[4,64,1536]{2,1,0:T(8,128)(2,1)S(1)} %pad_maximum_fusion), channel_id=1, replica_groups=mesh['dp'=8,'seq'=4] {'seq'}, dimensions={0} | all-to-all | bytes 1572864 | tf_op jit(solution)/shard_map/all_to_all | solution.py:99
  69.0 8.6 %collective-permute-done.5 = bf16[64,2048]{1,0:T(8,128)(2,1)S(1)} collective-permute-done((bf16[64,2048]{1,0:T(8,128)(2,1)S(1)}, bf16[64,2048]{1,0:T(8,128)(2,1)S(1)}, u32[]{:S(2)}, u32[]{:S(2)}) %collective-permute-start.5) | collective-permute-done | bytes 262176 | tf_op jit(solution)/shard_map/ppermute | solution.py:129
  92.1 40.0 %collective-permute-done.9.refs_1_ = bf16[256,2048]{1,0:T(8,128)(2,1)} collective-permute-done((bf16[256,2048]{1,0:T(8,128)(2,1)S(1)}, bf16[256,2048]{1,0:T(8,128)(2,1)}, u32[]{:S(2)}, u32[]{:S(2)}) %collective-permute-start.9) | collective-permute-done | bytes 1048608 | tf_op jit(solution)/shard_map/ppermute | solution.py:42
  133.5 9.1 %qkv_project.2 = (bf16[1024,2048]{1,0:T(8,128)(2,1)}, f32[1024,1536]{1,0:T(8,128)}, f32[4,8,256]{2,1,0:T(8,128)}) custom-call(s32[1]{0:T(128)} %bitcast.9.me_ref.refs_0_, bf16[256,2048]{1,0:T(8,128)(2,1)} %bitcast.64, bf16[256,2048]{1,0:T(8,128)(2,1)} %collective-permute-done.9.refs_1_, bf16[2048,1536]{1,0:T(8,128)(2,1)} %all-gather.5.cloned.1.call-done.refs_2_.refs_3_.w_ref), custom_call_target="tpu_custom_call" | custom-call | tf_op jit(solution)/shard_map/qkv_project/pallas_call | solution.py:602
  142.6 15.2 %collective-permute-done.10.refs_2_ = bf16[256,2048]{1,0:T(8,128)(2,1)} collective-permute-done((bf16[256,2048]{1,0:T(8,128)(2,1)}, bf16[256,2048]{1,0:T(8,128)(2,1)}, u32[]{:S(2)}, u32[]{:S(2)}) %collective-permute-start.10) | collective-permute-done | bytes 1048608 | tf_op jit(solution)/shard_map/ppermute | solution.py:45
  163.1 9.4 %qkv_project.3 = (bf16[1024,2048]{1,0:T(8,128)(2,1)}, f32[1024,1536]{1,0:T(8,128)}, f32[4,8,256]{2,1,0:T(8,128)}) custom-call(s32[1]{0:T(128)} %bitcast.9.me_ref.refs_0_, bf16[256,2048]{1,0:T(8,128)(2,1)} %copy-done.13, bf16[256,2048]{1,0:T(8,128)(2,1)} %copy-done.15, ...), custom_call_target="tpu_custom_call", output_to_operand_aliasing={{0}: (5, {}), {1}: (6, {}), {2}: (7, {})} | custom-call | tf_op jit(solution)/shard_map/qkv_project/pallas_call | solution.py:602
  198.9 16.1 %attend.1 = (bf16[1024,512]{1,0:T(8,128)(2,1)}, bf16[1024,512]{1,0:T(8,128)(2,1)}, bf16[1024,512]{1,0:T(8,128)(2,1)}, bf16[1024,512]{1,0:T(8,128)(2,1)}) custom-call(s32[1]{0:T(128)} %bitcast.9.me_ref.refs_0_, f32[1024,1536]{1,0:T(8,128)} %get-tuple-element.221.q_ref.k_ref.v_ref.refs_7_.refs_8_.qp_ref.kp_ref, ...), custom_call_target="tpu_custom_call" | custom-call | tf_op jit(solution)/shard_map/attend/pallas_call | solution.py:300
  223.0 43.0 %collective-permute-done.20.refs_3_.refs_2_ = bf16[1024,512]{1,0:T(8,128)(2,1)S(1)} collective-permute-done((bf16[1024,512]{1,0:T(8,128)(2,1)S(1)}, bf16[1024,512]{1,0:T(8,128)(2,1)S(1)}, u32[]{:S(2)}, u32[]{:S(2)}) %collective-permute-start.20) | collective-permute-done | bytes 1048608 | tf_op jit(solution)/shard_map/ppermute | solution.py:42
  267.3 22.2 %collective-permute-done.21 = bf16[1024,512]{1,0:T(8,128)(2,1)S(1)} collective-permute-done((bf16[1024,512]{1,0:T(8,128)(2,1)S(1)}, bf16[1024,512]{1,0:T(8,128)(2,1)S(1)}, u32[]{:S(2)}, u32[]{:S(2)}) %collective-permute-start.21) | collective-permute-done | bytes 1048608 | tf_op jit(solution)/shard_map/ppermute | solution.py:45
  290.9 17.5 %out_project.1 = (bf16[1024,2048]{1,0:T(8,128)(2,1)}, f32[256,2048]{1,0:T(8,128)}) custom-call(s32[1]{0:T(128)} %bitcast.9.me_ref.refs_0_, bf16[1024,512]{1,0:T(8,128)(2,1)} %get-tuple-element.243.refs_1_.refs_0_, bf16[1024,512]{1,0:T(8,128)(2,1)} %get-tuple-element.422.refs_2_.refs_1_, bf16[1024,512]{1,0:T(8,128)(2,1)} %copy-done.9, ...), custom_call_target="tpu_custom_call" | custom-call | tf_op jit(solution)/shard_map/out_project/pallas_call | solution.py:770
  308.5 15.3 %ff_forward.3 = (f32[1024,2048]{1,0:T(8,128)}, f32[1024,2048]{1,0:T(8,128)}, bf16[1024,2048]{1,0:T(8,128)(2,1)}, bf16[256,2048]{1,0:T(8,128)(2,1)}) custom-call(s32[1]{0:T(128)} %bitcast.9.me_ref.refs_0_, bf16[1024,2048]{1,0:T(8,128)(2,1)} %get-tuple-element.270.h_ref.refs_0_, ...), custom_call_target="tpu_custom_call" | custom-call | tf_op jit(solution)/shard_map/ff_forward/pallas_call | solution.py:697
  328.8 22.6 %ff_forward.4 = (f32[1024,2048]{1,0:T(8,128)}, f32[1024,2048]{1,0:T(8,128)}, bf16[1024,2048]{1,0:T(8,128)(2,1)}, bf16[256,2048]{1,0:T(8,128)(2,1)}, bf16[256,204...) custom-call(s32[1]{0:T(128)} %bitcast.9.me_ref.refs_0_, ...), custom_call_target="tpu_custom_call", output_to_operand_aliasing={{0}: (5, {}), {1}: (6, {}), {2}: (7, {})} | custom-call | tf_op jit(solution)/shard_map/ff_forward/pallas_call | solution.py:697
  360.9 15.8 %ff_forward.5 = (f32[1024,2048]{1,0:T(8,128)}, f32[1024,2048]{1,0:T(8,128)}, bf16[1024,2048]{1,0:T(8,128)(2,1)}, f32[256,2048]{1,0:T(8,128)}) custom-call(s32[1]{0:T(128)} %bitcast.9.me_ref.refs_0_, bf16[1024,2048]{1,0:T(8,128)(2,1)} %get-tuple-element.270.h_ref.refs_0_, ...), custom_call_target="tpu_custom_call", output_to_operand_aliasing={{0}: (5, {}), {1}: (6, {}), {2}: (7, {})} | custom-call | tf_op jit(solution)/shard_map/ff_forward/pallas_call | solution.py:697
  380.9 17.7 %collective-permute-done.27 = bf16[256,2048]{1,0:T(8,128)(2,1)S(1)} collective-permute-done((bf16[256,2048]{1,0:T(8,128)(2,1)}, bf16[256,2048]{1,0:T(8,128)(2,1)S(1)}, u32[]{:S(2)}, u32[]{:S(2)}) %collective-permute-start.27) | collective-permute-done | bytes 1048608 | tf_op jit(solution)/shard_map/ppermute | solution.py:59
  407.4 7.6 collective-permute-start.32
  416.3 16.1 %ff_backward.3 = (bf16[1024,4096]{1,0:T(8,128)(2,1)}, f32[256,2048]{1,0:T(8,128)}) custom-call(s32[1]{0:T(128)} %bitcast.9.me_ref.refs_0_, bf16[256,2048]{1,0:T(8,128)(2,1)} %get-tuple-element.301.refs_0_.refs_3_, bf16[2048,4096]{1,0:T(8,128)(2,1)} %all-gather.7.cloned.1.call-done.refs_5_.wg_ref.refs_1_.refs_2_.w_ref, ...), custom_call_target="tpu_custom_call" | custom-call | flops 99999997952 | tf_op jit(solution)/shard_map/ff_backward/pallas_call | solution.py:724
  432.3 22.2 %collective-permute-done.29.refs_0_.refs_2_ = bf16[256,2048]{1,0:T(8,128)(2,1)S(1)} collective-permute-done((bf16[256,2048]{1,0:T(8,128)(2,1)}, bf16[256,2048]{1,0:T(8,128)(2,1)S(1)}, u32[]{:S(2)}, u32[]{:S(2)}) %collective-permute-start.29) | collective-permute-done | bytes 1048608 | tf_op jit(solution)/shard_map/ppermute | solution.py:42
  456.3 15.8 %ff_backward.4 = (bf16[1024,4096]{1,0:T(8,128)(2,1)}, bf16[256,2048]{1,0:T(8,128)(2,1)}) custom-call(s32[1]{0:T(128)} %bitcast.9.me_ref.refs_0_, bf16[256,2048]{1,0:T(8,128)(2,1)} %copy-done.49, bf16[2048,4096]{1,0:T(8,128)(2,1)} %all-gather.7.cloned.1.call-done.refs_5_.wg_ref.refs_1_.refs_2_.w_ref, ...), custom_call_target="tpu_custom_call", output_to_operand_aliasing={{0}: (7, {})} | custom-call | flops 99999997952 | tf_op jit(solution)/shard_map/ff_backward/pallas_call | solution.py:724
  483.7 24.0 %ff_backward.5 = (bf16[1024,4096]{1,0:T(8,128)(2,1)}, bf16[256,2048]{1,0:T(8,128)(2,1)}, bf16[256,2048]{1,0:T(8,128)(2,1)}, bf16[256,2048]{1,0:T(8,128)(2,1)}) custom-call(s32[1]{0:T(128)} %bitcast.9.me_ref.refs_0_, bf16[256,2048]{1,0:T(8,128)(2,1)} %get-tuple-element.298.refs_0_, ...), custom_call_target="tpu_custom_call", output_to_operand_aliasing={{0}: (8, {})} | custom-call | flops 99999997952 | tf_op jit(solution)/shard_map/ff_backward/pallas_call | solution.py:724
  510.4 14.4 %weight_grad.2 = bf16[2048,2048]{1,0:T(8,128)(2,1)} custom-call(bf16[256,2048]{1,0:T(8,128)(2,1)} %get-tuple-element.298.refs_0_, bf16[256,2048]{1,0:T(8,128)(2,1)} %get-tuple-element.299.refs_1_, bf16[256,2048]{1,0:T(8,128)(2,1)} %copy-done.49, bf16[256,2048]{1,0:T(8,128)(2,1)} %get-tuple-element.301.refs_0_.refs_3_, ...), custom_call_target="tpu_custom_call" | custom-call | flops 99999997952 | tf_op jit(solution)/shard_map/weight_grad/pallas_call | solution.py:491
  540.1 28.0 %weight_grad.3 = bf16[2048,4096]{1,0:T(8,128)(2,1)} custom-call(bf16[1024,2048]{1,0:T(8,128)(2,1)} %get-tuple-element.270.h_ref.refs_0_, bf16[1024,4096]{1,0:T(8,128)(2,1)} %get-tuple-element.307.refs_1_), custom_call_target="tpu_custom_call" | custom-call | tf_op jit(solution)/shard_map/weight_grad/pallas_call | solution.py:491
  568.1 15.9 %collective-permute-done.37.c_ref = bf16[256,2048]{1,0:T(8,128)(2,1)} collective-permute-done((bf16[256,2048]{1,0:T(8,128)(2,1)}, bf16[256,2048]{1,0:T(8,128)(2,1)}, u32[]{:S(2)}, u32[]{:S(2)}) %collective-permute-start.37) | collective-permute-done | bytes 1048608 | tf_op jit(solution)/shard_map/ppermute | solution.py:60
  585.1 12.6 %residual_back.1 = (f32[256,2048]{1,0:T(8,128)}, bf16[256,2048]{1,0:T(8,128)(2,1)}, f32[8,2048]{1,0:T(8,128)}, bf16[256,512]{1,0:T(8,128)(2,1)}, bf16[256,512]{1...) custom-call(s32[1]{0:T(128)} %bitcast.9.me_ref.refs_0_, f32[256,2048]{1,0:T(8,128)} %get-tuple-element.283.own_ref, ...), custom_call_target="tpu_custom_call" | custom-call | flops 999999995904 | tf_op jit(solution)/shard_map/residual_back/pallas_call | solution.py:381
  599.9 7.6 collective-permute-done.38.refs_1_
  607.5 8.4 collective-permute-done.39.refs_2_
  623.2 23.4 %attend_back.1 = (f32[1024,512]{1,0:T(8,128)}, f32[1024,512]{1,0:T(8,128)}, bf16[1024,512]{1,0:T(8,128)(2,1)}, f32[4,8,256]{2,1,0:T(8,128)}, f32[2,8,512]{2,1,0:T(8,128)}) custom-call(s32[1]{0:T(128)} %bitcast.9.me_ref.refs_0_, bf16[256,512]{1,0:T(8,128)(2,1)} %get-tuple-element.317.refs_0_, bf16[256,512]{1,0:T(8,128)(2,1)} %copy-done.20, ...), custom_call_target="tpu_custom_call" | custom-call | tf_op jit(solution)/shard_map/attend_back/pallas_call | solution.py:323
  662.1 15.9 %input_back.1 = (bf16[1024,1536]{1,0:T(8,128)(2,1)}, bf16[256,2048]{1,0:T(8,128)(2,1)}, bf16[256,2048]{1,0:T(8,128)(2,1)}, bf16[256,2048]{1,0:T(8,128)(2,1)}, bf...) custom-call(s32[1]{0:T(128)} %bitcast.9.me_ref.refs_0_, f32[1024,512]{1,0:T(8,128)} %get-tuple-element.324.q_ref, ...), custom_call_target="tpu_custom_call" | custom-call | tf_op jit(solution)/shard_map/input_back/pallas_call | solution.py:431
  691.9 19.0 %attn_grad.1 = bf16[2048,2048]{1,0:T(8,128)(2,1)} custom-call(s32[1]{0:T(128)} %bitcast.9.me_ref.refs_0_, bf16[1024,2048]{1,0:T(8,128)(2,1)} %get-tuple-element.252.refs_6_.x_ref, bf16[1024,1536]{1,0:T(8,128)(2,1)} %get-tuple-element.347.d_ref, bf16[1024,512]{1,0:T(8,128)(2,1)} %get-tuple-element.243.refs_1_.refs_0_, ...), custom_call_target="tpu_custom_call" | custom-call | flops 99999997952 | tf_op jit(solution)/shard_map/attn_grad/pallas_call | solution.py:527
  714.8 9.6 %reduce-scatter.8.cloned.1.call-done = bf16[256,4096]{1,0:T(8,128)(2,1)} async-done(((bf16[2048,4096]{1,0:T(8,128)(2,1)}), bf16[256,4096]{1,0:T(8,128)(2,1)}) %reduce-scatter.8.cloned.1.call-update) | async-done | bytes 2097168 | tf_op jit(solution)/shard_map/reduce_scatter | solution.py:172
  735.2 17.7 %collective-permute-done.53.refs_4_ = bf16[256,2048]{1,0:T(8,128)(2,1)} collective-permute-done((bf16[256,2048]{1,0:T(8,128)(2,1)}, bf16[256,2048]{1,0:T(8,128)(2,1)}, u32[]{:S(2)}, u32[]{:S(2)}) %collective-permute-start.53) | collective-permute-done | bytes 1048608 | tf_op jit(solution)/shard_map/ppermute | solution.py:948
  752.9 32.3 %collective-permute-done.54.refs_5_ = bf16[256,2048]{1,0:T(8,128)(2,1)S(1)} collective-permute-done((bf16[256,2048]{1,0:T(8,128)(2,1)S(1)}, bf16[256,2048]{1,0:T(8,128)(2,1)S(1)}, u32[]{:S(2)}, u32[]{:S(2)}) %collective-permute-start.54) | collective-permute-done | bytes 1048608 | tf_op jit(solution)/shard_map/ppermute | solution.py:66
  825.6 8.3 collective-permute-done.64.refs_2_
  (329 shorter events, 251.2 us)
Async XLA Ops:
  7.2 126.3 %all-gather.5.cloned.1.call-start = ((), (), s32[]{:S(2)}) async-start(), calls=%async_computation.4 | async-start | bytes 7077888 | tf_op jit(solution)/shard_map/all_gather | solution.py:168
  35.9 255.1 %all-gather.7.cloned.1.call-start = ((), (), s32[]{:S(2)}) async-start(), calls=%async_computation.5 | async-start | bytes 18874368 | tf_op jit(solution)/shard_map/all_gather | solution.py:168
  82.5 225.9 %all-gather.9.cloned.1.call-start = ((), (), s32[]{:S(2)}) async-start(), calls=%async_computation.6 | async-start | bytes 9437184 | tf_op jit(solution)/shard_map/all_gather | solution.py:168
  82.6 49.5 %collective-permute-start.9 = (bf16[256,2048]{1,0:T(8,128)(2,1)S(1)}, bf16[256,2048]{1,0:T(8,128)(2,1)}, u32[]{:S(2)}, u32[]{:S(2)}) collective-permute-start(bf16[256,2048]{1,0:T(8,128)(2,1)S(1)} %bitcast.65), channel_id=1, source_target_pairs={{2,0},{3,1},{0,2},{1,3},{6,4},{7,5},{4,6},{5,7},{10,8},{11,9},{8,1... | collective-permute-start | bytes 3145736 | tf_op jit(solution)/shard_map/ppermute | solution.py:42
  85.3 57.3 %collective-permute-start.7 = (bf16[256,2048]{1,0:T(8,128)(2,1)S(1)}, bf16[256,2048]{1,0:T(8,128)(2,1)S(1)}, u32[]{:S(2)}, u32[]{:S(2)}) collective-permute-start(bf16[256,2048]{1,0:T(8,128)(2,1)S(1)} %bitcast.66), channel_id=1, source_target_pairs={{1,0},{2,1},{3,2},{5,4},{6,5},{7,6},{9,8},{10,9},{11,10},{13,12},{... | collective-permute-start | bytes 3145736 | tf_op jit(solution)/shard_map/ppermute | solution.py:43
  86.6 56.0 %collective-permute-start.8 = (bf16[256,2048]{1,0:T(8,128)(2,1)S(1)}, bf16[256,2048]{1,0:T(8,128)(2,1)S(1)}, u32[]{:S(2)}, u32[]{:S(2)}) collective-permute-start(bf16[256,2048]{1,0:T(8,128)(2,1)S(1)} %bitcast.67), channel_id=1, source_target_pairs={{0,1},{1,2},{2,3},{4,5},{5,6},{6,7},{8,9},{9,10},{10,11},{12,13},{... | collective-permute-start | bytes 3145736 | tf_op jit(solution)/shard_map/ppermute | solution.py:44
  180.3 128.1 %all-gather.11.cloned.1.call-start = ((), (), s32[]{:S(2)}) async-start(), calls=%async_computation.7 | async-start | bytes 9437184 | tf_op jit(solution)/shard_map/all_gather | solution.py:168
  216.3 430.3 %reduce-scatter.4.cloned.1.call-start = ((), (), s32[]{:S(2)}) async-start(), calls=%async_computation.8 | async-start | bytes 9437184 | tf_op jit(solution)/shard_map/reduce_scatter | solution.py:172
  216.4 49.6 %collective-permute-start.20 = (bf16[1024,512]{1,0:T(8,128)(2,1)S(1)}, bf16[1024,512]{1,0:T(8,128)(2,1)S(1)}, u32[]{:S(2)}, u32[]{:S(2)}) collective-permute-start(bf16[1024,512]{1,0:T(8,128)(2,1)S(1)} %copy-done.8), channel_id=1, source_target_pairs={{2,0},{3,1},{0,2},{1,3},{6,4},{7,5},{4,6},{5,7},{10,8},{11,9},{8,1... | collective-permute-start | bytes 3145736 | tf_op jit(solution)/shard_map/ppermute | solution.py:42
  218.4 48.8 %collective-permute-start.23 = (bf16[1024,512]{1,0:T(8,128)(2,1)S(1)}, bf16[1024,512]{1,0:T(8,128)(2,1)S(1)}, u32[]{:S(2)}, u32[]{:S(2)}) collective-permute-start(bf16[1024,512]{1,0:T(8,128)(2,1)S(1)} %copy-done.8), channel_id=1, source_target_pairs={{0,1},{1,2},{2,3},{4,5},{5,6},{6,7},{8,9},{9,10},{10,11},{12,13},{... | collective-permute-start | bytes 3145736 | tf_op jit(solution)/shard_map/ppermute | solution.py:44
  221.7 45.6 %collective-permute-start.22 = (bf16[1024,512]{1,0:T(8,128)(2,1)S(1)}, bf16[1024,512]{1,0:T(8,128)(2,1)S(1)}, u32[]{:S(2)}, u32[]{:S(2)}) collective-permute-start(bf16[1024,512]{1,0:T(8,128)(2,1)S(1)} %copy-done.8), channel_id=1, source_target_pairs={{1,0},{2,1},{3,2},{5,4},{6,5},{7,6},{9,8},{10,9},{11,10},{13,12},{... | collective-permute-start | bytes 3145736 | tf_op jit(solution)/shard_map/ppermute | solution.py:43
  323.8 27.6 %collective-permute-start.24 = (bf16[256,2048]{1,0:T(8,128)(2,1)}, bf16[256,2048]{1,0:T(8,128)(2,1)S(1)}, u32[]{:S(2)}, u32[]{:S(2)}) collective-permute-start(bf16[256,2048]{1,0:T(8,128)(2,1)} %get-tuple-element.269), channel_id=1, source_target_pairs={{0,2},{3,1},{4,6},{7,5},{8,10},{11,9},{12,14},{15,13},{16,18},{19,... | collective-permute-start | bytes 3145736 | tf_op jit(solution)/shard_map/ppermute | solution.py:882
  356.2 42.4 %collective-permute-start.27 = (bf16[256,2048]{1,0:T(8,128)(2,1)}, bf16[256,2048]{1,0:T(8,128)(2,1)S(1)}, u32[]{:S(2)}, u32[]{:S(2)}) collective-permute-start(bf16[256,2048]{1,0:T(8,128)(2,1)} %get-tuple-element.278), channel_id=1, source_target_pairs={{0,1},{1,2},{2,3},{4,5},{5,6},{6,7},{8,9},{9,10},{10,11},{12,13},{... | collective-permute-start | bytes 3145736 | tf_op jit(solution)/shard_map/ppermute | solution.py:59
  407.4 47.2 %collective-permute-start.29 = (bf16[256,2048]{1,0:T(8,128)(2,1)}, bf16[256,2048]{1,0:T(8,128)(2,1)S(1)}, u32[]{:S(2)}, u32[]{:S(2)}) collective-permute-start(bf16[256,2048]{1,0:T(8,128)(2,1)} %get-tuple-element.301.refs_0_.refs_3_), channel_id=1, source_target_pairs={{2,0},{3,1},{0,2},{1,3},{6,4},{7,5},{4,6},{5,7},{10,8},{11,9},{8,1... | collective-permute-start | bytes 3145736 | tf_op jit(solution)/shard_map/ppermute | solution.py:42
  407.4 64.7 %collective-permute-start.32 = (bf16[256,2048]{1,0:T(8,128)(2,1)}, bf16[256,2048]{1,0:T(8,128)(2,1)}, u32[]{:S(2)}, u32[]{:S(2)}) collective-permute-start(bf16[256,2048]{1,0:T(8,128)(2,1)} %get-tuple-element.301.refs_0_.refs_3_), channel_id=1, source_target_pairs={{0,1},{1,2},{2,3},{4,5},{5,6},{6,7},{8,9},{9,10},{10,11},{12,13},{... | collective-permute-start | bytes 3145736 | tf_op jit(solution)/shard_map/ppermute | solution.py:44
  415.0 57.1 %collective-permute-start.31 = (bf16[256,2048]{1,0:T(8,128)(2,1)}, bf16[256,2048]{1,0:T(8,128)(2,1)}, u32[]{:S(2)}, u32[]{:S(2)}) collective-permute-start(bf16[256,2048]{1,0:T(8,128)(2,1)} %get-tuple-element.301.refs_0_.refs_3_), channel_id=1, source_target_pairs={{1,0},{2,1},{3,2},{5,4},{6,5},{7,6},{9,8},{10,9},{11,10},{13,12},{... | collective-permute-start | bytes 3145736 | tf_op jit(solution)/shard_map/ppermute | solution.py:43
  531.7 192.7 %reduce-scatter.8.cloned.1.call-start = ((), (), s32[]{:S(2)}) async-start(), calls=%async_computation.10 | async-start | bytes 18874368 | tf_op jit(solution)/shard_map/reduce_scatter | solution.py:172
  531.8 36.3 %collective-permute-start.36 = (bf16[256,2048]{1,0:T(8,128)(2,1)}, bf16[256,2048]{1,0:T(8,128)(2,1)}, u32[]{:S(2)}, u32[]{:S(2)}) collective-permute-start(bf16[256,2048]{1,0:T(8,128)(2,1)} %get-tuple-element.304), channel_id=1, source_target_pairs={{0,1},{1,2},{2,3},{4,5},{5,6},{6,7},{8,9},{9,10},{10,11},{12,13},{... | collective-permute-start | bytes 3145736 | tf_op jit(solution)/shard_map/ppermute | solution.py:59
  537.1 47.0 %collective-permute-start.37 = (bf16[256,2048]{1,0:T(8,128)(2,1)}, bf16[256,2048]{1,0:T(8,128)(2,1)}, u32[]{:S(2)}, u32[]{:S(2)}) collective-permute-start(bf16[256,2048]{1,0:T(8,128)(2,1)} %get-tuple-element.305), channel_id=1, source_target_pairs={{1,0},{2,1},{3,2},{5,4},{6,5},{7,6},{9,8},{10,9},{11,10},{13,12},{... | collective-permute-start | bytes 3145736 | tf_op jit(solution)/shard_map/ppermute | solution.py:60
  538.8 45.3 %collective-permute-start.35 = (bf16[256,2048]{1,0:T(8,128)(2,1)S(1)}, bf16[256,2048]{1,0:T(8,128)(2,1)S(1)}, u32[]{:S(2)}, u32[]{:S(2)}) collective-permute-start(bf16[256,2048]{1,0:T(8,128)(2,1)S(1)} %add_convert_fusion.1), channel_id=1, source_target_pairs={{1,3},{2,0},{5,7},{6,4},{9,11},{10,8},{13,15},{14,12},{17,19},{18,... | collective-permute-start | bytes 3145736 | tf_op jit(solution)/shard_map/ppermute | solution.py:66
  585.1 226.8 %reduce-scatter.6.cloned.1.call-start = ((), (), s32[]{:S(2)}) async-start(), calls=%async_computation.9 | async-start | bytes 9437184 | tf_op jit(solution)/shard_map/reduce_scatter | solution.py:172
  618.4 30.3 %collective-permute-start.41 = (bf16[256,512]{1,0:T(8,128)(2,1)S(1)}, bf16[256,512]{1,0:T(8,128)(2,1)S(1)}, u32[]{:S(2)}, u32[]{:S(2)}) collective-permute-start(bf16[256,512]{1,0:T(8,128)(2,1)S(1)} %get-tuple-element.417), channel_id=1, source_target_pairs={{0,3},{1,0},{2,1},{3,2},{4,7},{5,4},{6,5},{7,6},{8,11},{9,8},{10,9... | collective-permute-start | bytes 786440 | tf_op jit(solution)/shard_map/ppermute | solution.py:794
  618.4 30.3 %collective-permute-start.42 = (bf16[256,512]{1,0:T(8,128)(2,1)S(1)}, bf16[256,512]{1,0:T(8,128)(2,1)S(1)}, u32[]{:S(2)}, u32[]{:S(2)}) collective-permute-start(bf16[256,512]{1,0:T(8,128)(2,1)S(1)} %get-tuple-element.416), channel_id=1, source_target_pairs={{0,2},{1,3},{2,0},{3,1},{4,6},{5,7},{6,4},{7,5},{8,10},{9,11},{10,... | collective-permute-start | bytes 786440 | tf_op jit(solution)/shard_map/ppermute | solution.py:794
  621.2 27.5 %collective-permute-start.43 = (bf16[256,512]{1,0:T(8,128)(2,1)S(1)}, bf16[256,512]{1,0:T(8,128)(2,1)S(1)}, u32[]{:S(2)}, u32[]{:S(2)}) collective-permute-start(bf16[256,512]{1,0:T(8,128)(2,1)S(1)} %get-tuple-element.415), channel_id=1, source_target_pairs={{0,1},{1,2},{2,3},{3,0},{4,5},{5,6},{6,7},{7,4},{8,9},{9,10},{10,1... | collective-permute-start | bytes 786440 | tf_op jit(solution)/shard_map/ppermute | solution.py:794
  678.9 32.0 %collective-permute-start.50 = (bf16[256,2048]{1,0:T(8,128)(2,1)}, bf16[256,2048]{1,0:T(8,128)(2,1)S(1)}, u32[]{:S(2)}, u32[]{:S(2)}) collective-permute-start(bf16[256,2048]{1,0:T(8,128)(2,1)} %get-tuple-element.346), channel_id=1, source_target_pairs={{0,1},{3,2},{4,5},{7,6},{8,9},{11,10},{12,13},{15,14},{16,17},{19,... | collective-permute-start | bytes 3145736 | tf_op jit(solution)/shard_map/ppermute | solution.py:57
  684.1 46.3 %collective-permute-start.51 = (bf16[256,2048]{1,0:T(8,128)(2,1)}, bf16[256,2048]{1,0:T(8,128)(2,1)}, u32[]{:S(2)}, u32[]{:S(2)}) collective-permute-start(bf16[256,2048]{1,0:T(8,128)(2,1)} %get-tuple-element.355), channel_id=1, source_target_pairs={{0,1},{1,2},{2,3},{4,5},{5,6},{6,7},{8,9},{9,10},{10,11},{12,13},{... | collective-permute-start | bytes 3145736 | tf_op jit(solution)/shard_map/ppermute | solution.py:59
  686.4 46.4 %collective-permute-start.52 = (bf16[256,2048]{1,0:T(8,128)(2,1)}, bf16[256,2048]{1,0:T(8,128)(2,1)}, u32[]{:S(2)}, u32[]{:S(2)}) collective-permute-start(bf16[256,2048]{1,0:T(8,128)(2,1)} %get-tuple-element.358), channel_id=1, source_target_pairs={{1,0},{2,1},{3,2},{5,4},{6,5},{7,6},{9,8},{10,9},{11,10},{13,12},{... | collective-permute-start | bytes 3145736 | tf_op jit(solution)/shard_map/ppermute | solution.py:60
  687.7 65.2 %collective-permute-start.53 = (bf16[256,2048]{1,0:T(8,128)(2,1)}, bf16[256,2048]{1,0:T(8,128)(2,1)}, u32[]{:S(2)}, u32[]{:S(2)}) collective-permute-start(bf16[256,2048]{1,0:T(8,128)(2,1)} %get-tuple-element.359), channel_id=1, source_target_pairs={{0,2},{3,1},{4,6},{7,5},{8,10},{11,9},{12,14},{15,13},{16,18},{19,... | collective-permute-start | bytes 3145736 | tf_op jit(solution)/shard_map/ppermute | solution.py:948
  711.4 73.8 %collective-permute-start.54 = (bf16[256,2048]{1,0:T(8,128)(2,1)S(1)}, bf16[256,2048]{1,0:T(8,128)(2,1)S(1)}, u32[]{:S(2)}, u32[]{:S(2)}) collective-permute-start(bf16[256,2048]{1,0:T(8,128)(2,1)S(1)} %add_convert_fusion), channel_id=1, source_target_pairs={{1,3},{2,0},{5,7},{6,4},{9,11},{10,8},{13,15},{14,12},{17,19},{18,... | collective-permute-start | bytes 3145736 | tf_op jit(solution)/shard_map/ppermute | solution.py:66
  730.4 81.6 %collective-permute-start.55 = (bf16[64,4096]{1,0:T(8,128)(2,1)}, bf16[64,4096]{1,0:T(8,128)(2,1)}, u32[]{:S(2)}, u32[]{:S(2)}) collective-permute-start(bf16[64,4096]{1,0:T(8,128)(2,1)} %get-tuple-element.365), channel_id=1, source_target_pairs={{0,1},{1,2},{2,3},{3,0},{4,5},{5,6},{6,7},{7,4},{8,9},{9,10},{10,1... | collective-permute-start | bytes 1572872 | tf_op jit(solution)/shard_map/ppermute | solution.py:129
  732.8 79.1 %collective-permute-start.56 = (bf16[64,4096]{1,0:T(8,128)(2,1)}, bf16[64,4096]{1,0:T(8,128)(2,1)}, u32[]{:S(2)}, u32[]{:S(2)}) collective-permute-start(bf16[64,4096]{1,0:T(8,128)(2,1)} %get-tuple-element.366), channel_id=1, source_target_pairs={{0,2},{1,3},{2,0},{3,1},{4,6},{5,7},{6,4},{7,5},{8,10},{9,11},{10,... | collective-permute-start | bytes 1572872 | tf_op jit(solution)/shard_map/ppermute | solution.py:129
  732.9 79.1 %collective-permute-start.57 = (bf16[64,4096]{1,0:T(8,128)(2,1)}, bf16[64,4096]{1,0:T(8,128)(2,1)}, u32[]{:S(2)}, u32[]{:S(2)}) collective-permute-start(bf16[64,4096]{1,0:T(8,128)(2,1)} %get-tuple-element.367), channel_id=1, source_target_pairs={{0,3},{1,0},{2,1},{3,2},{4,7},{5,4},{6,5},{7,6},{8,11},{9,8},{10,9... | collective-permute-start | bytes 1572872 | tf_op jit(solution)/shard_map/ppermute | solution.py:129
  (95 other events, 1446.0 us)
Sparse Core Ops, SparseCore 0:
  36.0 44.6 all-gather.4
  83.1 92.0 all-gather.6
  180.4 58.2 all-gather.8
  241.0 54.3 all-gather.10
  531.9 72.6 reduce-scatter.3
  608.4 115.9 reduce-scatter.7
  728.3 72.4 reduce-scatter.5
